TPU v7x, 32 devices: a whole 2x2x4 slice. The times are simulated.
32 devices in a mesh: rep: 4 (over y, x), fsdp: 2 (over core), tm: 4 (over z).
Axes of the slice: x: 2, y: 2, z: 4, core: 2. Of those that a mesh axis runs over, the one named last changes fastest.
Arguments:
- tokens: bfloat16 [8, 2048, 1024], P(('rep', 'fsdp'), 'tm'), may hold values from -6 to 6
- in_weight: float32 [1024, 4384], P('fsdp'), may hold values from -0.1875 to 0.1875
- out_weight: float32 [2048, 1024], P('fsdp'), may hold values from -0.125 to 0.125
- norm_gain: float32 [1024], P('fsdp'), may hold values from 0.5 to 1.5
- conv_weight: float32 [4, 2304], P(None, 'fsdp'), may hold values from -3 to 3
- conv_bias: float32 [2304], P('fsdp'), may hold values from -0.5 to 0.5
- dt_bias: float32 [32], P('fsdp'), may hold values from -1 to 1
- a_log: float32 [32], P('fsdp')
- d_skip: float32 [32], P('fsdp'), may hold values from 0.5 to 1.5
- gate_gain: float32 [2048], P('fsdp'), may hold values from 0.5 to 1.5
- lengths: int32 [8], P(('rep', 'fsdp')), may hold values from 512 to 2048, as said below
- starts: int32 [8], P(('rep', 'fsdp')), may hold values from 0 to 1536, as said below
- cotangent: bfloat16 [8, 2048, 1024], P(('rep', 'fsdp'), 'tm'), may hold values from -6 to 6
Outputs:
- output: bfloat16 [8, 2048, 1024], P(('rep', 'fsdp'), 'tm')
- input_grad: float32 [8, 2048, 1024], P(('rep', 'fsdp'), 'tm')
- grad_in_weight: float32 [1024, 4384], P('fsdp')
- grad_out_weight: float32 [2048, 1024], P('fsdp')
- grad_norm_gain: float32 [1024], P('fsdp')
- grad_conv_weight: float32 [4, 2304], P(None, 'fsdp')
- grad_conv_bias: float32 [2304], P('fsdp')
- grad_dt_bias: float32 [32], P('fsdp')
- grad_a_log: float32 [32], P('fsdp')
- grad_d_skip: float32 [32], P('fsdp')
- grad_gate_gain: float32 [2048], P('fsdp')
Inputs may be any that keep to these rules, and one draw needn't show every extreme that they name: Each row holds one sequence, starts + lengths <= 2048; some row has length 2048 and some other row length 512. starts + lengths <= 2048.
All inputs are finite; a program needn't handle non-finite values.
Results may differ from a plain program's by a relative error of at most 0.015.
The roundings to bfloat16 on the way count: a program that leaves them out, or rounds other values in their place, can miss the bound.
Values may be sent and summed in bfloat16 or wider, within the bound.
No kernel may reach another device: no remote copies, remote signals or barrier semaphores. Data moves between devices by JAX's collectives and lax.ppermute only.
A program may use at most 192 MiB of HBM per device.

v0:
```python
import jax
import jax.numpy as jnp
from jax import lax
from jax.sharding import PartitionSpec as P

H = 32
P_SIZE = 64
N = 128
K = 4
Q = 256
DIN = 2048
CONV = 2304


EPS = 1e-05
HIGHEST = lax.Precision.HIGHEST


def passed_along(shard, axis, by):
    length = lax.axis_size(axis)
    pairs = [(i, i + by) for i in range(length) if 0 <= i + by < length]
    return lax.ppermute(shard, axis, pairs)


def rms_scale(values, gain_row):
    return values * lax.rsqrt(jnp.mean(values * values, axis=-1, keepdims=True) + EPS) * gain_row


def block_terms(carried, inputs_x, steps_dt, rates, in_map, out_map):
    running = jnp.cumsum(steps_dt * rates[None, :], axis=0)
    length_q = inputs_x.shape[0]
    below_diag = (jnp.arange(length_q)[:, None] >= jnp.arange(length_q)[None, :])[:, :, None]
    spread = running[:, None, :] - running[None, :, :]
    decays = jnp.where(below_diag, jnp.exp(jnp.where(below_diag, spread, 0.0)), 0.0)
    scores = jnp.dot(out_map, in_map.T, precision=HIGHEST)
    weights = scores[:, :, None] * decays * steps_dt[None, :, :]
    within = jnp.einsum("ijh,jhp->ihp", weights, inputs_x, precision=HIGHEST)
    carry_term = jnp.exp(running)[:, :, None] * jnp.einsum(
        "in,hpn->ihp", out_map, carried, precision=HIGHEST
    )
    closing = jnp.exp(running[-1:, :] - running) * steps_dt
    fresh_terms = jnp.einsum("jh,jhp,jn->hpn", closing, inputs_x, in_map, precision=HIGHEST)
    new_state = jnp.exp(running[-1])[:, None, None] * carried + fresh_terms
    return (new_state, within + carry_term)


def block_scan(inputs_x, steps_dt, rates, in_map, out_map, carried, block_len):
    num_blocks = inputs_x.shape[0] // block_len
    head_count = inputs_x.shape[1]

    def advance(state_now, pieces):
        return block_terms(state_now, pieces[0], pieces[1], rates, pieces[2], pieces[3])

    final_state, outputs = lax.scan(
        jax.checkpoint(advance),
        carried,
        (
            inputs_x.reshape(num_blocks, block_len, head_count, -1),
            steps_dt.reshape(num_blocks, block_len, head_count),
            in_map.reshape(num_blocks, block_len, -1),
            out_map.reshape(num_blocks, block_len, -1),
        ),
    )
    return (outputs.reshape(inputs_x.shape), final_state)


def body(
    tokens,
    in_weight,
    out_weight,
    norm_gain,
    conv_weight,
    conv_bias,
    dt_bias,
    a_log,
    d_skip,
    gate_gain,
    lengths,
    starts,
    cotangent,
):
    bfloat = jnp.bfloat16
    gathered = (
        lax.all_gather(in_weight.astype(bfloat), "fsdp", axis=0, tiled=True),
        lax.all_gather(out_weight.astype(bfloat), "fsdp", axis=0, tiled=True),
        lax.all_gather(norm_gain.astype(bfloat), "fsdp", axis=0, tiled=True),
        lax.all_gather(conv_weight.astype(bfloat), "fsdp", axis=1, tiled=True),
        lax.all_gather(conv_bias.astype(bfloat), "fsdp", axis=0, tiled=True),
        lax.all_gather(dt_bias.astype(bfloat), "fsdp", axis=0, tiled=True),
        lax.all_gather(a_log.astype(bfloat), "fsdp", axis=0, tiled=True),
        lax.all_gather(d_skip.astype(bfloat), "fsdp", axis=0, tiled=True),
        lax.all_gather(gate_gain.astype(bfloat), "fsdp", axis=0, tiled=True),
    )
    in_low = gathered[0]
    out_low = gathered[1]
    norm_vec = gathered[2].astype(jnp.float32)
    conv_taps = gathered[3].astype(jnp.float32)
    conv_shift = gathered[4].astype(jnp.float32)
    dt_shift = gathered[5].astype(jnp.float32)
    decay_log = gathered[6].astype(jnp.float32)
    skip_vec = gathered[7].astype(jnp.float32)
    gate_vec = gathered[8].astype(jnp.float32)
    tok_count = tokens.shape[1]
    edge_start = tok_count - (K - 1)
    positions = lax.axis_index("tm") * tok_count + jnp.arange(tok_count)
    valid_rows = ((positions >= starts[0]) & (positions < starts[0] + lengths[0])).astype(
        jnp.float32
    )[:, None]
    residual = tokens[0].astype(jnp.float32)
    normed, norm_back = jax.vjp(rms_scale, residual, norm_vec)
    normed_low = normed.astype(bfloat)
    projected = jnp.dot(normed_low, in_low, preferred_element_type=jnp.float32).astype(bfloat)
    conv_input = projected[:, DIN : DIN + CONV] * valid_rows.astype(bfloat)
    earlier_rows = passed_along(conv_input[edge_start:], "tm", 1)

    def mixer_inputs(proj_full, edge_rows, taps, shifts, dt_offset, log_rates):
        gate_z = proj_full[:, :DIN]
        local_rows = proj_full[:, DIN : DIN + CONV] * valid_rows
        padded = jnp.concatenate([edge_rows, local_rows], axis=0)
        mixed = shifts[None, :] + sum(
            (taps[offset][None, :] * padded[offset : offset + tok_count] for offset in range(K))
        )
        active = jax.nn.silu(mixed)
        inputs_x = active[:, :DIN].reshape(tok_count, H, P_SIZE)
        in_map = active[:, DIN : DIN + N]
        out_map = active[:, DIN + N :]
        steps_dt = jax.nn.softplus(proj_full[:, DIN + CONV :] + dt_offset[None, :]) * valid_rows
        rates = -jnp.exp(log_rates)
        return (inputs_x, steps_dt, rates, in_map, out_map, gate_z)

    mixer_vals, mixer_back = jax.vjp(
        mixer_inputs,
        projected.astype(jnp.float32),
        earlier_rows.astype(jnp.float32),
        conv_taps,
        conv_shift,
        dt_shift,
        decay_log,
    )
    inputs_x, steps_dt, rates, in_map, out_map, gate_z = mixer_vals

    def local_scan(inputs_x, steps_dt, rates, in_map, out_map):
        zeros_state = jnp.zeros((H, P_SIZE, N), jnp.float32)
        outputs, final_state = block_scan(
            inputs_x, steps_dt, rates, in_map, out_map, zeros_state, Q
        )
        total_factor = jnp.exp(jnp.sum(steps_dt * rates[None, :], axis=0))
        return (outputs, final_state, total_factor)

    scan_vals, scan_back = jax.vjp(local_scan, inputs_x, steps_dt, rates, in_map, out_map)
    local_y, local_state, total_decay = scan_vals
    decay_col = total_decay[:, None, None]
    state_in = jnp.zeros_like(local_state)
    for rounds in range(lax.axis_size("tm") - 1):
        state_in = passed_along(decay_col * state_in + local_state, "tm", 1)

    def carried_term(steps_dt, rates, out_map, entering):
        running = jnp.cumsum(steps_dt * rates[None, :], axis=0)
        return jnp.exp(running)[:, :, None] * jnp.einsum(
            "in,hpn->ihp", out_map, entering, precision=HIGHEST
        )

    carried_y, carried_back = jax.vjp(carried_term, steps_dt, rates, out_map, state_in)

    def gated_output(mix_y, gate_in, inputs_in, skip_in, gain_in):
        full_y = (mix_y + skip_in[None, :, None] * inputs_in).reshape(tok_count, DIN)
        return rms_scale(full_y * jax.nn.silu(gate_in), gain_in) * valid_rows

    gated, gated_back = jax.vjp(
        gated_output, local_y + carried_y, gate_z, inputs_x, skip_vec, gate_vec
    )
    gated_low = gated.astype(bfloat)
    output = (residual + jnp.dot(gated_low, out_low, preferred_element_type=jnp.float32)).astype(
        bfloat
    )
    upstream = cotangent[0]
    grad_out_w = jnp.dot(gated_low.T, upstream, preferred_element_type=jnp.float32)
    grad_gated = jnp.dot(upstream, out_low.T, preferred_element_type=jnp.float32)
    grad_y, grad_z, grad_x_gate, grad_skip, grad_gate_vec = gated_back(grad_gated)
    grad_dt_c, grad_rates_c, grad_out_c, grad_state = carried_back(grad_y)
    later_grad = jnp.zeros_like(grad_state)
    for rounds in range(lax.axis_size("tm") - 1):
        later_grad = passed_along(grad_state + decay_col * later_grad, "tm", -1)
    grad_factor = jnp.sum(later_grad * state_in, axis=(1, 2))
    grad_x_scan, grad_dt_s, grad_rates_s, grad_in_map, grad_out_s = scan_back(
        (grad_y, later_grad, grad_factor)
    )
    grad_proj, grad_edge, grad_taps, grad_shifts, grad_dt_bias, grad_log = mixer_back(
        (
            grad_x_gate + grad_x_scan,
            grad_dt_c + grad_dt_s,
            grad_rates_c + grad_rates_s,
            grad_in_map,
            grad_out_c + grad_out_s,
            grad_z,
        )
    )
    from_next = passed_along(grad_edge, "tm", -1)
    grad_proj = grad_proj.at[edge_start:, DIN : DIN + CONV].add(from_next * valid_rows[edge_start:])
    grad_proj_low = grad_proj.astype(bfloat)
    grad_in_w = jnp.dot(normed_low.T, grad_proj_low, preferred_element_type=jnp.float32)
    grad_normed = jnp.dot(grad_proj_low, in_low.T, preferred_element_type=jnp.float32)
    grad_input, grad_norm_vec = norm_back(grad_normed)
    grad_tokens = upstream.astype(jnp.float32) + grad_input
    shares = (
        lax.psum_scatter(grad_in_w, "fsdp", scatter_dimension=0, tiled=True),
        lax.psum_scatter(grad_out_w, "fsdp", scatter_dimension=0, tiled=True),
        lax.psum_scatter(grad_norm_vec, "fsdp", scatter_dimension=0, tiled=True),
        lax.psum_scatter(grad_taps, "fsdp", scatter_dimension=1, tiled=True),
        lax.psum_scatter(grad_shifts, "fsdp", scatter_dimension=0, tiled=True),
        lax.psum_scatter(grad_dt_bias, "fsdp", scatter_dimension=0, tiled=True),
        lax.psum_scatter(grad_log, "fsdp", scatter_dimension=0, tiled=True),
        lax.psum_scatter(grad_skip, "fsdp", scatter_dimension=0, tiled=True),
        lax.psum_scatter(grad_gate_vec, "fsdp", scatter_dimension=0, tiled=True),
    )
    totals = lax.psum(
        (
            shares[0],
            shares[1],
            shares[2],
            shares[3],
            shares[4],
            shares[5],
            shares[6],
            shares[7],
            shares[8],
        ),
        ("rep", "tm"),
    )
    return (
        output[None],
        grad_tokens[None],
        totals[0],
        totals[1],
        totals[2],
        totals[3],
        totals[4],
        totals[5],
        totals[6],
        totals[7],
        totals[8],
    )


def solution(mesh):
    return jax.shard_map(
        body,
        mesh=mesh,
        in_specs=(
            P(("rep", "fsdp"), "tm", None),
            P("fsdp", None),
            P("fsdp", None),
            P("fsdp"),
            P(None, "fsdp"),
            P("fsdp"),
            P("fsdp"),
            P("fsdp"),
            P("fsdp"),
            P("fsdp"),
            P(("rep", "fsdp")),
            P(("rep", "fsdp")),
            P(("rep", "fsdp"), "tm", None),
        ),
        out_specs=(
            P(("rep", "fsdp"), "tm", None),
            P(("rep", "fsdp"), "tm", None),
            P("fsdp", None),
            P("fsdp", None),
            P("fsdp"),
            P(None, "fsdp"),
            P("fsdp"),
            P("fsdp"),
            P("fsdp"),
            P("fsdp"),
            P("fsdp"),
        ),
        check_vma=False,
    )
```

profile of v0, /device:TPU:0, one launch (start us, length us, event | category | flops | bytes accessed | tf_op | source)
XLA Modules:
  0.0 1151.7 jit_solution(16543430796936372421)
XLA Ops:
  7.2 6.2 convert_element_type.101
  26.5 11.2 all-gather.5.cloned.1.call-done
  37.6 10.3 fusion.170
  60.4 9.8 fusion.98
  75.2 5.3 copy.282
  80.5 5.9 reshape.395
  86.4 4.8 copy.284
  91.2 133.0 %while.45 = (s32[]{:T(128)}, f32[32,64,128]{2,1,0:T(8,128)S(1)}, f32[2,256,32,64]{1,0,3,2:T(2,128)}, f32[2,32,64,128]{3,2,1,0:T(8,128)}, f32[2,256,32]{1,2,0:T(8...) while((s32[]{:T(128)}, f32[32,64,128]{2,1,0:T(8,128)S(1)}, ...), condition=%wide.region_4.5_spmd.clone.clone, body=%wide.region_1.4_spmd.clone.clone.sunk | while | flops 3336339456 | bytes 26351332 | solution.py:54
  93.9 11.3 fusion.270
  110.3 42.6 %dynamic_update_slice.76 = f32[2,256,32,64]{1,0,3,2:T(2,128)} dynamic-update-slice(f32[2,256,32,64]{1,0,3,2:T(2,128)} %get-tuple-element.1108, f32[1,256,32,64]{1,0,3,2:T(1,128)S(1)} %copy.402, s32[]{:T(128)S(6)} %copy.416, s32[]{:T(128)} %constant.153.clone.1..sunk.1, s32[]{:T(128)} %constant.153.clone.1..sunk.1, s32[]{:T(128)} %constant.153.clone.1..sunk.1) | dynamic-update-slice | bytes 4194308 | tf_op jit(solution)/shard_map/jvp()/while/body/jit(dynamic_update_index_in_dim)/dynamic_update_slice | solution.py:54
  153.9 3.8 fusion.268
  160.3 11.3 fusion.270
  176.7 42.6 %dynamic_update_slice.76 = f32[2,256,32,64]{1,0,3,2:T(2,128)} dynamic-update-slice(f32[2,256,32,64]{1,0,3,2:T(2,128)} %get-tuple-element.1108, f32[1,256,32,64]{1,0,3,2:T(1,128)S(1)} %copy.402, s32[]{:T(128)S(6)} %copy.416, s32[]{:T(128)} %constant.153.clone.1..sunk.1, s32[]{:T(128)} %constant.153.clone.1..sunk.1, s32[]{:T(128)} %constant.153.clone.1..sunk.1) | dynamic-update-slice | bytes 4194308 | tf_op jit(solution)/shard_map/jvp()/while/body/jit(dynamic_update_index_in_dim)/dynamic_update_slice | solution.py:54
  220.3 3.8 fusion.268
  227.8 3.8 convert_element_type.120
  231.7 18.6 %collective-permute-done.1 = f32[32,64,128]{2,1,0:T(8,128)S(1)} collective-permute-done((f32[32,64,128]{2,1,0:T(8,128)S(1)}, f32[32,64,128]{2,1,0:T(8,128)S(1)}, u32[]{:S(2)}, u32[]{:S(2)}) %collective-permute-start.1) | collective-permute-done | bytes 1048608 | tf_op jit(solution)/shard_map/ppermute | solution.py:22
  250.5 4.5 collective-permute-start.2
  254.9 21.7 %collective-permute-done.2 = f32[32,64,128]{2,1,0:T(8,128)S(1)} collective-permute-done((f32[32,64,128]{2,1,0:T(8,128)S(1)}, f32[32,64,128]{2,1,0:T(8,128)S(1)}, u32[]{:S(2)}, u32[]{:S(2)}) %collective-permute-start.2) | collective-permute-done | bytes 1048608 | tf_op jit(solution)/shard_map/ppermute | solution.py:22
  276.8 4.5 collective-permute-start.3
  284.9 6.4 reshape.398
  291.4 10.7 collective-permute-done.3
  302.0 8.7 multiply_add_fusion.1
  310.8 5.4 copy.289
  316.1 6.7 multiply_reduce_fusion.12
  323.0 7.1 multiply_reduce_fusion.8
  330.1 7.5 multiply_reduce_fusion.9
  337.6 5.4 copy.290
  343.1 5.6 broadcast_add_fusion.2
  349.9 23.8 %collective-permute-done.4 = f32[32,64,128]{2,1,0:T(8,128)S(1)} collective-permute-done((f32[32,64,128]{2,1,0:T(8,128)S(1)}, f32[32,64,128]{2,1,0:T(8,128)S(1)}, u32[]{:S(2)}, u32[]{:S(2)}) %collective-permute-start.4) | collective-permute-done | bytes 1048608 | tf_op jit(solution)/shard_map/ppermute | solution.py:22
  377.5 21.4 %collective-permute-done.5 = f32[32,64,128]{2,1,0:T(8,128)S(1)} collective-permute-done((f32[32,64,128]{2,1,0:T(8,128)}, f32[32,64,128]{2,1,0:T(8,128)S(1)}, u32[]{:S(2)}, u32[]{:S(2)}) %collective-permute-start.5) | collective-permute-done | bytes 1048608 | tf_op jit(solution)/shard_map/ppermute | solution.py:22
  401.8 8.1 fusion.129
  410.0 7.8 reshape.457
  417.8 4.6 multiply_reduce_fusion.10
  422.5 5.0 reduce-window.80
  428.6 9.2 copy.295
  442.8 196.5 %while.44 = (s32[]{:T(128)}, f32[32]{0:T(128)}, f32[32,64,128]{2,1,0:T(8,128)S(1)}, f32[2,256,32,64]{1,3,2,0:T(8,128)}, f32[2,256,32]{2,1,0:T(8,128)}, /*index=5...) while((s32[]{:T(128)}, f32[32]{0:T(128)}, ...), condition=%wide.region_27.28_spmd.clone, body=%wide.region_14.27_spmd.clone.sunk | while | flops 7599751168 | bytes 98442416 | solution.py:54
  447.4 4.3 dynamic-slice_bitcast_fusion.13
  462.9 16.1 %fusion.250 = (f32[256,32]{0,1:T(8,128)}, f32[256,32]{0,1:T(8,128)}, f32[256,32]{0,1:T(8,128)}, f32[256,256]{1,0:T(8,128)}) fusion(f32[256,32]{0,1:T(8,128)} %copy.388, f32[256,32]{0,1:T(8,128)} %copy.389, f32[256,256]{1,0:T(8,128)S(1)} %fusion.249, pred[256,256]{1,0:T(8,128)(4,1)} %iota_compare_fusion.3, f32[256,32,64]{0,2,1:T(8,128)} %get-tuple-element.1061, ...), kind=kOutput, calls=%fused_computation.62.clone.1 | convolution fusion | flops 1641979904 | bytes 4947968 | tf_op jit(solution)/shard_map/transpose(jvp())/while/body/eval_jaxpr/checkpoint/ijh,jhp->ihp/dot_general | solution.py:37
  483.5 5.4 multiply_reduce_fusion.20
  495.3 3.8 reduce-window.98
  503.0 5.7 fusion.256
  514.1 4.8 fusion.258
  527.8 7.4 bitcast_dynamic-update-slice_fusion.6
  541.7 4.3 dynamic-slice_bitcast_fusion.13
  557.1 16.1 %fusion.250 = (f32[256,32]{0,1:T(8,128)}, f32[256,32]{0,1:T(8,128)}, f32[256,32]{0,1:T(8,128)}, f32[256,256]{1,0:T(8,128)}) fusion(f32[256,32]{0,1:T(8,128)} %copy.388, f32[256,32]{0,1:T(8,128)} %copy.389, f32[256,256]{1,0:T(8,128)S(1)} %fusion.249, pred[256,256]{1,0:T(8,128)(4,1)} %iota_compare_fusion.3, f32[256,32,64]{0,2,1:T(8,128)} %get-tuple-element.1061, ...), kind=kOutput, calls=%fused_computation.62.clone.1 | convolution fusion | flops 1641979904 | bytes 4947968 | tf_op jit(solution)/shard_map/transpose(jvp())/while/body/eval_jaxpr/checkpoint/ijh,jhp->ihp/dot_general | solution.py:37
  577.7 5.4 multiply_reduce_fusion.20
  589.5 3.8 reduce-window.98
  597.2 5.7 fusion.256
  609.1 4.8 fusion.258
  622.7 7.4 bitcast_dynamic-update-slice_fusion.6
  639.2 9.1 copy.307
  648.3 7.9 reshape.458
  656.3 8.7 fusion.126
  668.3 5.4 multiply_reduce_fusion.6
  673.8 7.3 broadcast_multiply_fusion.1
  690.8 4.0 pad_add_fusion
  700.3 12.4 %fusion.108 = f32[1024,4384]{0,1:T(8,128)} fusion(f32[512,4384]{1,0:T(8,128)} %scatter-add.4, bf16[1,512,1024]{2,1,0:T(8,128)(2,1)S(1)} %copy-done.12, f32[1024]{0:T(1024)S(1)} %bitcast.410, f32[512]{0:T(512)S(1)} %copy-done.50), kind=kOutput, calls=%fused_computation.177 | convolution fusion | flops 4601298944 | bytes 27990016 | tf_op jit(solution)/shard_map/dot_general | solution.py:201
  714.3 27.2 %reduce-scatter.6.cloned.1.call-done = f32[512,4384]{0,1:T(8,128)} async-done(((f32[1024,4384]{0,1:T(8,128)}), f32[512,4384]{0,1:T(8,128)}) %reduce-scatter.6.cloned.1.call-update) | async-done | bytes 8978448 | tf_op jit(solution)/shard_map/reduce_scatter | solution.py:206
  744.3 6.8 fusion.122
  751.1 11.8 %fusion.113 = (f32[1024]{0:T(1024)S(1)}, f32[512]{0:T(512)S(1)}, f32[512,1024]{1,0:T(8,128)}) fusion(bf16[1,512,1024]{2,1,0:T(8,128)(2,1)S(1)} %copy-done.12, f32[512]{0:T(512)S(1)} %copy-done.50, f32[1024]{0:T(1024)S(1)} %bitcast.411, bf16[1024,4384]{0,1:T(8,128)(2,1)} %all-gather.5.cloned.1.call-done, f32[512,4384]{1,0:T(8,128)} %scatter-add.4), kind=kOutput, calls=%fused_computation.182 | convolution fusion | flops 4602870272 | bytes 21114880 | tf_op jit(solution)/shard_map/dot_general | solution.py:202
  766.9 4.0 fusion.115
  772.1 83.3 %all-reduce.25 = (f32[512]{0:T(512)}, f32[4,1152]{1,0:T(4,128)}, f32[1152]{0:T(1024)}, f32[16]{0:T(128)}, f32[16]{0:T(128)}, /*index=5*/f32[16]{0:T(128)}, f32[1024]{0:T(1024)}) all-reduce(f32[512]{0:T(512)S(1)} %dynamic-slice.12, f32[4,1152]{1,0:T(4,128)S(1)} %copy.313, ...), channel_id=1, replica_groups=mesh['rep'=4,'fsdp'=2,'tm'=4] {'rep','tm'}, use_global_device_ids=true, to_apply=%region_35.36 | all-reduce | flops 7344 | bytes 58752 | tf_op jit(solution)/shard_map/psum | solution.py:216
  855.4 278.8 %all-reduce.31.cloned.1.call-done = (f32[512,4384]{0,1:T(8,128)}, f32[1024,1024]{1,0:T(8,128)}) async-done(((f32[512,4384]{0,1:T(8,128)}, f32[1024,1024]{1,0:T(8,128)}), (f32[512,4384]{0,1:T(8,128)}, f32[1024,1024]{1,0:T(8,128)})) %all-reduce.31.cloned.1.call-update) | async-done | bytes 13172752 | tf_op jit(solution)/shard_map/psum | solution.py:216
  1134.2 8.4 copy.457
  (449 shorter events, 188.1 us)
Async XLA Ops:
  7.2 30.5 %all-gather.5.cloned.1.call-start = ((), (), s32[]{:S(2)}) async-start(), calls=%async_computation.3 | async-start | bytes 13467648 | tf_op jit(solution)/shard_map/all_gather | solution.py:84
  13.5 10.6 copy-start.59
  13.5 12.6 %copy-start.11 = (bf16[1,512,1024]{2,1,0:T(8,128)(2,1)S(1)}, bf16[1,512,1024]{2,1,0:T(8,128)(2,1)}, u32[]{:S(2)}) copy-start(bf16[1,512,1024]{2,1,0:T(8,128)(2,1)} %param.19) | copy-start | bytes 3145732
  13.5 309.4 %all-gather.7.cloned.1.call-start = ((), (), s32[]{:S(2)}) async-start(), calls=%async_computation.4 | async-start | bytes 6291456 | tf_op jit(solution)/shard_map/all_gather | solution.py:85
  20.2 37.6 %copy-start.70 = (f32[32]{0:T(128)}, f32[32]{0:T(128)S(1)}, u32[]{:S(2)}) copy-start(f32[32]{0:T(128)S(1)} %convert_element_type.105) | copy-start | bytes 388
  22.2 25.8 %copy-start.33 = (f32[2,1,512]{2,1,0:T(1,128)}, f32[2,1,512]{2,1,0:T(1,128)S(1)}, u32[]{:S(2)}) copy-start(f32[2,1,512]{2,1,0:T(1,128)S(1)} %convert_element_type.125) | copy-start | bytes 12292
  25.9 375.9 %copy-start.39 = (f32[512]{0:T(512)}, f32[512]{0:T(512)S(1)}, u32[]{:S(2)}) copy-start(f32[512]{0:T(512)S(1)} %fusion.150) | copy-start | bytes 6148
  26.1 34.3 %copy-start.41 = (f32[2304]{0:T(1024)}, f32[2304]{0:T(1024)S(1)}, u32[]{:S(2)}) copy-start(f32[2304]{0:T(1024)S(1)} %get-tuple-element.762) | copy-start | bytes 27652
  26.1 34.3 %copy-start.43 = (f32[2304]{0:T(1024)}, f32[2304]{0:T(1024)S(1)}, u32[]{:S(2)}) copy-start(f32[2304]{0:T(1024)S(1)} %get-tuple-element.763) | copy-start | bytes 27652
  26.1 34.3 %copy-start.45 = (f32[2304]{0:T(1024)}, f32[2304]{0:T(1024)S(1)}, u32[]{:S(2)}) copy-start(f32[2304]{0:T(1024)S(1)} %get-tuple-element.764) | copy-start | bytes 27652
  26.1 34.3 %copy-start.47 = (f32[2304]{0:T(1024)}, f32[2304]{0:T(1024)S(1)}, u32[]{:S(2)}) copy-start(f32[2304]{0:T(1024)S(1)} %get-tuple-element.765) | copy-start | bytes 27652
  26.4 21.5 %copy-start.57 = (f32[512]{0:T(512)}, f32[512]{0:T(512)S(1)}, u32[]{:S(2)}) copy-start(f32[512]{0:T(512)S(1)} %fusion.116) | copy-start | bytes 6148
  26.5 21.5 %copy-start.49 = (f32[512]{0:T(512)}, f32[512]{0:T(512)S(1)}, u32[]{:S(2)}) copy-start(f32[512]{0:T(512)S(1)} %fusion.151) | copy-start | bytes 6148
  48.0 9.9 copy-start.8
  51.6 8.7 collective-permute-start
  58.7 11.5 copy-start.72
  60.3 9.9 copy-start.35
  91.2 133.0 %copy-start.74 = (f32[32]{0:T(128)S(1)}, f32[32]{0:T(128)}, u32[]{:S(2)}) copy-start(f32[32]{0:T(128)} %get-tuple-element.876) | copy-start | bytes 388
  91.3 14.0 %copy-start.51 = (pred[256,256]{1,0:T(8,128)(4,1)}, pred[256,256]{1,0:T(8,128)(4,1)S(1)}, u32[]{:S(2)}) copy-start(pred[256,256]{1,0:T(8,128)(4,1)S(1)} %get-tuple-element.1128) | copy-start | bytes 196612 | tf_op jit(solution)/shard_map/jvp()/while
  157.7 14.0 %copy-start.51 = (pred[256,256]{1,0:T(8,128)(4,1)}, pred[256,256]{1,0:T(8,128)(4,1)S(1)}, u32[]{:S(2)}) copy-start(pred[256,256]{1,0:T(8,128)(4,1)S(1)} %get-tuple-element.1128) | copy-start | bytes 196612 | tf_op jit(solution)/shard_map/jvp()/while
  224.3 26.0 %copy-start.64 = (f32[32]{0:T(128)S(1)}, f32[32]{0:T(128)}, u32[]{:S(2)}) copy-start(f32[32]{0:T(128)} %get-tuple-element.875) | copy-start | bytes 388
  224.3 26.0 %collective-permute-start.1 = (f32[32,64,128]{2,1,0:T(8,128)S(1)}, f32[32,64,128]{2,1,0:T(8,128)S(1)}, u32[]{:S(2)}, u32[]{:S(2)}) collective-permute-start(f32[32,64,128]{2,1,0:T(8,128)S(1)} %broadcast_add_fusion.3), channel_id=1, source_target_pairs={{0,1},{1,2},{2,3},{4,5},{5,6},{6,7},{8,9},{9,10},{10,11},{12,13},{... | collective-permute-start | bytes 3145736 | tf_op jit(solution)/shard_map/ppermute | solution.py:22
  231.6 49.6 %copy-start.76 = (bf16[32]{0:T(256)(128)(2,1)S(1)}, bf16[32]{0:T(256)(128)(2,1)}, u32[]{:S(2)}) copy-start(bf16[32]{0:T(256)(128)(2,1)} %get-tuple-element.831) | copy-start | bytes 196
  231.6 49.6 %copy-start.65 = (f32[1024]{0:T(1024)S(1)}, f32[1024]{0:T(1024)}, u32[]{:S(2)}) copy-start(f32[1024]{0:T(1024)} %param.28) | copy-start | bytes 12292
  231.6 482.7 %reduce-scatter.8.cloned.1.call-start = ((), (), s32[]{:S(2)}) async-start(), calls=%async_computation.6 | async-start | bytes 12582912 | tf_op jit(solution)/shard_map/reduce_scatter | solution.py:207
  250.5 26.1 %collective-permute-start.2 = (f32[32,64,128]{2,1,0:T(8,128)S(1)}, f32[32,64,128]{2,1,0:T(8,128)S(1)}, u32[]{:S(2)}, u32[]{:S(2)}) collective-permute-start(f32[32,64,128]{2,1,0:T(8,128)S(1)} %multiply_add_fusion.5), channel_id=1, source_target_pairs={{0,1},{1,2},{2,3},{4,5},{5,6},{6,7},{8,9},{9,10},{10,11},{12,13},{... | collective-permute-start | bytes 3145736 | tf_op jit(solution)/shard_map/ppermute | solution.py:22
  276.8 25.3 %collective-permute-start.3 = (f32[32,64,128]{2,1,0:T(8,128)S(1)}, f32[32,64,128]{2,1,0:T(8,128)S(1)}, u32[]{:S(2)}, u32[]{:S(2)}) collective-permute-start(f32[32,64,128]{2,1,0:T(8,128)S(1)} %multiply_add_fusion.4), channel_id=1, source_target_pairs={{0,1},{1,2},{2,3},{4,5},{5,6},{6,7},{8,9},{9,10},{10,11},{12,13},{... | collective-permute-start | bytes 3145736 | tf_op jit(solution)/shard_map/ppermute | solution.py:22
  283.1 118.7 %copy-start.37 = (f32[2048]{0:T(1024)}, f32[2048]{0:T(1024)S(1)}, u32[]{:S(2)}) copy-start(f32[2048]{0:T(1024)S(1)} %convert_element_type.118) | copy-start | bytes 24580
  284.9 58.2 %copy-start.25 = (f32[512,32]{0,1:T(8,128)}, f32[512,32]{0,1:T(8,128)S(1)}, u32[]{:S(2)}) copy-start(f32[512,32]{0,1:T(8,128)S(1)} %bitcast_bitcast_fusion.1) | copy-start | bytes 196612
  316.1 14.0 %slice-start = ((s8[4718592]{0:T(1024)(128)(4,1)}), s8[524288]{0:T(1024)(128)(4,1)S(1)}, s32[]{:S(2)}) async-start(s8[4718592]{0:T(1024)(128)(4,1)} %bitcast.389), calls=%async_computation.9 | async-start | bytes 1048576
  322.9 79.0 %copy-start.55 = (f32[512]{0:T(512)}, f32[512]{0:T(512)S(1)}, u32[]{:S(2)}) copy-start(f32[512]{0:T(512)S(1)} %fusion.152) | copy-start | bytes 6148
  348.6 25.1 %collective-permute-start.4 = (f32[32,64,128]{2,1,0:T(8,128)S(1)}, f32[32,64,128]{2,1,0:T(8,128)S(1)}, u32[]{:S(2)}, u32[]{:S(2)}) collective-permute-start(f32[32,64,128]{2,1,0:T(8,128)S(1)} %get-tuple-element.884), channel_id=1, source_target_pairs={{1,0},{2,1},{3,2},{5,4},{6,5},{7,6},{9,8},{10,9},{11,10},{13,12},{... | collective-permute-start | bytes 3145736 | tf_op jit(solution)/shard_map/ppermute | solution.py:22
  374.9 24.0 %collective-permute-start.5 = (f32[32,64,128]{2,1,0:T(8,128)}, f32[32,64,128]{2,1,0:T(8,128)S(1)}, u32[]{:S(2)}, u32[]{:S(2)}) collective-permute-start(f32[32,64,128]{2,1,0:T(8,128)} %multiply_add_fusion.3), channel_id=1, source_target_pairs={{1,0},{2,1},{3,2},{5,4},{6,5},{7,6},{9,8},{10,9},{11,10},{13,12},{... | collective-permute-start | bytes 3145736 | tf_op jit(solution)/shard_map/ppermute | solution.py:22
  400.1 37.7 %collective-permute-start.6 = (f32[32,64,128]{2,1,0:T(8,128)}, f32[32,64,128]{2,1,0:T(8,128)S(1)}, u32[]{:S(2)}, u32[]{:S(2)}) collective-permute-start(f32[32,64,128]{2,1,0:T(8,128)} %multiply_add_fusion.2), channel_id=1, source_target_pairs={{1,0},{2,1},{3,2},{5,4},{6,5},{7,6},{9,8},{10,9},{11,10},{13,12},{... | collective-permute-start | bytes 3145736 | tf_op jit(solution)/shard_map/ppermute | solution.py:22
  417.8 323.7 %reduce-scatter.6.cloned.1.call-start = ((), (), s32[]{:S(2)}) async-start(), calls=%async_computation.5 | async-start | bytes 26935296 | tf_op jit(solution)/shard_map/reduce_scatter | solution.py:206
  462.9 16.1 %copy-start.16 = (f32[256,256]{1,0:T(8,128)}, f32[256,256]{1,0:T(8,128)S(1)}, u32[]{:S(2)}) copy-start(f32[256,256]{1,0:T(8,128)S(1)} %fusion.249) | copy-start | bytes 786436 | tf_op jit(solution)/shard_map/transpose(jvp())/while
  503.0 21.7 %copy-start.61 = (f32[32]{0:T(128)S(1)}, f32[32]{0:T(128)}, u32[]{:S(2)}) copy-start(f32[32]{0:T(128)} %fusion.254) | copy-start | bytes 388 | tf_op jit(solution)/shard_map/transpose(jvp())/while
  514.1 13.6 %copy-start.2 = (f32[256,32,64]{0,2,1:T(8,128)S(1)}, f32[256,32,64]{0,2,1:T(8,128)}, u32[]{:S(2)}) copy-start(f32[256,32,64]{0,2,1:T(8,128)} %get-tuple-element.1075) | copy-start | bytes 6291460 | tf_op jit(solution)/shard_map/transpose(jvp())/while
  514.1 13.6 %copy-start.9 = (f32[2,256,32,64]{1,3,2,0:T(8,128)S(1)}, f32[2,256,32,64]{1,3,2,0:T(8,128)}, u32[]{:S(2)}) copy-start(f32[2,256,32,64]{1,3,2,0:T(8,128)} %get-tuple-element.1152) | copy-start | bytes 12582916 | tf_op jit(solution)/shard_map/transpose(jvp())/while
  514.1 13.6 %copy-start.17 = (f32[256,256]{1,0:T(8,128)S(1)}, f32[256,256]{1,0:T(8,128)}, u32[]{:S(2)}) copy-start(f32[256,256]{1,0:T(8,128)} %copy-done.16) | copy-start | bytes 786436 | tf_op jit(solution)/shard_map/transpose(jvp())/while
  514.1 13.6 %copy-start.23 = (f32[256,32]{0,1:T(8,128)S(1)}, f32[256,32]{0,1:T(8,128)}, u32[]{:S(2)}) copy-start(f32[256,32]{0,1:T(8,128)} %copy.398) | copy-start | bytes 98308 | tf_op jit(solution)/shard_map/transpose(jvp())/while
  514.1 13.6 %copy-start.24 = (pred[256,256]{1,0:T(8,128)(4,1)S(1)}, pred[256,256]{1,0:T(8,128)(4,1)}, u32[]{:S(2)}) copy-start(pred[256,256]{1,0:T(8,128)(4,1)} %iota_compare_fusion.3) | copy-start | bytes 196612 | tf_op jit(solution)/shard_map/transpose(jvp())/while
  514.1 13.6 %copy-start.31 = (f32[256,32]{0,1:T(8,128)S(1)}, f32[256,32]{0,1:T(8,128)}, u32[]{:S(2)}) copy-start(f32[256,32]{0,1:T(8,128)} %copy.389) | copy-start | bytes 98308 | tf_op jit(solution)/shard_map/transpose(jvp())/while
  514.1 13.6 %copy-start.32 = (f32[256,32]{0,1:T(8,128)S(1)}, f32[256,32]{0,1:T(8,128)}, u32[]{:S(2)}) copy-start(f32[256,32]{0,1:T(8,128)} %copy.388) | copy-start | bytes 98308 | tf_op jit(solution)/shard_map/transpose(jvp())/while
  557.1 16.1 %copy-start.16 = (f32[256,256]{1,0:T(8,128)}, f32[256,256]{1,0:T(8,128)S(1)}, u32[]{:S(2)}) copy-start(f32[256,256]{1,0:T(8,128)S(1)} %fusion.249) | copy-start | bytes 786436 | tf_op jit(solution)/shard_map/transpose(jvp())/while
  597.2 22.4 %copy-start.61 = (f32[32]{0:T(128)S(1)}, f32[32]{0:T(128)}, u32[]{:S(2)}) copy-start(f32[32]{0:T(128)} %fusion.254) | copy-start | bytes 388 | tf_op jit(solution)/shard_map/transpose(jvp())/while
  606.2 9.7 copy-start.7
  609.0 13.6 %copy-start.2 = (f32[256,32,64]{0,2,1:T(8,128)S(1)}, f32[256,32,64]{0,2,1:T(8,128)}, u32[]{:S(2)}) copy-start(f32[256,32,64]{0,2,1:T(8,128)} %get-tuple-element.1075) | copy-start | bytes 6291460 | tf_op jit(solution)/shard_map/transpose(jvp())/while
  609.0 13.6 %copy-start.9 = (f32[2,256,32,64]{1,3,2,0:T(8,128)S(1)}, f32[2,256,32,64]{1,3,2,0:T(8,128)}, u32[]{:S(2)}) copy-start(f32[2,256,32,64]{1,3,2,0:T(8,128)} %get-tuple-element.1152) | copy-start | bytes 12582916 | tf_op jit(solution)/shard_map/transpose(jvp())/while
  609.0 13.6 %copy-start.17 = (f32[256,256]{1,0:T(8,128)S(1)}, f32[256,256]{1,0:T(8,128)}, u32[]{:S(2)}) copy-start(f32[256,256]{1,0:T(8,128)} %copy-done.16) | copy-start | bytes 786436 | tf_op jit(solution)/shard_map/transpose(jvp())/while
  609.0 13.6 %copy-start.23 = (f32[256,32]{0,1:T(8,128)S(1)}, f32[256,32]{0,1:T(8,128)}, u32[]{:S(2)}) copy-start(f32[256,32]{0,1:T(8,128)} %copy.398) | copy-start | bytes 98308 | tf_op jit(solution)/shard_map/transpose(jvp())/while
  609.0 13.6 %copy-start.24 = (pred[256,256]{1,0:T(8,128)(4,1)S(1)}, pred[256,256]{1,0:T(8,128)(4,1)}, u32[]{:S(2)}) copy-start(pred[256,256]{1,0:T(8,128)(4,1)} %iota_compare_fusion.3) | copy-start | bytes 196612 | tf_op jit(solution)/shard_map/transpose(jvp())/while
  609.1 13.6 %copy-start.31 = (f32[256,32]{0,1:T(8,128)S(1)}, f32[256,32]{0,1:T(8,128)}, u32[]{:S(2)}) copy-start(f32[256,32]{0,1:T(8,128)} %copy.389) | copy-start | bytes 98308 | tf_op jit(solution)/shard_map/transpose(jvp())/while
  609.1 13.6 %copy-start.32 = (f32[256,32]{0,1:T(8,128)S(1)}, f32[256,32]{0,1:T(8,128)}, u32[]{:S(2)}) copy-start(f32[256,32]{0,1:T(8,128)} %copy.388) | copy-start | bytes 98308 | tf_op jit(solution)/shard_map/transpose(jvp())/while
  656.3 11.9 %slice-start.2 = ((s8[4718592]{0:T(1024)(128)(4,1)}), s8[4194304]{0:T(1024)(128)(4,1)S(1)}, s32[]{:S(2)}) async-start(s8[4718592]{0:T(1024)(128)(4,1)} %bitcast.391), calls=%async_computation.11 | async-start | bytes 8388608
  656.3 11.9 %slice-start.8 = ((s8[4718592]{0:T(1024)(128)(4,1)}), s8[4194304]{0:T(1024)(128)(4,1)S(1)}, s32[]{:S(2)}) async-start(s8[4718592]{0:T(1024)(128)(4,1)} %bitcast.398), calls=%async_computation.17 | async-start | bytes 8388608
  682.2 12.6 %collective-permute-start.7 = (f32[3,2304]{1,0:T(4,128)S(1)}, f32[3,2304]{1,0:T(4,128)S(1)}, u32[]{:S(2)}, u32[]{:S(2)}) collective-permute-start(f32[3,2304]{1,0:T(4,128)S(1)} %pad_add_fusion.2), channel_id=1, source_target_pairs={{1,0},{2,1},{3,2},{5,4},{6,5},{7,6},{9,8},{10,9},{11,10},{13,12},{... | collective-permute-start | bytes 82952 | tf_op jit(solution)/shard_map/ppermute | solution.py:22
  690.7 9.5 copy-start.34
  690.8 9.5 copy-start.50
  712.6 58.2 %reduce-scatter.10.cloned.1.call-start = ((), (), s32[]{:S(2)}) async-start(), calls=%async_computation.7 | async-start | bytes 1769472
  714.3 419.9 %all-reduce.31.cloned.1.call-start = ((), (), s32[]{:S(2)}) async-start(), calls=%async_computation.8 | async-start | bytes 26345472 | tf_op jit(solution)/shard_map/psum | solution.py:216
  751.1 11.8 %copy-start.62 = (f32[2048]{0:T(1024)S(1)}, f32[2048]{0:T(1024)}, u32[]{:S(2)}) copy-start(f32[2048]{0:T(1024)} %get-tuple-element.755) | copy-start | bytes 24580
  751.1 15.7 %copy-start.58 = (f32[512]{0:T(512)S(1)}, f32[512]{0:T(512)}, u32[]{:S(2)}) copy-start(f32[512]{0:T(512)} %copy-done.57) | copy-start | bytes 6148
  751.1 15.7 %copy-start.22 = (bf16[1,512,1024]{2,1,0:T(8,128)(2,1)S(1)}, bf16[1,512,1024]{2,1,0:T(8,128)(2,1)}, u32[]{:S(2)}) copy-start(bf16[1,512,1024]{2,1,0:T(8,128)(2,1)} %param.31) | copy-start | bytes 3145732
  (54 other events, 267.6 us)
Sparse Core Ops, SparseCore 0:
  13.7 23.9 all-gather.4
  231.8 12.6 all-gather.6
  417.9 18.4 reduce-scatter.7
  712.8 28.7 reduce-scatter.5
  744.2 9.7 reduce-scatter.9
  760.3 373.8 all-reduce.30
where the time goes:
time: 1170 us; the launch traced here: 1150 us
  waiting for transfers between devices  413 us (35%)
  local copies, waits for them, and re-layouts  254 us (22%)
  matrix products  220 us (19%)
  other arithmetic  117 us (10%)
  blocking collectives  97.2 us (8%)
  starting transfers between devices  22.1 us (2%)
  between operations  20.2 us (2%)
    psum x1, waiting for transfers between devices, body(): lax.psum((shares[0], shares[1], shares[2], shares[3], shares[4], shares[5...  279 us
    ppermute x8, waiting for transfers between devices, passed_along(): return lax.ppermute(shard, axis, pairs)  96.2 us
    dynamic_update_slice x6, local copies, waits for them, and re-layouts, block_scan(): lax.scan(jax.checkpoint(advance), carried, (inputs_x.reshape(num_blocks,...  92.5 us
    psum x1, blocking collectives, body(): lax.psum((shares[0], shares[1], shares[2], shares[3], shares[4], shares[5...  83.3 us
    dot_general x6, matrix products, block_terms(): within = jnp.einsum('ijh,jhp->ihp', weights, inputs_x, precision=HIGHEST)  69.7 us
    unnamed x175, local copies, waits for them, and re-layouts  35.1 us
    dot_general x6, matrix products, block_terms(): jnp.einsum('jh,jhp,jn->hpn', closing, inputs_x, in_map, precision=HIGHEST)  29.7 us
    dot_general x8, matrix products, block_terms(): jnp.einsum('in,hpn->ihp', out_map, carried, precision=HIGHEST)  27.4 us
  transfers between devices with their start and end apart: 14, of which 8 were waited for; matrix products, arithmetic and copies ran while one was open for 31% of the time, Pallas kernels for 0%

commit v1 on v0

v1 whole, which is shorter than its diff:
```python
import jax
import jax.numpy as jnp
from jax import lax
from jax.experimental import pallas as pl
from jax.experimental.pallas import tpu as pltpu
from jax.sharding import PartitionSpec as P

H = 32
P_SIZE = 64
N = 128
K = 4
DIN = 2048
CONV = 2304
EPS = 1e-05
QB = 128
HALO = 16
GROUP = 256
LANE = 128

bf16 = jnp.bfloat16
f32 = jnp.float32
HIGHEST = lax.Precision.HIGHEST

VMEM_LIMIT = 60 * 1024 * 1024


def nn(a, b):
    return lax.dot_general(a, b, (((1,), (0,)), ((), ())), preferred_element_type=f32)


def nt(a, b):
    return lax.dot_general(a, b, (((1,), (1,)), ((), ())), preferred_element_type=f32)


def exact_nn(a, b):
    return lax.dot_general(
        a, b, (((1,), (0,)), ((), ())), precision=HIGHEST, preferred_element_type=f32
    )


def iota(shape, dim):
    return lax.broadcasted_iota(jnp.int32, shape, dim)


def sigmoid(v):
    return 1.0 / (1.0 + jnp.exp(-v))


def split_two(v):
    hi = v.astype(bf16)
    lo = (v - hi.astype(f32)).astype(bf16)
    return hi, lo


def const_spec(shape):
    return pl.BlockSpec(shape, lambda *_: tuple(0 for _ in shape))


def params(steps=1):
    return pltpu.CompilerParams(
        dimension_semantics=("arbitrary",) * steps, vmem_limit_bytes=VMEM_LIMIT
    )


def call(kernel, grid, in_specs, out_specs, out_shape, scratch, flops, nbytes, name):
    return pl.pallas_call(
        kernel,
        grid_spec=pltpu.PrefetchScalarGridSpec(
            num_scalar_prefetch=1,
            grid=grid,
            in_specs=in_specs,
            out_specs=out_specs,
            scratch_shapes=scratch,
        ),
        out_shape=out_shape,
        compiler_params=params(len(grid)),
        cost_estimate=pl.CostEstimate(flops=flops, bytes_accessed=nbytes, transcendentals=0),
        name=name,
    )


def spread(cols, pair):
    left = cols[:, 2 * pair : 2 * pair + 1]
    right = cols[:, 2 * pair + 1 : 2 * pair + 2]
    lanes = iota((cols.shape[0], LANE), 1)
    return jnp.where(lanes < P_SIZE, left, right)


def spread_group(cols):
    return jnp.concatenate([spread(cols, 0), spread(cols, 1)], axis=1)


def block_diag(pair_low):
    lanes = iota(pair_low.shape, 1)
    zero = jnp.zeros_like(pair_low)
    return jnp.concatenate(
        [jnp.where(lanes < P_SIZE, pair_low, zero), jnp.where(lanes < P_SIZE, zero, pair_low)],
        axis=0,
    )


def head_columns(cols, group):
    return pltpu.roll(cols, lax.rem(LANE - 4 * group, LANE), 1)


def head_picker(lanes_in, first_head):
    rows = iota((lanes_in, LANE), 0) // P_SIZE + first_head
    return (rows == iota((lanes_in, LANE), 1)).astype(bf16)


def front_kernel(
    scal, tok, halo, gain, w_own, w_oth, r_own, r_oth, taps, heads,
    normed, u_out, act_out, dact_out, dt_out, sg_out, cum_out, cumt_out, st_out,
    ubuf, bt, ecl,
):
    step = pl.program_id(0)
    tok_count = tok.shape[0]
    half = w_own.shape[0]
    own = pl.ds(pl.multiple_of(scal[0] * half, LANE), half)
    oth = pl.ds(pl.multiple_of((1 - scal[0]) * half, LANE), half)
    lo = scal[1]
    hi = scal[2]

    @pl.when(step == 0)
    def _():
        def rows_of(src, base, dst, count):
            x = src[pl.ds(base, count), :].astype(f32)
            ms = jnp.mean(x * x, axis=-1, keepdims=True)
            normed[pl.ds(dst, count), :] = (x * lax.rsqrt(ms + EPS) * gain[...]).astype(bf16)

        rows_of(halo, 0, 0, HALO)

        def body(i, carry):
            base = pl.multiple_of(i * 64, 64)
            rows_of(tok, base, pl.multiple_of(base + HALO, 16), 64)
            return carry

        lax.fori_loop(0, tok_count // 64, body, 0)
        r = nn(normed[HALO:, own], r_own[...]) + nn(normed[HALO:, oth], r_oth[...])
        pre = r.astype(bf16).astype(f32) + heads[0:1, :]
        pos = iota((tok_count, LANE), 0)
        keep = (pos >= lo) & (pos < hi) & (iota((tok_count, LANE), 1) < H)
        soft = jnp.maximum(pre, 0.0) + jnp.log1p(jnp.exp(-jnp.abs(pre)))
        dt = jnp.where(keep, soft, 0.0)
        dt_out[...] = dt
        sg_out[...] = jnp.where(keep, sigmoid(pre), 0.0)
        da = dt * heads[1:2, :]
        tri = (iota((QB, QB), 0) >= iota((QB, QB), 1)).astype(f32)
        carry = jnp.zeros((1, LANE), f32)
        for q in range(tok_count // QB):
            cum = exact_nn(tri, da[q * QB : (q + 1) * QB]) + carry
            cum_out[q * QB : (q + 1) * QB, :] = cum
            cumt_out[:, q * QB : (q + 1) * QB] = cum.T
            carry = cum[QB - 1 : QB]
        ecl[...] = jnp.exp(carry - cum_out[...])

    u = nn(normed[:, own], w_own[...]) + nn(normed[:, oth], w_oth[...])
    pos = iota(u.shape, 0) - HALO
    u = jnp.where((pos >= lo) & (pos < hi), u, 0.0).astype(bf16)
    u_out[...] = u
    ubuf[...] = u.astype(f32)
    c = taps[4:5, :] + sum(
        taps[k : k + 1, :] * ubuf[HALO - 3 + k : HALO - 3 + k + tok_count, :] for k in range(K)
    )
    s = sigmoid(c)
    act = (c * s).astype(bf16)
    act_out[...] = act
    dact_out[...] = (s * (1.0 + c * (1.0 - s))).astype(bf16)

    @pl.when(step == 0)
    def _():
        bt[...] = act[:, :N].astype(f32).T.astype(bf16)

    @pl.when(step > 0)
    def _():
        group = step - 1
        dtg = spread_group(head_columns(dt_out[...], group))
        ecg = spread_group(head_columns(ecl[...], group))
        xt = (act.astype(f32) * dtg).astype(bf16)
        xw = (xt.astype(f32) * ecg).astype(bf16)
        st_out[...] = nn(bt[...], xw)


def front(scal, tok, halo, gain, wu_own, wu_oth, taps, heads):
    tok_count, d = tok.shape
    half = wu_own.shape[0]
    ext = tok_count + HALO
    groups = CONV // GROUP
    first = groups - 1

    def col(j, *_):
        return (0, (j + first) % groups)

    def weight(rows):
        return pl.BlockSpec((rows, GROUP), col)

    narrow = pl.BlockSpec((half, LANE), lambda j, *_: (0, CONV // LANE))
    return call(
        front_kernel,
        (groups,),
        [
            const_spec((tok_count, d)),
            const_spec((HALO, d)),
            const_spec((1, d)),
            weight(half),
            weight(half),
            narrow,
            narrow,
            weight(8),
            const_spec((8, LANE)),
        ],
        [
            const_spec((ext, d)),
            pl.BlockSpec((ext, GROUP), col),
            pl.BlockSpec((tok_count, GROUP), col),
            pl.BlockSpec((tok_count, GROUP), col),
            const_spec((tok_count, LANE)),
            const_spec((tok_count, LANE)),
            const_spec((tok_count, LANE)),
            const_spec((LANE, tok_count)),
            pl.BlockSpec((N, GROUP), lambda j, *_: (0, jnp.maximum(j - 1, 0))),
        ],
        [
            jax.ShapeDtypeStruct((ext, d), bf16),
            jax.ShapeDtypeStruct((ext, CONV), bf16),
            jax.ShapeDtypeStruct((tok_count, CONV), bf16),
            jax.ShapeDtypeStruct((tok_count, CONV), bf16),
            jax.ShapeDtypeStruct((tok_count, LANE), f32),
            jax.ShapeDtypeStruct((tok_count, LANE), f32),
            jax.ShapeDtypeStruct((tok_count, LANE), f32),
            jax.ShapeDtypeStruct((LANE, tok_count), f32),
            jax.ShapeDtypeStruct((N, DIN), f32),
        ],
        [
            pltpu.VMEM((ext, GROUP), f32),
            pltpu.VMEM((N, tok_count), bf16),
            pltpu.VMEM((tok_count, LANE), f32),
        ],
        2 * ext * d * (CONV + LANE),
        2 * (ext * d + d * CONV + 3 * ext * CONV),
        "front",
    )(scal, tok, halo, gain, wu_own, wu_oth, wu_own, wu_oth, taps, heads)


def intra_kernel(scal, x, bc, dt, cum, cumt, y_out, s0_out, scores, bt):
    group = pl.program_id(0)
    blocks = x.shape[0] // QB

    @pl.when(group == 0)
    def _():
        lower = iota((QB, QB), 0) >= iota((QB, QB), 1)
        bt[...] = bc[:, :N].astype(f32).T.astype(bf16)
        for q in range(blocks):
            rows = slice(q * QB, (q + 1) * QB)
            scores[q] = jnp.where(lower, nt(bc[rows, N:], bc[rows, :N]), 0.0)

    dtr = head_columns(dt[...], group)
    cumr = head_columns(cum[...], group)
    carry = jnp.zeros((N, GROUP), f32)
    for q in range(blocks):
        rows = slice(q * QB, (q + 1) * QB)
        cq = cumr[rows]
        end = cq[QB - 1 : QB]
        start = cumr[q * QB - 1 : q * QB] if q else jnp.zeros((1, LANE), f32)
        xt = (x[rows, :].astype(f32) * spread_group(dtr[rows])).astype(bf16)
        low_carry = carry.astype(bf16)
        s0_out[q] = low_carry
        ys = []
        for pair in range(2):
            mats = []
            for e in range(2):
                h = 2 * pair + e
                row = cumt[0, h : h + 1, rows]
                decay = jnp.exp(jnp.minimum(cq[:, h : h + 1] - row, 0.0))
                mats.append((decay * scores[q]).astype(bf16))
            ys.append(
                nn(
                    jnp.concatenate(mats, axis=1),
                    block_diag(xt[:, pair * LANE : (pair + 1) * LANE]),
                )
            )
        y = jnp.concatenate(ys, axis=1)
        if q:
            y = y + jnp.exp(spread_group(cq - start)) * nn(bc[rows, N:], low_carry)
        y_out[rows, :] = y
        if q < blocks - 1:
            xw = (xt.astype(f32) * jnp.exp(spread_group(end - cq))).astype(bf16)
            fresh = nn(bt[:, rows], xw)
            carry = fresh if q == 0 else fresh + carry * jnp.exp(spread_group(end - start))


def intra(scal, act, dt, cum, cumt):
    tok_count = act.shape[0]
    blocks = tok_count // QB
    groups = DIN // GROUP
    return call(
        intra_kernel,
        (groups,),
        [
            pl.BlockSpec((tok_count, GROUP), lambda j, *_: (0, j)),
            pl.BlockSpec((tok_count, GROUP), lambda j, *_: (0, groups)),
            const_spec((tok_count, LANE)),
            const_spec((tok_count, LANE)),
            pl.BlockSpec((1, 4, tok_count), lambda j, *_: (j, 0, 0)),
        ],
        [
            pl.BlockSpec((tok_count, GROUP), lambda j, *_: (0, j)),
            pl.BlockSpec((blocks, N, GROUP), lambda j, *_: (0, 0, j)),
        ],
        [
            jax.ShapeDtypeStruct((tok_count, DIN), f32),
            jax.ShapeDtypeStruct((blocks, N, DIN), bf16),
        ],
        [pltpu.VMEM((blocks, QB, QB), f32), pltpu.VMEM((N, tok_count), bf16)],
        2 * tok_count * DIN * 3 * N,
        8 * tok_count * DIN,
        "intra",
    )(scal, act, act, dt, cum, cumt)


def gate_kernel(
    scal, yloc, act, z, eg, cum, s_in, vecs,
    gated, ey_out, ez_out, r_loc, r_dev, dc_out, g_out, gs_out,
    pick, vbuf, ytbuf, ydbuf,
):
    step = pl.program_id(0)
    rows = yloc.shape[0]
    groups = DIN // GROUP

    @pl.when(step == 0)
    def _():
        pick[...] = head_picker(DIN, 0)
        g_out[...] = jnp.zeros_like(g_out)
        gs_out[...] = jnp.zeros_like(gs_out)

    pos = iota((rows, 1), 0) + step * rows
    valid = ((pos >= scal[1]) & (pos < scal[2])).astype(f32)
    cq = cum[...]
    ecq = jnp.exp(cq)
    cmat = act[:, DIN + N :]
    ssq = jnp.zeros((rows, GROUP), f32)
    for g in range(groups):
        cols = slice(g * GROUP, (g + 1) * GROUP)
        eg_cum = jnp.concatenate([spread(ecq, 2 * g), spread(ecq, 2 * g + 1)], axis=1)
        yd = eg_cum * nn(cmat, s_in[:, cols])
        ydbuf[:, cols] = yd
        yt = yloc[:, cols] + yd + vecs[1:2, cols] * act[:, cols].astype(f32)
        ytbuf[:, cols] = yt
        zz = z[:, cols].astype(f32)
        v = yt * (zz * sigmoid(zz))
        vbuf[:, cols] = v
        ssq = ssq + v * v
    rs = lax.rsqrt(jnp.sum(ssq, axis=-1, keepdims=True) / DIN + EPS)
    mixed = jnp.zeros((rows, GROUP), f32)
    for g in range(groups):
        cols = slice(g * GROUP, (g + 1) * GROUP)
        n = vbuf[:, cols] * rs
        vbuf[:, cols] = n
        gain = vecs[0:1, cols]
        gated[:, cols] = (n * gain * valid).astype(bf16)
        e = eg[:, cols].astype(f32) * valid
        gs_out[0:1, cols] += jnp.sum(e * n, axis=0, keepdims=True)
        mixed = mixed + e * gain * n
    m2 = jnp.sum(mixed, axis=-1, keepdims=True) / DIN
    rl = jnp.zeros((rows, LANE), f32)
    rd = jnp.zeros((rows, LANE), f32)
    dc = jnp.zeros((rows, N), f32)
    ct = cmat.astype(f32).T.astype(bf16)
    for g in range(groups):
        cols = slice(g * GROUP, (g + 1) * GROUP)
        n = vbuf[:, cols]
        e = eg[:, cols].astype(f32) * valid
        ev = rs * (e * vecs[0:1, cols] - n * m2)
        zz = z[:, cols].astype(f32)
        sz = sigmoid(zz)
        ey = ev * (zz * sz)
        ez_out[:, cols] = (ev * ytbuf[:, cols] * (sz * (1.0 + zz * (1.0 - sz)))).astype(bf16)
        gs_out[1:2, cols] += jnp.sum(ey * act[:, cols].astype(f32), axis=0, keepdims=True)
        low = ey.astype(bf16)
        ey_out[:, cols] = low
        eyf = low.astype(f32)
        ph, pl_ = split_two(eyf * yloc[:, cols])
        rl = rl + nn(ph, pick[cols, :]) + nn(pl_, pick[cols, :])
        rd = rd + nn((eyf * ydbuf[:, cols]).astype(bf16), pick[cols, :])
        eg_cum = jnp.concatenate([spread(ecq, 2 * g), spread(ecq, 2 * g + 1)], axis=1)
        eye = (eyf * eg_cum).astype(bf16)
        g_out[:, cols] += nn(ct, eye)
        dc = dc + nt(eye, s_in[:, cols])
    r_loc[...] = rl
    r_dev[...] = rd
    dc_out[...] = dc


def gate(scal, yloc, act, z, eg, cum, s_in, vecs):
    tok_count = act.shape[0]
    rows = QB

    def rowspec(width):
        return pl.BlockSpec((rows, width), lambda j, *_: (j, 0))

    def out(width, kind):
        return jax.ShapeDtypeStruct((tok_count, width), kind)

    return call(
        gate_kernel,
        (tok_count // rows,),
        [
            rowspec(DIN),
            rowspec(CONV),
            rowspec(DIN),
            rowspec(DIN),
            rowspec(LANE),
            const_spec((N, DIN)),
            const_spec((8, DIN)),
        ],
        [
            rowspec(DIN),
            rowspec(DIN),
            rowspec(DIN),
            rowspec(LANE),
            rowspec(LANE),
            rowspec(LANE),
            const_spec((N, DIN)),
            const_spec((8, DIN)),
        ],
        [
            out(DIN, bf16),
            out(DIN, bf16),
            out(DIN, bf16),
            out(LANE, f32),
            out(LANE, f32),
            out(LANE, f32),
            jax.ShapeDtypeStruct((N, DIN), f32),
            jax.ShapeDtypeStruct((8, DIN), f32),
        ],
        [
            pltpu.VMEM((DIN, LANE), bf16),
            pltpu.VMEM((rows, DIN), f32),
            pltpu.VMEM((rows, DIN), f32),
            pltpu.VMEM((rows, DIN), f32),
        ],
        2 * tok_count * DIN * 6 * N,
        20 * tok_count * DIN,
        "gate",
    )(scal, yloc, act, z, eg, cum, s_in, vecs)


def back_kernel(
    scal, x, bc, dt, cum, cumt, ey, s0,
    dxt_out, db_out, dc_out, r2_out, cq_out,
    scores, dscores, ct,
):
    group = pl.program_id(0)
    last = pl.num_programs(0) - 1
    blocks = x.shape[0] // QB
    upper = iota((QB, QB), 0) <= iota((QB, QB), 1)

    @pl.when(group == 0)
    def _():
        ct[...] = bc[:, N:].astype(f32).T.astype(bf16)
        for q in range(blocks):
            rows = slice(q * QB, (q + 1) * QB)
            scores[q] = jnp.where(upper, nt(bc[rows, :N], bc[rows, N:]), 0.0)
        dscores[...] = jnp.zeros_like(dscores)
        db_out[...] = jnp.zeros_like(db_out)
        dc_out[...] = jnp.zeros_like(dc_out)
        r2_out[...] = jnp.zeros_like(r2_out)
        cq_out[...] = jnp.zeros_like(cq_out)

    dtr = head_columns(dt[...], group)
    cumr = head_columns(cum[...], group)
    picks = [head_picker(LANE, 4 * group + 2 * pair) for pair in range(2)]
    picks2 = [jnp.concatenate([p, p], axis=0) for p in picks]
    pick_all = head_picker(GROUP, 4 * group).astype(f32)
    carry = None
    for q in reversed(range(blocks)):
        rows = slice(q * QB, (q + 1) * QB)
        cq = cumr[rows]
        end = cq[QB - 1 : QB]
        start = cumr[q * QB - 1 : q * QB] if q else jnp.zeros((1, LANE), f32)
        xt = (x[rows, :].astype(f32) * spread_group(dtr[rows])).astype(bf16)
        eyq = ey[rows, :]
        dxs = []
        ds = jnp.zeros((QB, QB), f32)
        for pair in range(2):
            lanes = slice(pair * LANE, (pair + 1) * LANE)
            eybd = block_diag(eyq[:, lanes])
            dm = nt(xt[:, lanes], eybd)
            mats = []
            for e in range(2):
                h = 2 * pair + e
                row = cumt[0, h : h + 1, rows]
                decay = jnp.exp(jnp.minimum(row - cq[:, h : h + 1], 0.0))
                mats.append((decay * scores[q]).astype(bf16))
                ds = ds + decay * dm[:, e * QB : (e + 1) * QB]
            dxs.append(nn(jnp.concatenate(mats, axis=1), eybd))
        dscores[q] += ds
        dx = jnp.concatenate(dxs, axis=1)
        xtf = xt.astype(f32)
        eye = None
        if q:
            eye = (eyq.astype(f32) * jnp.exp(spread_group(cq - start))).astype(bf16)
            dc_out[rows, :] += nt(eye, s0[q])
        if carry is not None:
            low = carry.astype(bf16)
            ecl = jnp.exp(spread_group(end - cq))
            dst = ecl * nn(bc[rows, :N], low)
            db_out[rows, :] += nt((xtf * ecl).astype(bf16), low)
            total = jnp.exp(spread_group(end - start))
            vec = jnp.sum(xtf * dst, axis=0, keepdims=True)
            if q:
                vec = vec + total * jnp.sum(carry * s0[q].astype(f32), axis=0, keepdims=True)
            cq_out[q : q + 1, :] += exact_nn(jnp.broadcast_to(vec, (8, GROUP)), pick_all)[0:1]
            dx = dx + dst
        if q:
            fresh = nn(ct[:, rows], eye)
            carry = fresh if carry is None else fresh + total * carry
        dxt_out[rows, :] = dx.astype(bf16)
        prod = xtf * dx
        acc = jnp.zeros((QB, LANE), f32)
        for pair in range(2):
            ph, pl_ = split_two(prod[:, pair * LANE : (pair + 1) * LANE])
            acc = acc + nn(jnp.concatenate([ph, pl_], axis=1), picks2[pair])
        r2_out[rows, :] += acc

    @pl.when(group == last)
    def _():
        for q in range(blocks):
            rows = slice(q * QB, (q + 1) * QB)
            ds = jnp.where(upper, dscores[q], 0.0)
            db_out[rows, :] += nn(ds.astype(bf16), bc[rows, N:])
            dc_out[rows, :] += nn(ds.T.astype(bf16), bc[rows, :N])


def back(scal, act, dt, cum, cumt, ey, s0):
    tok_count = act.shape[0]
    blocks = tok_count // QB
    groups = DIN // GROUP
    wide = pl.BlockSpec((tok_count, GROUP), lambda j, *_: (0, j))
    small = const_spec((tok_count, LANE))
    return call(
        back_kernel,
        (groups,),
        [
            wide,
            pl.BlockSpec((tok_count, GROUP), lambda j, *_: (0, groups)),
            small,
            small,
            pl.BlockSpec((1, 4, tok_count), lambda j, *_: (j, 0, 0)),
            wide,
            pl.BlockSpec((blocks, N, GROUP), lambda j, *_: (0, 0, j)),
        ],
        [wide, small, small, small, const_spec((8, LANE))],
        [
            jax.ShapeDtypeStruct((tok_count, DIN), bf16),
            jax.ShapeDtypeStruct((tok_count, LANE), f32),
            jax.ShapeDtypeStruct((tok_count, LANE), f32),
            jax.ShapeDtypeStruct((tok_count, LANE), f32),
            jax.ShapeDtypeStruct((8, LANE), f32),
        ],
        [
            pltpu.VMEM((blocks, QB, QB), f32),
            pltpu.VMEM((blocks, QB, QB), f32),
            pltpu.VMEM((N, tok_count), bf16),
        ],
        2 * tok_count * DIN * 8 * N,
        8 * tok_count * DIN,
        "back",
    )(scal, act, act, dt, cum, cumt, ey, s0)


def tail_kernel(
    scal, act, bc, dact, u, ey, dxt, taps, dt, sg, cum, g_in, s_in, skip, heads,
    db_loc, dc_loc, dc_dev, r_loc, r_dev, r2, cq,
    eu_out, er_out, gconv, ghead,
    ebuf, ubuf, p_acc, d_acc, db_acc, gs_acc,
):
    step = pl.program_id(0)
    last = pl.num_programs(0) - 1
    tok_count = act.shape[0]
    ext = tok_count + HALO
    lo = scal[1]
    hi = scal[2]

    @pl.when(step == 0)
    def _():
        p_acc[...] = jnp.zeros_like(p_acc)
        d_acc[...] = jnp.zeros_like(d_acc)
        db_acc[...] = jnp.zeros_like(db_acc)
        gs_acc[...] = jnp.zeros_like(gs_acc)
        ebuf[...] = jnp.zeros_like(ebuf)

    bmat = bc[:, :N]

    @pl.when(step < last)
    def _():
        cumr = head_columns(cum[...], step)
        dtr = spread_group(head_columns(dt[...], step))
        xf = act[...].astype(f32)
        xtf = (xf * dtr).astype(bf16).astype(f32)
        low = g_in[...]
        end = cumr[tok_count - 1 : tok_count]
        ecl = jnp.exp(spread_group(end - cumr))
        dxd = ecl * nn(bmat, low)
        dx = dxt[...].astype(f32) + dxd
        pick = head_picker(GROUP, 4 * step)
        p_acc[...] += nn((xtf * dxd).astype(bf16), pick)
        d_acc[...] += nn((xf * dx).astype(bf16), pick)
        db_acc[...] += nt((xtf * ecl).astype(bf16), low)
        vec = jnp.sum(low.astype(f32) * s_in[...].astype(f32), axis=0, keepdims=True)
        vec = vec * jnp.exp(spread_group(end))
        gs_acc[...] += exact_nn(jnp.broadcast_to(vec, (8, GROUP)), pick.astype(f32))
        ebuf[HALO : HALO + tok_count, :] = (
            dtr * dx + skip[0:1, :] * ey[...].astype(f32)
        ) * dact[...].astype(f32)

    @pl.when(step == last)
    def _():
        ebuf[HALO : HALO + tok_count, :N] = (db_loc[...] + db_acc[...]) * dact[:, :N].astype(f32)
        ebuf[HALO : HALO + tok_count, N:] = (dc_loc[...] + dc_dev[...]) * dact[:, N:].astype(f32)
        rate = heads[1:2, :]
        upper = (iota((QB, QB), 0) <= iota((QB, QB), 1)).astype(f32)
        strict = (iota((QB, QB), 0) > iota((QB, QB), 1)).astype(f32)
        blocks = tok_count // QB
        devs = jnp.zeros((1, LANE), f32)
        suffix = [None] * blocks
        for q in reversed(range(blocks)):
            rows = slice(q * QB, (q + 1) * QB)
            within = exact_nn(upper, r_loc[rows, :] - r2[rows, :]) + cq[q : q + 1, :]
            dev = exact_nn(upper, r_dev[rows, :]) + devs
            devs = dev[0:1]
            suffix[q] = within + dev
        before = gs_acc[0:1, :]
        glog = jnp.zeros((1, LANE), f32)
        gdt = jnp.zeros((1, LANE), f32)
        er_out[0:HALO, :] = jnp.zeros((HALO, LANE), bf16)
        for q in range(blocks):
            rows = slice(q * QB, (q + 1) * QB)
            pq = p_acc[rows, :]
            eda = suffix[q] + exact_nn(strict, pq) + before
            before = before + jnp.sum(pq, axis=0, keepdims=True)
            er = (d_acc[rows, :] + rate * eda) * sg[rows, :]
            gdt = gdt + jnp.sum(er, axis=0, keepdims=True)
            glog = glog + rate * jnp.sum(dt[rows, :] * eda, axis=0, keepdims=True)
            er_out[HALO + q * QB : HALO + (q + 1) * QB, :] = er.astype(bf16)
        ghead[...] = jnp.concatenate([gdt, glog, jnp.zeros((6, LANE), f32)], axis=0)

    ubuf[...] = u[...].astype(f32)
    ec = ebuf[HALO : HALO + tok_count, :]
    gs = [
        jnp.sum(ec * ubuf[HALO - 3 + k : HALO - 3 + k + tok_count, :], axis=0, keepdims=True)
        for k in range(K)
    ]
    gs.append(jnp.sum(ec, axis=0, keepdims=True))
    gs.append(jnp.zeros((3, ec.shape[1]), f32))
    gconv[...] = jnp.concatenate(gs, axis=0)
    eu = sum(taps[k : k + 1, :] * ebuf[3 - k : 3 - k + ext, :] for k in range(K))
    pos = iota(eu.shape, 0) - HALO
    eu_out[...] = jnp.where((pos >= lo) & (pos < hi), eu, 0.0).astype(bf16)


def tail(scal, act, dact, u, ey, dxt, taps, dt, sg, cum, g_in, s_in, skip, heads, smalls):
    tok_count = act.shape[0]
    ext = tok_count + HALO
    groups = DIN // GROUP

    def col(j, *_):
        return (0, j)

    def colx(j, *_):
        return (0, jnp.minimum(j, groups - 1))

    wide = pl.BlockSpec((tok_count, GROUP), col)
    widex = pl.BlockSpec((tok_count, GROUP), colx)
    small = const_spec((tok_count, LANE))
    return call(
        tail_kernel,
        (groups + 1,),
        [
            wide,
            pl.BlockSpec((tok_count, GROUP), lambda j, *_: (0, groups)),
            wide,
            pl.BlockSpec((ext, GROUP), col),
            widex,
            widex,
            pl.BlockSpec((8, GROUP), col),
            small,
            small,
            small,
            pl.BlockSpec((N, GROUP), colx),
            pl.BlockSpec((N, GROUP), colx),
            pl.BlockSpec((8, GROUP), colx),
            const_spec((8, LANE)),
            small,
            small,
            small,
            small,
            small,
            small,
            const_spec((8, LANE)),
        ],
        [
            pl.BlockSpec((ext, GROUP), col),
            const_spec((ext, LANE)),
            pl.BlockSpec((8, GROUP), col),
            const_spec((8, LANE)),
        ],
        [
            jax.ShapeDtypeStruct((ext, CONV), bf16),
            jax.ShapeDtypeStruct((ext, LANE), bf16),
            jax.ShapeDtypeStruct((8, CONV), f32),
            jax.ShapeDtypeStruct((8, LANE), f32),
        ],
        [
            pltpu.VMEM((ext + HALO, GROUP), f32),
            pltpu.VMEM((ext, GROUP), f32),
            pltpu.VMEM((tok_count, LANE), f32),
            pltpu.VMEM((tok_count, LANE), f32),
            pltpu.VMEM((tok_count, LANE), f32),
            pltpu.VMEM((8, LANE), f32),
        ],
        2 * tok_count * DIN * 4 * N,
        12 * tok_count * DIN,
        "tail",
    )(
        scal, act, act, dact, u, ey, dxt, taps, dt, sg, cum, g_in, s_in, skip, heads, *smalls
    )


def splitk_kernel(scal, a, w_own, w_oth, *rest):
    half = w_own.shape[0]
    own = pl.ds(pl.multiple_of(scal[0] * half, LANE), half)
    oth = pl.ds(pl.multiple_of((1 - scal[0]) * half, LANE), half)
    total = nn(a[:, own], w_own[...]) + nn(a[:, oth], w_oth[...])
    if len(rest) == 2:
        total = total + rest[0][...].astype(f32)
    out = rest[-1]
    out[...] = total.astype(out.dtype)


def splitk(scal, a, w_own, w_oth, add, name):
    rows, depth = a.shape
    width = w_own.shape[1]
    col = lambda j, *_: (0, j)
    specs = [
        const_spec((rows, depth)),
        pl.BlockSpec((depth // 2, GROUP), col),
        pl.BlockSpec((depth // 2, GROUP), col),
    ]
    args = [a, w_own, w_oth]
    if add is not None:
        specs.append(pl.BlockSpec((rows, GROUP), col))
        args.append(add)
    return call(
        splitk_kernel,
        (width // GROUP,),
        specs,
        pl.BlockSpec((rows, GROUP), col),
        jax.ShapeDtypeStruct((rows, width), bf16),
        [],
        2 * rows * depth * width,
        2 * (rows * depth + depth * width + rows * width),
        name,
    )(scal, *args)


def halves_kernel(scal, *refs):
    out = refs[-1]
    count = (len(refs) - 1) // 3
    steps = pl.num_programs(0) // 2
    step = pl.program_id(0)

    @pl.when(step < steps)
    def _():
        total = sum(nt(refs[3 * i][...], refs[3 * i + 1][...]) for i in range(count))
        out[...] = total.astype(out.dtype)

    @pl.when(step >= steps)
    def _():
        total = sum(nt(refs[3 * i][...], refs[3 * i + 2][...]) for i in range(count))
        out[...] = total.astype(out.dtype)


def halves(scal, terms, kind, name):
    rows = terms[0][0].shape[0]
    span = terms[0][1].shape[0]
    steps = span // GROUP
    specs = []
    args = []
    flops = 0
    for a, w_own, w_oth in terms:
        depth = a.shape[1]
        specs += [
            const_spec((rows, depth)),
            pl.BlockSpec((GROUP, depth), lambda j, *_: (jnp.minimum(j, steps - 1), 0)),
            pl.BlockSpec((GROUP, depth), lambda j, *_: (jnp.maximum(j - steps, 0), 0)),
        ]
        args += [a, w_own, w_oth]
        flops += 4 * rows * depth * span
    return call(
        halves_kernel,
        (2 * steps,),
        specs,
        pl.BlockSpec((rows, GROUP), lambda j, s: (0, lax.rem(j + steps * s[0], 2 * steps))),
        jax.ShapeDtypeStruct((rows, 2 * span), kind),
        [],
        flops,
        flops // rows,
        name,
    )(scal, *args)


def swap(x):
    return lax.ppermute(x, "fsdp", [(0, 1), (1, 0)])


def shifted(x, by):
    length = lax.axis_size("tm")
    return lax.ppermute(x, "tm", [(i, (i + by) % length) for i in range(length)])


def ordered(core, mine, other, axis):
    return jnp.where(
        core == 0,
        jnp.concatenate([mine, other], axis=axis),
        jnp.concatenate([other, mine], axis=axis),
    )


def bits_of(axis):
    return [(axis, 1 << b) for b in range((lax.axis_size(axis) - 1).bit_length())]


def across(x, axis, bit):
    return lax.ppermute(x, axis, [(i, i ^ bit) for i in range(lax.axis_size(axis))])


def reduced(buf, order):
    for axis, bit in order:
        n = buf.shape[0] // 2
        side = (lax.axis_index(axis) // bit) % 2
        send = lax.dynamic_slice_in_dim(buf, (1 - side) * n, n, 0)
        keep = lax.dynamic_slice_in_dim(buf, side * n, n, 0)
        got = across(send.astype(bf16), axis, bit)
        buf = (keep.astype(f32) + got.astype(f32)).astype(bf16)
    for axis, bit in reversed(order):
        n = buf.shape[0]
        side = (lax.axis_index(axis) // bit) % 2
        got = across(buf, axis, bit)
        both = jnp.zeros((2 * n,) + buf.shape[1:], bf16)
        both = lax.dynamic_update_slice_in_dim(both, buf, side * n, 0)
        buf = lax.dynamic_update_slice_in_dim(both, got, (1 - side) * n, 0)
    return buf


def summed(grad):
    rep = bits_of("rep")
    tm = bits_of("tm")
    cut = len(rep) // 2
    n = grad.shape[0] // 2
    first = reduced(grad[:n], rep + tm)
    second = reduced(grad[n:], rep[cut:] + rep[:cut] + tm)
    return jnp.concatenate([first, second], axis=0).astype(f32)


def body(
    tokens, in_weight, out_weight, norm_gain, conv_weight, conv_bias, dt_bias, a_log,
    d_skip, gate_gain, lengths, starts, cotangent,
):
    core = lax.axis_index("fsdp")
    tm = lax.axis_index("tm")
    tm_size = lax.axis_size("tm")
    tok = tokens[0]
    upstream = cotangent[0]
    tok_count, d = tok.shape
    half_d = in_weight.shape[0]
    half_in = out_weight.shape[0]
    half_conv = conv_bias.shape[0]
    half_heads = dt_bias.shape[0]

    lo = starts[0] - tm * tok_count
    scal = jnp.stack([core, lo, lo + lengths[0]]).astype(jnp.int32)

    def wide(v):
        return jnp.pad(v, (0, half_conv - v.shape[0]))[None]

    pack = jnp.concatenate(
        [
            conv_weight,
            conv_bias[None],
            wide(gate_gain),
            wide(norm_gain),
            wide(jnp.concatenate([dt_bias, a_log, d_skip])),
        ],
        axis=0,
    ).astype(bf16)
    pack_oth = swap(pack)
    halo = shifted(tok[tok_count - HALO :], 1)
    wu_own = jnp.pad(in_weight[:, DIN:], ((0, 0), (0, LANE - H))).astype(bf16)
    wu_oth = swap(wu_own)
    wz_own = in_weight[:, :DIN].astype(bf16)
    wz_oth = swap(wz_own)
    wo_own = out_weight.astype(bf16)
    wo_oth = swap(wo_own)

    def both(row, length):
        return ordered(core, pack[row, :length], pack_oth[row, :length], 0).astype(f32)

    def both_heads(i):
        part = slice(i * half_heads, (i + 1) * half_heads)
        return ordered(core, pack[7, part], pack_oth[7, part], 0).astype(f32)

    taps = jnp.pad(
        ordered(core, pack[:5], pack_oth[:5], 1).astype(f32), ((0, 3), (0, 0))
    )
    gate_vec = both(5, half_in)
    gain = both(6, half_d)[None]
    skip_vec = jnp.repeat(both_heads(2), P_SIZE)
    vecs = jnp.pad(jnp.stack([gate_vec, skip_vec]), ((0, 6), (0, 0)))
    skip8 = jnp.pad(skip_vec[None], ((0, 7), (0, 0)))
    heads = jnp.pad(
        jnp.stack([both_heads(0), -jnp.exp(both_heads(1))]), ((0, 6), (0, LANE - H))
    )

    normed, u, act, dact, dt, sg, cum, cumt, st = front(
        scal, tok, halo, gain, wu_own, wu_oth, taps, heads
    )
    cumt = cumt[:H].reshape(H // 4, 4, tok_count)
    total = jnp.exp(jnp.repeat(cum[tok_count - 1, :H], P_SIZE))[None]

    def chain(local, by, first):
        pieces = []
        for part in range(2):
            cols = slice(part * (DIN // 2), (part + 1) * (DIN // 2))
            send = local[:, cols].astype(bf16)
            got = None
            for hop in range(tm_size - 1):
                got = shifted(send, by)
                got = jnp.where(tm == first, jnp.zeros_like(got), got)
                if hop < tm_size - 2:
                    send = (local[:, cols] + total[:, cols] * got.astype(f32)).astype(bf16)
            pieces.append(got)
        return jnp.concatenate(pieces, axis=1)

    s_in = chain(st, 1, 0)
    z = splitk(scal, normed[HALO:], wz_own, wz_oth, None, "gate_proj")
    eg = halves(scal, [(upstream, wo_own, wo_oth)], bf16, "grad_gated")
    yloc, s0 = intra(scal, act, dt, cum, cumt)
    gated, ey, ez, r_loc, r_dev, dc_dev, g_loc, gs = gate(
        scal, yloc, act, z, eg, cum, s_in, vecs
    )

    def mine(x, half):
        return lax.dynamic_slice_in_dim(x, core * half, half, 1)

    def theirs(x, half):
        return lax.dynamic_slice_in_dim(x, (1 - core) * half, half, 1)

    def outer(a, b):
        return lax.dot_general(a, b, (((0,), (0,)), ((), ())), preferred_element_type=f32)

    up_oth = swap(upstream)
    normed_oth = swap(theirs(normed, half_d))
    normed_own = mine(normed, half_d)
    gated_oth = swap(theirs(gated, half_in))
    ez_oth = swap(ez)
    g_in = chain(g_loc, -1, tm_size - 1)
    grad_out = outer(mine(gated, half_in), upstream) + outer(gated_oth, up_oth)
    grad_z = outer(normed_own[HALO:], ez) + outer(normed_oth[HALO:], ez_oth)
    grad_out_w = summed(grad_out)
    grad_z_w = summed(grad_z)
    output = splitk(scal, gated, wo_own, wo_oth, tok, "out_proj")
    dxt, db_loc, dc_loc, r2, cq = back(scal, act, dt, cum, cumt, ey, s0)
    eu, er, gconv, ghead = tail(
        scal, act, dact, u, ey, dxt, taps, dt, sg, cum, g_in, s_in, skip8, heads,
        (db_loc, dc_loc, dc_dev, r_loc, r_dev, r2, cq),
    )
    eur = jnp.concatenate([eu, er], axis=1)
    eur_oth = swap(eur)
    grad_u = outer(normed_own, eur) + outer(normed_oth, eur_oth)
    grad_u_w = summed(grad_u)

    ez_ext = jnp.pad(ez, ((HALO, 0), (0, 0)))
    e_normed = halves(
        scal, [(ez_ext, wz_own, wz_oth), (eur, wu_own, wu_oth)], f32, "grad_normed"
    )
    ext_tok = jnp.concatenate([halo, tok], axis=0).astype(f32)
    rs = lax.rsqrt(jnp.mean(ext_tok * ext_tok, axis=-1, keepdims=True) + EPS)
    unit = ext_tok * rs
    scaled = e_normed * gain
    grad_in = rs * (scaled - unit * jnp.mean(scaled * unit, axis=-1, keepdims=True))
    grad_gain = jnp.sum(e_normed * unit, axis=0)
    edge = shifted(grad_in[:HALO], -1)
    edge = jnp.where(tm == tm_size - 1, jnp.zeros_like(edge), edge)
    input_grad = upstream.astype(f32) + grad_in[HALO:]
    input_grad = input_grad.at[tok_count - HALO :].add(edge)

    grad_skip = jnp.sum(gs[1].reshape(H, P_SIZE), axis=1)

    def side(v, half):
        return jnp.stack([v[:half], v[half : 2 * half]])

    def slot(v, half):
        return jnp.pad(side(v, half), ((0, 0), (0, half_conv - half)))[:, None]

    head_grads = jnp.stack([ghead[0, :H], ghead[1, :H], grad_skip])
    head_sides = jnp.stack(
        [head_grads[:, :half_heads].reshape(-1), head_grads[:, half_heads:].reshape(-1)]
    )
    packed = jnp.concatenate(
        [
            gconv[:5].reshape(5, 2, half_conv).transpose(1, 0, 2),
            slot(gs[0], half_in),
            slot(grad_gain, half_d),
            jnp.pad(head_sides, ((0, 0), (0, half_conv - 3 * half_heads)))[:, None],
        ],
        axis=1,
    )
    own = lax.dynamic_index_in_dim(packed, core, 0, keepdims=False)
    small = own + swap(lax.dynamic_index_in_dim(packed, 1 - core, 0, keepdims=False))
    for axis, bit in bits_of("rep") + bits_of("tm"):
        small = small + across(small, axis, bit)

    grad_in_w = jnp.concatenate([grad_z_w, grad_u_w[:, : CONV + H]], axis=1)
    hs = half_heads
    return (
        output[None],
        input_grad[None],
        grad_in_w,
        grad_out_w,
        small[6, :half_d],
        small[:4],
        small[4],
        small[7, :hs],
        small[7, hs : 2 * hs],
        small[7, 2 * hs : 3 * hs],
        small[5, :half_in],
    )


def solution(mesh):
    return jax.shard_map(
        body,
        mesh=mesh,
        in_specs=(
            P(("rep", "fsdp"), "tm", None),
            P("fsdp", None),
            P("fsdp", None),
            P("fsdp"),
            P(None, "fsdp"),
            P("fsdp"),
            P("fsdp"),
            P("fsdp"),
            P("fsdp"),
            P("fsdp"),
            P(("rep", "fsdp")),
            P(("rep", "fsdp")),
            P(("rep", "fsdp"), "tm", None),
        ),
        out_specs=(
            P(("rep", "fsdp"), "tm", None),
            P(("rep", "fsdp"), "tm", None),
            P("fsdp", None),
            P("fsdp", None),
            P("fsdp"),
            P(None, "fsdp"),
            P("fsdp"),
            P("fsdp"),
            P("fsdp"),
            P("fsdp"),
            P("fsdp"),
        ),
        check_vma=False,
    )
```

time: 1170 us -> 571 us (0.49)
  waiting for transfers between devices: 413 us -> 113 us
  matrix products: 220 us -> 18.4 us
  Pallas kernels: 0 us -> 135 us
  blocking collectives: 97.2 us -> 0 us
  local copies, waits for them, and re-layouts: 254 us -> 167 us
  other arithmetic: 117 us -> 43.2 us
  starting transfers between devices: 22.1 us -> 80.4 us
  between operations: 20.2 us -> 3.49 us
    psum x1 -> x0, waiting for transfers between devices: 279 us -> none  [body(): lax.psum((shares[0], shares[1], shares[2], shares[3], shares[4], shares[5...]
    dot_general x37 -> x6, matrix products: 220 us -> 18.4 us  [outer(): lax.dot_general(a, b, (((0,), (0,)), ((), ())), preferred_element_type=f32)]
    pallas_call x0 -> x9, Pallas kernels: none -> 135 us  [the longest x1 25.8 us: front(): call(front_kernel, (groups,), [const_spec((tok_count, d)), const_spec((HA...]
    psum x1 -> x0, blocking collectives: 83.3 us -> none  [body(): lax.psum((shares[0], shares[1], shares[2], shares[3], shares[4], shares[5...]
    ppermute x8 -> x76, starting transfers between devices: 21.9 us -> 80.4 us  [the longest x52 58 us: across(): lax.ppermute(x, axis, [(i, i ^ bit) for i in range(lax.axis_size(axis))])]
    reshape x10 -> x2, local copies, waits for them, and re-layouts: 42.5 us -> 0.67 us  [the longest x1 0.64 us: body(): cumt = cumt[:H].reshape(H // 4, 4, tok_count)]
    reduce_sum x13 -> x3, other arithmetic: 31.6 us -> 3.61 us  [the longest x1 2.44 us: body(): grad_gain = jnp.sum(e_normed * unit, axis=0)]
    reduce_scatter x2 -> x0, waiting for transfers between devices: 27.2 us -> none  [the longest x1 27.2 us: body(): lax.psum_scatter(grad_in_w, 'fsdp', scatter_dimension=0, tiled=True)]
  transfers between devices with their start and end apart: 14 -> 76, of which waited for: 8 -> 33; matrix products, arithmetic and copies ran while one was open for 31% -> 38% of each run, Pallas kernels for 0% -> 24%
where the time goes in v1:
time: 571 us; the launch traced here: 561 us
  local copies, waits for them, and re-layouts  167 us (29%)
  Pallas kernels  135 us (24%)
  waiting for transfers between devices  113 us (20%)
  starting transfers between devices  80.4 us (14%)
  other arithmetic  43.2 us (8%)
  matrix products  18.4 us (3%)
    ppermute x52, waiting for transfers between devices, across(): lax.ppermute(x, axis, [(i, i ^ bit) for i in range(lax.axis_size(axis))])  101 us
    ppermute x52, starting transfers between devices, across(): lax.ppermute(x, axis, [(i, i ^ bit) for i in range(lax.axis_size(axis))])  58 us
    dynamic_update_slice x26, local copies, waits for them, and re-layouts, reduced(): buf = lax.dynamic_update_slice_in_dim(both, got, (1 - side) * n, 0)  53.9 us
    dynamic_update_slice x20, local copies, waits for them, and re-layouts, reduced(): both = lax.dynamic_update_slice_in_dim(both, buf, side * n, 0)  43 us
    pallas_call x1, Pallas kernels, front(): call(front_kernel, (groups,), [const_spec((tok_count, d)), const_spec((HA...  25.8 us
    pallas_call x1, Pallas kernels, tail(): call(tail_kernel, (groups + 1,), [wide, pl.BlockSpec((tok_count, GROUP),...  23.4 us
    ppermute x14, starting transfers between devices, shifted(): lax.ppermute(x, 'tm', [(i, (i + by) % length) for i in range(length)])  21.2 us
    pallas_call x2, Pallas kernels, halves(): call(halves_kernel, (2 * steps,), specs, pl.BlockSpec((rows, GROUP), lamb...  20.8 us
  transfers between devices with their start and end apart: 76, of which 33 were waited for; matrix products, arithmetic and copies ran while one was open for 38% of the time, Pallas kernels for 24%

profile of v1, /device:TPU:0, one launch (start us, length us, event | category | flops | bytes accessed | tf_op | source)
XLA Modules:
  0.0 560.7 jit_solution(17173102040031793783)
XLA Ops:
  6.8 2.7 slice.257
  9.5 2.7 copy.47
  15.0 3.1 collective-permute-start
  18.2 3.8 slice.263
  21.9 3.9 copy.48.w_own.refs_1_
  25.9 3.9 convert_element_type.367.refs_1_.w_own
  49.4 25.8 %front.1 = (bf16[528,1024]{1,0:T(8,128)(2,1)}, bf16[528,2304]{1,0:T(8,128)(2,1)}, bf16[512,2304]{1,0:T(8,128)(2,1)}, bf16[512,2304]{1,0:T(8,128)(2,1)}, f32[512,...) custom-call(s32[3]{0:T(128)} %pad_add_fusion.scal, ...), custom_call_target="tpu_custom_call" | custom-call | flops 2629828608 | bytes 13099008 | tf_op jit(solution)/shard_map/front/pallas_call | solution.py:198
  80.6 7.0 %collective-permute-done.5 = bf16[128,1024]{1,0:T(8,128)(2,1)S(1)} collective-permute-done((bf16[128,1024]{1,0:T(8,128)(2,1)S(1)}, bf16[128,1024]{1,0:T(8,128)(2,1)S(1)}, u32[]{:S(2)}, u32[]{:S(2)}) %collective-permute-start.5) | collective-permute-done | bytes 262176 | tf_op jit(solution)/shard_map/ppermute | solution.py:819
  88.8 9.2 %grad_gated.1.eg = bf16[512,2048]{1,0:T(8,128)(2,1)} custom-call(s32[3]{0:T(128)} %pad_add_fusion.scal, bf16[512,1024]{1,0:T(8,128)(2,1)} %bitcast.67, bf16[1024,1024]{1,0:T(8,128)(2,1)} %convert_element_type.367.refs_1_.w_own, bf16[1024,1024]{1,0:T(8,128)(2,1)} %collective-permute-done.4.refs_2_.w_oth), custom_call_target="tpu_custom_call" | custom-call | flops 2147483648 | bytes 4194304 | tf_op jit(solution)/shard_map/grad_gated/pallas_call | solution.py:800
  103.0 8.8 %gate_proj.1.z = bf16[512,2048]{1,0:T(8,128)(2,1)} custom-call(s32[3]{0:T(128)} %pad_add_fusion.scal, bf16[512,1024]{1,0:T(8,128)(2,1)} %slice.214.a, bf16[512,2048]{1,0:T(8,128)(2,1)} %copy.48.w_own.refs_1_, bf16[512,2048]{1,0:T(8,128)(2,1)} %collective-permute-done.3.w_oth.refs_2_), custom_call_target="tpu_custom_call" | custom-call | flops 2147483648 | bytes 7340032 | tf_op jit(solution)/shard_map/gate_proj/pallas_call | solution.py:754
  112.8 2.9 collective-permute-start.10
  115.7 14.3 %intra.1 = (f32[512,2048]{1,0:T(8,128)}, bf16[4,128,2048]{2,1,0:T(8,128)(2,1)}) custom-call(s32[3]{0:T(128)} %pad_add_fusion.scal, bf16[512,2304]{1,0:T(8,128)(2,1)} %get-tuple-element.51.x.bc.act, bf16[512,2304]{1,0:T(8,128)(2,1)} %get-tuple-element.51.x.bc.act, f32[512,128]{1,0:T(8,128)} %get-tuple-element.52.dt, f32[512,128]{1,0:T(8,128)} %get-tuple-element.53.cum, ...), custom_call_target="tpu_custom_call" | custom-call | flops 805306368 | bytes 8388608 | tf_op jit(solution)/shard_map/intra/pallas_call | solution.py:296
  130.9 16.7 %gate.1 = (bf16[512,2048]{1,0:T(8,128)(2,1)}, bf16[512,2048]{1,0:T(8,128)(2,1)}, bf16[512,2048]{1,0:T(8,128)(2,1)}, f32[512,128]{1,0:T(8,128)}, f32[512,128]{1,0...) custom-call(s32[3]{0:T(128)} %pad_add_fusion.scal, f32[512,2048]{1,0:T(8,128)} %get-tuple-element.55.yloc, ...), custom_call_target="tpu_custom_call" | custom-call | flops 1610612736 | bytes 20971520 | tf_op jit(solution)/shard_map/gate/pallas_call | solution.py:404
  153.4 4.8 collective-permute-done.11
  159.0 3.0 collective-permute-start.12
  162.0 18.2 %back.1 = (bf16[512,2048]{1,0:T(8,128)(2,1)}, f32[512,128]{1,0:T(8,128)}, f32[512,128]{1,0:T(8,128)}, f32[512,128]{1,0:T(8,128)}, f32[8,128]{1,0:T(8,128)}) custom-call(s32[3]{0:T(128)} %pad_add_fusion.scal, bf16[512,2304]{1,0:T(8,128)(2,1)} %get-tuple-element.51.x.bc.act, bf16[512,2304]{1,0:T(8,128)(2,1)} %get-tuple-element.51.x.bc.act, ...), custom_call_target="tpu_custom_call" | custom-call | flops 2147483648 | bytes 8388608 | tf_op jit(solution)/shard_map/back/pallas_call | solution.py:541
  181.1 7.2 %out_proj.1 = bf16[512,1024]{1,0:T(8,128)(2,1)} custom-call(s32[3]{0:T(128)} %pad_add_fusion.scal, bf16[512,2048]{1,0:T(8,128)(2,1)} %get-tuple-element.58.a, bf16[1024,1024]{1,0:T(8,128)(2,1)} %convert_element_type.367.refs_1_.w_own, bf16[1024,1024]{1,0:T(8,128)(2,1)} %collective-permute-done.4.refs_2_.w_oth, bf16[512,1024]{1,0:T(8,128)(2,1)} %bitcast.61), custom_call_target="tpu_custom_call" | custom-call | flops 2147483648 | bytes 7340032 | tf_op jit(solution)/shard_map/out_proj/pallas_call | solution.py:754
  190.4 3.3 pad.64.refs_0_
  194.9 2.9 collective-permute-start.16
  198.8 2.7 fusion.47
  209.3 23.4 %tail.1 = (bf16[528,2304]{1,0:T(8,128)(2,1)}, bf16[528,128]{1,0:T(8,128)(2,1)}, f32[8,2304]{1,0:T(8,128)}, f32[8,128]{1,0:T(8,128)}) custom-call(s32[3]{0:T(128)} %pad_add_fusion.scal, bf16[512,2304]{1,0:T(8,128)(2,1)} %get-tuple-element.51.x.bc.act, bf16[512,2304]{1,0:T(8,128)(2,1)} %get-tuple-element.51.x.bc.act, ...), custom_call_target="tpu_custom_call" | custom-call | flops 1073741824 | bytes 12582912 | tf_op jit(solution)/shard_map/tail/pallas_call | solution.py:676
  233.7 3.3 constant_dynamic-update-slice_fusion.33
  237.6 11.6 %grad_normed.1 = f32[528,1024]{1,0:T(8,128)} custom-call(s32[3]{0:T(128)} %pad_add_fusion.scal, bf16[528,2048]{1,0:T(8,128)(2,1)} %pad.64.refs_0_, bf16[512,2048]{1,0:T(8,128)(2,1)} %copy.48.w_own.refs_1_, bf16[512,2048]{1,0:T(8,128)(2,1)} %collective-permute-done.3.w_oth.refs_2_, bf16[528,2432]{1,0:T(8,128)(2,1)} %constant_dynamic-update-slice_fusion.32.refs_3_, ...), custom_call_target="tpu_custom_call" | custom-call | flops 4844421120 | bytes 9175040 | tf_op jit(solution)/shard_map/grad_normed/pallas_call | solution.py:800
  249.3 2.4 fusion.8
  253.9 3.4 collective-permute-done.72
  267.8 4.2 collective-permute-done.75
  277.8 7.2 %collective-permute-done.56 = bf16[128,1024]{1,0:T(8,128)(2,1)S(1)} collective-permute-done((bf16[128,1024]{1,0:T(8,128)(2,1)S(1)}, bf16[128,1024]{1,0:T(8,128)(2,1)S(1)}, u32[]{:S(2)}, u32[]{:S(2)}) %collective-permute-start.56) | collective-permute-done | bytes 262176 | tf_op jit(solution)/shard_map/ppermute | solution.py:835
  287.4 4.2 collective-permute-done.57
  294.8 4.9 collective-permute-done.58
  302.8 2.3 collective-permute-done.59
  305.2 2.2 collective-permute-done.67
  308.0 3.1 fusion.12
  311.1 3.0 convolution_add_fusion.1
  320.8 10.6 %collective-permute-done.61 = bf16[128,1024]{1,0:T(8,128)(2,1)S(1)} collective-permute-done((bf16[128,1024]{1,0:T(8,128)(2,1)S(1)}, bf16[128,1024]{1,0:T(8,128)(2,1)S(1)}, u32[]{:S(2)}, u32[]{:S(2)}) %collective-permute-start.61) | collective-permute-done | bytes 262176 | tf_op jit(solution)/shard_map/ppermute | solution.py:835
  338.1 10.7 %collective-permute-done.21 = bf16[64,2048]{1,0:T(8,128)(2,1)S(1)} collective-permute-done((bf16[64,2048]{1,0:T(8,128)(2,1)S(1)}, bf16[64,2048]{1,0:T(8,128)(2,1)S(1)}, u32[]{:S(2)}, u32[]{:S(2)}) %collective-permute-start.21) | collective-permute-done | bytes 262176 | tf_op jit(solution)/shard_map/ppermute | solution.py:835
  351.1 3.0 collective-permute-done.22
  354.2 2.8 collective-permute-start.23
  359.7 2.6 collective-permute-start.24
  364.2 5.4 dynamic_update_slice.144
  370.6 6.1 %dynamic_update_slice.145 = bf16[32,2048]{0,1:T(8,128)(2,1)} dynamic-update-slice(bf16[32,2048]{0,1:T(8,128)(2,1)} %dynamic_update_slice.144, bf16[16,2048]{0,1:T(8,128)(2,1)} %copy.35, s32[]{:T(128)S(6)} %select_n.496, s32[]{:T(128)} %constant.310.clone.1) | dynamic-update-slice | bytes 131076 | tf_op jit(solution)/shard_map/dynamic_update_slice | solution.py:852
  379.7 5.2 dynamic_update_slice.146
  386.9 6.1 %dynamic_update_slice.147 = bf16[64,2048]{0,1:T(8,128)(2,1)} dynamic-update-slice(bf16[64,2048]{0,1:T(8,128)(2,1)} %dynamic_update_slice.146, bf16[32,2048]{0,1:T(8,128)(2,1)} %collective-permute-done.25, s32[]{:T(128)S(6)} %select_n.492, s32[]{:T(128)} %constant.310.clone.1) | dynamic-update-slice | bytes 262148 | tf_op jit(solution)/shard_map/dynamic_update_slice | solution.py:852
  398.1 5.2 dynamic_update_slice.152
  404.3 6.1 %dynamic_update_slice.153 = bf16[32,2048]{0,1:T(8,128)(2,1)} dynamic-update-slice(bf16[32,2048]{0,1:T(8,128)(2,1)} %dynamic_update_slice.152, bf16[16,2048]{0,1:T(8,128)(2,1)} %copy.37, s32[]{:T(128)S(6)} %select_n.496, s32[]{:T(128)} %constant.310.clone.1) | dynamic-update-slice | bytes 131076 | tf_op jit(solution)/shard_map/dynamic_update_slice | solution.py:852
  410.4 2.5 maximum_convert_fusion
  413.7 5.2 dynamic_update_slice.154
  419.8 5.0 dynamic_update_slice.148
  424.8 6.1 %dynamic_update_slice.155 = bf16[64,2048]{0,1:T(8,128)(2,1)} dynamic-update-slice(bf16[64,2048]{0,1:T(8,128)(2,1)} %dynamic_update_slice.154, bf16[32,2048]{0,1:T(8,128)(2,1)} %collective-permute-done.33, s32[]{:T(128)S(6)} %select_n.492, s32[]{:T(128)} %constant.310.clone.1) | dynamic-update-slice | bytes 262148 | tf_op jit(solution)/shard_map/dynamic_update_slice | solution.py:852
  431.0 4.7 dynamic_update_slice.156
  435.7 6.3 %dynamic_update_slice.149 = bf16[128,2048]{0,1:T(8,128)(2,1)} dynamic-update-slice(bf16[128,2048]{0,1:T(8,128)(2,1)} %dynamic_update_slice.148, bf16[64,2048]{0,1:T(8,128)(2,1)} %collective-permute-done.26, s32[]{:T(128)S(6)} %select_n.489, s32[]{:T(128)} %constant.310.clone.1) | dynamic-update-slice | bytes 524292 | tf_op jit(solution)/shard_map/dynamic_update_slice | solution.py:852
  442.0 3.1 collective-permute-start.27
  445.1 4.1 fusion.46
  449.2 4.1 convolution_add_fusion
  457.3 6.3 %dynamic_update_slice.157 = bf16[128,2048]{0,1:T(8,128)(2,1)} dynamic-update-slice(bf16[128,2048]{0,1:T(8,128)(2,1)} %copy-done.18, bf16[64,2048]{0,1:T(8,128)(2,1)} %collective-permute-done.34, s32[]{:T(128)S(6)} %select_n.500, s32[]{:T(128)} %constant.310.clone.1) | dynamic-update-slice | bytes 524292 | tf_op jit(solution)/shard_map/dynamic_update_slice | solution.py:852
  470.1 14.6 %collective-permute-done.45 = bf16[128,2432]{1,0:T(8,128)(2,1)S(1)} collective-permute-done((bf16[128,2432]{1,0:T(8,128)(2,1)S(1)}, bf16[128,2432]{1,0:T(8,128)(2,1)S(1)}, u32[]{:S(2)}, u32[]{:S(2)}) %collective-permute-start.45) | collective-permute-done | bytes 622624 | tf_op jit(solution)/shard_map/ppermute | solution.py:835
  496.4 2.5 collective-permute-done.47
  507.4 2.4 collective-permute-done.49
  518.9 3.4 dynamic_update_slice.164
  522.4 3.4 dynamic_update_slice.172
  527.1 5.5 dynamic_update_slice.165
  532.6 3.2 collective-permute-start.44
  537.2 5.5 dynamic_update_slice.173
  545.4 7.5 %collective-permute-done.52 = bf16[128,2432]{0,1:T(8,128)(2,1)S(1)} collective-permute-done((bf16[128,2432]{0,1:T(8,128)(2,1)S(1)}, bf16[128,2432]{0,1:T(8,128)(2,1)S(1)}, u32[]{:S(2)}, u32[]{:S(2)}) %collective-permute-start.52) | collective-permute-done | bytes 622624 | tf_op jit(solution)/shard_map/ppermute | solution.py:835
  553.1 7.4 %fusion.1 = f32[512,4384]{0,1:T(8,128)} fusion(bf16[256,2432]{0,1:T(8,128)(2,1)S(1)} %constant_dynamic-update-slice_fusion.16, bf16[256,2432]{0,1:T(8,128)(2,1)S(1)} %constant_dynamic-update-slice_fusion.22, bf16[256,2048]{0,1:T(8,128)(2,1)} %constant_dynamic-update-slice_fusion.28, bf16[256,2048]{0,1:T(8,128)(2,1)S(1)} %constant_dynamic-update-slice_fusion.30), kind=kLoop, calls=%fused_computation.3 | loop fusion | flops 17956864 | bytes 13565952 | tf_op jit(solution)/shard_map/concatenate | solution.py:1024
  (385 shorter events, 168.5 us)
Async XLA Ops:
  6.2 29.1 %collective-permute-start.1 = (bf16[8,1152]{1,0:T(8,128)(2,1)}, bf16[8,1152]{1,0:T(8,128)(2,1)}, u32[]{:S(2)}, u32[]{:S(2)}) collective-permute-start(bf16[8,1152]{1,0:T(8,128)(2,1)} %concatenate.146), channel_id=1, source_target_pairs={{0,4},{4,0},{1,5},{5,1},{2,6},{6,2},{3,7},{7,3},{8,12},{12,8},{9,1... | collective-permute-start | bytes 55304 | tf_op jit(solution)/shard_map/ppermute | solution.py:814
  14.2 35.3 %collective-permute-start.2 = (bf16[512,2432]{1,0:T(8,128)(2,1)S(1)}, bf16[512,2432]{1,0:T(8,128)(2,1)}, u32[]{:S(2)}, u32[]{:S(2)}) collective-permute-start(bf16[512,2432]{1,0:T(8,128)(2,1)S(1)} %pad.59.w_own.r_own.refs_4_), channel_id=1, source_target_pairs={{0,4},{4,0},{1,5},{5,1},{2,6},{6,2},{3,7},{7,3},{8,12},{12,8},{9,1... | collective-permute-start | bytes 7471112 | tf_op jit(solution)/shard_map/ppermute | solution.py:814
  15.0 33.3 %collective-permute-start = (bf16[16,1024]{1,0:T(8,128)(2,1)}, bf16[16,1024]{1,0:T(8,128)(2,1)}, u32[]{:S(2)}, u32[]{:S(2)}) collective-permute-start(bf16[16,1024]{1,0:T(8,128)(2,1)} %slice_bitcast_fusion), channel_id=1, source_target_pairs={{0,1},{1,2},{2,3},{3,0},{4,5},{5,6},{6,7},{7,4},{8,9},{9,10},{10,1... | collective-permute-start | bytes 98312 | tf_op jit(solution)/shard_map/ppermute | solution.py:819
  25.9 77.1 %collective-permute-start.3 = (bf16[512,2048]{1,0:T(8,128)(2,1)}, bf16[512,2048]{1,0:T(8,128)(2,1)}, u32[]{:S(2)}, u32[]{:S(2)}) collective-permute-start(bf16[512,2048]{1,0:T(8,128)(2,1)} %copy.48.w_own.refs_1_), channel_id=1, source_target_pairs={{0,4},{4,0},{1,5},{5,1},{2,6},{6,2},{3,7},{7,3},{8,12},{12,8},{9,1... | collective-permute-start | bytes 6291464 | tf_op jit(solution)/shard_map/ppermute | solution.py:814
  29.8 59.0 %collective-permute-start.4 = (bf16[1024,1024]{1,0:T(8,128)(2,1)}, bf16[1024,1024]{1,0:T(8,128)(2,1)}, u32[]{:S(2)}, u32[]{:S(2)}) collective-permute-start(bf16[1024,1024]{1,0:T(8,128)(2,1)} %convert_element_type.367.refs_1_.w_own), channel_id=1, source_target_pairs={{0,4},{4,0},{1,5},{5,1},{2,6},{6,2},{3,7},{7,3},{8,12},{12,8},{9,1... | collective-permute-start | bytes 6291464 | tf_op jit(solution)/shard_map/ppermute | solution.py:814
  35.4 163.4 %collective-permute-start.54 = (bf16[512,1024]{1,0:T(8,128)(2,1)}, bf16[512,1024]{1,0:T(8,128)(2,1)}, u32[]{:S(2)}, u32[]{:S(2)}) collective-permute-start(bf16[512,1024]{1,0:T(8,128)(2,1)} %bitcast.66), channel_id=1, source_target_pairs={{0,4},{4,0},{1,5},{5,1},{2,6},{6,2},{3,7},{7,3},{8,12},{12,8},{9,1... | collective-permute-start | bytes 3145736 | tf_op jit(solution)/shard_map/ppermute | solution.py:814
  76.6 11.0 %collective-permute-start.5 = (bf16[128,1024]{1,0:T(8,128)(2,1)S(1)}, bf16[128,1024]{1,0:T(8,128)(2,1)S(1)}, u32[]{:S(2)}, u32[]{:S(2)}) collective-permute-start(bf16[128,1024]{1,0:T(8,128)(2,1)S(1)} %get-tuple-element.101), channel_id=1, source_target_pairs={{0,1},{1,2},{2,3},{3,0},{4,5},{5,6},{6,7},{7,4},{8,9},{9,10},{10,1... | collective-permute-start | bytes 786440 | tf_op jit(solution)/shard_map/ppermute | solution.py:819
  79.0 19.0 %collective-permute-start.8 = (bf16[128,1024]{1,0:T(8,128)(2,1)S(1)}, bf16[128,1024]{1,0:T(8,128)(2,1)S(1)}, u32[]{:S(2)}, u32[]{:S(2)}) collective-permute-start(bf16[128,1024]{1,0:T(8,128)(2,1)S(1)} %get-tuple-element.102), channel_id=1, source_target_pairs={{0,1},{1,2},{2,3},{3,0},{4,5},{5,6},{6,7},{7,4},{8,9},{9,10},{10,1... | collective-permute-start | bytes 786440 | tf_op jit(solution)/shard_map/ppermute | solution.py:819
  88.7 9.6 %collective-permute-start.6 = (bf16[128,1024]{1,0:T(8,128)(2,1)S(1)}, bf16[128,1024]{1,0:T(8,128)(2,1)S(1)}, u32[]{:S(2)}, u32[]{:S(2)}) collective-permute-start(bf16[128,1024]{1,0:T(8,128)(2,1)S(1)} %add_convert_fusion.19), channel_id=1, source_target_pairs={{0,1},{1,2},{2,3},{3,0},{4,5},{5,6},{6,7},{7,4},{8,9},{9,10},{10,1... | collective-permute-start | bytes 786440 | tf_op jit(solution)/shard_map/ppermute | solution.py:819
  98.5 14.2 %collective-permute-start.9 = (bf16[128,1024]{1,0:T(8,128)(2,1)S(1)}, bf16[128,1024]{1,0:T(8,128)(2,1)S(1)}, u32[]{:S(2)}, u32[]{:S(2)}) collective-permute-start(bf16[128,1024]{1,0:T(8,128)(2,1)S(1)} %get-tuple-element.100), channel_id=1, source_target_pairs={{0,1},{1,2},{2,3},{3,0},{4,5},{5,6},{6,7},{7,4},{8,9},{9,10},{10,1... | collective-permute-start | bytes 786440 | tf_op jit(solution)/shard_map/ppermute | solution.py:819
  102.9 205.0 %collective-permute-start.18 = (bf16[528,512]{1,0:T(8,128)(2,1)}, bf16[528,512]{1,0:T(8,128)(2,1)}, u32[]{:S(2)}, u32[]{:S(2)}) collective-permute-start(bf16[528,512]{1,0:T(8,128)(2,1)} %constant_dynamic-slice_fusion.21), channel_id=1, source_target_pairs={{0,4},{4,0},{1,5},{5,1},{2,6},{6,2},{3,7},{7,3},{8,12},{12,8},{9,1... | collective-permute-start | bytes 1622024 | tf_op jit(solution)/shard_map/ppermute | solution.py:814
  111.7 18.2 %collective-permute-start.7 = (bf16[128,1024]{1,0:T(8,128)(2,1)S(1)}, bf16[128,1024]{1,0:T(8,128)(2,1)S(1)}, u32[]{:S(2)}, u32[]{:S(2)}) collective-permute-start(bf16[128,1024]{1,0:T(8,128)(2,1)S(1)} %get-tuple-element.99), channel_id=1, source_target_pairs={{0,1},{1,2},{2,3},{3,0},{4,5},{5,6},{6,7},{7,4},{8,9},{9,10},{10,1... | collective-permute-start | bytes 786440 | tf_op jit(solution)/shard_map/ppermute | solution.py:819
  112.8 17.2 %collective-permute-start.10 = (bf16[128,1024]{1,0:T(8,128)(2,1)S(1)}, bf16[128,1024]{1,0:T(8,128)(2,1)S(1)}, u32[]{:S(2)}, u32[]{:S(2)}) collective-permute-start(bf16[128,1024]{1,0:T(8,128)(2,1)S(1)} %add_convert_fusion.16), channel_id=1, source_target_pairs={{0,1},{1,2},{2,3},{3,0},{4,5},{5,6},{6,7},{7,4},{8,9},{9,10},{10,1... | collective-permute-start | bytes 786440 | tf_op jit(solution)/shard_map/ppermute | solution.py:819
  149.0 9.2 %collective-permute-start.11 = (bf16[128,1024]{1,0:T(8,128)(2,1)S(1)}, bf16[128,1024]{1,0:T(8,128)(2,1)S(1)}, u32[]{:S(2)}, u32[]{:S(2)}) collective-permute-start(bf16[128,1024]{1,0:T(8,128)(2,1)S(1)} %get-tuple-element.97), channel_id=1, source_target_pairs={{0,3},{1,0},{2,1},{3,2},{4,7},{5,4},{6,5},{7,6},{8,11},{9,8},{10,9... | collective-permute-start | bytes 786440 | tf_op jit(solution)/shard_map/ppermute | solution.py:819
  150.2 30.0 %collective-permute-start.14 = (bf16[128,1024]{1,0:T(8,128)(2,1)S(1)}, bf16[128,1024]{1,0:T(8,128)(2,1)S(1)}, u32[]{:S(2)}, u32[]{:S(2)}) collective-permute-start(bf16[128,1024]{1,0:T(8,128)(2,1)S(1)} %get-tuple-element.98), channel_id=1, source_target_pairs={{0,3},{1,0},{2,1},{3,2},{4,7},{5,4},{6,5},{7,6},{8,11},{9,8},{10,9... | collective-permute-start | bytes 786440 | tf_op jit(solution)/shard_map/ppermute | solution.py:819
  152.6 46.2 %collective-permute-start.53 = (bf16[512,1024]{1,0:T(8,128)(2,1)S(1)}, bf16[512,1024]{1,0:T(8,128)(2,1)S(1)}, u32[]{:S(2)}, u32[]{:S(2)}) collective-permute-start(bf16[512,1024]{1,0:T(8,128)(2,1)S(1)} %constant_dynamic-slice_fusion.8), channel_id=1, source_target_pairs={{0,4},{4,0},{1,5},{5,1},{2,6},{6,2},{3,7},{7,3},{8,12},{12,8},{9,1... | collective-permute-start | bytes 3145736 | tf_op jit(solution)/shard_map/ppermute | solution.py:814
  159.0 21.2 %collective-permute-start.12 = (bf16[128,1024]{1,0:T(8,128)(2,1)}, bf16[128,1024]{1,0:T(8,128)(2,1)S(1)}, u32[]{:S(2)}, u32[]{:S(2)}) collective-permute-start(bf16[128,1024]{1,0:T(8,128)(2,1)} %add_convert_fusion.15), channel_id=1, source_target_pairs={{0,3},{1,0},{2,1},{3,2},{4,7},{5,4},{6,5},{7,6},{8,11},{9,8},{10,9... | collective-permute-start | bytes 786440 | tf_op jit(solution)/shard_map/ppermute | solution.py:819
  181.1 12.5 %collective-permute-start.15 = (bf16[128,1024]{1,0:T(8,128)(2,1)}, bf16[128,1024]{1,0:T(8,128)(2,1)}, u32[]{:S(2)}, u32[]{:S(2)}) collective-permute-start(bf16[128,1024]{1,0:T(8,128)(2,1)} %get-tuple-element.96), channel_id=1, source_target_pairs={{0,3},{1,0},{2,1},{3,2},{4,7},{5,4},{6,5},{7,6},{8,11},{9,8},{10,9... | collective-permute-start | bytes 786440 | tf_op jit(solution)/shard_map/ppermute | solution.py:819
  188.4 6.5 %collective-permute-start.13 = (bf16[128,1024]{1,0:T(8,128)(2,1)S(1)}, bf16[128,1024]{1,0:T(8,128)(2,1)}, u32[]{:S(2)}, u32[]{:S(2)}) collective-permute-start(bf16[128,1024]{1,0:T(8,128)(2,1)S(1)} %get-tuple-element.95), channel_id=1, source_target_pairs={{0,3},{1,0},{2,1},{3,2},{4,7},{5,4},{6,5},{7,6},{8,11},{9,8},{10,9... | collective-permute-start | bytes 786440 | tf_op jit(solution)/shard_map/ppermute | solution.py:819
  193.7 114.3 %collective-permute-start.19 = (bf16[512,2048]{1,0:T(8,128)(2,1)}, bf16[512,2048]{1,0:T(8,128)(2,1)}, u32[]{:S(2)}, u32[]{:S(2)}) collective-permute-start(bf16[512,2048]{1,0:T(8,128)(2,1)} %get-tuple-element.59), channel_id=1, source_target_pairs={{0,4},{4,0},{1,5},{5,1},{2,6},{6,2},{3,7},{7,3},{8,12},{12,8},{9,1... | collective-permute-start | bytes 6291464 | tf_op jit(solution)/shard_map/ppermute | solution.py:814
  194.9 13.6 %collective-permute-start.16 = (bf16[128,1024]{1,0:T(8,128)(2,1)S(1)}, bf16[128,1024]{1,0:T(8,128)(2,1)S(1)}, u32[]{:S(2)}, u32[]{:S(2)}) collective-permute-start(bf16[128,1024]{1,0:T(8,128)(2,1)S(1)} %add_convert_fusion.12), channel_id=1, source_target_pairs={{0,3},{1,0},{2,1},{3,2},{4,7},{5,4},{6,5},{7,6},{8,11},{9,8},{10,9... | collective-permute-start | bytes 786440 | tf_op jit(solution)/shard_map/ppermute | solution.py:819
  206.9 68.1 %collective-permute-start.55 = (bf16[256,1024]{1,0:T(8,128)(2,1)}, bf16[256,1024]{1,0:T(8,128)(2,1)}, u32[]{:S(2)}, u32[]{:S(2)}) collective-permute-start(bf16[256,1024]{1,0:T(8,128)(2,1)} %dynamic-slice_convert_fusion.3), channel_id=1, source_target_pairs={{0,8},{8,0},{16,24},{24,16},{1,9},{9,1},{17,25},{25,17},{2,10},{10... | collective-permute-start | bytes 1572872 | tf_op jit(solution)/shard_map/ppermute | solution.py:835
  260.2 6.7 %collective-permute-start.17 = (f32[16,1024]{1,0:T(8,128)S(1)}, f32[16,1024]{1,0:T(8,128)S(1)}, u32[]{:S(2)}, u32[]{:S(2)}) collective-permute-start(f32[16,1024]{1,0:T(8,128)S(1)} %slice.272), channel_id=1, source_target_pairs={{0,3},{1,0},{2,1},{3,2},{4,7},{5,4},{6,5},{7,6},{8,11},{9,8},{10,9... | collective-permute-start | bytes 196616 | tf_op jit(solution)/shard_map/ppermute | solution.py:819
  265.3 11.7 %collective-permute-start.63 = (bf16[256,1024]{1,0:T(8,128)(2,1)S(1)}, bf16[256,1024]{1,0:T(8,128)(2,1)S(1)}, u32[]{:S(2)}, u32[]{:S(2)}) collective-permute-start(bf16[256,1024]{1,0:T(8,128)(2,1)S(1)} %dynamic-slice_convert_fusion.2), channel_id=1, source_target_pairs={{0,16},{8,24},{16,0},{24,8},{1,17},{9,25},{17,1},{25,9},{2,18},{10... | collective-permute-start | bytes 1572872 | tf_op jit(solution)/shard_map/ppermute | solution.py:835
  272.0 173.1 %collective-permute-start.36 = (bf16[528,2432]{1,0:T(8,128)(2,1)}, bf16[528,2432]{1,0:T(8,128)(2,1)}, u32[]{:S(2)}, u32[]{:S(2)}) collective-permute-start(bf16[528,2432]{1,0:T(8,128)(2,1)} %constant_dynamic-update-slice_fusion.32.refs_3_), channel_id=1, source_target_pairs={{0,4},{4,0},{1,5},{5,1},{2,6},{6,2},{3,7},{7,3},{8,12},{12,8},{9,1... | collective-permute-start | bytes 7704584 | tf_op jit(solution)/shard_map/ppermute | solution.py:814
  276.3 8.8 %collective-permute-start.56 = (bf16[128,1024]{1,0:T(8,128)(2,1)S(1)}, bf16[128,1024]{1,0:T(8,128)(2,1)S(1)}, u32[]{:S(2)}, u32[]{:S(2)}) collective-permute-start(bf16[128,1024]{1,0:T(8,128)(2,1)S(1)} %constant_dynamic-slice_fusion.7), channel_id=1, source_target_pairs={{0,16},{8,24},{16,0},{24,8},{1,17},{9,25},{17,1},{25,9},{2,18},{10... | collective-permute-start | bytes 786440 | tf_op jit(solution)/shard_map/ppermute | solution.py:835
  277.2 8.1 %collective-permute-start.64 = (bf16[128,1024]{1,0:T(8,128)(2,1)S(1)}, bf16[128,1024]{1,0:T(8,128)(2,1)S(1)}, u32[]{:S(2)}, u32[]{:S(2)}) collective-permute-start(bf16[128,1024]{1,0:T(8,128)(2,1)S(1)} %constant_dynamic-slice_fusion.4), channel_id=1, source_target_pairs={{0,8},{8,0},{16,24},{24,16},{1,9},{9,1},{17,25},{25,17},{2,10},{10... | collective-permute-start | bytes 786440 | tf_op jit(solution)/shard_map/ppermute | solution.py:835
  285.1 6.4 %collective-permute-start.57 = (bf16[64,1024]{1,0:T(8,128)(2,1)S(1)}, bf16[64,1024]{1,0:T(8,128)(2,1)S(1)}, u32[]{:S(2)}, u32[]{:S(2)}) collective-permute-start(bf16[64,1024]{1,0:T(8,128)(2,1)S(1)} %constant_dynamic-slice_fusion.6), channel_id=1, source_target_pairs={{0,1},{1,0},{2,3},{3,2},{4,5},{5,4},{6,7},{7,6},{8,9},{9,8},{10,11... | collective-permute-start | bytes 393224 | tf_op jit(solution)/shard_map/ppermute | solution.py:835
  285.5 8.0 %collective-permute-start.65 = (bf16[64,1024]{1,0:T(8,128)(2,1)S(1)}, bf16[64,1024]{1,0:T(8,128)(2,1)S(1)}, u32[]{:S(2)}, u32[]{:S(2)}) collective-permute-start(bf16[64,1024]{1,0:T(8,128)(2,1)S(1)} %constant_dynamic-slice_fusion.3), channel_id=1, source_target_pairs={{0,1},{1,0},{2,3},{3,2},{4,5},{5,4},{6,7},{7,6},{8,9},{9,8},{10,11... | collective-permute-start | bytes 393224 | tf_op jit(solution)/shard_map/ppermute | solution.py:835
  291.6 8.0 %collective-permute-start.58 = (bf16[32,1024]{1,0:T(8,128)(2,1)S(1)}, bf16[32,1024]{1,0:T(8,128)(2,1)S(1)}, u32[]{:S(2)}, u32[]{:S(2)}) collective-permute-start(bf16[32,1024]{1,0:T(8,128)(2,1)S(1)} %constant_dynamic-slice_fusion.5), channel_id=1, source_target_pairs={{0,2},{1,3},{2,0},{3,1},{4,6},{5,7},{6,4},{7,5},{8,10},{9,11},{10,... | collective-permute-start | bytes 196616 | tf_op jit(solution)/shard_map/ppermute | solution.py:835
  293.5 8.1 %collective-permute-start.66 = (bf16[32,1024]{1,0:T(8,128)(2,1)S(1)}, bf16[32,1024]{1,0:T(8,128)(2,1)S(1)}, u32[]{:S(2)}, u32[]{:S(2)}) collective-permute-start(bf16[32,1024]{1,0:T(8,128)(2,1)S(1)} %constant_dynamic-slice_fusion.2), channel_id=1, source_target_pairs={{0,2},{1,3},{2,0},{3,1},{4,6},{5,7},{6,4},{7,5},{8,10},{9,11},{10,... | collective-permute-start | bytes 196616 | tf_op jit(solution)/shard_map/ppermute | solution.py:835
  301.7 5.7 %collective-permute-start.67 = (bf16[32,1024]{1,0:T(8,128)(2,1)S(1)}, bf16[32,1024]{1,0:T(8,128)(2,1)S(1)}, u32[]{:S(2)}, u32[]{:S(2)}) collective-permute-start(bf16[32,1024]{1,0:T(8,128)(2,1)S(1)} %get-tuple-element.84), channel_id=1, source_target_pairs={{0,2},{1,3},{2,0},{3,1},{4,6},{5,7},{6,4},{7,5},{8,10},{9,11},{10,... | collective-permute-start | bytes 196616 | tf_op jit(solution)/shard_map/ppermute | solution.py:835
  305.1 10.6 %collective-permute-start.60 = (bf16[64,1024]{1,0:T(8,128)(2,1)S(1)}, bf16[64,1024]{1,0:T(8,128)(2,1)S(1)}, u32[]{:S(2)}, u32[]{:S(2)}) collective-permute-start(bf16[64,1024]{1,0:T(8,128)(2,1)S(1)} %constant_dynamic-update-slice_fusion.14), channel_id=1, source_target_pairs={{0,1},{1,0},{2,3},{3,2},{4,5},{5,4},{6,7},{7,6},{8,9},{9,8},{10,11... | collective-permute-start | bytes 393224 | tf_op jit(solution)/shard_map/ppermute | solution.py:835
  307.4 10.1 %collective-permute-start.68 = (bf16[64,1024]{1,0:T(8,128)(2,1)S(1)}, bf16[64,1024]{1,0:T(8,128)(2,1)S(1)}, u32[]{:S(2)}, u32[]{:S(2)}) collective-permute-start(bf16[64,1024]{1,0:T(8,128)(2,1)S(1)} %constant_dynamic-update-slice_fusion.6), channel_id=1, source_target_pairs={{0,1},{1,0},{2,3},{3,2},{4,5},{5,4},{6,7},{7,6},{8,9},{9,8},{10,11... | collective-permute-start | bytes 393224 | tf_op jit(solution)/shard_map/ppermute | solution.py:835
  314.7 21.1 %collective-permute-start.20 = (bf16[128,2048]{1,0:T(8,128)(2,1)S(1)}, bf16[128,2048]{1,0:T(8,128)(2,1)S(1)}, u32[]{:S(2)}, u32[]{:S(2)}) collective-permute-start(bf16[128,2048]{1,0:T(8,128)(2,1)S(1)} %dynamic-slice_convert_fusion.5), channel_id=1, source_target_pairs={{0,8},{8,0},{16,24},{24,16},{1,9},{9,1},{17,25},{25,17},{2,10},{10... | collective-permute-start | bytes 1572872 | tf_op jit(solution)/shard_map/ppermute | solution.py:835
  315.3 22.4 %collective-permute-start.28 = (bf16[128,2048]{1,0:T(8,128)(2,1)S(1)}, bf16[128,2048]{1,0:T(8,128)(2,1)S(1)}, u32[]{:S(2)}, u32[]{:S(2)}) collective-permute-start(bf16[128,2048]{1,0:T(8,128)(2,1)S(1)} %dynamic-slice_convert_fusion.4), channel_id=1, source_target_pairs={{0,16},{8,24},{16,0},{24,8},{1,17},{9,25},{17,1},{25,9},{2,18},{10... | collective-permute-start | bytes 1572872 | tf_op jit(solution)/shard_map/ppermute | solution.py:835
  315.8 15.6 %collective-permute-start.61 = (bf16[128,1024]{1,0:T(8,128)(2,1)S(1)}, bf16[128,1024]{1,0:T(8,128)(2,1)S(1)}, u32[]{:S(2)}, u32[]{:S(2)}) collective-permute-start(bf16[128,1024]{1,0:T(8,128)(2,1)S(1)} %constant_dynamic-update-slice_fusion.12), channel_id=1, source_target_pairs={{0,16},{8,24},{16,0},{24,8},{1,17},{9,25},{17,1},{25,9},{2,18},{10... | collective-permute-start | bytes 786440 | tf_op jit(solution)/shard_map/ppermute | solution.py:835
  317.5 15.9 %collective-permute-start.69 = (bf16[128,1024]{1,0:T(8,128)(2,1)S(1)}, bf16[128,1024]{1,0:T(8,128)(2,1)S(1)}, u32[]{:S(2)}, u32[]{:S(2)}) collective-permute-start(bf16[128,1024]{1,0:T(8,128)(2,1)S(1)} %constant_dynamic-update-slice_fusion.4), channel_id=1, source_target_pairs={{0,8},{8,0},{16,24},{24,16},{1,9},{9,1},{17,25},{25,17},{2,10},{10... | collective-permute-start | bytes 786440 | tf_op jit(solution)/shard_map/ppermute | solution.py:835
  331.4 30.8 %collective-permute-start.62 = (bf16[256,1024]{1,0:T(8,128)(2,1)S(1)}, bf16[256,1024]{1,0:T(8,128)(2,1)S(1)}, u32[]{:S(2)}, u32[]{:S(2)}) collective-permute-start(bf16[256,1024]{1,0:T(8,128)(2,1)S(1)} %constant_dynamic-update-slice_fusion.10), channel_id=1, source_target_pairs={{0,8},{8,0},{16,24},{24,16},{1,9},{9,1},{17,25},{25,17},{2,10},{10... | collective-permute-start | bytes 1572872 | tf_op jit(solution)/shard_map/ppermute | solution.py:835
  334.1 61.0 %collective-permute-start.70 = (bf16[256,1024]{1,0:T(8,128)(2,1)}, bf16[256,1024]{1,0:T(8,128)(2,1)}, u32[]{:S(2)}, u32[]{:S(2)}) collective-permute-start(bf16[256,1024]{1,0:T(8,128)(2,1)} %constant_dynamic-update-slice_fusion.2), channel_id=1, source_target_pairs={{0,16},{8,24},{16,0},{24,8},{1,17},{9,25},{17,1},{25,9},{2,18},{10... | collective-permute-start | bytes 1572872 | tf_op jit(solution)/shard_map/ppermute | solution.py:835
  335.9 12.8 %collective-permute-start.21 = (bf16[64,2048]{1,0:T(8,128)(2,1)S(1)}, bf16[64,2048]{1,0:T(8,128)(2,1)S(1)}, u32[]{:S(2)}, u32[]{:S(2)}) collective-permute-start(bf16[64,2048]{1,0:T(8,128)(2,1)S(1)} %constant_dynamic-slice_fusion.20), channel_id=1, source_target_pairs={{0,16},{8,24},{16,0},{24,8},{1,17},{9,25},{17,1},{25,9},{2,18},{10... | collective-permute-start | bytes 786440 | tf_op jit(solution)/shard_map/ppermute | solution.py:835
  337.9 12.8 %collective-permute-start.29 = (bf16[64,2048]{1,0:T(8,128)(2,1)S(1)}, bf16[64,2048]{1,0:T(8,128)(2,1)S(1)}, u32[]{:S(2)}, u32[]{:S(2)}) collective-permute-start(bf16[64,2048]{1,0:T(8,128)(2,1)S(1)} %constant_dynamic-slice_fusion.17), channel_id=1, source_target_pairs={{0,8},{8,0},{16,24},{24,16},{1,9},{9,1},{17,25},{25,17},{2,10},{10... | collective-permute-start | bytes 786440 | tf_op jit(solution)/shard_map/ppermute | solution.py:835
  350.8 6.2 %collective-permute-start.30 = (bf16[32,2048]{1,0:T(8,128)(2,1)S(1)}, bf16[32,2048]{1,0:T(8,128)(2,1)S(1)}, u32[]{:S(2)}, u32[]{:S(2)}) collective-permute-start(bf16[32,2048]{1,0:T(8,128)(2,1)S(1)} %constant_dynamic-slice_fusion.16), channel_id=1, source_target_pairs={{0,1},{1,0},{2,3},{3,2},{4,5},{5,4},{6,7},{7,6},{8,9},{9,8},{10,11... | collective-permute-start | bytes 393224 | tf_op jit(solution)/shard_map/ppermute | solution.py:835
  357.7 19.0 %collective-permute-start.31 = (bf16[16,2048]{1,0:T(8,128)(2,1)}, bf16[16,2048]{1,0:T(8,128)(2,1)S(1)}, u32[]{:S(2)}, u32[]{:S(2)}) collective-permute-start(bf16[16,2048]{1,0:T(8,128)(2,1)} %constant_dynamic-slice_fusion.15), channel_id=1, source_target_pairs={{0,2},{1,3},{2,0},{3,1},{4,6},{5,7},{6,4},{7,5},{8,10},{9,11},{10,... | collective-permute-start | bytes 196616 | tf_op jit(solution)/shard_map/ppermute | solution.py:835
  359.7 9.9 %collective-permute-start.24 = (bf16[16,2048]{1,0:T(8,128)(2,1)S(1)}, bf16[16,2048]{1,0:T(8,128)(2,1)S(1)}, u32[]{:S(2)}, u32[]{:S(2)}) collective-permute-start(bf16[16,2048]{1,0:T(8,128)(2,1)S(1)} %add_convert_fusion.31), channel_id=1, source_target_pairs={{0,2},{1,3},{2,0},{3,1},{4,6},{5,7},{6,4},{7,5},{8,10},{9,11},{10,... | collective-permute-start | bytes 196616 | tf_op jit(solution)/shard_map/ppermute | solution.py:835
  376.7 10.2 %collective-permute-start.25 = (bf16[32,2048]{0,1:T(8,128)(2,1)}, bf16[32,2048]{0,1:T(8,128)(2,1)}, u32[]{:S(2)}, u32[]{:S(2)}) collective-permute-start(bf16[32,2048]{0,1:T(8,128)(2,1)} %dynamic_update_slice.145), channel_id=1, source_target_pairs={{0,1},{1,0},{2,3},{3,2},{4,5},{5,4},{6,7},{7,6},{8,9},{9,8},{10,11... | collective-permute-start | bytes 393224 | tf_op jit(solution)/shard_map/ppermute | solution.py:835
  376.7 26.6 %collective-permute-start.32 = (bf16[16,2048]{1,0:T(8,128)(2,1)S(1)}, bf16[16,2048]{1,0:T(8,128)(2,1)S(1)}, u32[]{:S(2)}, u32[]{:S(2)}) collective-permute-start(bf16[16,2048]{1,0:T(8,128)(2,1)S(1)} %add_convert_fusion.30), channel_id=1, source_target_pairs={{0,2},{1,3},{2,0},{3,1},{4,6},{5,7},{6,4},{7,5},{8,10},{9,11},{10,... | collective-permute-start | bytes 196616 | tf_op jit(solution)/shard_map/ppermute | solution.py:835
  393.0 42.8 %collective-permute-start.26 = (bf16[64,2048]{0,1:T(8,128)(2,1)}, bf16[64,2048]{0,1:T(8,128)(2,1)}, u32[]{:S(2)}, u32[]{:S(2)}) collective-permute-start(bf16[64,2048]{0,1:T(8,128)(2,1)} %dynamic_update_slice.147), channel_id=1, source_target_pairs={{0,16},{8,24},{16,0},{24,8},{1,17},{9,25},{17,1},{25,9},{2,18},{10... | collective-permute-start | bytes 786440 | tf_op jit(solution)/shard_map/ppermute | solution.py:835
  410.4 14.4 %collective-permute-start.33 = (bf16[32,2048]{0,1:T(8,128)(2,1)}, bf16[32,2048]{0,1:T(8,128)(2,1)}, u32[]{:S(2)}, u32[]{:S(2)}) collective-permute-start(bf16[32,2048]{0,1:T(8,128)(2,1)} %dynamic_update_slice.153), channel_id=1, source_target_pairs={{0,1},{1,0},{2,3},{3,2},{4,5},{5,4},{6,7},{7,6},{8,9},{9,8},{10,11... | collective-permute-start | bytes 393224 | tf_op jit(solution)/shard_map/ppermute | solution.py:835
  430.9 26.4 %collective-permute-start.34 = (bf16[64,2048]{0,1:T(8,128)(2,1)}, bf16[64,2048]{0,1:T(8,128)(2,1)}, u32[]{:S(2)}, u32[]{:S(2)}) collective-permute-start(bf16[64,2048]{0,1:T(8,128)(2,1)} %dynamic_update_slice.155), channel_id=1, source_target_pairs={{0,8},{8,0},{16,24},{24,16},{1,9},{9,1},{17,25},{25,17},{2,10},{10... | collective-permute-start | bytes 786440 | tf_op jit(solution)/shard_map/ppermute | solution.py:835
  442.0 74.1 %collective-permute-start.27 = (bf16[128,2048]{0,1:T(8,128)(2,1)}, bf16[128,2048]{0,1:T(8,128)(2,1)}, u32[]{:S(2)}, u32[]{:S(2)}) collective-permute-start(bf16[128,2048]{0,1:T(8,128)(2,1)} %dynamic_update_slice.149), channel_id=1, source_target_pairs={{0,8},{8,0},{16,24},{24,16},{1,9},{9,1},{17,25},{25,17},{2,10},{10... | collective-permute-start | bytes 1572872 | tf_op jit(solution)/shard_map/ppermute | solution.py:835
  456.0 12.8 %collective-permute-start.37 = (bf16[128,2432]{1,0:T(8,128)(2,1)}, bf16[128,2432]{1,0:T(8,128)(2,1)}, u32[]{:S(2)}, u32[]{:S(2)}) collective-permute-start(bf16[128,2432]{1,0:T(8,128)(2,1)} %dynamic-slice_convert_fusion.1), channel_id=1, source_target_pairs={{0,8},{8,0},{16,24},{24,16},{1,9},{9,1},{17,25},{25,17},{2,10},{10... | collective-permute-start | bytes 1867784 | tf_op jit(solution)/shard_map/ppermute | solution.py:835
  463.6 53.6 %collective-permute-start.35 = (bf16[128,2048]{0,1:T(8,128)(2,1)}, bf16[128,2048]{0,1:T(8,128)(2,1)S(1)}, u32[]{:S(2)}, u32[]{:S(2)}) collective-permute-start(bf16[128,2048]{0,1:T(8,128)(2,1)} %dynamic_update_slice.157), channel_id=1, source_target_pairs={{0,16},{8,24},{16,0},{24,8},{1,17},{9,25},{17,1},{25,9},{2,18},{10... | collective-permute-start | bytes 1572872 | tf_op jit(solution)/shard_map/ppermute | solution.py:835
  466.7 18.0 %collective-permute-start.45 = (bf16[128,2432]{1,0:T(8,128)(2,1)S(1)}, bf16[128,2432]{1,0:T(8,128)(2,1)S(1)}, u32[]{:S(2)}, u32[]{:S(2)}) collective-permute-start(bf16[128,2432]{1,0:T(8,128)(2,1)S(1)} %dynamic-slice_convert_fusion), channel_id=1, source_target_pairs={{0,16},{8,24},{16,0},{24,8},{1,17},{9,25},{17,1},{25,9},{2,18},{10... | collective-permute-start | bytes 1867784 | tf_op jit(solution)/shard_map/ppermute | solution.py:835
  470.0 18.0 %collective-permute-start.38 = (bf16[64,2432]{1,0:T(8,128)(2,1)S(1)}, bf16[64,2432]{1,0:T(8,128)(2,1)S(1)}, u32[]{:S(2)}, u32[]{:S(2)}) collective-permute-start(bf16[64,2432]{1,0:T(8,128)(2,1)S(1)} %constant_dynamic-slice_fusion.14), channel_id=1, source_target_pairs={{0,16},{8,24},{16,0},{24,8},{1,17},{9,25},{17,1},{25,9},{2,18},{10... | collective-permute-start | bytes 933896 | tf_op jit(solution)/shard_map/ppermute | solution.py:835
  484.9 7.0 %collective-permute-start.46 = (bf16[64,2432]{1,0:T(8,128)(2,1)S(1)}, bf16[64,2432]{1,0:T(8,128)(2,1)S(1)}, u32[]{:S(2)}, u32[]{:S(2)}) collective-permute-start(bf16[64,2432]{1,0:T(8,128)(2,1)S(1)} %constant_dynamic-slice_fusion.11), channel_id=1, source_target_pairs={{0,8},{8,0},{16,24},{24,16},{1,9},{9,1},{17,25},{25,17},{2,10},{10... | collective-permute-start | bytes 933896 | tf_op jit(solution)/shard_map/ppermute | solution.py:835
  488.2 7.0 %collective-permute-start.39 = (bf16[32,2432]{1,0:T(8,128)(2,1)S(1)}, bf16[32,2432]{1,0:T(8,128)(2,1)S(1)}, u32[]{:S(2)}, u32[]{:S(2)}) collective-permute-start(bf16[32,2432]{1,0:T(8,128)(2,1)S(1)} %constant_dynamic-slice_fusion.13), channel_id=1, source_target_pairs={{0,1},{1,0},{2,3},{3,2},{4,5},{5,4},{6,7},{7,6},{8,9},{9,8},{10,11... | collective-permute-start | bytes 466952 | tf_op jit(solution)/shard_map/ppermute | solution.py:835
  492.0 7.0 %collective-permute-start.47 = (bf16[32,2432]{1,0:T(8,128)(2,1)S(1)}, bf16[32,2432]{1,0:T(8,128)(2,1)S(1)}, u32[]{:S(2)}, u32[]{:S(2)}) collective-permute-start(bf16[32,2432]{1,0:T(8,128)(2,1)S(1)} %constant_dynamic-slice_fusion.10), channel_id=1, source_target_pairs={{0,1},{1,0},{2,3},{3,2},{4,5},{5,4},{6,7},{7,6},{8,9},{9,8},{10,11... | collective-permute-start | bytes 466952 | tf_op jit(solution)/shard_map/ppermute | solution.py:835
  495.2 6.2 %collective-permute-start.40 = (bf16[16,2432]{1,0:T(8,128)(2,1)S(1)}, bf16[16,2432]{1,0:T(8,128)(2,1)S(1)}, u32[]{:S(2)}, u32[]{:S(2)}) collective-permute-start(bf16[16,2432]{1,0:T(8,128)(2,1)S(1)} %constant_dynamic-slice_fusion.12), channel_id=1, source_target_pairs={{0,2},{1,3},{2,0},{3,1},{4,6},{5,7},{6,4},{7,5},{8,10},{9,11},{10,... | collective-permute-start | bytes 233480 | tf_op jit(solution)/shard_map/ppermute | solution.py:835
  501.4 5.8 %collective-permute-start.41 = (bf16[16,2432]{1,0:T(8,128)(2,1)S(1)}, bf16[16,2432]{1,0:T(8,128)(2,1)S(1)}, u32[]{:S(2)}, u32[]{:S(2)}) collective-permute-start(bf16[16,2432]{1,0:T(8,128)(2,1)S(1)} %get-tuple-element.86), channel_id=1, source_target_pairs={{0,2},{1,3},{2,0},{3,1},{4,6},{5,7},{6,4},{7,5},{8,10},{9,11},{10,... | collective-permute-start | bytes 233480 | tf_op jit(solution)/shard_map/ppermute | solution.py:835
  512.5 13.3 %collective-permute-start.43 = (bf16[64,2432]{1,0:T(8,128)(2,1)S(1)}, bf16[64,2432]{1,0:T(8,128)(2,1)}, u32[]{:S(2)}, u32[]{:S(2)}) collective-permute-start(bf16[64,2432]{1,0:T(8,128)(2,1)S(1)} %constant_dynamic-update-slice_fusion.24), channel_id=1, source_target_pairs={{0,16},{8,24},{16,0},{24,8},{1,17},{9,25},{17,1},{25,9},{2,18},{10... | collective-permute-start | bytes 933896 | tf_op jit(solution)/shard_map/ppermute | solution.py:835
  515.1 20.8 %collective-permute-start.51 = (bf16[64,2432]{1,0:T(8,128)(2,1)S(1)}, bf16[64,2432]{1,0:T(8,128)(2,1)}, u32[]{:S(2)}, u32[]{:S(2)}) collective-permute-start(bf16[64,2432]{1,0:T(8,128)(2,1)S(1)} %constant_dynamic-update-slice_fusion.18), channel_id=1, source_target_pairs={{0,8},{8,0},{16,24},{24,16},{1,9},{9,1},{17,25},{25,17},{2,10},{10... | collective-permute-start | bytes 933896 | tf_op jit(solution)/shard_map/ppermute | solution.py:835
  532.6 11.6 %collective-permute-start.44 = (bf16[128,2432]{0,1:T(8,128)(2,1)S(1)}, bf16[128,2432]{0,1:T(8,128)(2,1)}, u32[]{:S(2)}, u32[]{:S(2)}) collective-permute-start(bf16[128,2432]{0,1:T(8,128)(2,1)S(1)} %dynamic_update_slice.165), channel_id=1, source_target_pairs={{0,8},{8,0},{16,24},{24,16},{1,9},{9,1},{17,25},{25,17},{2,10},{10... | collective-permute-start | bytes 1867784 | tf_op jit(solution)/shard_map/ppermute | solution.py:835
  542.7 10.3 %collective-permute-start.52 = (bf16[128,2432]{0,1:T(8,128)(2,1)S(1)}, bf16[128,2432]{0,1:T(8,128)(2,1)S(1)}, u32[]{:S(2)}, u32[]{:S(2)}) collective-permute-start(bf16[128,2432]{0,1:T(8,128)(2,1)S(1)} %dynamic_update_slice.173), channel_id=1, source_target_pairs={{0,16},{8,24},{16,0},{24,8},{1,17},{9,25},{17,1},{25,9},{2,18},{10... | collective-permute-start | bytes 1867784 | tf_op jit(solution)/shard_map/ppermute | solution.py:835
  (38 other events, 223.9 us)

commit v2 on v1

--- a/solution.py
+++ b/solution.py
@@ -42,8 +42,12 @@
     return lax.broadcasted_iota(jnp.int32, shape, dim)
 
 
+def tn(a, b):
+    return lax.dot_general(a, b, (((0,), (0,)), ((), ())), preferred_element_type=f32)
+
+
 def sigmoid(v):
-    return 1.0 / (1.0 + jnp.exp(-v))
+    return 0.5 + 0.5 * jnp.tanh(0.5 * v)
 
 
 def split_two(v):
@@ -108,14 +112,68 @@
     return (rows == iota((lanes_in, LANE), 1)).astype(bf16)
 
 
+def pack_kernel(scal, own, oth, taps, vecs, heads, gain):
+    core = scal[0]
+    span = own.shape[1]
+    half_in = vecs.shape[1] // 2
+    half_d = gain.shape[1] // 2
+    taps[...] = jnp.zeros_like(taps)
+    vecs[...] = jnp.zeros_like(vecs)
+    sides = []
+    for src, place in ((own, core), (oth, 1 - core)):
+        block = src[...].astype(f32)
+
+        def at(width):
+            return pl.ds(pl.multiple_of(place * width, LANE), width)
+
+        taps[0:5, at(span)] = block[0:5]
+        vecs[0:1, at(half_in)] = block[5:6, :half_in]
+        gain[0:1, at(half_d)] = block[6:7, :half_d]
+        sides.append(jnp.broadcast_to(block[7:8, :LANE], (8, LANE)))
+    width = H // 2
+    lanes = iota((8, LANE), 1)
+    rows = []
+    for i in range(3):
+        first = jnp.where(core == 0, sides[0], sides[1])
+        second = jnp.where(core == 0, sides[1], sides[0])
+        low = pltpu.roll(first, (LANE - i * width) % LANE, 1)
+        high = pltpu.roll(second, (LANE - i * width + width) % LANE, 1)
+        rows.append(jnp.where(lanes < width, low, jnp.where(lanes < H, high, 0.0)))
+    rate = jnp.where(lanes < H, -jnp.exp(rows[1]), 0.0)
+    pick = iota((8, LANE), 0)
+    heads[...] = jnp.where(pick == 0, rows[0], jnp.where(pick == 1, rate, 0.0))
+    skip = rows[2].astype(bf16)
+    expand = (iota((LANE, DIN), 1) // P_SIZE == iota((LANE, DIN), 0)).astype(bf16)
+    vecs[1:2, :] = nn(skip, expand)[0:1]
+
+
+def pack_vectors(scal, own, oth, d):
+    return call(
+        pack_kernel,
+        (1,),
+        [const_spec(own.shape), const_spec(oth.shape)],
+        [const_spec((8, CONV)), const_spec((8, DIN)), const_spec((8, LANE)), const_spec((1, d))],
+        [
+            jax.ShapeDtypeStruct((8, CONV), f32),
+            jax.ShapeDtypeStruct((8, DIN), f32),
+            jax.ShapeDtypeStruct((8, LANE), f32),
+            jax.ShapeDtypeStruct((1, d), f32),
+        ],
+        [],
+        10**6,
+        10**5,
+        "vectors",
+    )(scal, own, oth)
+
+
 def front_kernel(
     scal, tok, halo, gain, w_own, w_oth, r_own, r_oth, taps, heads,
-    normed, u_out, act_out, dact_out, dt_out, sg_out, cum_out, cumt_out, st_out,
+    n_own, n_oth, u_out, act_out, dact_out, dt_out, sg_out, cum_out, cumt_out, st_out,
     ubuf, bt, ecl,
 ):
     step = pl.program_id(0)
     tok_count = tok.shape[0]
-    half = w_own.shape[0]
+    half = w_own.shape[1]
     own = pl.ds(pl.multiple_of(scal[0] * half, LANE), half)
     oth = pl.ds(pl.multiple_of((1 - scal[0]) * half, LANE), half)
     lo = scal[1]
@@ -125,8 +183,10 @@
     def _():
         def rows_of(src, base, dst, count):
             x = src[pl.ds(base, count), :].astype(f32)
-            ms = jnp.mean(x * x, axis=-1, keepdims=True)
-            normed[pl.ds(dst, count), :] = (x * lax.rsqrt(ms + EPS) * gain[...]).astype(bf16)
+            rs = lax.rsqrt(jnp.mean(x * x, axis=-1, keepdims=True) + EPS)
+            for out, cols in ((n_own, own), (n_oth, oth)):
+                part = src[pl.ds(base, count), cols].astype(f32)
+                out[pl.ds(dst, count), :] = (part * rs * gain[:, cols]).astype(bf16)
 
         rows_of(halo, 0, 0, HALO)
 
@@ -136,14 +196,14 @@
             return carry
 
         lax.fori_loop(0, tok_count // 64, body, 0)
-        r = nn(normed[HALO:, own], r_own[...]) + nn(normed[HALO:, oth], r_oth[...])
+        r = nt(n_own[HALO:, :], r_own[...]) + nt(n_oth[HALO:, :], r_oth[...])
         pre = r.astype(bf16).astype(f32) + heads[0:1, :]
         pos = iota((tok_count, LANE), 0)
         keep = (pos >= lo) & (pos < hi) & (iota((tok_count, LANE), 1) < H)
         soft = jnp.maximum(pre, 0.0) + jnp.log1p(jnp.exp(-jnp.abs(pre)))
         dt = jnp.where(keep, soft, 0.0)
         dt_out[...] = dt
-        sg_out[...] = jnp.where(keep, sigmoid(pre), 0.0)
+        sg_out[...] = jnp.where(keep, 1.0 / (1.0 + jnp.exp(-pre)), 0.0)
         da = dt * heads[1:2, :]
         tri = (iota((QB, QB), 0) >= iota((QB, QB), 1)).astype(f32)
         carry = jnp.zeros((1, LANE), f32)
@@ -154,7 +214,7 @@
             carry = cum[QB - 1 : QB]
         ecl[...] = jnp.exp(carry - cum_out[...])
 
-    u = nn(normed[:, own], w_own[...]) + nn(normed[:, oth], w_oth[...])
+    u = nt(n_own[...], w_own[...]) + nt(n_oth[...], w_oth[...])
     pos = iota(u.shape, 0) - HALO
     u = jnp.where((pos >= lo) & (pos < hi), u, 0.0).astype(bf16)
     u_out[...] = u
@@ -183,7 +243,7 @@
 
 def front(scal, tok, halo, gain, wu_own, wu_oth, taps, heads):
     tok_count, d = tok.shape
-    half = wu_own.shape[0]
+    half = wu_own.shape[1]
     ext = tok_count + HALO
     groups = CONV // GROUP
     first = groups - 1
@@ -191,10 +251,8 @@
     def col(j, *_):
         return (0, (j + first) % groups)
 
-    def weight(rows):
-        return pl.BlockSpec((rows, GROUP), col)
-
-    narrow = pl.BlockSpec((half, LANE), lambda j, *_: (0, CONV // LANE))
+    weight = pl.BlockSpec((GROUP, half), lambda j, *_: ((j + first) % groups, 0))
+    narrow = pl.BlockSpec((LANE, half), lambda j, *_: (CONV // LANE, 0))
     return call(
         front_kernel,
         (groups,),
@@ -202,15 +260,16 @@
             const_spec((tok_count, d)),
             const_spec((HALO, d)),
             const_spec((1, d)),
-            weight(half),
-            weight(half),
+            weight,
+            weight,
             narrow,
             narrow,
-            weight(8),
+            pl.BlockSpec((8, GROUP), col),
             const_spec((8, LANE)),
         ],
         [
-            const_spec((ext, d)),
+            const_spec((ext, half)),
+            const_spec((ext, half)),
             pl.BlockSpec((ext, GROUP), col),
             pl.BlockSpec((tok_count, GROUP), col),
             pl.BlockSpec((tok_count, GROUP), col),
@@ -221,7 +280,8 @@
             pl.BlockSpec((N, GROUP), lambda j, *_: (0, jnp.maximum(j - 1, 0))),
         ],
         [
-            jax.ShapeDtypeStruct((ext, d), bf16),
+            jax.ShapeDtypeStruct((ext, half), bf16),
+            jax.ShapeDtypeStruct((ext, half), bf16),
             jax.ShapeDtypeStruct((ext, CONV), bf16),
             jax.ShapeDtypeStruct((tok_count, CONV), bf16),
             jax.ShapeDtypeStruct((tok_count, CONV), bf16),
@@ -326,6 +386,7 @@
     step = pl.program_id(0)
     rows = yloc.shape[0]
     groups = DIN // GROUP
+    per = groups // 2
 
     @pl.when(step == 0)
     def _():
@@ -357,8 +418,10 @@
         n = vbuf[:, cols] * rs
         vbuf[:, cols] = n
         gain = vecs[0:1, cols]
-        gated[:, cols] = (n * gain * valid).astype(bf16)
-        e = eg[:, cols].astype(f32) * valid
+        side = (g // per) ^ scal[0]
+        local = slice((g % per) * GROUP, (g % per + 1) * GROUP)
+        gated[side, :, local] = (n * gain * valid).astype(bf16)
+        e = eg[side, :, local].astype(f32) * valid
         gs_out[0:1, cols] += jnp.sum(e * n, axis=0, keepdims=True)
         mixed = mixed + e * gain * n
     m2 = jnp.sum(mixed, axis=-1, keepdims=True) / DIN
@@ -369,7 +432,9 @@
     for g in range(groups):
         cols = slice(g * GROUP, (g + 1) * GROUP)
         n = vbuf[:, cols]
-        e = eg[:, cols].astype(f32) * valid
+        side = (g // per) ^ scal[0]
+        local = slice((g % per) * GROUP, (g % per + 1) * GROUP)
+        e = eg[side, :, local].astype(f32) * valid
         ev = rs * (e * vecs[0:1, cols] - n * m2)
         zz = z[:, cols].astype(f32)
         sz = sigmoid(zz)
@@ -401,6 +466,8 @@
     def out(width, kind):
         return jax.ShapeDtypeStruct((tok_count, width), kind)
 
+    sides = pl.BlockSpec((2, rows, DIN // 2), lambda j, *_: (0, j, 0))
+
     return call(
         gate_kernel,
         (tok_count // rows,),
@@ -408,13 +475,13 @@
             rowspec(DIN),
             rowspec(CONV),
             rowspec(DIN),
-            rowspec(DIN),
+            sides,
             rowspec(LANE),
             const_spec((N, DIN)),
             const_spec((8, DIN)),
         ],
         [
-            rowspec(DIN),
+            sides,
             rowspec(DIN),
             rowspec(DIN),
             rowspec(LANE),
@@ -424,7 +491,7 @@
             const_spec((8, DIN)),
         ],
         [
-            out(DIN, bf16),
+            jax.ShapeDtypeStruct((2, tok_count, DIN // 2), bf16),
             out(DIN, bf16),
             out(DIN, bf16),
             out(LANE, f32),
@@ -572,11 +639,11 @@
 def tail_kernel(
     scal, act, bc, dact, u, ey, dxt, taps, dt, sg, cum, g_in, s_in, skip, heads,
     db_loc, dc_loc, dc_dev, r_loc, r_dev, r2, cq,
-    eu_out, er_out, gconv, ghead,
+    eu_out, gconv, ghead,
     ebuf, ubuf, p_acc, d_acc, db_acc, gs_acc,
 ):
     step = pl.program_id(0)
-    last = pl.num_programs(0) - 1
+    last = pl.num_programs(0) - 2
     tok_count = act.shape[0]
     ext = tok_count + HALO
     lo = scal[1]
@@ -611,13 +678,16 @@
         vec = vec * jnp.exp(spread_group(end))
         gs_acc[...] += exact_nn(jnp.broadcast_to(vec, (8, GROUP)), pick.astype(f32))
         ebuf[HALO : HALO + tok_count, :] = (
-            dtr * dx + skip[0:1, :] * ey[...].astype(f32)
+            dtr * dx + skip[1:2, :] * ey[...].astype(f32)
         ) * dact[...].astype(f32)
 
     @pl.when(step == last)
     def _():
         ebuf[HALO : HALO + tok_count, :N] = (db_loc[...] + db_acc[...]) * dact[:, :N].astype(f32)
         ebuf[HALO : HALO + tok_count, N:] = (dc_loc[...] + dc_dev[...]) * dact[:, N:].astype(f32)
+
+    @pl.when(step > last)
+    def _():
         rate = heads[1:2, :]
         upper = (iota((QB, QB), 0) <= iota((QB, QB), 1)).astype(f32)
         strict = (iota((QB, QB), 0) > iota((QB, QB), 1)).astype(f32)
@@ -633,7 +703,7 @@
         before = gs_acc[0:1, :]
         glog = jnp.zeros((1, LANE), f32)
         gdt = jnp.zeros((1, LANE), f32)
-        er_out[0:HALO, :] = jnp.zeros((HALO, LANE), bf16)
+        eu_out[...] = jnp.zeros_like(eu_out)
         for q in range(blocks):
             rows = slice(q * QB, (q + 1) * QB)
             pq = p_acc[rows, :]
@@ -642,21 +712,23 @@
             er = (d_acc[rows, :] + rate * eda) * sg[rows, :]
             gdt = gdt + jnp.sum(er, axis=0, keepdims=True)
             glog = glog + rate * jnp.sum(dt[rows, :] * eda, axis=0, keepdims=True)
-            er_out[HALO + q * QB : HALO + (q + 1) * QB, :] = er.astype(bf16)
+            eu_out[HALO + q * QB : HALO + (q + 1) * QB, :LANE] = er.astype(bf16)
         ghead[...] = jnp.concatenate([gdt, glog, jnp.zeros((6, LANE), f32)], axis=0)
 
-    ubuf[...] = u[...].astype(f32)
-    ec = ebuf[HALO : HALO + tok_count, :]
-    gs = [
-        jnp.sum(ec * ubuf[HALO - 3 + k : HALO - 3 + k + tok_count, :], axis=0, keepdims=True)
-        for k in range(K)
-    ]
-    gs.append(jnp.sum(ec, axis=0, keepdims=True))
-    gs.append(jnp.zeros((3, ec.shape[1]), f32))
-    gconv[...] = jnp.concatenate(gs, axis=0)
-    eu = sum(taps[k : k + 1, :] * ebuf[3 - k : 3 - k + ext, :] for k in range(K))
-    pos = iota(eu.shape, 0) - HALO
-    eu_out[...] = jnp.where((pos >= lo) & (pos < hi), eu, 0.0).astype(bf16)
+    @pl.when(step <= last)
+    def _():
+        ubuf[...] = u[...].astype(f32)
+        ec = ebuf[HALO : HALO + tok_count, :]
+        gs = [
+            jnp.sum(ec * ubuf[HALO - 3 + k : HALO - 3 + k + tok_count, :], axis=0, keepdims=True)
+            for k in range(K)
+        ]
+        gs.append(jnp.sum(ec, axis=0, keepdims=True))
+        gs.append(jnp.zeros((3, ec.shape[1]), f32))
+        gconv[...] = jnp.concatenate(gs, axis=0)
+        eu = sum(taps[k : k + 1, :] * ebuf[3 - k : 3 - k + ext, :] for k in range(K))
+        pos = iota(eu.shape, 0) - HALO
+        eu_out[...] = jnp.where((pos >= lo) & (pos < hi), eu, 0.0).astype(bf16)
 
 
 def tail(scal, act, dact, u, ey, dxt, taps, dt, sg, cum, g_in, s_in, skip, heads, smalls):
@@ -665,7 +737,7 @@
     groups = DIN // GROUP
 
     def col(j, *_):
-        return (0, j)
+        return (0, jnp.minimum(j, groups))
 
     def colx(j, *_):
         return (0, jnp.minimum(j, groups - 1))
@@ -675,7 +747,7 @@
     small = const_spec((tok_count, LANE))
     return call(
         tail_kernel,
-        (groups + 1,),
+        (groups + 2,),
         [
             wide,
             pl.BlockSpec((tok_count, GROUP), lambda j, *_: (0, groups)),
@@ -689,7 +761,7 @@
             small,
             pl.BlockSpec((N, GROUP), colx),
             pl.BlockSpec((N, GROUP), colx),
-            pl.BlockSpec((8, GROUP), colx),
+            pl.BlockSpec((8, GROUP), lambda j, *_: (0, jnp.minimum(j, groups - 1))),
             const_spec((8, LANE)),
             small,
             small,
@@ -700,14 +772,12 @@
             const_spec((8, LANE)),
         ],
         [
-            pl.BlockSpec((ext, GROUP), col),
-            const_spec((ext, LANE)),
+            pl.BlockSpec((ext, GROUP), lambda j, *_: (0, j)),
             pl.BlockSpec((8, GROUP), col),
             const_spec((8, LANE)),
         ],
         [
-            jax.ShapeDtypeStruct((ext, CONV), bf16),
-            jax.ShapeDtypeStruct((ext, LANE), bf16),
+            jax.ShapeDtypeStruct((ext, CONV + GROUP), bf16),
             jax.ShapeDtypeStruct((8, CONV), f32),
             jax.ShapeDtypeStruct((8, LANE), f32),
         ],
@@ -727,87 +797,339 @@
     )
 
 
-def splitk_kernel(scal, a, w_own, w_oth, *rest):
-    half = w_own.shape[0]
-    own = pl.ds(pl.multiple_of(scal[0] * half, LANE), half)
-    oth = pl.ds(pl.multiple_of((1 - scal[0]) * half, LANE), half)
-    total = nn(a[:, own], w_own[...]) + nn(a[:, oth], w_oth[...])
-    if len(rest) == 2:
-        total = total + rest[0][...].astype(f32)
-    out = rest[-1]
-    out[...] = total.astype(out.dtype)
-
-
-def splitk(scal, a, w_own, w_oth, add, name):
-    rows, depth = a.shape
-    width = w_own.shape[1]
-    col = lambda j, *_: (0, j)
+def gate_proj_kernel(scal, a_own, a_oth, w_own, w_oth, out):
+    out[...] = (
+        nt(a_own[HALO:, :], w_own[...]) + nt(a_oth[HALO:, :], w_oth[...])
+    ).astype(bf16)
+
+
+def gate_proj(scal, n_own, n_oth, wz_own, wz_oth):
+    ext, half = n_own.shape
+    rows = ext - HALO
+    wide = 2 * GROUP
+    weight = pl.BlockSpec((wide, half), lambda j, *_: (j, 0))
+    return call(
+        gate_proj_kernel,
+        (DIN // wide,),
+        [const_spec((ext, half)), const_spec((ext, half)), weight, weight],
+        pl.BlockSpec((rows, wide), lambda j, *_: (0, j)),
+        jax.ShapeDtypeStruct((rows, DIN), bf16),
+        [],
+        4 * rows * half * DIN,
+        4 * DIN * half,
+        "gate_proj",
+    )(scal, n_own, n_oth, wz_own, wz_oth)
+
+
+def grad_gated_kernel(scal, e, w_own, w_oth, out):
+    out[0] = nt(e[...], w_own[...]).astype(bf16)
+    out[1] = nt(e[...], w_oth[...]).astype(bf16)
+
+
+def grad_gated(scal, e, wo_own, wo_oth):
+    rows, d = e.shape
+    half = wo_own.shape[0]
+    weight = pl.BlockSpec((GROUP, d), lambda j, *_: (j, 0))
+    return call(
+        grad_gated_kernel,
+        (half // GROUP,),
+        [const_spec((rows, d)), weight, weight],
+        pl.BlockSpec((2, rows, GROUP), lambda j, *_: (0, 0, j)),
+        jax.ShapeDtypeStruct((2, rows, half), bf16),
+        [],
+        4 * rows * half * d,
+        4 * d * half,
+        "grad_gated",
+    )(scal, e, wo_own, wo_oth)
+
+
+def out_proj_kernel(scal, a, w_own, w_oth, tok, out):
+    total = tok[...].astype(f32) + nn(a[0], w_own[...]) + nn(a[1], w_oth[...])
+    out[...] = total.astype(bf16)
+
+
+def out_proj(scal, gated, wo_own, wo_oth, tok):
+    rows, d = tok.shape
+    half = wo_own.shape[0]
+    wide = 2 * GROUP
+    weight = pl.BlockSpec((half, wide), lambda j, *_: (0, j))
+    cols = pl.BlockSpec((rows, wide), lambda j, *_: (0, j))
+    return call(
+        out_proj_kernel,
+        (d // wide,),
+        [const_spec(gated.shape), weight, weight, cols],
+        cols,
+        jax.ShapeDtypeStruct((rows, d), bf16),
+        [],
+        4 * rows * half * d,
+        4 * d * half,
+        "out_proj",
+    )(scal, gated, wo_own, wo_oth, tok)
+
+
+def input_back_kernel(
+    scal, ez, eu, wz_own, wz_oth, wu_own, wu_oth, tok, halo, up, gain,
+    grad_out, edge_out, gain_out,
+    acc,
+):
+    step = pl.program_id(0)
+    per = pl.num_programs(0) // 2
+    half = acc.shape[1] // 2
+    side = jnp.where(step < per, scal[0], 1 - scal[0])
+    place = pl.ds(pl.multiple_of(side * half + lax.rem(step, per) * GROUP, GROUP), GROUP)
+
+    def fill(wz, wu):
+        part = nn(eu[...], wu[...])
+        acc[0:HALO, place] = part[0:HALO]
+        acc[HALO:, place] = part[HALO:] + nn(ez[...], wz[...])
+
+    @pl.when(step < per)
+    def _():
+        fill(wz_own, wu_own)
+
+    @pl.when(step >= per)
+    def _():
+        fill(wz_oth, wu_oth)
+
+    def norm_back(x, rows):
+        rs = lax.rsqrt(jnp.mean(x * x, axis=-1, keepdims=True) + EPS)
+        unit = x * rs
+        en = acc[rows, :]
+        scaled = en * gain[...]
+        gain_out[0:1, :] += jnp.sum(en * unit, axis=0, keepdims=True)
+        return rs * (scaled - unit * jnp.mean(scaled * unit, axis=-1, keepdims=True))
+
+    @pl.when(step == 2 * per - 1)
+    def _():
+        gain_out[...] = jnp.zeros_like(gain_out)
+        edge_out[...] = norm_back(halo[...].astype(f32), pl.ds(0, HALO))
+
+        def body(i, carry):
+            rows = pl.ds(pl.multiple_of(i * 64, 64), 64)
+            ext_rows = pl.ds(pl.multiple_of(i * 64 + HALO, 16), 64)
+            grad_out[rows, :] = up[rows, :].astype(f32) + norm_back(
+                tok[rows, :].astype(f32), ext_rows
+            )
+            return carry
+
+        lax.fori_loop(0, tok.shape[0] // 64, body, 0)
+
+
+def input_back(scal, ez, eu, wz_own, wz_oth, wu_own, wu_oth, tok, halo, up, gain):
+    rows, d = tok.shape
+    ext = rows + HALO
+    half = wz_own.shape[1]
+    per = half // GROUP
+
+    def own(depth):
+        return pl.BlockSpec((depth, GROUP), lambda j, *_: (0, jnp.minimum(j, per - 1)))
+
+    def oth(depth):
+        return pl.BlockSpec((depth, GROUP), lambda j, *_: (0, jnp.maximum(j - per, 0)))
+
+    zd = wz_own.shape[0]
+    ud = wu_own.shape[0]
+    return call(
+        input_back_kernel,
+        (2 * per,),
+        [
+            const_spec(ez.shape),
+            const_spec(eu.shape),
+            own(zd),
+            oth(zd),
+            own(ud),
+            oth(ud),
+            const_spec((rows, d)),
+            const_spec((HALO, d)),
+            const_spec((rows, d)),
+            const_spec((1, d)),
+        ],
+        [const_spec((rows, d)), const_spec((HALO, d)), const_spec((8, d))],
+        [
+            jax.ShapeDtypeStruct((rows, d), f32),
+            jax.ShapeDtypeStruct((HALO, d), f32),
+            jax.ShapeDtypeStruct((8, d), f32),
+        ],
+        [pltpu.VMEM((ext, d), f32)],
+        2 * ext * d * (zd + ud),
+        2 * d * (zd + ud) + 8 * rows * d,
+        "input_back",
+    )(scal, ez, eu, wz_own, wz_oth, wu_own, wu_oth, tok, halo, up, gain)
+
+
+BLOCKS = 16
+
+
+def outer_kernel(spans, keys, offset, has_rates, scal, l1, l2, r1, r2, *rest):
+    if has_rates:
+        e1, e2 = rest[:2]
+        rest = rest[2:]
+    step = pl.program_id(0)
+    rows = l1.shape[1]
+    total = rest[0].shape[1]
+    count = rows // total
+    tail = r1.shape[0] - l1.shape[0] if offset else 0
+    acc = tn(l1[...], r1[tail:, :]) + tn(l2[...], r2[tail:, :])
+    low = acc.astype(bf16)
+    for i, (span, key) in enumerate(zip(spans, keys)):
+        keep, send = rest[2 * i], rest[2 * i + 1]
+        for t in range(count):
+            place = (step * count + t) ^ scal[key]
+            part = low[t * total : (t + 1) * total, span]
+
+            @pl.when(place < BLOCKS // 2)
+            def _():
+                keep[place] = part
+
+            @pl.when(place >= BLOCKS // 2)
+            def _():
+                send[place - BLOCKS // 2] = part
+
+    if has_rates:
+        @pl.when(step == 0)
+        def _():
+            rest[-1][...] = (tn(e1[...], r1[...]) + tn(e2[...], r2[...]))[:H]
+
+
+def outer(scal, l1, l2, r1, r2, width, rows, step_rows, spans, keys, rates, name):
+    toks = l1.shape[0]
+    ext = r1.shape[0]
+    cols = r1.shape[1]
     specs = [
-        const_spec((rows, depth)),
-        pl.BlockSpec((depth // 2, GROUP), col),
-        pl.BlockSpec((depth // 2, GROUP), col),
+        pl.BlockSpec((toks, step_rows), lambda j, *_: (0, j)),
+        pl.BlockSpec((toks, step_rows), lambda j, *_: (0, j)),
+        const_spec((ext, cols)),
+        const_spec((ext, cols)),
     ]
-    args = [a, w_own, w_oth]
-    if add is not None:
-        specs.append(pl.BlockSpec((rows, GROUP), col))
-        args.append(add)
+    args = [l1, l2, r1, r2]
+    if rates:
+        spec = pl.BlockSpec((toks, LANE), lambda j, *_: (0, CONV // LANE))
+        specs += [spec, spec]
+        args += [l1, l2]
+    outs = []
+    for span in spans:
+        shape = (BLOCKS // 2, rows, span.stop - span.start)
+        outs += [shape, shape]
+    shapes = [jax.ShapeDtypeStruct(o, bf16) for o in outs]
+    if rates:
+        outs.append((H, cols))
+        shapes.append(jax.ShapeDtypeStruct((H, cols), f32))
+
+    def kernel(*refs):
+        outer_kernel(spans, keys, ext != toks, rates, *refs)
+
     return call(
-        splitk_kernel,
-        (width // GROUP,),
+        kernel,
+        (width // step_rows,),
         specs,
-        pl.BlockSpec((rows, GROUP), col),
-        jax.ShapeDtypeStruct((rows, width), bf16),
+        [const_spec(o) for o in outs],
+        shapes,
         [],
-        2 * rows * depth * width,
-        2 * (rows * depth + depth * width + rows * width),
+        4 * toks * width * cols,
+        4 * toks * width,
         name,
     )(scal, *args)
 
 
-def halves_kernel(scal, *refs):
-    out = refs[-1]
-    count = (len(refs) - 1) // 3
-    steps = pl.num_programs(0) // 2
-    step = pl.program_id(0)
-
-    @pl.when(step < steps)
-    def _():
-        total = sum(nt(refs[3 * i][...], refs[3 * i + 1][...]) for i in range(count))
-        out[...] = total.astype(out.dtype)
-
-    @pl.when(step >= steps)
-    def _():
-        total = sum(nt(refs[3 * i][...], refs[3 * i + 2][...]) for i in range(count))
-        out[...] = total.astype(out.dtype)
-
-
-def halves(scal, terms, kind, name):
-    rows = terms[0][0].shape[0]
-    span = terms[0][1].shape[0]
-    steps = span // GROUP
-    specs = []
-    args = []
-    flops = 0
-    for a, w_own, w_oth in terms:
-        depth = a.shape[1]
-        specs += [
-            const_spec((rows, depth)),
-            pl.BlockSpec((GROUP, depth), lambda j, *_: (jnp.minimum(j, steps - 1), 0)),
-            pl.BlockSpec((GROUP, depth), lambda j, *_: (jnp.maximum(j - steps, 0), 0)),
-        ]
-        args += [a, w_own, w_oth]
-        flops += 4 * rows * depth * span
+def finish_kernel(key, scal, near, far, *rest):
+    out = rest[-1]
+    place = pl.program_id(0) ^ scal[key]
+
+    @pl.when(place < BLOCKS // 2)
+    def _():
+        out[...] = near[0].astype(f32)
+
+    @pl.when(place >= BLOCKS // 2)
+    def _():
+        out[...] = far[0].astype(f32)
+
+
+def finish(scal, near, far, key, height, name):
+    half, rows, cols = near.shape
+
+    def near_map(j, s):
+        return (jnp.minimum(j ^ s[key], half - 1), 0, 0)
+
+    def far_map(j, s):
+        return (jnp.maximum((j ^ s[key]) - half, 0), 0, 0)
+
+    def kernel(*refs):
+        finish_kernel(key, *refs)
+
     return call(
-        halves_kernel,
-        (2 * steps,),
-        specs,
-        pl.BlockSpec((rows, GROUP), lambda j, s: (0, lax.rem(j + steps * s[0], 2 * steps))),
-        jax.ShapeDtypeStruct((rows, 2 * span), kind),
+        kernel,
+        (BLOCKS,),
+        [pl.BlockSpec((1, rows, cols), near_map), pl.BlockSpec((1, rows, cols), far_map)],
+        pl.BlockSpec((rows, cols), lambda j, *_: (j, 0)),
+        jax.ShapeDtypeStruct((height, cols), f32),
         [],
-        flops,
-        flops // rows,
+        0,
+        6 * BLOCKS * rows * cols,
         name,
-    )(scal, *args)
+    )(scal, near, far)
+
+
+def finish_conv_kernel(spans, keys, scal, rates, *rest):
+    streams = rest[: 2 * len(spans)]
+    out, buf, sems = rest[2 * len(spans) + 1 :]
+    half, rows, _ = streams[0].shape
+    last = pltpu.make_async_copy(
+        rates, out.at[pl.ds(DIN + CONV, H), :], sems.at[BLOCKS]
+    )
+    last.start()
+    copies = [last]
+    for t in range(BLOCKS):
+        for i, (span, key) in enumerate(zip(spans, keys)):
+            near, far = streams[2 * i], streams[2 * i + 1]
+            place = t ^ scal[key]
+            dst = slice(t * rows, (t + 1) * rows)
+
+            @pl.when(place < half)
+            def _():
+                buf[dst, span] = near[place].astype(f32)
+
+            @pl.when(place >= half)
+            def _():
+                buf[dst, span] = far[place - half].astype(f32)
+
+        copy = pltpu.make_async_copy(
+            buf.at[pl.ds(t * rows, rows), :],
+            out.at[pl.ds(DIN + t * rows, rows), :],
+            sems.at[t],
+        )
+        copy.start()
+        copies.append(copy)
+    for copy in copies:
+        copy.wait()
+
+
+def finish_conv(scal, streams, spans, keys, rates, target):
+    def kernel(*refs):
+        finish_conv_kernel(spans, keys, *refs)
+
+    count = len(streams)
+    return pl.pallas_call(
+        kernel,
+        grid_spec=pltpu.PrefetchScalarGridSpec(
+            num_scalar_prefetch=1,
+            grid=(1,),
+            in_specs=[const_spec(rates.shape)]
+            + [const_spec(s.shape) for s in streams]
+            + [pl.BlockSpec(memory_space=pl.ANY)],
+            out_specs=pl.BlockSpec(memory_space=pl.ANY),
+            scratch_shapes=[
+                pltpu.VMEM((CONV, target.shape[1]), f32),
+                pltpu.SemaphoreType.DMA((BLOCKS + 1,)),
+            ],
+        ),
+        out_shape=jax.ShapeDtypeStruct(target.shape, f32),
+        input_output_aliases={2 + count: 0},
+        compiler_params=params(1),
+        cost_estimate=pl.CostEstimate(
+            flops=0, bytes_accessed=6 * CONV * target.shape[1], transcendentals=0
+        ),
+        name="finish_conv",
+    )(scal, rates, *streams, target)
 
 
 def swap(x):
@@ -819,14 +1141,6 @@
     return lax.ppermute(x, "tm", [(i, (i + by) % length) for i in range(length)])
 
 
-def ordered(core, mine, other, axis):
-    return jnp.where(
-        core == 0,
-        jnp.concatenate([mine, other], axis=axis),
-        jnp.concatenate([other, mine], axis=axis),
-    )
-
-
 def bits_of(axis):
     return [(axis, 1 << b) for b in range((lax.axis_size(axis) - 1).bit_length())]
 
@@ -835,32 +1149,59 @@
     return lax.ppermute(x, axis, [(i, i ^ bit) for i in range(lax.axis_size(axis))])
 
 
-def reduced(buf, order):
-    for axis, bit in order:
-        n = buf.shape[0] // 2
-        side = (lax.axis_index(axis) // bit) % 2
-        send = lax.dynamic_slice_in_dim(buf, (1 - side) * n, n, 0)
-        keep = lax.dynamic_slice_in_dim(buf, side * n, n, 0)
-        got = across(send.astype(bf16), axis, bit)
-        buf = (keep.astype(f32) + got.astype(f32)).astype(bf16)
-    for axis, bit in reversed(order):
-        n = buf.shape[0]
-        side = (lax.axis_index(axis) // bit) % 2
-        got = across(buf, axis, bit)
-        both = jnp.zeros((2 * n,) + buf.shape[1:], bf16)
-        both = lax.dynamic_update_slice_in_dim(both, buf, side * n, 0)
-        buf = lax.dynamic_update_slice_in_dim(both, got, (1 - side) * n, 0)
-    return buf
-
-
-def summed(grad):
+def orders():
     rep = bits_of("rep")
-    tm = bits_of("tm")
+    tm = bits_of("tm")[::-1]
     cut = len(rep) // 2
-    n = grad.shape[0] // 2
-    first = reduced(grad[:n], rep + tm)
-    second = reduced(grad[n:], rep[cut:] + rep[:cut] + tm)
-    return jnp.concatenate([first, second], axis=0).astype(f32)
+    depth = BLOCKS.bit_length() - 1
+    found = []
+    for lead in (rep, rep[cut:] + rep[:cut]):
+        every = lead + tm
+        found.append((every[:depth], every[depth:]))
+    return found
+
+
+def code_of(order):
+    place = 0
+    for axis, bit in order[0]:
+        place = 2 * place + (lax.axis_index(axis) // bit) % 2
+    return place
+
+
+def reduce_blocks(keep, send, order):
+    first, extra = order
+    for axis, bit in first[:-2]:
+        got = across(send, axis, bit)
+        n = keep.shape[0] // 2
+        total = keep.astype(f32) + got.astype(f32)
+        last = (axis, bit) == first[-3]
+        low = total.astype(bf16)
+        keep, send = (low, None) if last else (low[:n], low[n:])
+    axis, high = first[-2]
+    step = first[-1][1]
+    total = keep[0:1].astype(f32)
+    for k in range(1, 4):
+        mask = (high if k & 2 else 0) ^ (step if k & 1 else 0)
+        total = total + across(keep[k : k + 1], axis, mask).astype(f32)
+    piece = total.astype(bf16)
+    for axis_, bit in extra:
+        piece = (piece.astype(f32) + across(piece, axis_, bit).astype(f32)).astype(bf16)
+    return piece
+
+
+def spread_blocks(piece, order):
+    first = order[0]
+    axis, high = first[-2]
+    step = first[-1][1]
+    parts = [piece]
+    for k in range(1, 4):
+        mask = (high if k & 2 else 0) ^ (step if k & 1 else 0)
+        parts.append(across(piece, axis, mask))
+    near = jnp.concatenate(parts, axis=0)
+    middle = first[1:-2]
+    for axis_, bit in reversed(middle):
+        near = jnp.concatenate([near, across(near, axis_, bit)], axis=0)
+    return near, across(near, *first[0])
 
 
 def body(
@@ -877,54 +1218,39 @@
     half_in = out_weight.shape[0]
     half_conv = conv_bias.shape[0]
     half_heads = dt_bias.shape[0]
+    order_a, order_b = orders()
 
     lo = starts[0] - tm * tok_count
-    scal = jnp.stack([core, lo, lo + lengths[0]]).astype(jnp.int32)
-
-    def wide(v):
-        return jnp.pad(v, (0, half_conv - v.shape[0]))[None]
+    scal = jnp.stack(
+        [core, lo, lo + lengths[0], code_of(order_a), code_of(order_b)]
+    ).astype(jnp.int32)
+
+    def fill(v):
+        return [v, jnp.zeros((half_conv - v.shape[0],), f32)]
 
     pack = jnp.concatenate(
-        [
-            conv_weight,
-            conv_bias[None],
-            wide(gate_gain),
-            wide(norm_gain),
-            wide(jnp.concatenate([dt_bias, a_log, d_skip])),
-        ],
-        axis=0,
-    ).astype(bf16)
+        [conv_weight.reshape(-1), conv_bias]
+        + fill(gate_gain)
+        + fill(norm_gain)
+        + [dt_bias, a_log, d_skip, jnp.zeros((half_conv - 3 * half_heads,), f32)]
+    )
+    pack = pack.reshape(8, half_conv).astype(bf16)
     pack_oth = swap(pack)
     halo = shifted(tok[tok_count - HALO :], 1)
-    wu_own = jnp.pad(in_weight[:, DIN:], ((0, 0), (0, LANE - H))).astype(bf16)
+    w_t = in_weight.T
+    wu_own = jnp.pad(w_t[DIN:], ((0, GROUP - H), (0, 0))).astype(bf16)
     wu_oth = swap(wu_own)
-    wz_own = in_weight[:, :DIN].astype(bf16)
+    wz_own = w_t[:DIN].astype(bf16)
     wz_oth = swap(wz_own)
     wo_own = out_weight.astype(bf16)
     wo_oth = swap(wo_own)
-
-    def both(row, length):
-        return ordered(core, pack[row, :length], pack_oth[row, :length], 0).astype(f32)
-
-    def both_heads(i):
-        part = slice(i * half_heads, (i + 1) * half_heads)
-        return ordered(core, pack[7, part], pack_oth[7, part], 0).astype(f32)
-
-    taps = jnp.pad(
-        ordered(core, pack[:5], pack_oth[:5], 1).astype(f32), ((0, 3), (0, 0))
-    )
-    gate_vec = both(5, half_in)
-    gain = both(6, half_d)[None]
-    skip_vec = jnp.repeat(both_heads(2), P_SIZE)
-    vecs = jnp.pad(jnp.stack([gate_vec, skip_vec]), ((0, 6), (0, 0)))
-    skip8 = jnp.pad(skip_vec[None], ((0, 7), (0, 0)))
-    heads = jnp.pad(
-        jnp.stack([both_heads(0), -jnp.exp(both_heads(1))]), ((0, 6), (0, LANE - H))
-    )
-
-    normed, u, act, dact, dt, sg, cum, cumt, st = front(
+    up_oth = swap(upstream)
+
+    taps, vecs, heads, gain = pack_vectors(scal, pack, pack_oth, d)
+    n_own, n_oth, u, act, dact, dt, sg, cum, cumt, st = front(
         scal, tok, halo, gain, wu_own, wu_oth, taps, heads
     )
+    n_got = swap(n_oth)
     cumt = cumt[:H].reshape(H // 4, 4, tok_count)
     total = jnp.exp(jnp.repeat(cum[tok_count - 1, :H], P_SIZE))[None]
 
@@ -943,57 +1269,53 @@
         return jnp.concatenate(pieces, axis=1)
 
     s_in = chain(st, 1, 0)
-    z = splitk(scal, normed[HALO:], wz_own, wz_oth, None, "gate_proj")
-    eg = halves(scal, [(upstream, wo_own, wo_oth)], bf16, "grad_gated")
+    z = gate_proj(scal, n_own, n_oth, wz_own, wz_oth)
+    eg = grad_gated(scal, upstream, wo_own, wo_oth)
     yloc, s0 = intra(scal, act, dt, cum, cumt)
     gated, ey, ez, r_loc, r_dev, dc_dev, g_loc, gs = gate(
         scal, yloc, act, z, eg, cum, s_in, vecs
     )
 
-    def mine(x, half):
-        return lax.dynamic_slice_in_dim(x, core * half, half, 1)
-
-    def theirs(x, half):
-        return lax.dynamic_slice_in_dim(x, (1 - core) * half, half, 1)
-
-    def outer(a, b):
-        return lax.dot_general(a, b, (((0,), (0,)), ((), ())), preferred_element_type=f32)
-
-    up_oth = swap(upstream)
-    normed_oth = swap(theirs(normed, half_d))
-    normed_own = mine(normed, half_d)
-    gated_oth = swap(theirs(gated, half_in))
-    ez_oth = swap(ez)
+    gated_got = swap(gated[1])
+    ez_got = swap(ez)
     g_in = chain(g_loc, -1, tm_size - 1)
-    grad_out = outer(mine(gated, half_in), upstream) + outer(gated_oth, up_oth)
-    grad_z = outer(normed_own[HALO:], ez) + outer(normed_oth[HALO:], ez_oth)
-    grad_out_w = summed(grad_out)
-    grad_z_w = summed(grad_z)
-    output = splitk(scal, gated, wo_own, wo_oth, tok, "out_proj")
+    full = [slice(0, d)]
+    a_keep, a_send = outer(
+        scal, gated[0], gated_got, upstream, up_oth,
+        half_in, half_in // BLOCKS, GROUP, full, [3], False, "grad_out",
+    )
+    half_span = [slice(0, half_d)]
+    b_keep, b_send = outer(
+        scal, ez, ez_got, n_own, n_got,
+        DIN, DIN // BLOCKS, 2 * GROUP, half_span, [4], False, "grad_z",
+    )
+    a_piece = reduce_blocks(a_keep, a_send, order_a)
+    b_piece = reduce_blocks(b_keep, b_send, order_b)
+    a_near, a_far = spread_blocks(a_piece, order_a)
+    b_near, b_far = spread_blocks(b_piece, order_b)
+    output = out_proj(scal, gated, wo_own, wo_oth, tok)
     dxt, db_loc, dc_loc, r2, cq = back(scal, act, dt, cum, cumt, ey, s0)
-    eu, er, gconv, ghead = tail(
-        scal, act, dact, u, ey, dxt, taps, dt, sg, cum, g_in, s_in, skip8, heads,
+    eu, gconv, ghead = tail(
+        scal, act, dact, u, ey, dxt, taps, dt, sg, cum, g_in, s_in, vecs, heads,
         (db_loc, dc_loc, dc_dev, r_loc, r_dev, r2, cq),
     )
-    eur = jnp.concatenate([eu, er], axis=1)
-    eur_oth = swap(eur)
-    grad_u = outer(normed_own, eur) + outer(normed_oth, eur_oth)
-    grad_u_w = summed(grad_u)
-
-    ez_ext = jnp.pad(ez, ((HALO, 0), (0, 0)))
-    e_normed = halves(
-        scal, [(ez_ext, wz_own, wz_oth), (eur, wu_own, wu_oth)], f32, "grad_normed"
-    )
-    ext_tok = jnp.concatenate([halo, tok], axis=0).astype(f32)
-    rs = lax.rsqrt(jnp.mean(ext_tok * ext_tok, axis=-1, keepdims=True) + EPS)
-    unit = ext_tok * rs
-    scaled = e_normed * gain
-    grad_in = rs * (scaled - unit * jnp.mean(scaled * unit, axis=-1, keepdims=True))
-    grad_gain = jnp.sum(e_normed * unit, axis=0)
-    edge = shifted(grad_in[:HALO], -1)
+    eu_got = swap(eu)
+    spans = [slice(0, half_d // 2), slice(half_d // 2, half_d)]
+    c1_keep, c1_send, c2_keep, c2_send, g_rates = outer(
+        scal, eu, eu_got, n_own, n_got,
+        CONV, CONV // BLOCKS, CONV // 2, spans, [3, 4], True, "grad_u",
+    )
+    c1_piece = reduce_blocks(c1_keep, c1_send, order_a)
+    c2_piece = reduce_blocks(c2_keep, c2_send, order_b)
+    c1_near, c1_far = spread_blocks(c1_piece, order_a)
+    c2_near, c2_far = spread_blocks(c2_piece, order_b)
+
+    grad_in, edge, ggain = input_back(
+        scal, ez, eu, wz_own, wz_oth, wu_own, wu_oth, tok, halo, upstream, gain
+    )
+    edge = shifted(edge, -1)
     edge = jnp.where(tm == tm_size - 1, jnp.zeros_like(edge), edge)
-    input_grad = upstream.astype(f32) + grad_in[HALO:]
-    input_grad = input_grad.at[tok_count - HALO :].add(edge)
+    input_grad = grad_in.at[tok_count - HALO :].add(edge)
 
     grad_skip = jnp.sum(gs[1].reshape(H, P_SIZE), axis=1)
 
@@ -1011,26 +1333,32 @@
         [
             gconv[:5].reshape(5, 2, half_conv).transpose(1, 0, 2),
             slot(gs[0], half_in),
-            slot(grad_gain, half_d),
+            slot(ggain[0], half_d),
             jnp.pad(head_sides, ((0, 0), (0, half_conv - 3 * half_heads)))[:, None],
         ],
         axis=1,
     )
     own = lax.dynamic_index_in_dim(packed, core, 0, keepdims=False)
     small = own + swap(lax.dynamic_index_in_dim(packed, 1 - core, 0, keepdims=False))
+    small = jnp.concatenate([small, g_rates.reshape(8, -1)], axis=1)
     for axis, bit in bits_of("rep") + bits_of("tm"):
         small = small + across(small, axis, bit)
-
-    grad_in_w = jnp.concatenate([grad_z_w, grad_u_w[:, : CONV + H]], axis=1)
+    rates = small[:, half_conv:].reshape(H, half_d)
+
+    grad_out_w = finish(scal, a_near, a_far, 3, half_in, "finish_out")
+    grad_in_t = finish(scal, b_near, b_far, 4, DIN + CONV + H, "finish_z")
+    grad_in_t = finish_conv(
+        scal, [c1_near, c1_far, c2_near, c2_far], spans, [3, 4], rates, grad_in_t
+    )
     hs = half_heads
     return (
         output[None],
         input_grad[None],
-        grad_in_w,
+        grad_in_t.T,
         grad_out_w,
         small[6, :half_d],
-        small[:4],
-        small[4],
+        small[:4, :half_conv],
+        small[4, :half_conv],
         small[7, :hs],
         small[7, hs : 2 * hs],
         small[7, 2 * hs : 3 * hs],

time: 571 us -> 457 us (0.80); the launches traced: 561 us -> 455 us
  local copies, waits for them, and re-layouts: 167 us -> 36.1 us
  Pallas kernels: 135 us -> 186 us
  other arithmetic: 43.2 us -> 19 us
  waiting for transfers between devices: 113 us -> 132 us
  matrix products: 18.4 us -> 0 us
    dynamic_update_slice x46 -> x0, local copies, waits for them, and re-layouts: 96.9 us -> none  [the longest x26 53.9 us: reduced(): buf = lax.dynamic_update_slice_in_dim(both, got, (1 - side) * n, 0)]
    pallas_call x5 -> x12, Pallas kernels: 60.2 us -> 111 us  [the longest x1 23.8 us: tail(): call(tail_kernel, (groups + 2,), [wide, pl.BlockSpec((tok_count, GROUP),...]
    dot_general x6 -> x0, matrix products: 18.4 us -> none  [outer(): lax.dot_general(a, b, (((0,), (0,)), ((), ())), preferred_element_type=f32)]
    ppermute x14, waiting for transfers between devices: 12.3 us -> 30 us  [shifted(): lax.ppermute(x, 'tm', [(i, (i + by) % length) for i in range(length)])]
    slice x14 -> x13, local copies, waits for them, and re-layouts: 14.6 us -> 4.6 us  [the longest x1 1.47 us: body(): wz_own = w_t[:DIN].astype(bf16)]
    another operation x25 -> x1, local copies, waits for them, and re-layouts: 8.59 us -> 0.63 us  [body(): jnp.stack([core, lo, lo + lengths[0], code_of(order_a), code_of(order_b)])]
    concatenate x2 -> x5, other arithmetic: 7.48 us -> 0.22 us  [the longest x4 0.21 us: spread_blocks(): near = jnp.concatenate(parts, axis=0)]
    ppermute x52 -> x44, starting transfers between devices: 58 us -> 51.9 us  [across(): lax.ppermute(x, axis, [(i, i ^ bit) for i in range(lax.axis_size(axis))])]
  transfers between devices with their start and end apart: 76 -> 68, of which waited for: 33 -> 28; matrix products, arithmetic and copies ran while one was open for 38% -> 10% of each run, Pallas kernels for 24% -> 40%
where the time goes in v2:
time: 457 us; the launch traced here: 455 us
  Pallas kernels  186 us (41%)
  waiting for transfers between devices  132 us (29%)
  starting transfers between devices  79.1 us (17%)
  local copies, waits for them, and re-layouts  36.1 us (8%)
  other arithmetic  19 us (4%)
    ppermute x44, waiting for transfers between devices, across(): lax.ppermute(x, axis, [(i, i ^ bit) for i in range(lax.axis_size(axis))])  102 us
    ppermute x44, starting transfers between devices, across(): lax.ppermute(x, axis, [(i, i ^ bit) for i in range(lax.axis_size(axis))])  51.9 us
    ppermute x14, waiting for transfers between devices, shifted(): lax.ppermute(x, 'tm', [(i, (i + by) % length) for i in range(length)])  30 us
    pallas_call x1, Pallas kernels, front(): call(front_kernel, (groups,), [const_spec((tok_count, d)), const_spec((HA...  25.7 us
    ppermute x14, starting transfers between devices, shifted(): lax.ppermute(x, 'tm', [(i, (i + by) % length) for i in range(length)])  25.7 us
    pallas_call x1, Pallas kernels, tail(): call(tail_kernel, (groups + 2,), [wide, pl.BlockSpec((tok_count, GROUP),...  23.8 us
    pallas_call x3, Pallas kernels, outer(): call(kernel, (width // step_rows,), specs, [const_spec(o) for o in outs],...  23.8 us
    pallas_call x2, Pallas kernels, finish(): call(kernel, (BLOCKS,), [pl.BlockSpec((1, rows, cols), near_map), pl.Bloc...  21.3 us
  transfers between devices with their start and end apart: 68, of which 28 were waited for; matrix products, arithmetic and copies ran while one was open for 10% of the time, Pallas kernels for 40%

profile of v2, /device:TPU:0, one launch (start us, length us, event | category | flops | bytes accessed | tf_op | source)
XLA Modules:
  0.0 454.8 jit_solution(17574723020836623866)
XLA Ops:
  0.6 4.1 convert_bitcast_fusion
  5.7 2.4 copy-done.5
  8.1 1.7 convert_element_type.209.w_own
  12.7 3.1 collective-permute-start
  18.8 2.2 vectors.1
  21.7 25.7 %front.1 = (bf16[528,512]{1,0:T(8,128)(2,1)}, bf16[528,512]{1,0:T(8,128)(2,1)}, bf16[528,2304]{1,0:T(8,128)(2,1)}, bf16[512,2304]{1,0:T(8,128)(2,1)}, bf16[512,2...) custom-call(s32[5]{0:T(128)} %stack.43.scal.refs_0_, ...), custom_call_target="tpu_custom_call" | custom-call | flops 2629828608 | bytes 13099008 | tf_op jit(solution)/shard_map/front/pallas_call | solution.py:256
  48.8 2.4 collective-permute-start.5
  52.0 1.6 collective-permute-start.8
  53.6 6.8 %collective-permute-done.5 = bf16[128,1024]{1,0:T(8,128)(2,1)S(1)} collective-permute-done((bf16[128,1024]{1,0:T(8,128)(2,1)S(1)}, bf16[128,1024]{1,0:T(8,128)(2,1)S(1)}, u32[]{:S(2)}, u32[]{:S(2)}) %collective-permute-start.5) | collective-permute-done | bytes 262176 | tf_op jit(solution)/shard_map/ppermute | solution.py:1141
  61.6 4.3 collective-permute-done.8
  65.9 5.1 %collective-permute-done.6 = bf16[128,1024]{1,0:T(8,128)(2,1)S(1)} collective-permute-done((bf16[128,1024]{1,0:T(8,128)(2,1)S(1)}, bf16[128,1024]{1,0:T(8,128)(2,1)S(1)}, u32[]{:S(2)}, u32[]{:S(2)}) %collective-permute-start.6) | collective-permute-done | bytes 262176 | tf_op jit(solution)/shard_map/ppermute | solution.py:1141
  71.3 6.8 %grad_gated.1.eg = bf16[2,512,1024]{2,1,0:T(8,128)(2,1)} custom-call(s32[5]{0:T(128)} %stack.43.scal.refs_0_, bf16[512,1024]{1,0:T(8,128)(2,1)} %bitcast.71, bf16[1024,1024]{1,0:T(8,128)(2,1)} %convert_element_type.209.w_own, bf16[1024,1024]{1,0:T(8,128)(2,1)} %collective-permute-done.4.w_oth), custom_call_target="tpu_custom_call" | custom-call | flops 2147483648 | bytes 4194304 | tf_op jit(solution)/shard_map/grad_gated/pallas_call | solution.py:833
  79.6 6.8 %gate_proj.1.z = bf16[512,2048]{1,0:T(8,128)(2,1)} custom-call(s32[5]{0:T(128)} %stack.43.scal.refs_0_, bf16[528,512]{1,0:T(8,128)(2,1)} %get-tuple-element.75.a_own.refs_3_, bf16[528,512]{1,0:T(8,128)(2,1)} %get-tuple-element.76.a_oth, bf16[2048,512]{1,0:T(8,128)(2,1)} %slice.269.w_own.wz_own, bf16[2048,512]{1,0:T(8,128)(2,1)} %collective-permute-done.3.w_oth.wz_oth), custom_call_target="tpu_custom_call" | custom-call | flops 2147483648 | bytes 4194304 | tf_op jit(solution)/shard_map/gate_proj/pallas_call | solution.py:811
  87.8 1.8 collective-permute-start.10
  89.6 14.3 %intra.1 = (f32[512,2048]{1,0:T(8,128)}, bf16[4,128,2048]{2,1,0:T(8,128)(2,1)}) custom-call(s32[5]{0:T(128)} %stack.43.scal.refs_0_, bf16[512,2304]{1,0:T(8,128)(2,1)} %get-tuple-element.70.x.bc.act, bf16[512,2304]{1,0:T(8,128)(2,1)} %get-tuple-element.70.x.bc.act, f32[512,128]{1,0:T(8,128)} %get-tuple-element.71.dt, f32[512,128]{1,0:T(8,128)} %get-tuple-element.72.cum, ...), custom_call_target="tpu_custom_call" | custom-call | flops 805306368 | bytes 8388608 | tf_op jit(solution)/shard_map/intra/pallas_call | solution.py:356
  104.8 16.8 %gate.1 = (bf16[2,512,1024]{2,1,0:T(8,128)(2,1)}, bf16[512,2048]{1,0:T(8,128)(2,1)}, bf16[512,2048]{1,0:T(8,128)(2,1)}, f32[512,128]{1,0:T(8,128)}, f32[512,128]...) custom-call(s32[5]{0:T(128)} %stack.43.scal.refs_0_, ...), custom_call_target="tpu_custom_call" | custom-call | flops 1610612736 | bytes 20971520 | tf_op jit(solution)/shard_map/gate/pallas_call | solution.py:471
  122.8 2.3 collective-permute-start.11
  125.9 2.8 slice_bitcast_fusion
  128.7 3.5 collective-permute-done.11
  132.2 4.0 collective-permute-start.12
  137.7 4.9 %collective-permute-done.12 = bf16[128,1024]{1,0:T(8,128)(2,1)S(1)} collective-permute-done((bf16[128,1024]{1,0:T(8,128)(2,1)S(1)}, bf16[128,1024]{1,0:T(8,128)(2,1)S(1)}, u32[]{:S(2)}, u32[]{:S(2)}) %collective-permute-start.12) | collective-permute-done | bytes 262176 | tf_op jit(solution)/shard_map/ppermute | solution.py:1141
  142.8 3.8 collective-permute-start.15
  146.6 18.2 %back.1 = (bf16[512,2048]{1,0:T(8,128)(2,1)}, f32[512,128]{1,0:T(8,128)}, f32[512,128]{1,0:T(8,128)}, f32[512,128]{1,0:T(8,128)}, f32[8,128]{1,0:T(8,128)}) custom-call(s32[5]{0:T(128)} %stack.43.scal.refs_0_, bf16[512,2304]{1,0:T(8,128)(2,1)} %get-tuple-element.70.x.bc.act, bf16[512,2304]{1,0:T(8,128)(2,1)} %get-tuple-element.70.x.bc.act, ...), custom_call_target="tpu_custom_call" | custom-call | flops 2147483648 | bytes 8388608 | tf_op jit(solution)/shard_map/back/pallas_call | solution.py:608
  167.0 4.8 %collective-permute-done.13 = bf16[128,1024]{1,0:T(8,128)(2,1)S(1)} collective-permute-done((bf16[128,1024]{1,0:T(8,128)(2,1)S(1)}, bf16[128,1024]{1,0:T(8,128)(2,1)S(1)}, u32[]{:S(2)}, u32[]{:S(2)}) %collective-permute-start.13) | collective-permute-done | bytes 262176 | tf_op jit(solution)/shard_map/ppermute | solution.py:1141
  171.8 2.1 collective-permute-start.16
  174.0 7.3 %grad_out.1 = (bf16[8,64,1024]{2,1,0:T(8,128)(2,1)}, bf16[8,64,1024]{2,1,0:T(8,128)(2,1)}) custom-call(s32[5]{0:T(128)} %stack.43.scal.refs_0_, bf16[512,1024]{1,0:T(8,128)(2,1)} %get-tuple-element.120.refs_1_, bf16[512,1024]{1,0:T(8,128)(2,1)} %collective-permute-done.56.refs_2_, bf16[512,1024]{1,0:T(8,128)(2,1)} %bitcast.72, ...), custom_call_target="tpu_custom_call" | custom-call | flops 2147483648 | bytes 2097152 | tf_op jit(solution)/shard_map/grad_out/pallas_call | solution.py:1021
  183.6 23.8 %tail.1 = (bf16[528,2560]{1,0:T(8,128)(2,1)}, f32[8,2304]{1,0:T(8,128)}, f32[8,128]{1,0:T(8,128)}) custom-call(s32[5]{0:T(128)} %stack.43.scal.refs_0_, bf16[512,2304]{1,0:T(8,128)(2,1)} %get-tuple-element.70.x.bc.act, bf16[512,2304]{1,0:T(8,128)(2,1)} %get-tuple-element.70.x.bc.act, bf16[512,2304]{1,0:T(8,128)(2,1)} %get-tuple-element.81.dact, ...), custom_call_target="tpu_custom_call" | custom-call | flops 1073741824 | bytes 12582912 | tf_op jit(solution)/shard_map/tail/pallas_call | solution.py:748
  208.2 14.4 %input_back.1 = (f32[512,1024]{1,0:T(8,128)}, f32[16,1024]{1,0:T(8,128)}, f32[8,1024]{1,0:T(8,128)}) custom-call(s32[5]{0:T(128)} %stack.43.scal.refs_0_, bf16[512,2048]{1,0:T(8,128)(2,1)} %get-tuple-element.80.ez.refs_1_, bf16[528,2560]{1,0:T(8,128)(2,1)} %get-tuple-element.95.eu.refs_1_.refs_5_, bf16[2048,512]{1,0:T(8,128)(2,1)} %slice.269.w_own.wz_own, ...), custom_call_target="tpu_custom_call" | custom-call | flops 4982833152 | bytes 13631488 | tf_op jit(solution)/shard_map/input_back/pallas_call | solution.py:932
  223.4 2.0 add_convert_fusion
  229.8 7.3 %grad_z.1 = (bf16[8,128,512]{2,1,0:T(8,128)(2,1)}, bf16[8,128,512]{2,1,0:T(8,128)(2,1)}) custom-call(s32[5]{0:T(128)} %stack.43.scal.refs_0_, bf16[512,2048]{1,0:T(8,128)(2,1)} %get-tuple-element.80.ez.refs_1_, bf16[512,2048]{1,0:T(8,128)(2,1)} %collective-permute-done.45.refs_2_, bf16[528,512]{1,0:T(8,128)(2,1)} %get-tuple-element.75.a_own.refs_3_, ...), custom_call_target="tpu_custom_call" | custom-call | flops 2147483648 | bytes 4194304 | tf_op jit(solution)/shard_map/grad_z/pallas_call | solution.py:1021
  237.6 4.7 %collective-permute-done.59 = bf16[4,64,1024]{2,1,0:T(8,128)(2,1)} collective-permute-done((bf16[4,64,1024]{2,1,0:T(8,128)(2,1)}, bf16[4,64,1024]{2,1,0:T(8,128)(2,1)}, u32[]{:S(2)}, u32[]{:S(2)}) %collective-permute-start.59) | collective-permute-done | bytes 524320 | tf_op jit(solution)/shard_map/ppermute | solution.py:1149
  245.2 3.0 collective-permute-start.60
  248.2 3.7 collective-permute-done.62
  252.0 4.4 collective-permute-done.61
  257.1 1.7 collective-permute-start.64
  258.8 2.7 collective-permute-start.65
  262.3 2.5 collective-permute-start.17
  264.8 4.4 collective-permute-done.64
  269.2 1.6 collective-permute-start.66
  273.9 9.8 %collective-permute-done.66 = bf16[4,64,1024]{2,1,0:T(8,128)(2,1)S(1)} collective-permute-done((bf16[4,64,1024]{2,1,0:T(8,128)(2,1)S(1)}, bf16[4,64,1024]{2,1,0:T(8,128)(2,1)S(1)}, u32[]{:S(2)}, u32[]{:S(2)}) %collective-permute-start.66) | collective-permute-done | bytes 524320 | tf_op jit(solution)/shard_map/ppermute | solution.py:1149
  286.2 2.6 collective-permute-start.50
  288.9 1.7 collective-permute-start.48
  290.6 9.2 %grad_u.1 = (bf16[8,144,256]{2,1,0:T(8,128)(2,1)}, bf16[8,144,256]{2,1,0:T(8,128)(2,1)}, bf16[8,144,256]{2,1,0:T(8,128)(2,1)}, bf16[8,144,256]{2,1,0:T(8,128)(2,1)}, f32[32,512]{1,0:T(8,128)}) custom-call(s32[5]{0:T(128)} %stack.43.scal.refs_0_, bf16[528,2560]{1,0:T(8,128)(2,1)} %get-tuple-element.95.eu.refs_1_.refs_5_, bf16[528,2560]{1,0:T(8,128)(2,1)} %copy-done.1, ...), custom_call_target="tpu_custom_call" | custom-call | flops 2491416576 | bytes 4866048 | tf_op jit(solution)/shard_map/grad_u/pallas_call | solution.py:1021
  303.9 1.6 collective-permute-start.51
  305.5 7.4 %collective-permute-done.21 = f32[8,3200]{1,0:T(8,128)S(1)} collective-permute-done((f32[8,3200]{1,0:T(8,128)S(1)}, f32[8,3200]{1,0:T(8,128)S(1)}, u32[]{:S(2)}, u32[]{:S(2)}) %collective-permute-start.21) | collective-permute-done | bytes 102432 | tf_op jit(solution)/shard_map/ppermute | solution.py:1149
  314.0 1.7 collective-permute-start.53
  315.7 7.0 %collective-permute-done.52 = bf16[1,128,512]{2,1,0:T(8,128)(2,1)S(1)} collective-permute-done((bf16[1,128,512]{2,1,0:T(8,128)(2,1)S(1)}, bf16[1,128,512]{2,1,0:T(8,128)(2,1)S(1)}, u32[]{:S(2)}, u32[]{:S(2)}) %collective-permute-start.52) | collective-permute-done | bytes 131104 | tf_op jit(solution)/shard_map/ppermute | solution.py:1149
  324.9 15.0 %collective-permute-done.22 = f32[8,3200]{1,0:T(8,128)S(1)} collective-permute-done((f32[8,3200]{1,0:T(8,128)S(1)}, f32[8,3200]{1,0:T(8,128)S(1)}, u32[]{:S(2)}, u32[]{:S(2)}) %collective-permute-start.22) | collective-permute-done | bytes 102432 | tf_op jit(solution)/shard_map/ppermute | solution.py:1149
  340.7 1.6 collective-permute-start.26
  344.0 10.7 %collective-permute-done.54 = bf16[4,128,512]{2,1,0:T(8,128)(2,1)S(1)} collective-permute-done((bf16[4,128,512]{2,1,0:T(8,128)(2,1)S(1)}, bf16[4,128,512]{2,1,0:T(8,128)(2,1)S(1)}, u32[]{:S(2)}, u32[]{:S(2)}) %collective-permute-start.54) | collective-permute-done | bytes 524320 | tf_op jit(solution)/shard_map/ppermute | solution.py:1149
  355.0 3.7 collective-permute-done.36
  359.4 1.8 collective-permute-done.29
  363.3 3.3 collective-permute-start.37
  369.0 4.2 collective-permute-start.32
  374.4 1.5 collective-permute-start.41
  376.6 3.0 collective-permute-start.42
  379.6 1.6 collective-permute-start.55
  387.3 18.1 %collective-permute-done.33 = bf16[4,144,256]{2,1,0:T(8,128)(2,1)S(1)} collective-permute-done((bf16[4,144,256]{2,1,0:T(8,128)(2,1)S(1)}, bf16[4,144,256]{2,1,0:T(8,128)(2,1)S(1)}, u32[]{:S(2)}, u32[]{:S(2)}) %collective-permute-start.33) | collective-permute-done | bytes 294944 | tf_op jit(solution)/shard_map/ppermute | solution.py:1149
  407.4 2.6 collective-permute-done.23
  411.5 7.0 %out_proj.1 = bf16[512,1024]{1,0:T(8,128)(2,1)} custom-call(s32[5]{0:T(128)} %stack.43.scal.refs_0_, bf16[2,512,1024]{2,1,0:T(8,128)(2,1)} %get-tuple-element.79.a, bf16[1024,1024]{1,0:T(8,128)(2,1)} %convert_element_type.209.w_own, bf16[1024,1024]{1,0:T(8,128)(2,1)} %collective-permute-done.4.w_oth, bf16[512,1024]{1,0:T(8,128)(2,1)} %bitcast.53), custom_call_target="tpu_custom_call" | custom-call | flops 2147483648 | bytes 4194304 | tf_op jit(solution)/shard_map/out_proj/pallas_call | solution.py:857
  421.1 3.9 collective-permute-done.24
  428.7 10.6 %finish_out.1 = f32[1024,1024]{1,0:T(8,128)} custom-call(s32[5]{0:T(128)} %stack.43.scal.refs_0_, bf16[8,64,1024]{2,1,0:T(8,128)(2,1)} %constant_dynamic-update-slice_fusion.15.refs_1_, bf16[8,64,1024]{2,1,0:T(8,128)(2,1)} %collective-permute-done.67.refs_2_), custom_call_target="tpu_custom_call" | custom-call | bytes 6291456 | tf_op jit(solution)/shard_map/finish_out/pallas_call | solution.py:1059
  439.3 10.6 %finish_z.1.refs_6_ = f32[4384,512]{1,0:T(8,128)} custom-call(s32[5]{0:T(128)} %stack.43.scal.refs_0_, bf16[8,128,512]{2,1,0:T(8,128)(2,1)} %copy-done.8, bf16[8,128,512]{2,1,0:T(8,128)(2,1)} %collective-permute-done.55.refs_2_), custom_call_target="tpu_custom_call" | custom-call | bytes 6291456 | tf_op jit(solution)/shard_map/finish_z/pallas_call | solution.py:1059
  449.9 4.6 %finish_conv.1 = f32[4384,512]{1,0:T(8,128)} custom-call(s32[5]{0:T(128)} %stack.43.scal.refs_0_, f32[32,512]{1,0:T(8,128)} %reshape.94.refs_1_, bf16[8,144,256]{2,1,0:T(8,128)(2,1)} %constant_dynamic-update-slice_fusion.refs_2_, bf16[8,144,256]{2,1,0:T(8,128)(2,1)} %collective-permute-done.34.refs_3_, ...), custom_call_target="tpu_custom_call", output_to_operand_aliasing={{}: (6, {})} | custom-call | bytes 7077888 | tf_op jit(solution)/shard_map/finish_conv/pallas_call | solution.py:1111
  (249 shorter events, 71.2 us)
Async XLA Ops:
  5.1 15.9 %collective-permute-start.2 = (bf16[2560,512]{1,0:T(8,128)(2,1)S(1)}, bf16[2560,512]{1,0:T(8,128)(2,1)}, u32[]{:S(2)}, u32[]{:S(2)}) collective-permute-start(bf16[2560,512]{1,0:T(8,128)(2,1)S(1)} %pad.19.w_own.r_own.wu_own), channel_id=1, source_target_pairs={{0,4},{4,0},{1,5},{5,1},{2,6},{6,2},{3,7},{7,3},{8,12},{12,8},{9,1... | collective-permute-start | bytes 7864328 | tf_op jit(solution)/shard_map/ppermute | solution.py:1136
  9.9 61.4 %collective-permute-start.4 = (bf16[1024,1024]{1,0:T(8,128)(2,1)}, bf16[1024,1024]{1,0:T(8,128)(2,1)}, u32[]{:S(2)}, u32[]{:S(2)}) collective-permute-start(bf16[1024,1024]{1,0:T(8,128)(2,1)} %convert_element_type.209.w_own), channel_id=1, source_target_pairs={{0,4},{4,0},{1,5},{5,1},{2,6},{6,2},{3,7},{7,3},{8,12},{12,8},{9,1... | collective-permute-start | bytes 6291464 | tf_op jit(solution)/shard_map/ppermute | solution.py:1136
  11.9 67.7 %collective-permute-start.3 = (bf16[2048,512]{1,0:T(8,128)(2,1)}, bf16[2048,512]{1,0:T(8,128)(2,1)}, u32[]{:S(2)}, u32[]{:S(2)}) collective-permute-start(bf16[2048,512]{1,0:T(8,128)(2,1)} %slice.269.w_own.wz_own), channel_id=1, source_target_pairs={{0,4},{4,0},{1,5},{5,1},{2,6},{6,2},{3,7},{7,3},{8,12},{12,8},{9,1... | collective-permute-start | bytes 6291464 | tf_op jit(solution)/shard_map/ppermute | solution.py:1136
  12.7 8.3 %collective-permute-start = (bf16[16,1024]{1,0:T(8,128)(2,1)S(1)}, bf16[16,1024]{1,0:T(8,128)(2,1)S(1)}, u32[]{:S(2)}, u32[]{:S(2)}) collective-permute-start(bf16[16,1024]{1,0:T(8,128)(2,1)S(1)} %slice_bitcast_fusion.2), channel_id=1, source_target_pairs={{0,1},{1,2},{2,3},{3,0},{4,5},{5,6},{6,7},{7,4},{8,9},{9,10},{10,1... | collective-permute-start | bytes 98312 | tf_op jit(solution)/shard_map/ppermute | solution.py:1141
  48.8 11.6 %collective-permute-start.5 = (bf16[128,1024]{1,0:T(8,128)(2,1)S(1)}, bf16[128,1024]{1,0:T(8,128)(2,1)S(1)}, u32[]{:S(2)}, u32[]{:S(2)}) collective-permute-start(bf16[128,1024]{1,0:T(8,128)(2,1)S(1)} %get-tuple-element.127), channel_id=1, source_target_pairs={{0,1},{1,2},{2,3},{3,0},{4,5},{5,6},{6,7},{7,4},{8,9},{9,10},{10,1... | collective-permute-start | bytes 786440 | tf_op jit(solution)/shard_map/ppermute | solution.py:1141
  52.0 13.9 %collective-permute-start.8 = (bf16[128,1024]{1,0:T(8,128)(2,1)S(1)}, bf16[128,1024]{1,0:T(8,128)(2,1)S(1)}, u32[]{:S(2)}, u32[]{:S(2)}) collective-permute-start(bf16[128,1024]{1,0:T(8,128)(2,1)S(1)} %get-tuple-element.128), channel_id=1, source_target_pairs={{0,1},{1,2},{2,3},{3,0},{4,5},{5,6},{6,7},{7,4},{8,9},{9,10},{10,1... | collective-permute-start | bytes 786440 | tf_op jit(solution)/shard_map/ppermute | solution.py:1141
  61.5 9.5 %collective-permute-start.6 = (bf16[128,1024]{1,0:T(8,128)(2,1)S(1)}, bf16[128,1024]{1,0:T(8,128)(2,1)S(1)}, u32[]{:S(2)}, u32[]{:S(2)}) collective-permute-start(bf16[128,1024]{1,0:T(8,128)(2,1)S(1)} %add_convert_fusion.15), channel_id=1, source_target_pairs={{0,1},{1,2},{2,3},{3,0},{4,5},{5,6},{6,7},{7,4},{8,9},{9,10},{10,1... | collective-permute-start | bytes 786440 | tf_op jit(solution)/shard_map/ppermute | solution.py:1141
  61.5 112.4 %collective-permute-start.57 = (bf16[512,1024]{1,0:T(8,128)(2,1)}, bf16[512,1024]{1,0:T(8,128)(2,1)}, u32[]{:S(2)}, u32[]{:S(2)}) collective-permute-start(bf16[512,1024]{1,0:T(8,128)(2,1)} %bitcast.70), channel_id=1, source_target_pairs={{0,4},{4,0},{1,5},{5,1},{2,6},{6,2},{3,7},{7,3},{8,12},{12,8},{9,1... | collective-permute-start | bytes 3145736 | tf_op jit(solution)/shard_map/ppermute | solution.py:1136
  71.2 16.5 %collective-permute-start.9 = (bf16[128,1024]{1,0:T(8,128)(2,1)S(1)}, bf16[128,1024]{1,0:T(8,128)(2,1)S(1)}, u32[]{:S(2)}, u32[]{:S(2)}) collective-permute-start(bf16[128,1024]{1,0:T(8,128)(2,1)S(1)} %get-tuple-element.126), channel_id=1, source_target_pairs={{0,1},{1,2},{2,3},{3,0},{4,5},{5,6},{6,7},{7,4},{8,9},{9,10},{10,1... | collective-permute-start | bytes 786440 | tf_op jit(solution)/shard_map/ppermute | solution.py:1141
  79.6 149.4 %collective-permute-start.20 = (bf16[528,512]{1,0:T(8,128)(2,1)}, bf16[528,512]{1,0:T(8,128)(2,1)S(1)}, u32[]{:S(2)}, u32[]{:S(2)}) collective-permute-start(bf16[528,512]{1,0:T(8,128)(2,1)} %get-tuple-element.76.a_oth), channel_id=1, source_target_pairs={{0,4},{4,0},{1,5},{5,1},{2,6},{6,2},{3,7},{7,3},{8,12},{12,8},{9,1... | collective-permute-start | bytes 1622024 | tf_op jit(solution)/shard_map/ppermute | solution.py:1136
  86.4 17.5 %collective-permute-start.7 = (bf16[128,1024]{1,0:T(8,128)(2,1)S(1)}, bf16[128,1024]{1,0:T(8,128)(2,1)S(1)}, u32[]{:S(2)}, u32[]{:S(2)}) collective-permute-start(bf16[128,1024]{1,0:T(8,128)(2,1)S(1)} %get-tuple-element.125), channel_id=1, source_target_pairs={{0,1},{1,2},{2,3},{3,0},{4,5},{5,6},{6,7},{7,4},{8,9},{9,10},{10,1... | collective-permute-start | bytes 786440 | tf_op jit(solution)/shard_map/ppermute | solution.py:1141
  87.8 16.2 %collective-permute-start.10 = (bf16[128,1024]{1,0:T(8,128)(2,1)S(1)}, bf16[128,1024]{1,0:T(8,128)(2,1)S(1)}, u32[]{:S(2)}, u32[]{:S(2)}) collective-permute-start(bf16[128,1024]{1,0:T(8,128)(2,1)S(1)} %add_convert_fusion.12), channel_id=1, source_target_pairs={{0,1},{1,2},{2,3},{3,0},{4,5},{5,6},{6,7},{7,4},{8,9},{9,10},{10,1... | collective-permute-start | bytes 786440 | tf_op jit(solution)/shard_map/ppermute | solution.py:1141
  122.8 9.3 %collective-permute-start.11 = (bf16[128,1024]{1,0:T(8,128)(2,1)S(1)}, bf16[128,1024]{1,0:T(8,128)(2,1)S(1)}, u32[]{:S(2)}, u32[]{:S(2)}) collective-permute-start(bf16[128,1024]{1,0:T(8,128)(2,1)S(1)} %get-tuple-element.123), channel_id=1, source_target_pairs={{0,3},{1,0},{2,1},{3,2},{4,7},{5,4},{6,5},{7,6},{8,11},{9,8},{10,9... | collective-permute-start | bytes 786440 | tf_op jit(solution)/shard_map/ppermute | solution.py:1141
  125.1 12.6 %collective-permute-start.14 = (bf16[128,1024]{1,0:T(8,128)(2,1)S(1)}, bf16[128,1024]{1,0:T(8,128)(2,1)S(1)}, u32[]{:S(2)}, u32[]{:S(2)}) collective-permute-start(bf16[128,1024]{1,0:T(8,128)(2,1)S(1)} %get-tuple-element.124), channel_id=1, source_target_pairs={{0,3},{1,0},{2,1},{3,2},{4,7},{5,4},{6,5},{7,6},{8,11},{9,8},{10,9... | collective-permute-start | bytes 786440 | tf_op jit(solution)/shard_map/ppermute | solution.py:1141
  132.2 10.4 %collective-permute-start.12 = (bf16[128,1024]{1,0:T(8,128)(2,1)S(1)}, bf16[128,1024]{1,0:T(8,128)(2,1)S(1)}, u32[]{:S(2)}, u32[]{:S(2)}) collective-permute-start(bf16[128,1024]{1,0:T(8,128)(2,1)S(1)} %add_convert_fusion.11), channel_id=1, source_target_pairs={{0,3},{1,0},{2,1},{3,2},{4,7},{5,4},{6,5},{7,6},{8,11},{9,8},{10,9... | collective-permute-start | bytes 786440 | tf_op jit(solution)/shard_map/ppermute | solution.py:1141
  137.0 37.0 %collective-permute-start.56 = (bf16[512,1024]{1,0:T(8,128)(2,1)S(1)}, bf16[512,1024]{1,0:T(8,128)(2,1)}, u32[]{:S(2)}, u32[]{:S(2)}) collective-permute-start(bf16[512,1024]{1,0:T(8,128)(2,1)S(1)} %get-tuple-element.119), channel_id=1, source_target_pairs={{0,4},{4,0},{1,5},{5,1},{2,6},{6,2},{3,7},{7,3},{8,12},{12,8},{9,1... | collective-permute-start | bytes 3145736 | tf_op jit(solution)/shard_map/ppermute | solution.py:1136
  142.8 23.1 %collective-permute-start.15 = (bf16[128,1024]{1,0:T(8,128)(2,1)S(1)}, bf16[128,1024]{1,0:T(8,128)(2,1)}, u32[]{:S(2)}, u32[]{:S(2)}) collective-permute-start(bf16[128,1024]{1,0:T(8,128)(2,1)S(1)} %get-tuple-element.122), channel_id=1, source_target_pairs={{0,3},{1,0},{2,1},{3,2},{4,7},{5,4},{6,5},{7,6},{8,11},{9,8},{10,9... | collective-permute-start | bytes 786440 | tf_op jit(solution)/shard_map/ppermute | solution.py:1141
  164.8 7.1 %collective-permute-start.13 = (bf16[128,1024]{1,0:T(8,128)(2,1)S(1)}, bf16[128,1024]{1,0:T(8,128)(2,1)S(1)}, u32[]{:S(2)}, u32[]{:S(2)}) collective-permute-start(bf16[128,1024]{1,0:T(8,128)(2,1)S(1)} %get-tuple-element.121), channel_id=1, source_target_pairs={{0,3},{1,0},{2,1},{3,2},{4,7},{5,4},{6,5},{7,6},{8,11},{9,8},{10,9... | collective-permute-start | bytes 786440 | tf_op jit(solution)/shard_map/ppermute | solution.py:1141
  165.9 63.1 %collective-permute-start.45 = (bf16[512,2048]{1,0:T(8,128)(2,1)}, bf16[512,2048]{1,0:T(8,128)(2,1)}, u32[]{:S(2)}, u32[]{:S(2)}) collective-permute-start(bf16[512,2048]{1,0:T(8,128)(2,1)} %get-tuple-element.80.ez.refs_1_), channel_id=1, source_target_pairs={{0,4},{4,0},{1,5},{5,1},{2,6},{6,2},{3,7},{7,3},{8,12},{12,8},{9,1... | collective-permute-start | bytes 6291464 | tf_op jit(solution)/shard_map/ppermute | solution.py:1136
  171.8 10.9 %collective-permute-start.16 = (bf16[128,1024]{1,0:T(8,128)(2,1)S(1)}, bf16[128,1024]{1,0:T(8,128)(2,1)S(1)}, u32[]{:S(2)}, u32[]{:S(2)}) collective-permute-start(bf16[128,1024]{1,0:T(8,128)(2,1)S(1)} %add_convert_fusion.8), channel_id=1, source_target_pairs={{0,3},{1,0},{2,1},{3,2},{4,7},{5,4},{6,5},{7,6},{8,11},{9,8},{10,9... | collective-permute-start | bytes 786440 | tf_op jit(solution)/shard_map/ppermute | solution.py:1141
  181.3 42.1 %collective-permute-start.58 = (bf16[8,64,1024]{2,1,0:T(8,128)(2,1)}, bf16[8,64,1024]{2,1,0:T(8,128)(2,1)}, u32[]{:S(2)}, u32[]{:S(2)}) collective-permute-start(bf16[8,64,1024]{2,1,0:T(8,128)(2,1)} %get-tuple-element.110), channel_id=1, source_target_pairs={{0,8},{8,0},{16,24},{24,16},{1,9},{9,1},{17,25},{25,17},{2,10},{10... | collective-permute-start | bytes 3145736 | tf_op jit(solution)/shard_map/ppermute | solution.py:1149
  207.5 81.4 %collective-permute-start.19 = (bf16[528,2560]{1,0:T(8,128)(2,1)}, bf16[528,2560]{1,0:T(8,128)(2,1)S(1)}, u32[]{:S(2)}, u32[]{:S(2)}) collective-permute-start(bf16[528,2560]{1,0:T(8,128)(2,1)} %get-tuple-element.95.eu.refs_1_.refs_5_), channel_id=1, source_target_pairs={{0,4},{4,0},{1,5},{5,1},{2,6},{6,2},{3,7},{7,3},{8,12},{12,8},{9,1... | collective-permute-start | bytes 8110088 | tf_op jit(solution)/shard_map/ppermute | solution.py:1136
  227.2 15.1 %collective-permute-start.59 = (bf16[4,64,1024]{2,1,0:T(8,128)(2,1)}, bf16[4,64,1024]{2,1,0:T(8,128)(2,1)}, u32[]{:S(2)}, u32[]{:S(2)}) collective-permute-start(bf16[4,64,1024]{2,1,0:T(8,128)(2,1)} %slice.292), channel_id=1, source_target_pairs={{0,16},{8,24},{16,0},{24,8},{1,17},{9,25},{17,1},{25,9},{2,18},{10... | collective-permute-start | bytes 1572872 | tf_op jit(solution)/shard_map/ppermute | solution.py:1149
  237.2 33.7 %collective-permute-start.46 = (bf16[8,128,512]{2,1,0:T(8,128)(2,1)}, bf16[8,128,512]{2,1,0:T(8,128)(2,1)S(1)}, u32[]{:S(2)}, u32[]{:S(2)}) collective-permute-start(bf16[8,128,512]{2,1,0:T(8,128)(2,1)} %get-tuple-element.108), channel_id=1, source_target_pairs={{0,16},{8,24},{16,0},{24,8},{1,17},{9,25},{17,1},{25,9},{2,18},{10... | collective-permute-start | bytes 3145736 | tf_op jit(solution)/shard_map/ppermute | solution.py:1149
  243.7 8.2 %collective-permute-start.62 = (bf16[1,64,1024]{2,1,0:T(8,128)(2,1)S(1)}, bf16[1,64,1024]{2,1,0:T(8,128)(2,1)S(1)}, u32[]{:S(2)}, u32[]{:S(2)}) collective-permute-start(bf16[1,64,1024]{2,1,0:T(8,128)(2,1)S(1)} %get-tuple-element.130), channel_id=1, source_target_pairs={{0,3},{1,2},{2,1},{3,0},{4,7},{5,6},{6,5},{7,4},{8,11},{9,10},{10,... | collective-permute-start | bytes 393224 | tf_op jit(solution)/shard_map/ppermute | solution.py:1149
  243.8 12.6 %collective-permute-start.61 = (bf16[1,64,1024]{2,1,0:T(8,128)(2,1)S(1)}, bf16[1,64,1024]{2,1,0:T(8,128)(2,1)S(1)}, u32[]{:S(2)}, u32[]{:S(2)}) collective-permute-start(bf16[1,64,1024]{2,1,0:T(8,128)(2,1)S(1)} %get-tuple-element.131), channel_id=1, source_target_pairs={{0,2},{1,3},{2,0},{3,1},{4,6},{5,7},{6,4},{7,5},{8,10},{9,11},{10,... | collective-permute-start | bytes 393224 | tf_op jit(solution)/shard_map/ppermute | solution.py:1149
  245.2 11.2 %collective-permute-start.60 = (bf16[1,64,1024]{2,1,0:T(8,128)(2,1)S(1)}, bf16[1,64,1024]{2,1,0:T(8,128)(2,1)S(1)}, u32[]{:S(2)}, u32[]{:S(2)}) collective-permute-start(bf16[1,64,1024]{2,1,0:T(8,128)(2,1)S(1)} %get-tuple-element.129), channel_id=1, source_target_pairs={{0,1},{1,0},{2,3},{3,2},{4,5},{5,4},{6,7},{7,6},{8,9},{9,8},{10,11... | collective-permute-start | bytes 393224 | tf_op jit(solution)/shard_map/ppermute | solution.py:1149
  257.1 5.2 %collective-permute-start.63 = (bf16[1,64,1024]{2,1,0:T(8,128)(2,1)S(1)}, bf16[1,64,1024]{2,1,0:T(8,128)(2,1)S(1)}, u32[]{:S(2)}, u32[]{:S(2)}) collective-permute-start(bf16[1,64,1024]{2,1,0:T(8,128)(2,1)S(1)} %get-tuple-element.112), channel_id=1, source_target_pairs={{0,1},{1,0},{2,3},{3,2},{4,5},{5,4},{6,7},{7,6},{8,9},{9,8},{10,11... | collective-permute-start | bytes 393224 | tf_op jit(solution)/shard_map/ppermute | solution.py:1149
  257.1 12.0 %collective-permute-start.64 = (bf16[1,64,1024]{2,1,0:T(8,128)(2,1)S(1)}, bf16[1,64,1024]{2,1,0:T(8,128)(2,1)S(1)}, u32[]{:S(2)}, u32[]{:S(2)}) collective-permute-start(bf16[1,64,1024]{2,1,0:T(8,128)(2,1)S(1)} %get-tuple-element.112), channel_id=1, source_target_pairs={{0,2},{1,3},{2,0},{3,1},{4,6},{5,7},{6,4},{7,5},{8,10},{9,11},{10,... | collective-permute-start | bytes 393224 | tf_op jit(solution)/shard_map/ppermute | solution.py:1149
  258.8 10.4 %collective-permute-start.65 = (bf16[1,64,1024]{2,1,0:T(8,128)(2,1)S(1)}, bf16[1,64,1024]{2,1,0:T(8,128)(2,1)S(1)}, u32[]{:S(2)}, u32[]{:S(2)}) collective-permute-start(bf16[1,64,1024]{2,1,0:T(8,128)(2,1)S(1)} %get-tuple-element.112), channel_id=1, source_target_pairs={{0,3},{1,2},{2,1},{3,0},{4,7},{5,6},{6,5},{7,4},{8,11},{9,10},{10,... | collective-permute-start | bytes 393224 | tf_op jit(solution)/shard_map/ppermute | solution.py:1149
  262.3 156.5 %collective-permute-start.17 = (f32[16,1024]{1,0:T(8,128)}, f32[16,1024]{1,0:T(8,128)}, u32[]{:S(2)}, u32[]{:S(2)}) collective-permute-start(f32[16,1024]{1,0:T(8,128)} %get-tuple-element.97), channel_id=1, source_target_pairs={{0,3},{1,0},{2,1},{3,2},{4,7},{5,4},{6,5},{7,6},{8,11},{9,8},{10,9... | collective-permute-start | bytes 196616 | tf_op jit(solution)/shard_map/ppermute | solution.py:1141
  269.2 14.4 %collective-permute-start.66 = (bf16[4,64,1024]{2,1,0:T(8,128)(2,1)S(1)}, bf16[4,64,1024]{2,1,0:T(8,128)(2,1)S(1)}, u32[]{:S(2)}, u32[]{:S(2)}) collective-permute-start(bf16[4,64,1024]{2,1,0:T(8,128)(2,1)S(1)} %pad_maximum_fusion.3), channel_id=1, source_target_pairs={{0,16},{8,24},{16,0},{24,8},{1,17},{9,25},{17,1},{25,9},{2,18},{10... | collective-permute-start | bytes 1572872 | tf_op jit(solution)/shard_map/ppermute | solution.py:1149
  271.2 14.1 %collective-permute-start.47 = (bf16[4,128,512]{2,1,0:T(8,128)(2,1)S(1)}, bf16[4,128,512]{2,1,0:T(8,128)(2,1)S(1)}, u32[]{:S(2)}, u32[]{:S(2)}) collective-permute-start(bf16[4,128,512]{2,1,0:T(8,128)(2,1)S(1)} %slice.286), channel_id=1, source_target_pairs={{0,8},{8,0},{16,24},{24,16},{1,9},{9,1},{17,25},{25,17},{2,10},{10... | collective-permute-start | bytes 1572872 | tf_op jit(solution)/shard_map/ppermute | solution.py:1149
  284.5 144.2 %collective-permute-start.67 = (bf16[8,64,1024]{2,1,0:T(8,128)(2,1)}, bf16[8,64,1024]{2,1,0:T(8,128)(2,1)}, u32[]{:S(2)}, u32[]{:S(2)}) collective-permute-start(bf16[8,64,1024]{2,1,0:T(8,128)(2,1)} %constant_dynamic-update-slice_fusion.15.refs_1_), channel_id=1, source_target_pairs={{0,8},{8,0},{16,24},{24,16},{1,9},{9,1},{17,25},{25,17},{2,10},{10... | collective-permute-start | bytes 3145736 | tf_op jit(solution)/shard_map/ppermute | solution.py:1149
  286.2 14.6 %collective-permute-start.50 = (bf16[1,128,512]{2,1,0:T(8,128)(2,1)}, bf16[1,128,512]{2,1,0:T(8,128)(2,1)S(1)}, u32[]{:S(2)}, u32[]{:S(2)}) collective-permute-start(bf16[1,128,512]{2,1,0:T(8,128)(2,1)} %get-tuple-element.133), channel_id=1, source_target_pairs={{0,3},{1,2},{2,1},{3,0},{4,7},{5,6},{6,5},{7,4},{8,11},{9,10},{10,... | collective-permute-start | bytes 393224 | tf_op jit(solution)/shard_map/ppermute | solution.py:1149
  288.9 13.2 %collective-permute-start.49 = (bf16[1,128,512]{2,1,0:T(8,128)(2,1)}, bf16[1,128,512]{2,1,0:T(8,128)(2,1)S(1)}, u32[]{:S(2)}, u32[]{:S(2)}) collective-permute-start(bf16[1,128,512]{2,1,0:T(8,128)(2,1)} %get-tuple-element.134), channel_id=1, source_target_pairs={{0,2},{1,3},{2,0},{3,1},{4,6},{5,7},{6,4},{7,5},{8,10},{9,11},{10,... | collective-permute-start | bytes 393224 | tf_op jit(solution)/shard_map/ppermute | solution.py:1149
  288.9 14.0 %collective-permute-start.48 = (bf16[1,128,512]{2,1,0:T(8,128)(2,1)}, bf16[1,128,512]{2,1,0:T(8,128)(2,1)}, u32[]{:S(2)}, u32[]{:S(2)}) collective-permute-start(bf16[1,128,512]{2,1,0:T(8,128)(2,1)} %get-tuple-element.132), channel_id=1, source_target_pairs={{0,1},{1,0},{2,3},{3,2},{4,5},{5,4},{6,7},{7,6},{8,9},{9,8},{10,11... | collective-permute-start | bytes 393224 | tf_op jit(solution)/shard_map/ppermute | solution.py:1149
  300.8 12.1 %collective-permute-start.21 = (f32[8,3200]{1,0:T(8,128)S(1)}, f32[8,3200]{1,0:T(8,128)S(1)}, u32[]{:S(2)}, u32[]{:S(2)}) collective-permute-start(f32[8,3200]{1,0:T(8,128)S(1)} %pad_maximum_fusion.6), channel_id=1, source_target_pairs={{0,8},{8,0},{16,24},{24,16},{1,9},{9,1},{17,25},{25,17},{2,10},{10... | collective-permute-start | bytes 307208 | tf_op jit(solution)/shard_map/ppermute | solution.py:1149
  302.1 38.4 %collective-permute-start.25 = (bf16[8,144,256]{2,1,0:T(8,128)(2,1)}, bf16[8,144,256]{2,1,0:T(8,128)(2,1)S(1)}, u32[]{:S(2)}, u32[]{:S(2)}) collective-permute-start(bf16[8,144,256]{2,1,0:T(8,128)(2,1)} %get-tuple-element.104), channel_id=1, source_target_pairs={{0,8},{8,0},{16,24},{24,16},{1,9},{9,1},{17,25},{25,17},{2,10},{10... | collective-permute-start | bytes 1769480 | tf_op jit(solution)/shard_map/ppermute | solution.py:1149
  303.9 10.1 %collective-permute-start.51 = (bf16[1,128,512]{2,1,0:T(8,128)(2,1)S(1)}, bf16[1,128,512]{2,1,0:T(8,128)(2,1)S(1)}, u32[]{:S(2)}, u32[]{:S(2)}) collective-permute-start(bf16[1,128,512]{2,1,0:T(8,128)(2,1)S(1)} %get-tuple-element.114), channel_id=1, source_target_pairs={{0,1},{1,0},{2,3},{3,2},{4,5},{5,4},{6,7},{7,6},{8,9},{9,8},{10,11... | collective-permute-start | bytes 393224 | tf_op jit(solution)/shard_map/ppermute | solution.py:1149
  312.9 9.8 %collective-permute-start.52 = (bf16[1,128,512]{2,1,0:T(8,128)(2,1)S(1)}, bf16[1,128,512]{2,1,0:T(8,128)(2,1)S(1)}, u32[]{:S(2)}, u32[]{:S(2)}) collective-permute-start(bf16[1,128,512]{2,1,0:T(8,128)(2,1)S(1)} %get-tuple-element.114), channel_id=1, source_target_pairs={{0,2},{1,3},{2,0},{3,1},{4,6},{5,7},{6,4},{7,5},{8,10},{9,11},{10,... | collective-permute-start | bytes 393224 | tf_op jit(solution)/shard_map/ppermute | solution.py:1149
  314.0 10.3 %collective-permute-start.53 = (bf16[1,128,512]{2,1,0:T(8,128)(2,1)S(1)}, bf16[1,128,512]{2,1,0:T(8,128)(2,1)S(1)}, u32[]{:S(2)}, u32[]{:S(2)}) collective-permute-start(bf16[1,128,512]{2,1,0:T(8,128)(2,1)S(1)} %get-tuple-element.114), channel_id=1, source_target_pairs={{0,3},{1,2},{2,1},{3,0},{4,7},{5,6},{6,5},{7,4},{8,11},{9,10},{10,... | collective-permute-start | bytes 393224 | tf_op jit(solution)/shard_map/ppermute | solution.py:1149
  322.7 19.6 %collective-permute-start.35 = (bf16[8,144,256]{2,1,0:T(8,128)(2,1)}, bf16[8,144,256]{2,1,0:T(8,128)(2,1)S(1)}, u32[]{:S(2)}, u32[]{:S(2)}) collective-permute-start(bf16[8,144,256]{2,1,0:T(8,128)(2,1)} %get-tuple-element.106), channel_id=1, source_target_pairs={{0,16},{8,24},{16,0},{24,8},{1,17},{9,25},{17,1},{25,9},{2,18},{10... | collective-permute-start | bytes 1769480 | tf_op jit(solution)/shard_map/ppermute | solution.py:1149
  324.3 15.6 %collective-permute-start.22 = (f32[8,3200]{1,0:T(8,128)S(1)}, f32[8,3200]{1,0:T(8,128)S(1)}, u32[]{:S(2)}, u32[]{:S(2)}) collective-permute-start(f32[8,3200]{1,0:T(8,128)S(1)} %fusion.3), channel_id=1, source_target_pairs={{0,16},{8,24},{16,0},{24,8},{1,17},{9,25},{17,1},{25,9},{2,18},{10... | collective-permute-start | bytes 307208 | tf_op jit(solution)/shard_map/ppermute | solution.py:1149
  339.9 14.8 %collective-permute-start.54 = (bf16[4,128,512]{2,1,0:T(8,128)(2,1)S(1)}, bf16[4,128,512]{2,1,0:T(8,128)(2,1)S(1)}, u32[]{:S(2)}, u32[]{:S(2)}) collective-permute-start(bf16[4,128,512]{2,1,0:T(8,128)(2,1)S(1)} %pad_maximum_fusion.2), channel_id=1, source_target_pairs={{0,8},{8,0},{16,24},{24,16},{1,9},{9,1},{17,25},{25,17},{2,10},{10... | collective-permute-start | bytes 1572872 | tf_op jit(solution)/shard_map/ppermute | solution.py:1149
  340.7 14.0 %collective-permute-start.26 = (bf16[4,144,256]{2,1,0:T(8,128)(2,1)S(1)}, bf16[4,144,256]{2,1,0:T(8,128)(2,1)S(1)}, u32[]{:S(2)}, u32[]{:S(2)}) collective-permute-start(bf16[4,144,256]{2,1,0:T(8,128)(2,1)S(1)} %slice.274), channel_id=1, source_target_pairs={{0,16},{8,24},{16,0},{24,8},{1,17},{9,25},{17,1},{25,9},{2,18},{10... | collective-permute-start | bytes 884744 | tf_op jit(solution)/shard_map/ppermute | solution.py:1149
  342.5 16.2 %collective-permute-start.36 = (bf16[4,144,256]{2,1,0:T(8,128)(2,1)S(1)}, bf16[4,144,256]{2,1,0:T(8,128)(2,1)S(1)}, u32[]{:S(2)}, u32[]{:S(2)}) collective-permute-start(bf16[4,144,256]{2,1,0:T(8,128)(2,1)S(1)} %slice.280), channel_id=1, source_target_pairs={{0,8},{8,0},{16,24},{24,16},{1,9},{9,1},{17,25},{25,17},{2,10},{10... | collective-permute-start | bytes 884744 | tf_op jit(solution)/shard_map/ppermute | solution.py:1149
  354.8 6.3 %collective-permute-start.29 = (bf16[1,144,256]{2,1,0:T(8,128)(2,1)S(1)}, bf16[1,144,256]{2,1,0:T(8,128)(2,1)S(1)}, u32[]{:S(2)}, u32[]{:S(2)}) collective-permute-start(bf16[1,144,256]{2,1,0:T(8,128)(2,1)S(1)} %get-tuple-element.139), channel_id=1, source_target_pairs={{0,3},{1,2},{2,1},{3,0},{4,7},{5,6},{6,5},{7,4},{8,11},{9,10},{10,... | collective-permute-start | bytes 221192 | tf_op jit(solution)/shard_map/ppermute | solution.py:1149
  354.9 6.3 %collective-permute-start.28 = (bf16[1,144,256]{2,1,0:T(8,128)(2,1)S(1)}, bf16[1,144,256]{2,1,0:T(8,128)(2,1)S(1)}, u32[]{:S(2)}, u32[]{:S(2)}) collective-permute-start(bf16[1,144,256]{2,1,0:T(8,128)(2,1)S(1)} %get-tuple-element.140), channel_id=1, source_target_pairs={{0,2},{1,3},{2,0},{3,1},{4,6},{5,7},{6,4},{7,5},{8,10},{9,11},{10,... | collective-permute-start | bytes 221192 | tf_op jit(solution)/shard_map/ppermute | solution.py:1149
  361.2 6.3 %collective-permute-start.39 = (bf16[1,144,256]{2,1,0:T(8,128)(2,1)S(1)}, bf16[1,144,256]{2,1,0:T(8,128)(2,1)S(1)}, u32[]{:S(2)}, u32[]{:S(2)}) collective-permute-start(bf16[1,144,256]{2,1,0:T(8,128)(2,1)S(1)} %get-tuple-element.136), channel_id=1, source_target_pairs={{0,3},{1,2},{2,1},{3,0},{4,7},{5,6},{6,5},{7,4},{8,11},{9,10},{10,... | collective-permute-start | bytes 221192 | tf_op jit(solution)/shard_map/ppermute | solution.py:1149
  361.2 6.3 %collective-permute-start.38 = (bf16[1,144,256]{2,1,0:T(8,128)(2,1)S(1)}, bf16[1,144,256]{2,1,0:T(8,128)(2,1)S(1)}, u32[]{:S(2)}, u32[]{:S(2)}) collective-permute-start(bf16[1,144,256]{2,1,0:T(8,128)(2,1)S(1)} %get-tuple-element.137), channel_id=1, source_target_pairs={{0,2},{1,3},{2,0},{3,1},{4,6},{5,7},{6,4},{7,5},{8,10},{9,11},{10,... | collective-permute-start | bytes 221192 | tf_op jit(solution)/shard_map/ppermute | solution.py:1149
  363.3 5.7 %collective-permute-start.37 = (bf16[1,144,256]{2,1,0:T(8,128)(2,1)S(1)}, bf16[1,144,256]{2,1,0:T(8,128)(2,1)S(1)}, u32[]{:S(2)}, u32[]{:S(2)}) collective-permute-start(bf16[1,144,256]{2,1,0:T(8,128)(2,1)S(1)} %get-tuple-element.135), channel_id=1, source_target_pairs={{0,1},{1,0},{2,3},{3,2},{4,5},{5,4},{6,7},{7,6},{8,9},{9,8},{10,11... | collective-permute-start | bytes 221192 | tf_op jit(solution)/shard_map/ppermute | solution.py:1149
  367.5 6.4 %collective-permute-start.30 = (bf16[1,144,256]{2,1,0:T(8,128)(2,1)S(1)}, bf16[1,144,256]{2,1,0:T(8,128)(2,1)S(1)}, u32[]{:S(2)}, u32[]{:S(2)}) collective-permute-start(bf16[1,144,256]{2,1,0:T(8,128)(2,1)S(1)} %get-tuple-element.118), channel_id=1, source_target_pairs={{0,1},{1,0},{2,3},{3,2},{4,5},{5,4},{6,7},{7,6},{8,9},{9,8},{10,11... | collective-permute-start | bytes 221192 | tf_op jit(solution)/shard_map/ppermute | solution.py:1149
  367.5 6.9 %collective-permute-start.31 = (bf16[1,144,256]{2,1,0:T(8,128)(2,1)S(1)}, bf16[1,144,256]{2,1,0:T(8,128)(2,1)S(1)}, u32[]{:S(2)}, u32[]{:S(2)}) collective-permute-start(bf16[1,144,256]{2,1,0:T(8,128)(2,1)S(1)} %get-tuple-element.118), channel_id=1, source_target_pairs={{0,2},{1,3},{2,0},{3,1},{4,6},{5,7},{6,4},{7,5},{8,10},{9,11},{10,... | collective-permute-start | bytes 221192 | tf_op jit(solution)/shard_map/ppermute | solution.py:1149
  369.0 7.6 %collective-permute-start.32 = (bf16[1,144,256]{2,1,0:T(8,128)(2,1)S(1)}, bf16[1,144,256]{2,1,0:T(8,128)(2,1)S(1)}, u32[]{:S(2)}, u32[]{:S(2)}) collective-permute-start(bf16[1,144,256]{2,1,0:T(8,128)(2,1)S(1)} %get-tuple-element.118), channel_id=1, source_target_pairs={{0,3},{1,2},{2,1},{3,0},{4,7},{5,6},{6,5},{7,4},{8,11},{9,10},{10,... | collective-permute-start | bytes 221192 | tf_op jit(solution)/shard_map/ppermute | solution.py:1149
  373.9 5.7 %collective-permute-start.40 = (bf16[1,144,256]{2,1,0:T(8,128)(2,1)S(1)}, bf16[1,144,256]{2,1,0:T(8,128)(2,1)S(1)}, u32[]{:S(2)}, u32[]{:S(2)}) collective-permute-start(bf16[1,144,256]{2,1,0:T(8,128)(2,1)S(1)} %get-tuple-element.116), channel_id=1, source_target_pairs={{0,1},{1,0},{2,3},{3,2},{4,5},{5,4},{6,7},{7,6},{8,9},{9,8},{10,11... | collective-permute-start | bytes 221192 | tf_op jit(solution)/shard_map/ppermute | solution.py:1149
  374.4 6.8 %collective-permute-start.41 = (bf16[1,144,256]{2,1,0:T(8,128)(2,1)S(1)}, bf16[1,144,256]{2,1,0:T(8,128)(2,1)S(1)}, u32[]{:S(2)}, u32[]{:S(2)}) collective-permute-start(bf16[1,144,256]{2,1,0:T(8,128)(2,1)S(1)} %get-tuple-element.116), channel_id=1, source_target_pairs={{0,2},{1,3},{2,0},{3,1},{4,6},{5,7},{6,4},{7,5},{8,10},{9,11},{10,... | collective-permute-start | bytes 221192 | tf_op jit(solution)/shard_map/ppermute | solution.py:1149
  376.6 6.2 %collective-permute-start.42 = (bf16[1,144,256]{2,1,0:T(8,128)(2,1)S(1)}, bf16[1,144,256]{2,1,0:T(8,128)(2,1)S(1)}, u32[]{:S(2)}, u32[]{:S(2)}) collective-permute-start(bf16[1,144,256]{2,1,0:T(8,128)(2,1)S(1)} %get-tuple-element.116), channel_id=1, source_target_pairs={{0,3},{1,2},{2,1},{3,0},{4,7},{5,6},{6,5},{7,4},{8,11},{9,10},{10,... | collective-permute-start | bytes 221192 | tf_op jit(solution)/shard_map/ppermute | solution.py:1149
  379.6 59.7 %collective-permute-start.55 = (bf16[8,128,512]{2,1,0:T(8,128)(2,1)S(1)}, bf16[8,128,512]{2,1,0:T(8,128)(2,1)}, u32[]{:S(2)}, u32[]{:S(2)}) collective-permute-start(bf16[8,128,512]{2,1,0:T(8,128)(2,1)S(1)} %constant_dynamic-update-slice_fusion.10.refs_1_), channel_id=1, source_target_pairs={{0,16},{8,24},{16,0},{24,8},{1,17},{9,25},{17,1},{25,9},{2,18},{10... | collective-permute-start | bytes 3145736 | tf_op jit(solution)/shard_map/ppermute | solution.py:1149
  381.2 24.2 %collective-permute-start.33 = (bf16[4,144,256]{2,1,0:T(8,128)(2,1)S(1)}, bf16[4,144,256]{2,1,0:T(8,128)(2,1)S(1)}, u32[]{:S(2)}, u32[]{:S(2)}) collective-permute-start(bf16[4,144,256]{2,1,0:T(8,128)(2,1)S(1)} %pad_maximum_fusion.4), channel_id=1, source_target_pairs={{0,16},{8,24},{16,0},{24,8},{1,17},{9,25},{17,1},{25,9},{2,18},{10... | collective-permute-start | bytes 884744 | tf_op jit(solution)/shard_map/ppermute | solution.py:1149
  382.8 23.3 %collective-permute-start.43 = (bf16[4,144,256]{2,1,0:T(8,128)(2,1)S(1)}, bf16[4,144,256]{2,1,0:T(8,128)(2,1)S(1)}, u32[]{:S(2)}, u32[]{:S(2)}) collective-permute-start(bf16[4,144,256]{2,1,0:T(8,128)(2,1)S(1)} %pad_maximum_fusion.5), channel_id=1, source_target_pairs={{0,8},{8,0},{16,24},{24,16},{1,9},{9,1},{17,25},{25,17},{2,10},{10... | collective-permute-start | bytes 884744 | tf_op jit(solution)/shard_map/ppermute | solution.py:1149
  406.1 43.8 %collective-permute-start.34 = (bf16[8,144,256]{2,1,0:T(8,128)(2,1)}, bf16[8,144,256]{2,1,0:T(8,128)(2,1)}, u32[]{:S(2)}, u32[]{:S(2)}) collective-permute-start(bf16[8,144,256]{2,1,0:T(8,128)(2,1)} %constant_dynamic-update-slice_fusion.refs_2_), channel_id=1, source_target_pairs={{0,8},{8,0},{16,24},{24,16},{1,9},{9,1},{17,25},{25,17},{2,10},{10... | collective-permute-start | bytes 1769480 | tf_op jit(solution)/shard_map/ppermute | solution.py:1149
  410.0 39.9 %collective-permute-start.44 = (bf16[8,144,256]{2,1,0:T(8,128)(2,1)}, bf16[8,144,256]{2,1,0:T(8,128)(2,1)}, u32[]{:S(2)}, u32[]{:S(2)}) collective-permute-start(bf16[8,144,256]{2,1,0:T(8,128)(2,1)} %constant_dynamic-update-slice_fusion.5.refs_4_), channel_id=1, source_target_pairs={{0,16},{8,24},{16,0},{24,8},{1,17},{9,25},{17,1},{25,9},{2,18},{10... | collective-permute-start | bytes 1769480 | tf_op jit(solution)/shard_map/ppermute | solution.py:1149
  418.8 6.2 %collective-permute-start.24 = (f32[8,3200]{1,0:T(8,128)S(1)}, f32[8,3200]{1,0:T(8,128)S(1)}, u32[]{:S(2)}, u32[]{:S(2)}) collective-permute-start(f32[8,3200]{1,0:T(8,128)S(1)} %add.189), channel_id=1, source_target_pairs={{0,2},{1,3},{2,0},{3,1},{4,6},{5,7},{6,4},{7,5},{8,10},{9,11},{10,... | collective-permute-start | bytes 307208 | tf_op jit(solution)/shard_map/ppermute | solution.py:1149
  (28 other events, 240.6 us)

commit v3 on v2

--- a/solution.py
+++ b/solution.py
@@ -22,6 +22,9 @@
 HIGHEST = lax.Precision.HIGHEST
 
 VMEM_LIMIT = 60 * 1024 * 1024
+COST = 1000
+CHUNKS = 4
+BLOCKS = 16
 
 
 def nn(a, b):
@@ -78,7 +81,9 @@
         ),
         out_shape=out_shape,
         compiler_params=params(len(grid)),
-        cost_estimate=pl.CostEstimate(flops=flops, bytes_accessed=nbytes, transcendentals=0),
+        cost_estimate=pl.CostEstimate(
+            flops=flops // COST, bytes_accessed=nbytes // COST, transcendentals=0
+        ),
         name=name,
     )
 
@@ -380,7 +385,7 @@
 
 def gate_kernel(
     scal, yloc, act, z, eg, cum, s_in, vecs,
-    gated, ey_out, ez_out, r_loc, r_dev, dc_out, g_out, gs_out,
+    own_out, oth_out, ey_out, ez_out, r_loc, r_dev, dc_out, g_out, gs_out,
     pick, vbuf, ytbuf, ydbuf,
 ):
     step = pl.program_id(0)
@@ -413,17 +418,22 @@
         ssq = ssq + v * v
     rs = lax.rsqrt(jnp.sum(ssq, axis=-1, keepdims=True) / DIN + EPS)
     mixed = jnp.zeros((rows, GROUP), f32)
-    for g in range(groups):
-        cols = slice(g * GROUP, (g + 1) * GROUP)
-        n = vbuf[:, cols] * rs
-        vbuf[:, cols] = n
-        gain = vecs[0:1, cols]
-        side = (g // per) ^ scal[0]
-        local = slice((g % per) * GROUP, (g % per + 1) * GROUP)
-        gated[side, :, local] = (n * gain * valid).astype(bf16)
-        e = eg[side, :, local].astype(f32) * valid
-        gs_out[0:1, cols] += jnp.sum(e * n, axis=0, keepdims=True)
-        mixed = mixed + e * gain * n
+    low_half = scal[0] == 0
+    for i in range(per):
+        local = slice(i * GROUP, (i + 1) * GROUP)
+        outs = []
+        for half in range(2):
+            g = half * per + i
+            cols = slice(g * GROUP, (g + 1) * GROUP)
+            n = vbuf[:, cols] * rs
+            vbuf[:, cols] = n
+            gain = vecs[0:1, cols]
+            outs.append((n * gain * valid).astype(bf16))
+            e = eg[half ^ scal[0], :, local].astype(f32) * valid
+            gs_out[0:1, cols] += jnp.sum(e * n, axis=0, keepdims=True)
+            mixed = mixed + e * gain * n
+        own_out[:, local] = jnp.where(low_half, outs[0], outs[1])
+        oth_out[:, local] = jnp.where(low_half, outs[1], outs[0])
     m2 = jnp.sum(mixed, axis=-1, keepdims=True) / DIN
     rl = jnp.zeros((rows, LANE), f32)
     rd = jnp.zeros((rows, LANE), f32)
@@ -481,7 +491,8 @@
             const_spec((8, DIN)),
         ],
         [
-            sides,
+            rowspec(DIN // 2),
+            rowspec(DIN // 2),
             rowspec(DIN),
             rowspec(DIN),
             rowspec(LANE),
@@ -491,7 +502,8 @@
             const_spec((8, DIN)),
         ],
         [
-            jax.ShapeDtypeStruct((2, tok_count, DIN // 2), bf16),
+            out(DIN // 2, bf16),
+            out(DIN // 2, bf16),
             out(DIN, bf16),
             out(DIN, bf16),
             out(LANE, f32),
@@ -639,9 +651,11 @@
 def tail_kernel(
     scal, act, bc, dact, u, ey, dxt, taps, dt, sg, cum, g_in, s_in, skip, heads,
     db_loc, dc_loc, dc_dev, r_loc, r_dev, r2, cq,
-    eu_out, gconv, ghead,
-    ebuf, ubuf, p_acc, d_acc, db_acc, gs_acc,
+    *rest,
 ):
+    chunks = rest[: CHUNKS + 1]
+    gconv, ghead, ebuf, ubuf, p_acc, d_acc, db_acc, gs_acc = rest[CHUNKS + 1 :]
+    eu_out = chunks[-1]
     step = pl.program_id(0)
     last = pl.num_programs(0) - 2
     tok_count = act.shape[0]
@@ -728,7 +742,11 @@
         gconv[...] = jnp.concatenate(gs, axis=0)
         eu = sum(taps[k : k + 1, :] * ebuf[3 - k : 3 - k + ext, :] for k in range(K))
         pos = iota(eu.shape, 0) - HALO
-        eu_out[...] = jnp.where((pos >= lo) & (pos < hi), eu, 0.0).astype(bf16)
+        eu = jnp.where((pos >= lo) & (pos < hi), eu, 0.0).astype(bf16)
+        for c, chunk in enumerate(chunks):
+            @pl.when(step // 2 == c)
+            def _():
+                chunk[...] = eu
 
 
 def tail(scal, act, dact, u, ey, dxt, taps, dt, sg, cum, g_in, s_in, skip, heads, smalls):
@@ -741,6 +759,9 @@
 
     def colx(j, *_):
         return (0, jnp.minimum(j, groups - 1))
+
+    def chunk(c):
+        return pl.BlockSpec((ext, GROUP), lambda j, *_: (0, jnp.clip(j - 2 * c, 0, 1)))
 
     wide = pl.BlockSpec((tok_count, GROUP), col)
     widex = pl.BlockSpec((tok_count, GROUP), colx)
@@ -772,12 +793,12 @@
             const_spec((8, LANE)),
         ],
         [
-            pl.BlockSpec((ext, GROUP), lambda j, *_: (0, j)),
+            *[chunk(c) for c in range(CHUNKS + 1)],
             pl.BlockSpec((8, GROUP), col),
             const_spec((8, LANE)),
         ],
         [
-            jax.ShapeDtypeStruct((ext, CONV + GROUP), bf16),
+            *[jax.ShapeDtypeStruct((ext, 2 * GROUP), bf16)] * (CHUNKS + 1),
             jax.ShapeDtypeStruct((8, CONV), f32),
             jax.ShapeDtypeStruct((8, LANE), f32),
         ],
@@ -843,12 +864,12 @@
     )(scal, e, wo_own, wo_oth)
 
 
-def out_proj_kernel(scal, a, w_own, w_oth, tok, out):
-    total = tok[...].astype(f32) + nn(a[0], w_own[...]) + nn(a[1], w_oth[...])
+def out_proj_kernel(scal, a_own, a_oth, w_own, w_oth, tok, out):
+    total = tok[...].astype(f32) + nn(a_own[...], w_own[...]) + nn(a_oth[...], w_oth[...])
     out[...] = total.astype(bf16)
 
 
-def out_proj(scal, gated, wo_own, wo_oth, tok):
+def out_proj(scal, g_own, g_oth, wo_own, wo_oth, tok):
     rows, d = tok.shape
     half = wo_own.shape[0]
     wide = 2 * GROUP
@@ -857,21 +878,21 @@
     return call(
         out_proj_kernel,
         (d // wide,),
-        [const_spec(gated.shape), weight, weight, cols],
+        [const_spec(g_own.shape), const_spec(g_oth.shape), weight, weight, cols],
         cols,
         jax.ShapeDtypeStruct((rows, d), bf16),
         [],
         4 * rows * half * d,
         4 * d * half,
         "out_proj",
-    )(scal, gated, wo_own, wo_oth, tok)
+    )(scal, g_own, g_oth, wo_own, wo_oth, tok)
 
 
 def input_back_kernel(
-    scal, ez, eu, wz_own, wz_oth, wu_own, wu_oth, tok, halo, up, gain,
-    grad_out, edge_out, gain_out,
-    acc,
+    scal, ez, wz_own, wz_oth, wu_own, wu_oth, tok, halo, up, gain, *rest
 ):
+    chunks = rest[: CHUNKS + 1]
+    grad_out, edge_out, gain_out, acc = rest[CHUNKS + 1 :]
     step = pl.program_id(0)
     per = pl.num_programs(0) // 2
     half = acc.shape[1] // 2
@@ -879,7 +900,8 @@
     place = pl.ds(pl.multiple_of(side * half + lax.rem(step, per) * GROUP, GROUP), GROUP)
 
     def fill(wz, wu):
-        part = nn(eu[...], wu[...])
+        deep = chunks[0].shape[1]
+        part = sum(nn(e[...], wu[c * deep : (c + 1) * deep]) for c, e in enumerate(chunks))
         acc[0:HALO, place] = part[0:HALO]
         acc[HALO:, place] = part[HALO:] + nn(ez[...], wz[...])
 
@@ -934,7 +956,6 @@
         (2 * per,),
         [
             const_spec(ez.shape),
-            const_spec(eu.shape),
             own(zd),
             oth(zd),
             own(ud),
@@ -943,6 +964,7 @@
             const_spec((HALO, d)),
             const_spec((rows, d)),
             const_spec((1, d)),
+            *[const_spec(e.shape) for e in eu],
         ],
         [const_spec((rows, d)), const_spec((HALO, d)), const_spec((8, d))],
         [
@@ -954,182 +976,210 @@
         2 * ext * d * (zd + ud),
         2 * d * (zd + ud) + 8 * rows * d,
         "input_back",
-    )(scal, ez, eu, wz_own, wz_oth, wu_own, wu_oth, tok, halo, up, gain)
-
-
-BLOCKS = 16
-
-
-def outer_kernel(spans, keys, offset, has_rates, scal, l1, l2, r1, r2, *rest):
-    if has_rates:
-        e1, e2 = rest[:2]
-        rest = rest[2:]
+    )(scal, ez, wz_own, wz_oth, wu_own, wu_oth, tok, halo, up, gain, *eu)
+
+
+SIDE = 4
+
+
+def place_blocks(groups, base, group, parts, rows):
+    where = group ^ (base // SIDE)
+    within = lax.rem(base, SIDE)
+    for k in range(SIDE):
+        @pl.when(where == k)
+        def _():
+            for i, part in enumerate(parts):
+                for span, value in zip(rows, part):
+                    groups[k][i ^ within, span, :] = value
+
+
+def outer_ab_kernel(scal, a1, a2, ra1, ra2, b1, b2, rb1, rb2, *groups):
     step = pl.program_id(0)
-    rows = l1.shape[1]
-    total = rest[0].shape[1]
-    count = rows // total
-    tail = r1.shape[0] - l1.shape[0] if offset else 0
-    acc = tn(l1[...], r1[tail:, :]) + tn(l2[...], r2[tail:, :])
-    low = acc.astype(bf16)
-    for i, (span, key) in enumerate(zip(spans, keys)):
-        keep, send = rest[2 * i], rest[2 * i + 1]
-        for t in range(count):
-            place = (step * count + t) ^ scal[key]
-            part = low[t * total : (t + 1) * total, span]
-
-            @pl.when(place < BLOCKS // 2)
+    base = scal[3]
+    width = groups[0].shape[2]
+    high = a1.shape[1] // SIDE
+    deep = b1.shape[1] // SIDE
+
+    @pl.when(step < SIDE)
+    def _():
+        low = (tn(a1[...], ra1[...]) + tn(a2[...], ra2[...])).astype(bf16)
+        parts = [
+            (low[i * high : (i + 1) * high, :width], low[i * high : (i + 1) * high, width:])
+            for i in range(SIDE)
+        ]
+        place_blocks(groups, base, step, parts, [slice(0, high), slice(high, 2 * high)])
+
+    @pl.when(step >= SIDE)
+    def _():
+        low = (tn(b1[...], rb1[HALO:, :]) + tn(b2[...], rb2[HALO:, :])).astype(bf16)
+        parts = [(low[i * deep : (i + 1) * deep],) for i in range(SIDE)]
+        place_blocks(groups, base, step - SIDE, parts, [slice(2 * high, 2 * high + deep)])
+
+
+def outer_ab(scal, a1, a2, ra1, ra2, b1, b2, rb1, rb2):
+    toks = a1.shape[0]
+    width = rb1.shape[1]
+    a_cols = a1.shape[1] // SIDE
+    b_cols = b1.shape[1] // SIDE
+    shape = (SIDE, 2 * a_cols // SIDE + b_cols // SIDE, width)
+    a_spec = pl.BlockSpec((toks, a_cols), lambda j, *_: (0, jnp.minimum(j, SIDE - 1)))
+    b_spec = pl.BlockSpec((toks, b_cols), lambda j, *_: (0, jnp.maximum(j - SIDE, 0)))
+    return call(
+        outer_ab_kernel,
+        (2 * SIDE,),
+        [
+            a_spec,
+            a_spec,
+            const_spec(ra1.shape),
+            const_spec(ra2.shape),
+            b_spec,
+            b_spec,
+            const_spec(rb1.shape),
+            const_spec(rb2.shape),
+        ],
+        [const_spec(shape)] * SIDE,
+        [jax.ShapeDtypeStruct(shape, bf16)] * SIDE,
+        [],
+        8 * toks * a1.shape[1] * ra1.shape[1],
+        10**7,
+        "outer_ab",
+    )(scal, a1, a2, ra1, ra2, b1, b2, rb1, rb2)
+
+
+def outer_c_kernel(scal, *rest):
+    mine = rest[: CHUNKS + 1]
+    other = rest[CHUNKS + 1 : 2 * CHUNKS + 2]
+    r1, r2 = rest[2 * CHUNKS + 2 : 2 * CHUNKS + 4]
+    groups = rest[2 * CHUNKS + 4 : 2 * CHUNKS + 4 + SIDE]
+    base = scal[3]
+    within = lax.rem(base, SIDE)
+    offset = 0
+    for c in range(CHUNKS + 1):
+        acc = tn(mine[c][...], r1[...]) + tn(other[c][...], r2[...])
+        low = acc.astype(bf16)
+        height = (low.shape[0] if c < CHUNKS else 2 * N) // BLOCKS
+        span = slice(offset, offset + height)
+        offset += height
+        for k in range(SIDE):
+            @pl.when(base // SIDE == k)
             def _():
-                keep[place] = part
-
-            @pl.when(place >= BLOCKS // 2)
-            def _():
-                send[place - BLOCKS // 2] = part
-
-    if has_rates:
-        @pl.when(step == 0)
-        def _():
-            rest[-1][...] = (tn(e1[...], r1[...]) + tn(e2[...], r2[...]))[:H]
-
-
-def outer(scal, l1, l2, r1, r2, width, rows, step_rows, spans, keys, rates, name):
-    toks = l1.shape[0]
-    ext = r1.shape[0]
-    cols = r1.shape[1]
-    specs = [
-        pl.BlockSpec((toks, step_rows), lambda j, *_: (0, j)),
-        pl.BlockSpec((toks, step_rows), lambda j, *_: (0, j)),
-        const_spec((ext, cols)),
-        const_spec((ext, cols)),
-    ]
-    args = [l1, l2, r1, r2]
-    if rates:
-        spec = pl.BlockSpec((toks, LANE), lambda j, *_: (0, CONV // LANE))
-        specs += [spec, spec]
-        args += [l1, l2]
-    outs = []
-    for span in spans:
-        shape = (BLOCKS // 2, rows, span.stop - span.start)
-        outs += [shape, shape]
-    shapes = [jax.ShapeDtypeStruct(o, bf16) for o in outs]
-    if rates:
-        outs.append((H, cols))
-        shapes.append(jax.ShapeDtypeStruct((H, cols), f32))
-
-    def kernel(*refs):
-        outer_kernel(spans, keys, ext != toks, rates, *refs)
-
+                for t in range(BLOCKS):
+                    groups[(t // SIDE) ^ k][(t % SIDE) ^ within, span, :] = low[
+                        t * height : (t + 1) * height
+                    ]
+    rest[-1][...] = acc[2 * N : 2 * N + H]
+
+
+def outer_c(scal, mine, other, r1, r2):
+    toks, width = r1.shape
+    shape = (SIDE, CONV // BLOCKS, width)
+    args = [*mine, *other, r1, r2]
     return call(
-        kernel,
-        (width // step_rows,),
-        specs,
-        [const_spec(o) for o in outs],
-        shapes,
+        outer_c_kernel,
+        (1,),
+        [const_spec(a.shape) for a in args],
+        [const_spec(shape)] * SIDE + [const_spec((H, width))],
+        [jax.ShapeDtypeStruct(shape, bf16)] * SIDE + [jax.ShapeDtypeStruct((H, width), f32)],
         [],
-        4 * toks * width * cols,
-        4 * toks * width,
-        name,
+        4 * toks * CONV * width,
+        10**7,
+        "outer_c",
     )(scal, *args)
 
 
-def finish_kernel(key, scal, near, far, *rest):
-    out = rest[-1]
-    place = pl.program_id(0) ^ scal[key]
-
-    @pl.when(place < BLOCKS // 2)
-    def _():
-        out[...] = near[0].astype(f32)
-
-    @pl.when(place >= BLOCKS // 2)
-    def _():
-        out[...] = far[0].astype(f32)
-
-
-def finish(scal, near, far, key, height, name):
-    half, rows, cols = near.shape
-
-    def near_map(j, s):
-        return (jnp.minimum(j ^ s[key], half - 1), 0, 0)
-
-    def far_map(j, s):
-        return (jnp.maximum((j ^ s[key]) - half, 0), 0, 0)
-
-    def kernel(*refs):
-        finish_kernel(key, *refs)
-
-    return call(
-        kernel,
-        (BLOCKS,),
-        [pl.BlockSpec((1, rows, cols), near_map), pl.BlockSpec((1, rows, cols), far_map)],
-        pl.BlockSpec((rows, cols), lambda j, *_: (j, 0)),
-        jax.ShapeDtypeStruct((height, cols), f32),
-        [],
-        0,
-        6 * BLOCKS * rows * cols,
-        name,
-    )(scal, near, far)
-
-
-def finish_conv_kernel(spans, keys, scal, rates, *rest):
-    streams = rest[: 2 * len(spans)]
-    out, buf, sems = rest[2 * len(spans) + 1 :]
-    half, rows, _ = streams[0].shape
-    last = pltpu.make_async_copy(
-        rates, out.at[pl.ds(DIN + CONV, H), :], sems.at[BLOCKS]
-    )
-    last.start()
-    copies = [last]
-    for t in range(BLOCKS):
-        for i, (span, key) in enumerate(zip(spans, keys)):
-            near, far = streams[2 * i], streams[2 * i + 1]
-            place = t ^ scal[key]
-            dst = slice(t * rows, (t + 1) * rows)
-
-            @pl.when(place < half)
-            def _():
-                buf[dst, span] = near[place].astype(f32)
-
-            @pl.when(place >= half)
-            def _():
-                buf[dst, span] = far[place - half].astype(f32)
-
-        copy = pltpu.make_async_copy(
-            buf.at[pl.ds(t * rows, rows), :],
-            out.at[pl.ds(DIN + t * rows, rows), :],
-            sems.at[t],
-        )
-        copy.start()
-        copies.append(copy)
-    for copy in copies:
-        copy.wait()
-
-
-def finish_conv(scal, streams, spans, keys, rates, target):
-    def kernel(*refs):
-        finish_conv_kernel(spans, keys, *refs)
-
-    count = len(streams)
+def own_copies(kernel, args, outs, scratch, aliases, name):
     return pl.pallas_call(
         kernel,
         grid_spec=pltpu.PrefetchScalarGridSpec(
             num_scalar_prefetch=1,
             grid=(1,),
-            in_specs=[const_spec(rates.shape)]
-            + [const_spec(s.shape) for s in streams]
-            + [pl.BlockSpec(memory_space=pl.ANY)],
-            out_specs=pl.BlockSpec(memory_space=pl.ANY),
-            scratch_shapes=[
-                pltpu.VMEM((CONV, target.shape[1]), f32),
-                pltpu.SemaphoreType.DMA((BLOCKS + 1,)),
-            ],
+            in_specs=[pl.BlockSpec(memory_space=pl.ANY)] * (len(args) - 1),
+            out_specs=[pl.BlockSpec(memory_space=pl.ANY)] * len(outs),
+            scratch_shapes=scratch,
         ),
-        out_shape=jax.ShapeDtypeStruct(target.shape, f32),
-        input_output_aliases={2 + count: 0},
+        out_shape=outs,
+        input_output_aliases=aliases,
         compiler_params=params(1),
-        cost_estimate=pl.CostEstimate(
-            flops=0, bytes_accessed=6 * CONV * target.shape[1], transcendentals=0
-        ),
-        name="finish_conv",
-    )(scal, rates, *streams, target)
+        cost_estimate=pl.CostEstimate(flops=0, bytes_accessed=10**4, transcendentals=0),
+        name=name,
+    )(*args)
+
+
+def unload(scal, ab, c, first, targets, shapes, rates, name):
+    _, rows_ab, width = ab[0].shape
+    rows_c = c[0].shape[1]
+    half_in, d = shapes[0]
+    high = half_in // BLOCKS
+    deep = DIN // BLOCKS
+    tall = DIN // (CHUNKS * BLOCKS)
+    pieces = [(DIN + i * tall * BLOCKS, tall, i * tall) for i in range(CHUNKS)]
+    pieces.append((DIN + CONV - 2 * N, 2 * N // BLOCKS, CHUNKS * tall))
+    count = len(ab)
+    blocks = sum(p.shape[0] for p in ab)
+    extra = [rates] if rates is not None else []
+    skip = 2 * count + len(extra) + len(targets)
+
+    def kernel(scal, *refs):
+        out_a, out_b, ab_buf, c_buf, wide_a, wide_b, wide_c, in_sems, sems = refs[skip:]
+        stores = []
+
+        def send(src, dst, sem):
+            store = pltpu.make_async_copy(src, dst, sem)
+            store.start()
+            stores.append(store)
+
+        def rows_at(ref, start, t, size):
+            return ref.at[pl.ds(pl.multiple_of(start + t * size, size), size), :]
+
+        loads = []
+        row = 0
+        for i in range(count):
+            n = ab[i].shape[0]
+            for j, (src, buf) in enumerate(((refs[i], ab_buf), (refs[count + i], c_buf))):
+                load = pltpu.make_async_copy(src, buf.at[pl.ds(row, n)], in_sems.at[j, i])
+                load.start()
+                loads.append((load, j, row, n))
+            row += n
+        if extra:
+            send(refs[2 * count], out_b.at[pl.ds(DIN + CONV, H), :], sems.at[blocks, 0])
+        for load, kind, row, n in loads:
+            load.wait()
+            for p in range(row, row + n):
+                t = (first + p) ^ scal[3]
+                if kind == 0:
+                    wide_a[p, :, 0:width] = ab_buf[p, 0:high].astype(f32)
+                    wide_a[p, :, width:] = ab_buf[p, high : 2 * high].astype(f32)
+                    wide_b[p] = ab_buf[p, 2 * high :].astype(f32)
+                    send(wide_a.at[p], rows_at(out_a, 0, t, high), sems.at[p, 0])
+                    send(wide_b.at[p], rows_at(out_b, 0, t, deep), sems.at[p, 1])
+                    continue
+                wide_c[p] = c_buf[p].astype(f32)
+                for i, (start, height, inner) in enumerate(pieces):
+                    send(
+                        wide_c.at[p, pl.ds(inner, height)],
+                        rows_at(out_b, start, t, height),
+                        sems.at[p, 2 + i],
+                    )
+        for store in stores:
+            store.wait()
+
+    args = [scal, *ab, *c, *extra, *targets]
+    return own_copies(
+        kernel,
+        args,
+        [jax.ShapeDtypeStruct(shape, f32) for shape in shapes],
+        [
+            pltpu.VMEM((blocks, rows_ab, width), bf16),
+            pltpu.VMEM((blocks, rows_c, width), bf16),
+            pltpu.VMEM((blocks, high, d), f32),
+            pltpu.VMEM((blocks, deep, width), f32),
+            pltpu.VMEM((blocks, rows_c, width), f32),
+            pltpu.SemaphoreType.DMA((2, count)),
+            pltpu.SemaphoreType.DMA((blocks + 1, 2 + len(pieces))),
+        ],
+        {len(args) - 2 + i: i for i in range(len(targets))},
+        name,
+    )
 
 
 def swap(x):
@@ -1141,67 +1191,100 @@
     return lax.ppermute(x, "tm", [(i, (i + by) % length) for i in range(length)])
 
 
-def bits_of(axis):
-    return [(axis, 1 << b) for b in range((lax.axis_size(axis) - 1).bit_length())]
-
-
-def across(x, axis, bit):
-    return lax.ppermute(x, axis, [(i, i ^ bit) for i in range(lax.axis_size(axis))])
-
-
-def orders():
-    rep = bits_of("rep")
-    tm = bits_of("tm")[::-1]
-    cut = len(rep) // 2
-    depth = BLOCKS.bit_length() - 1
-    found = []
-    for lead in (rep, rep[cut:] + rep[:cut]):
-        every = lead + tm
-        found.append((every[:depth], every[depth:]))
-    return found
-
-
-def code_of(order):
-    place = 0
-    for axis, bit in order[0]:
-        place = 2 * place + (lax.axis_index(axis) // bit) % 2
-    return place
-
-
-def reduce_blocks(keep, send, order):
-    first, extra = order
-    for axis, bit in first[:-2]:
-        got = across(send, axis, bit)
-        n = keep.shape[0] // 2
-        total = keep.astype(f32) + got.astype(f32)
-        last = (axis, bit) == first[-3]
-        low = total.astype(bf16)
-        keep, send = (low, None) if last else (low[:n], low[n:])
-    axis, high = first[-2]
-    step = first[-1][1]
-    total = keep[0:1].astype(f32)
-    for k in range(1, 4):
-        mask = (high if k & 2 else 0) ^ (step if k & 1 else 0)
-        total = total + across(keep[k : k + 1], axis, mask).astype(f32)
-    piece = total.astype(bf16)
-    for axis_, bit in extra:
-        piece = (piece.astype(f32) + across(piece, axis_, bit).astype(f32)).astype(bf16)
+def across(x, axis, mask):
+    return lax.ppermute(x, axis, [(i, i ^ mask) for i in range(lax.axis_size(axis))])
+
+
+def after(value, *deps):
+    return lax.optimization_barrier((value, *deps))[0]
+
+
+def sum_low(values):
+    return sum(v.astype(f32) for v in values).astype(bf16)
+
+
+def exchange_corner(groups):
+    half = SIDE // 2
+    return across(groups[3][:half], "rep", 2), across(groups[3][half:], "rep", 1)
+
+
+def exchange_sides(groups, corner, *cover):
+    half = SIDE // 2
+    lo, hi = corner
+    first = after(groups[1], *cover)
+    by_x = jnp.concatenate([sum_low([first[:half], lo]), first[half:]])
+    by_y = jnp.concatenate([groups[2][:half], sum_low([groups[2][half:], hi])])
+    return across(by_x, "rep", 1), across(by_y, "rep", 2)
+
+
+def sum_parts(own, got, *cover):
+    every = [after(own, *cover), *got]
+    return [sum_low([g[m] for g in every]) for m in range(SIDE)]
+
+
+def reduce_times(parts, *cover):
+    got = [across(parts[m], "tm", m) for m in range(1, SIDE)]
+    piece = sum_low([after(parts[0], *cover), *got])
+    for axis in ("rep", "tm"):
+        bit = SIDE
+        while bit < lax.axis_size(axis):
+            piece = sum_low([piece, across(piece, axis, bit)])
+            bit *= 2
     return piece
 
 
-def spread_blocks(piece, order):
-    first = order[0]
-    axis, high = first[-2]
-    step = first[-1][1]
-    parts = [piece]
-    for k in range(1, 4):
-        mask = (high if k & 2 else 0) ^ (step if k & 1 else 0)
-        parts.append(across(piece, axis, mask))
-    near = jnp.concatenate(parts, axis=0)
-    middle = first[1:-2]
-    for axis_, bit in reversed(middle):
-        near = jnp.concatenate([near, across(near, axis_, bit)], axis=0)
-    return near, across(near, *first[0])
+def gather_times(piece, *cover):
+    got = [across(piece, "tm", m) for m in range(1, SIDE)]
+    return jnp.stack([after(piece, *cover), *got])
+
+
+def gather_replicas(near):
+    by_x = across(near, "rep", 1)
+    by_y = across(near, "rep", 2)
+    return by_x, by_y
+
+
+def gather_corner(by_x, by_y):
+    return across(by_x[: SIDE // 2], "rep", 2), across(by_y[SIDE // 2 :], "rep", 1)
+
+
+def chain(local, total, logs, by, *cover):
+    size = lax.axis_size("tm")
+    tm = lax.axis_index("tm")
+
+    def widen(row):
+        return jnp.exp(jnp.repeat(row[0, :H], P_SIZE))[None]
+
+    def moved(v, hops):
+        return shifted(v, by * hops)
+
+    def inside(v, hops):
+        outside = tm < hops if by > 0 else tm >= size - hops
+        return jnp.where(outside, 0.0, v.astype(f32))
+
+    def inclusive(held):
+        return (local + total * held).astype(bf16)
+
+    first = moved(local.astype(bf16), 1)
+    reach = moved(logs, 1)
+    total = after(total, *cover)
+    held = inside(first, 1)
+    sent = inclusive(held)
+    got = moved(sent, 2)
+
+    def finish(*cover):
+        nonlocal held, got, reach
+        span = 1
+        reach = after(reach, *cover)
+        while True:
+            held = held + widen(reach) * inside(got, span + 1)
+            if 2 * span + 1 >= size - 1:
+                return held.astype(bf16)
+            reach = reach + moved(logs + reach, span + 1)
+            span = 2 * span + 1
+            got = moved(inclusive(held), span + 1)
+
+    return sent, finish
 
 
 def body(
@@ -1218,11 +1301,15 @@
     half_in = out_weight.shape[0]
     half_conv = conv_bias.shape[0]
     half_heads = dt_bias.shape[0]
-    order_a, order_b = orders()
 
     lo = starts[0] - tm * tok_count
     scal = jnp.stack(
-        [core, lo, lo + lengths[0], code_of(order_a), code_of(order_b)]
+        [
+            core,
+            lo,
+            lo + lengths[0],
+            SIDE * (lax.axis_index("rep") % SIDE) + tm % SIDE,
+        ]
     ).astype(jnp.int32)
 
     def fill(v):
@@ -1236,87 +1323,57 @@
     )
     pack = pack.reshape(8, half_conv).astype(bf16)
     pack_oth = swap(pack)
-    halo = shifted(tok[tok_count - HALO :], 1)
-    w_t = in_weight.T
+    edge_tok = tok[tok_count - HALO :]
+    halo = shifted(edge_tok, 1)
+    w_t = after(in_weight.T, edge_tok)
     wu_own = jnp.pad(w_t[DIN:], ((0, GROUP - H), (0, 0))).astype(bf16)
     wu_oth = swap(wu_own)
+    taps, vecs, heads, gain = pack_vectors(scal, pack, pack_oth, d)
     wz_own = w_t[:DIN].astype(bf16)
     wz_oth = swap(wz_own)
-    wo_own = out_weight.astype(bf16)
+    wo_own = after(out_weight, wu_own).astype(bf16)
     wo_oth = swap(wo_own)
     up_oth = swap(upstream)
 
-    taps, vecs, heads, gain = pack_vectors(scal, pack, pack_oth, d)
     n_own, n_oth, u, act, dact, dt, sg, cum, cumt, st = front(
-        scal, tok, halo, gain, wu_own, wu_oth, taps, heads
+        scal, tok, halo, gain, after(wu_own, wz_own, wo_own), wu_oth, taps, heads
     )
     n_got = swap(n_oth)
     cumt = cumt[:H].reshape(H // 4, 4, tok_count)
     total = jnp.exp(jnp.repeat(cum[tok_count - 1, :H], P_SIZE))[None]
 
-    def chain(local, by, first):
-        pieces = []
-        for part in range(2):
-            cols = slice(part * (DIN // 2), (part + 1) * (DIN // 2))
-            send = local[:, cols].astype(bf16)
-            got = None
-            for hop in range(tm_size - 1):
-                got = shifted(send, by)
-                got = jnp.where(tm == first, jnp.zeros_like(got), got)
-                if hop < tm_size - 2:
-                    send = (local[:, cols] + total[:, cols] * got.astype(f32)).astype(bf16)
-            pieces.append(got)
-        return jnp.concatenate(pieces, axis=1)
-
-    s_in = chain(st, 1, 0)
+    logs = cum[tok_count - 1 :]
     z = gate_proj(scal, n_own, n_oth, wz_own, wz_oth)
     eg = grad_gated(scal, upstream, wo_own, wo_oth)
-    yloc, s0 = intra(scal, act, dt, cum, cumt)
-    gated, ey, ez, r_loc, r_dev, dc_dev, g_loc, gs = gate(
+    sent, finish = chain(st, total, logs, 1, z, eg)
+    yloc, s0 = intra(scal, after(act, sent), dt, cum, cumt)
+    s_in = finish(yloc)
+    g_own, g_oth, ey, ez, r_loc, r_dev, dc_dev, g_loc, gs = gate(
         scal, yloc, act, z, eg, cum, s_in, vecs
     )
 
-    gated_got = swap(gated[1])
+    gated_got = swap(g_oth)
     ez_got = swap(ez)
-    g_in = chain(g_loc, -1, tm_size - 1)
-    full = [slice(0, d)]
-    a_keep, a_send = outer(
-        scal, gated[0], gated_got, upstream, up_oth,
-        half_in, half_in // BLOCKS, GROUP, full, [3], False, "grad_out",
-    )
-    half_span = [slice(0, half_d)]
-    b_keep, b_send = outer(
-        scal, ez, ez_got, n_own, n_got,
-        DIN, DIN // BLOCKS, 2 * GROUP, half_span, [4], False, "grad_z",
-    )
-    a_piece = reduce_blocks(a_keep, a_send, order_a)
-    b_piece = reduce_blocks(b_keep, b_send, order_b)
-    a_near, a_far = spread_blocks(a_piece, order_a)
-    b_near, b_far = spread_blocks(b_piece, order_b)
-    output = out_proj(scal, gated, wo_own, wo_oth, tok)
-    dxt, db_loc, dc_loc, r2, cq = back(scal, act, dt, cum, cumt, ey, s0)
-    eu, gconv, ghead = tail(
-        scal, act, dact, u, ey, dxt, taps, dt, sg, cum, g_in, s_in, vecs, heads,
+    ab = outer_ab(scal, g_own, gated_got, upstream, up_oth, ez, ez_got, n_own, n_got)
+    sent, finish = chain(g_loc, total, logs, -1, ab[0])
+    dxt, db_loc, dc_loc, r2, cq = back(scal, after(act, sent), dt, cum, cumt, ey, s0)
+    g_in = finish(dxt)
+    ab_corner = exchange_corner(ab)
+    ab_got = exchange_sides(ab, ab_corner, dxt)
+    *eu, gconv, ghead = tail(
+        scal, after(act, *ab_corner), dact, u, ey, dxt, taps, dt, sg, cum, g_in, s_in, vecs, heads,
         (db_loc, dc_loc, dc_dev, r_loc, r_dev, r2, cq),
     )
-    eu_got = swap(eu)
-    spans = [slice(0, half_d // 2), slice(half_d // 2, half_d)]
-    c1_keep, c1_send, c2_keep, c2_send, g_rates = outer(
-        scal, eu, eu_got, n_own, n_got,
-        CONV, CONV // BLOCKS, CONV // 2, spans, [3, 4], True, "grad_u",
-    )
-    c1_piece = reduce_blocks(c1_keep, c1_send, order_a)
-    c2_piece = reduce_blocks(c2_keep, c2_send, order_b)
-    c1_near, c1_far = spread_blocks(c1_piece, order_a)
-    c2_near, c2_far = spread_blocks(c2_piece, order_b)
-
+    eu_got = [swap(e) for e in eu]
+    ab_parts = sum_parts(ab[0], ab_got, gconv)
+    *c, g_rates = outer_c(scal, eu, eu_got, after(n_own, *ab_parts), n_got)
+    output = out_proj(scal, g_own, g_oth, wo_own, wo_oth, after(tok, c[0]))
+    c_corner = exchange_corner(c)
+    c_got = exchange_sides(c, c_corner, output)
+    ab_piece = reduce_times(ab_parts, output)
     grad_in, edge, ggain = input_back(
-        scal, ez, eu, wz_own, wz_oth, wu_own, wu_oth, tok, halo, upstream, gain
-    )
-    edge = shifted(edge, -1)
-    edge = jnp.where(tm == tm_size - 1, jnp.zeros_like(edge), edge)
-    input_grad = grad_in.at[tok_count - HALO :].add(edge)
-
+        scal, ez, eu, wz_own, wz_oth, wu_own, wu_oth, after(tok, ab_piece, *c_corner), halo, upstream, gain
+    )
     grad_skip = jnp.sum(gs[1].reshape(H, P_SIZE), axis=1)
 
     def side(v, half):
@@ -1338,17 +1395,40 @@
         ],
         axis=1,
     )
+    ab_near = gather_times(ab_piece, packed)
+    c_parts = sum_parts(c[0], c_got, ab_near)
+    packed = after(packed, *c_parts)
     own = lax.dynamic_index_in_dim(packed, core, 0, keepdims=False)
     small = own + swap(lax.dynamic_index_in_dim(packed, 1 - core, 0, keepdims=False))
     small = jnp.concatenate([small, g_rates.reshape(8, -1)], axis=1)
-    for axis, bit in bits_of("rep") + bits_of("tm"):
-        small = small + across(small, axis, bit)
+
+    def total_over(v, axis):
+        v = v + sum(across(v, axis, mask) for mask in range(1, SIDE))
+        bit = SIDE
+        while bit < lax.axis_size(axis):
+            v = v + across(v, axis, bit)
+            bit *= 2
+        return v
+
+    small = total_over(small, "rep")
+    ab_x, ab_y = gather_replicas(ab_near)
+    c_piece = reduce_times(c_parts)
+    c_near = gather_times(c_piece)
+    small = total_over(after(small, c_piece), "tm")
+    edge = shifted(edge, -1)
+    edge = jnp.where(tm == tm_size - 1, jnp.zeros_like(edge), edge)
+    input_grad = grad_in.at[tok_count - HALO :].add(edge)
+    c_x, c_y = gather_replicas(c_near)
+    ab_lo, ab_hi = gather_corner(ab_x, ab_y)
+    c_lo, c_hi = gather_corner(c_x, c_y)
     rates = small[:, half_conv:].reshape(H, half_d)
 
-    grad_out_w = finish(scal, a_near, a_far, 3, half_in, "finish_out")
-    grad_in_t = finish(scal, b_near, b_far, 4, DIN + CONV + H, "finish_z")
-    grad_in_t = finish_conv(
-        scal, [c1_near, c1_far, c2_near, c2_far], spans, [3, 4], rates, grad_in_t
+    shapes = [(half_in, d), (DIN + CONV + H, half_d)]
+    near = unload(
+        scal, [ab_near, ab_x, ab_y], [c_near, c_x, c_y], 0, [], shapes, rates, "finish_near"
+    )
+    grad_out_w, grad_in_t = unload(
+        scal, [ab_lo, ab_hi], [c_lo, c_hi], 3 * SIDE, near, shapes, None, "finish_far"
     )
     hs = half_heads
     return (

time: 457 us -> 346 us (0.76)
  waiting for transfers between devices: 132 us -> 62.5 us
  starting transfers between devices: 79.1 us -> 57.8 us
  Pallas kernels: 186 us -> 171 us
  local copies, waits for them, and re-layouts: 36.1 us -> 29.3 us
    ppermute x44 -> x34, waiting for transfers between devices: 102 us -> 51.7 us  [across(): lax.ppermute(x, axis, [(i, i ^ mask) for i in range(lax.axis_size(axis))])]
    ppermute x14 -> x8, waiting for transfers between devices: 30 us -> 7.97 us  [shifted(): lax.ppermute(x, 'tm', [(i, (i + by) % length) for i in range(length)])]
    pallas_call x8 -> x6, Pallas kernels: 71.1 us -> 54.4 us  [the longest x1 14.4 us: input_back(): call(input_back_kernel, (2 * per,), [const_spec(ez.shape), own(zd), oth(z...]
    ppermute x44 -> x34, starting transfers between devices: 51.9 us -> 39.2 us  [across(): lax.ppermute(x, axis, [(i, i ^ mask) for i in range(lax.axis_size(axis))])]
    ppermute x14 -> x8, starting transfers between devices: 25.7 us -> 15 us  [shifted(): lax.ppermute(x, 'tm', [(i, (i + by) % length) for i in range(length)])]
    convert_element_type x15, other arithmetic: 8.72 us -> 14.5 us  [the longest x8 6.11 us: sum_low(): return sum((v.astype(f32) for v in values)).astype(bf16)]
    unnamed x62 -> x80, local copies, waits for them, and re-layouts: 12.8 us -> 8.47 us
  transfers between devices with their start and end apart: 68 -> 56, of which waited for: 28 -> 17; matrix products, arithmetic and copies ran while one was open for 10% -> 11% of each run, Pallas kernels for 40% -> 44%
where the time goes in v3:
time: 346 us; the launch traced here: 345 us
  Pallas kernels  171 us (49%)
  waiting for transfers between devices  62.5 us (18%)
  starting transfers between devices  57.8 us (17%)
  local copies, waits for them, and re-layouts  29.3 us (8%)
  other arithmetic  21.7 us (6%)
    ppermute x34, waiting for transfers between devices, across(): lax.ppermute(x, axis, [(i, i ^ mask) for i in range(lax.axis_size(axis))])  51.7 us
    ppermute x34, starting transfers between devices, across(): lax.ppermute(x, axis, [(i, i ^ mask) for i in range(lax.axis_size(axis))])  39.2 us
    pallas_call x1, Pallas kernels, front(): call(front_kernel, (groups,), [const_spec((tok_count, d)), const_spec((HA...  25.8 us
    pallas_call x1, Pallas kernels, tail(): call(tail_kernel, (groups + 2,), [wide, pl.BlockSpec((tok_count, GROUP),...  25.2 us
    pallas_call x1, Pallas kernels, back(): call(back_kernel, (groups,), [wide, pl.BlockSpec((tok_count, GROUP), lamb...  18.3 us
    pallas_call x1, Pallas kernels, gate(): call(gate_kernel, (tok_count // rows,), [rowspec(DIN), rowspec(CONV), row...  16.6 us
    ppermute x8, starting transfers between devices, shifted(): lax.ppermute(x, 'tm', [(i, (i + by) % length) for i in range(length)])  15 us
    pallas_call x1, Pallas kernels, input_back(): call(input_back_kernel, (2 * per,), [const_spec(ez.shape), own(zd), oth(z...  14.4 us
  transfers between devices with their start and end apart: 56, of which 17 were waited for; matrix products, arithmetic and copies ran while one was open for 11% of the time, Pallas kernels for 44%

profile of v3, /device:TPU:0, one launch (start us, length us, event | category | flops | bytes accessed | tf_op | source)
XLA Modules:
  0.0 344.8 jit_solution(17430793491214768087)
XLA Ops:
  1.4 4.1 %convert.41 = bf16[4384,512]{1,0:T(8,128)(2,1)S(1)} convert(f32[4384,512]{1,0:T(8,128)} %bitcast.79) | non-fusion elementwise | flops 2244608 | bytes 13467648 | tf_op jit(solution)/shard_map/convert.3
  6.5 2.4 copy-done.5
  8.8 1.6 convert_element_type.257.w_own
  11.1 1.6 slice.299.w_own.wz_own
  12.6 3.1 collective-permute-start
  18.8 2.3 vectors.1
  21.7 25.8 %front.1 = (bf16[528,512]{1,0:T(8,128)(2,1)}, bf16[528,512]{1,0:T(8,128)(2,1)}, bf16[528,2304]{1,0:T(8,128)(2,1)}, bf16[512,2304]{1,0:T(8,128)(2,1)}, bf16[512,2...) custom-call(s32[4]{0:T(128)} %pad_add_fusion.scal, ...), custom_call_target="tpu_custom_call" | custom-call | flops 2629828 | bytes 13099 | tf_op jit(solution)/shard_map/front/pallas_call | solution.py:261
  47.5 1.3 convert_element_type.258
  48.8 3.0 collective-permute-start.5
  51.7 6.8 %grad_gated.1.eg = bf16[2,512,1024]{2,1,0:T(8,128)(2,1)} custom-call(s32[4]{0:T(128)} %pad_add_fusion.scal, bf16[512,1024]{1,0:T(8,128)(2,1)} %bitcast.75, bf16[1024,1024]{1,0:T(8,128)(2,1)} %convert_element_type.257.w_own, bf16[1024,1024]{1,0:T(8,128)(2,1)} %collective-permute-done.4.w_oth), custom_call_target="tpu_custom_call" | custom-call | flops 2147483 | bytes 4194 | tf_op jit(solution)/shard_map/grad_gated/pallas_call | solution.py:854
  59.4 6.9 %gate_proj.1.z = bf16[512,2048]{1,0:T(8,128)(2,1)} custom-call(s32[4]{0:T(128)} %pad_add_fusion.scal, bf16[528,512]{1,0:T(8,128)(2,1)} %get-tuple-element.148.a_own.rb1.rest_10_, bf16[528,512]{1,0:T(8,128)(2,1)} %get-tuple-element.107.a_oth, bf16[2048,512]{1,0:T(8,128)(2,1)} %slice.299.w_own.wz_own, bf16[2048,512]{1,0:T(8,128)(2,1)} %collective-permute-done.3.w_oth.wz_oth), custom_call_target="tpu_custom_call" | custom-call | flops 2147483 | bytes 4194 | tf_op jit(solution)/shard_map/gate_proj/pallas_call | solution.py:832
  66.5 2.6 collective-permute-start.7
  71.3 14.3 %intra.1 = (f32[512,2048]{1,0:T(8,128)}, bf16[4,128,2048]{2,1,0:T(8,128)(2,1)}) custom-call(s32[4]{0:T(128)} %pad_add_fusion.scal, bf16[512,2304]{1,0:T(8,128)(2,1)} %get-tuple-element.126.x.bc.act, bf16[512,2304]{1,0:T(8,128)(2,1)} %get-tuple-element.126.x.bc.act, f32[512,128]{1,0:T(8,128)} %get-tuple-element.110.dt, f32[512,128]{1,0:T(8,128)} %get-tuple-element.105.cum, ...), custom_call_target="tpu_custom_call" | custom-call | flops 805306 | bytes 8388 | tf_op jit(solution)/shard_map/intra/pallas_call | solution.py:361
  85.8 6.6 %collective-permute-done.7 = bf16[128,2048]{1,0:T(8,128)(2,1)S(1)} collective-permute-done((bf16[128,2048]{1,0:T(8,128)(2,1)S(1)}, bf16[128,2048]{1,0:T(8,128)(2,1)S(1)}, u32[]{:S(2)}, u32[]{:S(2)}) %collective-permute-start.7) | collective-permute-done | bytes 524320 | tf_op jit(solution)/shard_map/ppermute | solution.py:1191
  93.4 16.6 %gate.1 = (bf16[512,1024]{1,0:T(8,128)(2,1)}, bf16[512,1024]{1,0:T(8,128)(2,1)}, bf16[512,2048]{1,0:T(8,128)(2,1)}, bf16[512,2048]{1,0:T(8,128)(2,1)}, f32[512,1...) custom-call(s32[4]{0:T(128)} %pad_add_fusion.scal, ...), custom_call_target="tpu_custom_call" | custom-call | flops 1610612 | bytes 20971 | tf_op jit(solution)/shard_map/gate/pallas_call | solution.py:481
  111.1 2.1 convert_element_type.263
  113.2 2.3 collective-permute-start.14
  116.0 2.3 collective-permute-done.11.rb2.rest_11_
  119.1 12.7 %outer_ab.1 = (bf16[4,256,512]{2,1,0:T(8,128)(2,1)}, bf16[4,256,512]{2,1,0:T(8,128)(2,1)}, bf16[4,256,512]{2,1,0:T(8,128)(2,1)}, bf16[4,256,512]{2,1,0:T(8,128)(2,1)}) custom-call(s32[4]{0:T(128)} %pad_add_fusion.scal, bf16[512,1024]{1,0:T(8,128)(2,1)} %get-tuple-element.115.a1.a_own, bf16[512,1024]{1,0:T(8,128)(2,1)} %collective-permute-done.8.a2, ...), custom_call_target="tpu_custom_call" | custom-call | flops 4294967 | bytes 10000 | tf_op jit(solution)/shard_map/outer_ab/pallas_call | solution.py:1027
  131.8 2.4 fusion.11
  134.2 1.5 collective-permute-start.12
  135.7 2.3 collective-permute-start.15
  138.0 1.5 collective-permute-start.13
  139.8 18.3 %back.1 = (bf16[512,2048]{1,0:T(8,128)(2,1)}, f32[512,128]{1,0:T(8,128)}, f32[512,128]{1,0:T(8,128)}, f32[512,128]{1,0:T(8,128)}, f32[8,128]{1,0:T(8,128)}) custom-call(s32[4]{0:T(128)} %pad_add_fusion.scal, bf16[512,2304]{1,0:T(8,128)(2,1)} %get-tuple-element.126.x.bc.act, bf16[512,2304]{1,0:T(8,128)(2,1)} %get-tuple-element.126.x.bc.act, ...), custom_call_target="tpu_custom_call" | custom-call | flops 2147483 | bytes 8388 | tf_op jit(solution)/shard_map/back/pallas_call | solution.py:620
  158.2 1.2 add_convert_fusion.1
  162.9 1.4 collective-permute-done.16
  164.3 2.1 add_convert_fusion.2.g_in
  166.4 25.2 %tail.1 = (bf16[528,512]{1,0:T(8,128)(2,1)}, bf16[528,512]{1,0:T(8,128)(2,1)}, bf16[528,512]{1,0:T(8,128)(2,1)}, bf16[528,512]{1,0:T(8,128)(2,1)}, bf16[528,512]...) custom-call(s32[4]{0:T(128)} %pad_add_fusion.scal, bf16[512,2304]{1,0:T(8,128)(2,1)} %get-tuple-element.126.x.bc.act, ...), custom_call_target="tpu_custom_call" | custom-call | flops 1073741 | bytes 12582 | tf_op jit(solution)/shard_map/tail/pallas_call | solution.py:769
  193.6 3.1 fusion.3
  196.8 2.1 collective-permute-start.25
  199.0 2.2 collective-permute-start.26
  202.8 10.4 %outer_c.1 = (bf16[4,144,512]{2,1,0:T(8,128)(2,1)}, bf16[4,144,512]{2,1,0:T(8,128)(2,1)}, bf16[4,144,512]{2,1,0:T(8,128)(2,1)}, bf16[4,144,512]{2,1,0:T(8,128)(2,1)}, f32[32,512]{1,0:T(8,128)}) custom-call(s32[4]{0:T(128)} %pad_add_fusion.scal, bf16[528,512]{1,0:T(8,128)(2,1)} %get-tuple-element.138.rest_0_, bf16[528,512]{1,0:T(8,128)(2,1)} %get-tuple-element.139.rest_1_, ...), custom_call_target="tpu_custom_call" | custom-call | flops 2491416 | bytes 10000 | tf_op jit(solution)/shard_map/outer_c/pallas_call | solution.py:1077
  213.2 1.1 fusion.12
  214.9 1.2 collective-permute-start.28
  217.3 6.8 %out_proj.1 = bf16[512,1024]{1,0:T(8,128)(2,1)} custom-call(s32[4]{0:T(128)} %pad_add_fusion.scal, bf16[512,1024]{1,0:T(8,128)(2,1)} %get-tuple-element.115.a1.a_own, bf16[512,1024]{1,0:T(8,128)(2,1)} %get-tuple-element.116.a_oth, bf16[1024,1024]{1,0:T(8,128)(2,1)} %convert_element_type.257.w_own, bf16[1024,1024]{1,0:T(8,128)(2,1)} %collective-permute-done.4.w_oth, ...), custom_call_target="tpu_custom_call" | custom-call | flops 2147483 | bytes 4194 | tf_op jit(solution)/shard_map/out_proj/pallas_call | solution.py:878
  225.1 1.2 add_convert_fusion.8
  226.9 2.4 collective-permute-start.31
  229.4 1.4 collective-permute-start.32
  230.8 14.4 %input_back.1 = (f32[512,1024]{1,0:T(8,128)}, f32[16,1024]{1,0:T(8,128)}, f32[8,1024]{1,0:T(8,128)}) custom-call(s32[4]{0:T(128)} %pad_add_fusion.scal, bf16[512,2048]{1,0:T(8,128)(2,1)} %get-tuple-element.117.b1.ez, bf16[2048,512]{1,0:T(8,128)(2,1)} %slice.299.w_own.wz_own, bf16[2048,512]{1,0:T(8,128)(2,1)} %collective-permute-done.3.w_oth.wz_oth, ...), custom_call_target="tpu_custom_call" | custom-call | flops 4982833 | bytes 13631 | tf_op jit(solution)/shard_map/input_back/pallas_call | solution.py:954
  247.2 1.6 collective-permute-start.38
  249.7 1.6 collective-permute-start.29
  251.3 1.1 pad_maximum_fusion.2.refs_0_
  252.4 7.5 %collective-permute-done.37 = bf16[4,144,512]{2,1,0:T(8,128)(2,1)S(1)} collective-permute-done((bf16[4,144,512]{2,1,0:T(8,128)(2,1)S(1)}, bf16[4,144,512]{2,1,0:T(8,128)(2,1)S(1)}, u32[]{:S(2)}, u32[]{:S(2)}) %collective-permute-start.37) | collective-permute-done | bytes 589856 | tf_op jit(solution)/shard_map/ppermute | solution.py:1195
  260.8 1.5 collective-permute-start.33
  262.9 2.9 collective-permute-start.40
  265.8 1.5 collective-permute-start.41
  267.4 3.8 %collective-permute-done.39 = bf16[144,512]{1,0:T(8,128)(2,1)S(1)} collective-permute-done((bf16[144,512]{1,0:T(8,128)(2,1)S(1)}, bf16[144,512]{1,0:T(8,128)(2,1)S(1)}, u32[]{:S(2)}, u32[]{:S(2)}) %collective-permute-start.39) | collective-permute-done | bytes 147488 | tf_op jit(solution)/shard_map/ppermute | solution.py:1195
  271.1 1.1 collective-permute-start.50
  272.3 4.6 %collective-permute-done.40 = bf16[144,512]{1,0:T(8,128)(2,1)S(1)} collective-permute-done((bf16[144,512]{1,0:T(8,128)(2,1)S(1)}, bf16[144,512]{1,0:T(8,128)(2,1)S(1)}, u32[]{:S(2)}, u32[]{:S(2)}) %collective-permute-start.40) | collective-permute-done | bytes 147488 | tf_op jit(solution)/shard_map/ppermute | solution.py:1195
  276.9 1.5 collective-permute-start.51
  278.3 1.5 collective-permute-start.52
  279.9 9.2 %collective-permute-done.50 = f32[8,3200]{1,0:T(8,128)S(1)} collective-permute-done((f32[8,3200]{1,0:T(8,128)S(1)}, f32[8,3200]{1,0:T(8,128)S(1)}, u32[]{:S(2)}, u32[]{:S(2)}) %collective-permute-start.50) | collective-permute-done | bytes 102432 | tf_op jit(solution)/shard_map/ppermute | solution.py:1195
  289.1 2.9 collective-permute-done.51
  292.8 1.6 collective-permute-start.44
  294.4 1.4 collective-permute-done.42
  295.8 8.3 %collective-permute-done.43 = bf16[144,512]{1,0:T(8,128)(2,1)S(1)} collective-permute-done((bf16[144,512]{1,0:T(8,128)(2,1)S(1)}, bf16[144,512]{1,0:T(8,128)(2,1)S(1)}, u32[]{:S(2)}, u32[]{:S(2)}) %collective-permute-start.43) | collective-permute-done | bytes 147488 | tf_op jit(solution)/shard_map/ppermute | solution.py:1195
  304.1 3.0 collective-permute-start.55
  307.2 2.3 collective-permute-start.45
  316.7 7.0 %collective-permute-done.45.refs_4_ = bf16[4,144,512]{2,1,0:T(8,128)(2,1)S(1)} collective-permute-done((bf16[4,144,512]{2,1,0:T(8,128)(2,1)S(1)}, bf16[4,144,512]{2,1,0:T(8,128)(2,1)S(1)}, u32[]{:S(2)}, u32[]{:S(2)}) %collective-permute-start.45) | collective-permute-done | bytes 589856 | tf_op jit(solution)/shard_map/ppermute | solution.py:1195
  323.7 1.7 collective-permute-start.46
  325.4 1.1 collective-permute-done.47.refs_5_
  328.7 6.4 %finish_near.1 = (f32[1024,1024]{1,0:T(8,128)}, f32[4384,512]{1,0:T(8,128)}) custom-call(s32[4]{0:T(128)} %pad_add_fusion.scal, bf16[4,256,512]{2,1,0:T(8,128)(2,1)} %copy-done.2, bf16[4,256,512]{2,1,0:T(8,128)(2,1)} %copy-done.7, bf16[4,256,512]{2,1,0:T(8,128)(2,1)} %copy-done.8, bf16[4,144,512]{2,1,0:T(8,128)(2,1)} %copy-done.6, ...), custom_call_target="tpu_custom_call" | custom-call | bytes 10000 | tf_op jit(solution)/shard_map/finish_near/pallas_call | solution.py:1091
  335.1 4.9 %collective-permute-done.46.refs_2_ = bf16[2,144,512]{2,1,0:T(8,128)(2,1)} collective-permute-done((bf16[2,144,512]{2,1,0:T(8,128)(2,1)S(1)}, bf16[2,144,512]{2,1,0:T(8,128)(2,1)}, u32[]{:S(2)}, u32[]{:S(2)}) %collective-permute-start.46) | collective-permute-done | bytes 294944 | tf_op jit(solution)/shard_map/ppermute | solution.py:1195
  340.9 3.7 %finish_far.1 = (f32[1024,1024]{1,0:T(8,128)}, f32[4384,512]{1,0:T(8,128)}) custom-call(s32[4]{0:T(128)} %pad_add_fusion.scal, bf16[2,256,512]{2,1,0:T(8,128)(2,1)} %copy-done.24, bf16[2,256,512]{2,1,0:T(8,128)(2,1)} %collective-permute-done.36.refs_1_, ...), custom_call_target="tpu_custom_call", output_to_operand_aliasing={{0}: (5, {}), {1}: (6, {})} | custom-call | bytes 10000 | tf_op jit(solution)/shard_map/finish_far/pallas_call | solution.py:1091
  (232 shorter events, 37.6 us)
Async XLA Ops:
  5.9 15.2 %collective-permute-start.2 = (bf16[2560,512]{1,0:T(8,128)(2,1)S(1)}, bf16[2560,512]{1,0:T(8,128)(2,1)}, u32[]{:S(2)}, u32[]{:S(2)}) collective-permute-start(bf16[2560,512]{1,0:T(8,128)(2,1)S(1)} %pad.19.w_own.r_own.wu_own), channel_id=1, source_target_pairs={{0,4},{4,0},{1,5},{5,1},{2,6},{6,2},{3,7},{7,3},{8,12},{12,8},{9,1... | collective-permute-start | bytes 7864328 | tf_op jit(solution)/shard_map/ppermute | solution.py:1186
  10.5 41.2 %collective-permute-start.4 = (bf16[1024,1024]{1,0:T(8,128)(2,1)}, bf16[1024,1024]{1,0:T(8,128)(2,1)}, u32[]{:S(2)}, u32[]{:S(2)}) collective-permute-start(bf16[1024,1024]{1,0:T(8,128)(2,1)} %convert_element_type.257.w_own), channel_id=1, source_target_pairs={{0,4},{4,0},{1,5},{5,1},{2,6},{6,2},{3,7},{7,3},{8,12},{12,8},{9,1... | collective-permute-start | bytes 6291464 | tf_op jit(solution)/shard_map/ppermute | solution.py:1186
  12.6 46.7 %collective-permute-start.3 = (bf16[2048,512]{1,0:T(8,128)(2,1)}, bf16[2048,512]{1,0:T(8,128)(2,1)}, u32[]{:S(2)}, u32[]{:S(2)}) collective-permute-start(bf16[2048,512]{1,0:T(8,128)(2,1)} %slice.299.w_own.wz_own), channel_id=1, source_target_pairs={{0,4},{4,0},{1,5},{5,1},{2,6},{6,2},{3,7},{7,3},{8,12},{12,8},{9,1... | collective-permute-start | bytes 6291464 | tf_op jit(solution)/shard_map/ppermute | solution.py:1186
  12.6 8.4 %collective-permute-start = (bf16[16,1024]{1,0:T(8,128)(2,1)S(1)}, bf16[16,1024]{1,0:T(8,128)(2,1)S(1)}, u32[]{:S(2)}, u32[]{:S(2)}) collective-permute-start(bf16[16,1024]{1,0:T(8,128)(2,1)S(1)} %slice_bitcast_fusion), channel_id=1, source_target_pairs={{0,1},{1,2},{2,3},{3,0},{4,5},{5,6},{6,7},{7,4},{8,9},{9,10},{10,1... | collective-permute-start | bytes 98312 | tf_op jit(solution)/shard_map/ppermute | solution.py:1191
  16.1 2.2 collective-permute-start.1
  48.8 17.6 %collective-permute-start.5 = (bf16[128,2048]{1,0:T(8,128)(2,1)S(1)}, bf16[128,2048]{1,0:T(8,128)(2,1)S(1)}, u32[]{:S(2)}, u32[]{:S(2)}) collective-permute-start(bf16[128,2048]{1,0:T(8,128)(2,1)S(1)} %convert_element_type.258), channel_id=1, source_target_pairs={{0,1},{1,2},{2,3},{3,0},{4,5},{5,6},{6,7},{7,4},{8,9},{9,10},{10,1... | collective-permute-start | bytes 1572872 | tf_op jit(solution)/shard_map/ppermute | solution.py:1191
  66.5 25.9 %collective-permute-start.7 = (bf16[128,2048]{1,0:T(8,128)(2,1)S(1)}, bf16[128,2048]{1,0:T(8,128)(2,1)S(1)}, u32[]{:S(2)}, u32[]{:S(2)}) collective-permute-start(bf16[128,2048]{1,0:T(8,128)(2,1)S(1)} %add_convert_fusion.5), channel_id=1, source_target_pairs={{0,2},{1,3},{2,0},{3,1},{4,6},{5,7},{6,4},{7,5},{8,10},{9,11},{10,... | collective-permute-start | bytes 1572872 | tf_op jit(solution)/shard_map/ppermute | solution.py:1191
  69.8 15.8 %collective-permute-start.6 = (f32[1,128]{1,0:T(1,128)S(1)}, f32[1,128]{1,0:T(1,128)S(1)}, u32[]{:S(2)}, u32[]{:S(2)}) collective-permute-start(f32[1,128]{1,0:T(1,128)S(1)} %slice.237), channel_id=1, source_target_pairs={{0,1},{1,2},{2,3},{3,0},{4,5},{5,6},{6,7},{7,4},{8,9},{9,10},{10,1... | collective-permute-start | bytes 1544 | tf_op jit(solution)/shard_map/ppermute | solution.py:1191
  93.4 17.3 %copy-start.23 = (bf16[528,512]{1,0:T(8,128)(2,1)S(1)}, bf16[528,512]{1,0:T(8,128)(2,1)}, u32[]{:S(2)}) copy-start(bf16[528,512]{1,0:T(8,128)(2,1)} %get-tuple-element.107.a_oth) | copy-start | bytes 1622020
  110.1 8.2 %collective-permute-start.10 = (bf16[512,2048]{1,0:T(8,128)(2,1)}, bf16[512,2048]{1,0:T(8,128)(2,1)}, u32[]{:S(2)}, u32[]{:S(2)}) collective-permute-start(bf16[512,2048]{1,0:T(8,128)(2,1)} %get-tuple-element.117.b1.ez), channel_id=1, source_target_pairs={{0,4},{4,0},{1,5},{5,1},{2,6},{6,2},{3,7},{7,3},{8,12},{12,8},{9,1... | collective-permute-start | bytes 6291464 | tf_op jit(solution)/shard_map/ppermute | solution.py:1186
  110.1 5.8 %collective-permute-start.9 = (bf16[512,1024]{1,0:T(8,128)(2,1)S(1)}, bf16[512,1024]{1,0:T(8,128)(2,1)S(1)}, u32[]{:S(2)}, u32[]{:S(2)}) collective-permute-start(bf16[512,1024]{1,0:T(8,128)(2,1)S(1)} %bitcast.78), channel_id=1, source_target_pairs={{0,4},{4,0},{1,5},{5,1},{2,6},{6,2},{3,7},{7,3},{8,12},{12,8},{9,1... | collective-permute-start | bytes 3145736 | tf_op jit(solution)/shard_map/ppermute | solution.py:1186
  110.6 7.6 %collective-permute-start.8 = (bf16[512,1024]{1,0:T(8,128)(2,1)}, bf16[512,1024]{1,0:T(8,128)(2,1)}, u32[]{:S(2)}, u32[]{:S(2)}) collective-permute-start(bf16[512,1024]{1,0:T(8,128)(2,1)} %get-tuple-element.116.a_oth), channel_id=1, source_target_pairs={{0,4},{4,0},{1,5},{5,1},{2,6},{6,2},{3,7},{7,3},{8,12},{12,8},{9,1... | collective-permute-start | bytes 3145736 | tf_op jit(solution)/shard_map/ppermute | solution.py:1186
  110.7 7.5 %collective-permute-start.11 = (bf16[528,512]{1,0:T(8,128)(2,1)S(1)}, bf16[528,512]{1,0:T(8,128)(2,1)S(1)}, u32[]{:S(2)}, u32[]{:S(2)}) collective-permute-start(bf16[528,512]{1,0:T(8,128)(2,1)S(1)} %copy-done.23), channel_id=1, source_target_pairs={{0,4},{4,0},{1,5},{5,1},{2,6},{6,2},{3,7},{7,3},{8,12},{12,8},{9,1... | collective-permute-start | bytes 1622024 | tf_op jit(solution)/shard_map/ppermute | solution.py:1186
  113.2 26.3 %collective-permute-start.14 = (bf16[128,2048]{1,0:T(8,128)(2,1)}, bf16[128,2048]{1,0:T(8,128)(2,1)S(1)}, u32[]{:S(2)}, u32[]{:S(2)}) collective-permute-start(bf16[128,2048]{1,0:T(8,128)(2,1)} %convert_element_type.263), channel_id=1, source_target_pairs={{0,3},{1,0},{2,1},{3,2},{4,7},{5,4},{6,5},{7,6},{8,11},{9,8},{10,9... | collective-permute-start | bytes 1572872 | tf_op jit(solution)/shard_map/ppermute | solution.py:1191
  134.2 24.0 %collective-permute-start.12 = (bf16[2,256,512]{2,1,0:T(8,128)(2,1)}, bf16[2,256,512]{2,1,0:T(8,128)(2,1)}, u32[]{:S(2)}, u32[]{:S(2)}) collective-permute-start(bf16[2,256,512]{2,1,0:T(8,128)(2,1)} %get-tuple-element.180), channel_id=1, source_target_pairs={{0,16},{8,24},{16,0},{24,8},{1,17},{9,25},{17,1},{25,9},{2,18},{10... | collective-permute-start | bytes 1572872 | tf_op jit(solution)/shard_map/ppermute | solution.py:1195
  135.7 27.1 %collective-permute-start.15 = (f32[1,128]{1,0:T(1,128)S(1)}, f32[1,128]{1,0:T(1,128)S(1)}, u32[]{:S(2)}, u32[]{:S(2)}) collective-permute-start(f32[1,128]{1,0:T(1,128)S(1)} %slice.237), channel_id=1, source_target_pairs={{0,3},{1,0},{2,1},{3,2},{4,7},{5,4},{6,5},{7,6},{8,11},{9,8},{10,9... | collective-permute-start | bytes 1544 | tf_op jit(solution)/shard_map/ppermute | solution.py:1191
  138.0 22.1 %collective-permute-start.13 = (bf16[2,256,512]{2,1,0:T(8,128)(2,1)}, bf16[2,256,512]{2,1,0:T(8,128)(2,1)S(1)}, u32[]{:S(2)}, u32[]{:S(2)}) collective-permute-start(bf16[2,256,512]{2,1,0:T(8,128)(2,1)} %get-tuple-element.179), channel_id=1, source_target_pairs={{0,8},{8,0},{16,24},{24,16},{1,9},{9,1},{17,25},{25,17},{2,10},{10... | collective-permute-start | bytes 1572872 | tf_op jit(solution)/shard_map/ppermute | solution.py:1195
  139.7 24.6 %collective-permute-start.16 = (bf16[128,2048]{1,0:T(8,128)(2,1)S(1)}, bf16[128,2048]{1,0:T(8,128)(2,1)}, u32[]{:S(2)}, u32[]{:S(2)}) collective-permute-start(bf16[128,2048]{1,0:T(8,128)(2,1)S(1)} %add_convert_fusion.3), channel_id=1, source_target_pairs={{0,2},{1,3},{2,0},{3,1},{4,6},{5,7},{6,4},{7,5},{8,10},{9,11},{10,... | collective-permute-start | bytes 1572872 | tf_op jit(solution)/shard_map/ppermute | solution.py:1191
  139.8 18.3 %copy-start.16 = (bf16[4,256,512]{2,1,0:T(8,128)(2,1)S(1)}, bf16[4,256,512]{2,1,0:T(8,128)(2,1)}, u32[]{:S(2)}) copy-start(bf16[4,256,512]{2,1,0:T(8,128)(2,1)} %get-tuple-element.146) | copy-start | bytes 3145732
  139.8 18.4 %copy-start.15 = (bf16[4,256,512]{2,1,0:T(8,128)(2,1)S(1)}, bf16[4,256,512]{2,1,0:T(8,128)(2,1)}, u32[]{:S(2)}) copy-start(bf16[4,256,512]{2,1,0:T(8,128)(2,1)} %get-tuple-element.147) | copy-start | bytes 3145732
  159.5 33.4 %collective-permute-start.22 = (bf16[4,256,512]{2,1,0:T(8,128)(2,1)S(1)}, bf16[4,256,512]{2,1,0:T(8,128)(2,1)}, u32[]{:S(2)}, u32[]{:S(2)}) collective-permute-start(bf16[4,256,512]{2,1,0:T(8,128)(2,1)S(1)} %pad_maximum_fusion), channel_id=1, source_target_pairs={{0,8},{8,0},{16,24},{24,16},{1,9},{9,1},{17,25},{25,17},{2,10},{10... | collective-permute-start | bytes 3145736 | tf_op jit(solution)/shard_map/ppermute | solution.py:1195
  160.4 33.0 %collective-permute-start.23 = (bf16[4,256,512]{2,1,0:T(8,128)(2,1)S(1)}, bf16[4,256,512]{2,1,0:T(8,128)(2,1)}, u32[]{:S(2)}, u32[]{:S(2)}) collective-permute-start(bf16[4,256,512]{2,1,0:T(8,128)(2,1)S(1)} %pad_maximum_fusion.1), channel_id=1, source_target_pairs={{0,16},{8,24},{16,0},{24,8},{1,17},{9,25},{17,1},{25,9},{2,18},{10... | collective-permute-start | bytes 3145736 | tf_op jit(solution)/shard_map/ppermute | solution.py:1195
  191.5 5.2 %collective-permute-start.17 = (bf16[528,512]{1,0:T(8,128)(2,1)}, bf16[528,512]{1,0:T(8,128)(2,1)S(1)}, u32[]{:S(2)}, u32[]{:S(2)}) collective-permute-start(bf16[528,512]{1,0:T(8,128)(2,1)} %get-tuple-element.138.rest_0_), channel_id=1, source_target_pairs={{0,4},{4,0},{1,5},{5,1},{2,6},{6,2},{3,7},{7,3},{8,12},{12,8},{9,1... | collective-permute-start | bytes 1622024 | tf_op jit(solution)/shard_map/ppermute | solution.py:1186
  191.6 5.2 %collective-permute-start.18 = (bf16[528,512]{1,0:T(8,128)(2,1)}, bf16[528,512]{1,0:T(8,128)(2,1)}, u32[]{:S(2)}, u32[]{:S(2)}) collective-permute-start(bf16[528,512]{1,0:T(8,128)(2,1)} %get-tuple-element.139.rest_1_), channel_id=1, source_target_pairs={{0,4},{4,0},{1,5},{5,1},{2,6},{6,2},{3,7},{7,3},{8,12},{12,8},{9,1... | collective-permute-start | bytes 1622024 | tf_op jit(solution)/shard_map/ppermute | solution.py:1186
  192.1 6.9 %collective-permute-start.19 = (bf16[528,512]{1,0:T(8,128)(2,1)}, bf16[528,512]{1,0:T(8,128)(2,1)}, u32[]{:S(2)}, u32[]{:S(2)}) collective-permute-start(bf16[528,512]{1,0:T(8,128)(2,1)} %get-tuple-element.140.rest_2_), channel_id=1, source_target_pairs={{0,4},{4,0},{1,5},{5,1},{2,6},{6,2},{3,7},{7,3},{8,12},{12,8},{9,1... | collective-permute-start | bytes 1622024 | tf_op jit(solution)/shard_map/ppermute | solution.py:1186
  192.9 8.3 %collective-permute-start.20 = (bf16[528,512]{1,0:T(8,128)(2,1)}, bf16[528,512]{1,0:T(8,128)(2,1)S(1)}, u32[]{:S(2)}, u32[]{:S(2)}) collective-permute-start(bf16[528,512]{1,0:T(8,128)(2,1)} %get-tuple-element.141.rest_3_), channel_id=1, source_target_pairs={{0,4},{4,0},{1,5},{5,1},{2,6},{6,2},{3,7},{7,3},{8,12},{12,8},{9,1... | collective-permute-start | bytes 1622024 | tf_op jit(solution)/shard_map/ppermute | solution.py:1186
  193.3 7.9 %collective-permute-start.21 = (bf16[528,512]{1,0:T(8,128)(2,1)}, bf16[528,512]{1,0:T(8,128)(2,1)S(1)}, u32[]{:S(2)}, u32[]{:S(2)}) collective-permute-start(bf16[528,512]{1,0:T(8,128)(2,1)} %get-tuple-element.142.rest_4_), channel_id=1, source_target_pairs={{0,4},{4,0},{1,5},{5,1},{2,6},{6,2},{3,7},{7,3},{8,12},{12,8},{9,1... | collective-permute-start | bytes 1622024 | tf_op jit(solution)/shard_map/ppermute | solution.py:1186
  196.7 19.9 %copy-start.28 = (f32[8,2304]{1,0:T(8,128)S(1)}, f32[8,2304]{1,0:T(8,128)}, u32[]{:S(2)}) copy-start(f32[8,2304]{1,0:T(8,128)} %get-tuple-element.143) | copy-start | bytes 221188
  196.8 28.3 %collective-permute-start.24 = (bf16[256,512]{1,0:T(8,128)(2,1)}, bf16[256,512]{1,0:T(8,128)(2,1)}, u32[]{:S(2)}, u32[]{:S(2)}) collective-permute-start(bf16[256,512]{1,0:T(8,128)(2,1)} %get-tuple-element.173), channel_id=1, source_target_pairs={{0,1},{1,0},{2,3},{3,2},{4,5},{5,4},{6,7},{7,6},{8,9},{9,8},{10,11... | collective-permute-start | bytes 786440 | tf_op jit(solution)/shard_map/ppermute | solution.py:1195
  196.8 28.2 %collective-permute-start.25 = (bf16[256,512]{1,0:T(8,128)(2,1)}, bf16[256,512]{1,0:T(8,128)(2,1)}, u32[]{:S(2)}, u32[]{:S(2)}) collective-permute-start(bf16[256,512]{1,0:T(8,128)(2,1)} %get-tuple-element.172), channel_id=1, source_target_pairs={{0,2},{1,3},{2,0},{3,1},{4,6},{5,7},{6,4},{7,5},{8,10},{9,11},{10,... | collective-permute-start | bytes 786440 | tf_op jit(solution)/shard_map/ppermute | solution.py:1195
  199.0 26.1 %collective-permute-start.26 = (bf16[256,512]{1,0:T(8,128)(2,1)S(1)}, bf16[256,512]{1,0:T(8,128)(2,1)}, u32[]{:S(2)}, u32[]{:S(2)}) collective-permute-start(bf16[256,512]{1,0:T(8,128)(2,1)S(1)} %get-tuple-element.171), channel_id=1, source_target_pairs={{0,3},{1,2},{2,1},{3,0},{4,7},{5,6},{6,5},{7,4},{8,11},{9,10},{10,... | collective-permute-start | bytes 786440 | tf_op jit(solution)/shard_map/ppermute | solution.py:1195
  214.3 16.5 %collective-permute-start.27 = (bf16[2,144,512]{2,1,0:T(8,128)(2,1)S(1)}, bf16[2,144,512]{2,1,0:T(8,128)(2,1)S(1)}, u32[]{:S(2)}, u32[]{:S(2)}) collective-permute-start(bf16[2,144,512]{2,1,0:T(8,128)(2,1)S(1)} %get-tuple-element.182), channel_id=1, source_target_pairs={{0,16},{8,24},{16,0},{24,8},{1,17},{9,25},{17,1},{25,9},{2,18},{10... | collective-permute-start | bytes 884744 | tf_op jit(solution)/shard_map/ppermute | solution.py:1195
  214.9 15.9 %collective-permute-start.28 = (bf16[2,144,512]{2,1,0:T(8,128)(2,1)S(1)}, bf16[2,144,512]{2,1,0:T(8,128)(2,1)S(1)}, u32[]{:S(2)}, u32[]{:S(2)}) collective-permute-start(bf16[2,144,512]{2,1,0:T(8,128)(2,1)S(1)} %get-tuple-element.181), channel_id=1, source_target_pairs={{0,8},{8,0},{16,24},{24,16},{1,9},{9,1},{17,25},{25,17},{2,10},{10... | collective-permute-start | bytes 884744 | tf_op jit(solution)/shard_map/ppermute | solution.py:1195
  226.3 22.8 %collective-permute-start.30 = (bf16[256,512]{1,0:T(8,128)(2,1)S(1)}, bf16[256,512]{1,0:T(8,128)(2,1)S(1)}, u32[]{:S(2)}, u32[]{:S(2)}) collective-permute-start(bf16[256,512]{1,0:T(8,128)(2,1)S(1)} %add_convert_fusion.8), channel_id=1, source_target_pairs={{0,1},{1,0},{2,3},{3,2},{4,5},{5,4},{6,7},{7,6},{8,9},{9,8},{10,11... | collective-permute-start | bytes 786440 | tf_op jit(solution)/shard_map/ppermute | solution.py:1195
  226.9 24.4 %collective-permute-start.31 = (bf16[256,512]{1,0:T(8,128)(2,1)S(1)}, bf16[256,512]{1,0:T(8,128)(2,1)S(1)}, u32[]{:S(2)}, u32[]{:S(2)}) collective-permute-start(bf16[256,512]{1,0:T(8,128)(2,1)S(1)} %add_convert_fusion.8), channel_id=1, source_target_pairs={{0,2},{1,3},{2,0},{3,1},{4,6},{5,7},{6,4},{7,5},{8,10},{9,11},{10,... | collective-permute-start | bytes 786440 | tf_op jit(solution)/shard_map/ppermute | solution.py:1195
  229.4 21.9 %collective-permute-start.32 = (bf16[256,512]{1,0:T(8,128)(2,1)S(1)}, bf16[256,512]{1,0:T(8,128)(2,1)}, u32[]{:S(2)}, u32[]{:S(2)}) collective-permute-start(bf16[256,512]{1,0:T(8,128)(2,1)S(1)} %add_convert_fusion.8), channel_id=1, source_target_pairs={{0,3},{1,2},{2,1},{3,0},{4,7},{5,6},{6,5},{7,4},{8,11},{9,10},{10,... | collective-permute-start | bytes 786440 | tf_op jit(solution)/shard_map/ppermute | solution.py:1195
  246.1 13.8 %collective-permute-start.37 = (bf16[4,144,512]{2,1,0:T(8,128)(2,1)S(1)}, bf16[4,144,512]{2,1,0:T(8,128)(2,1)S(1)}, u32[]{:S(2)}, u32[]{:S(2)}) collective-permute-start(bf16[4,144,512]{2,1,0:T(8,128)(2,1)S(1)} %pad_maximum_fusion.3), channel_id=1, source_target_pairs={{0,8},{8,0},{16,24},{24,16},{1,9},{9,1},{17,25},{25,17},{2,10},{10... | collective-permute-start | bytes 1769480 | tf_op jit(solution)/shard_map/ppermute | solution.py:1195
  247.2 13.2 %collective-permute-start.38 = (bf16[4,144,512]{2,1,0:T(8,128)(2,1)S(1)}, bf16[4,144,512]{2,1,0:T(8,128)(2,1)S(1)}, u32[]{:S(2)}, u32[]{:S(2)}) collective-permute-start(bf16[4,144,512]{2,1,0:T(8,128)(2,1)S(1)} %pad_maximum_fusion.4), channel_id=1, source_target_pairs={{0,16},{8,24},{16,0},{24,8},{1,17},{9,25},{17,1},{25,9},{2,18},{10... | collective-permute-start | bytes 1769480 | tf_op jit(solution)/shard_map/ppermute | solution.py:1195
  249.7 11.1 %collective-permute-start.29 = (f32[16,1024]{1,0:T(8,128)S(1)}, f32[16,1024]{1,0:T(8,128)S(1)}, u32[]{:S(2)}, u32[]{:S(2)}) collective-permute-start(f32[16,1024]{1,0:T(8,128)S(1)} %copy-done.35), channel_id=1, source_target_pairs={{0,3},{1,0},{2,1},{3,2},{4,7},{5,4},{6,5},{7,6},{8,11},{9,8},{10,9... | collective-permute-start | bytes 196616 | tf_op jit(solution)/shard_map/ppermute | solution.py:1191
  252.4 42.1 %copy-start.2 = (bf16[4,256,512]{2,1,0:T(8,128)(2,1)}, bf16[4,256,512]{2,1,0:T(8,128)(2,1)S(1)}, u32[]{:S(2)}) copy-start(bf16[4,256,512]{2,1,0:T(8,128)(2,1)S(1)} %pad_maximum_fusion.2.refs_0_) | copy-start | bytes 3145732
  260.7 5.1 %collective-permute-start.49 = (f32[8,1152]{1,0:T(8,128)S(1)}, f32[8,1152]{1,0:T(8,128)S(1)}, u32[]{:S(2)}, u32[]{:S(2)}) collective-permute-start(f32[8,1152]{1,0:T(8,128)S(1)} %bitcast.94), channel_id=1, source_target_pairs={{0,4},{4,0},{1,5},{5,1},{2,6},{6,2},{3,7},{7,3},{8,12},{12,8},{9,1... | collective-permute-start | bytes 110600 | tf_op jit(solution)/shard_map/ppermute | solution.py:1186
  260.8 51.3 %copy-start.11 = (f32[1,512,1024]{2,1,0:T(8,128)}, f32[1,512,1024]{2,1,0:T(8,128)S(1)}, u32[]{:S(2)}) copy-start(f32[1,512,1024]{2,1,0:T(8,128)S(1)} %bitcast_dynamic-update-slice_fusion) | copy-start | bytes 6291460
  260.8 46.4 %collective-permute-start.33 = (bf16[4,256,512]{2,1,0:T(8,128)(2,1)S(1)}, bf16[4,256,512]{2,1,0:T(8,128)(2,1)S(1)}, u32[]{:S(2)}, u32[]{:S(2)}) collective-permute-start(bf16[4,256,512]{2,1,0:T(8,128)(2,1)S(1)} %pad_maximum_fusion.2.refs_0_), channel_id=1, source_target_pairs={{0,8},{8,0},{16,24},{24,16},{1,9},{9,1},{17,25},{25,17},{2,10},{10... | collective-permute-start | bytes 3145736 | tf_op jit(solution)/shard_map/ppermute | solution.py:1195
  262.3 48.0 %collective-permute-start.35 = (bf16[4,256,512]{2,1,0:T(8,128)(2,1)S(1)}, bf16[4,256,512]{2,1,0:T(8,128)(2,1)S(1)}, u32[]{:S(2)}, u32[]{:S(2)}) collective-permute-start(bf16[4,256,512]{2,1,0:T(8,128)(2,1)S(1)} %pad_maximum_fusion.2.refs_0_), channel_id=1, source_target_pairs={{0,16},{8,24},{16,0},{24,8},{1,17},{9,25},{17,1},{25,9},{2,18},{10... | collective-permute-start | bytes 3145736 | tf_op jit(solution)/shard_map/ppermute | solution.py:1195
  262.9 8.2 %collective-permute-start.39 = (bf16[144,512]{1,0:T(8,128)(2,1)S(1)}, bf16[144,512]{1,0:T(8,128)(2,1)S(1)}, u32[]{:S(2)}, u32[]{:S(2)}) collective-permute-start(bf16[144,512]{1,0:T(8,128)(2,1)S(1)} %get-tuple-element.178), channel_id=1, source_target_pairs={{0,1},{1,0},{2,3},{3,2},{4,5},{5,4},{6,7},{7,6},{8,9},{9,8},{10,11... | collective-permute-start | bytes 442376 | tf_op jit(solution)/shard_map/ppermute | solution.py:1195
  262.9 13.9 %collective-permute-start.40 = (bf16[144,512]{1,0:T(8,128)(2,1)S(1)}, bf16[144,512]{1,0:T(8,128)(2,1)S(1)}, u32[]{:S(2)}, u32[]{:S(2)}) collective-permute-start(bf16[144,512]{1,0:T(8,128)(2,1)S(1)} %get-tuple-element.177), channel_id=1, source_target_pairs={{0,2},{1,3},{2,0},{3,1},{4,6},{5,7},{6,4},{7,5},{8,10},{9,11},{10,... | collective-permute-start | bytes 442376 | tf_op jit(solution)/shard_map/ppermute | solution.py:1195
  265.8 12.5 %collective-permute-start.41 = (bf16[144,512]{1,0:T(8,128)(2,1)S(1)}, bf16[144,512]{1,0:T(8,128)(2,1)S(1)}, u32[]{:S(2)}, u32[]{:S(2)}) collective-permute-start(bf16[144,512]{1,0:T(8,128)(2,1)S(1)} %get-tuple-element.176), channel_id=1, source_target_pairs={{0,3},{1,2},{2,1},{3,0},{4,7},{5,6},{6,5},{7,4},{8,11},{9,10},{10,... | collective-permute-start | bytes 442376 | tf_op jit(solution)/shard_map/ppermute | solution.py:1195
  271.1 18.0 %collective-permute-start.50 = (f32[8,3200]{1,0:T(8,128)S(1)}, f32[8,3200]{1,0:T(8,128)S(1)}, u32[]{:S(2)}, u32[]{:S(2)}) collective-permute-start(f32[8,3200]{1,0:T(8,128)S(1)} %pad_maximum_fusion.6), channel_id=1, source_target_pairs={{0,8},{8,0},{16,24},{24,16},{1,9},{9,1},{17,25},{25,17},{2,10},{10... | collective-permute-start | bytes 307208 | tf_op jit(solution)/shard_map/ppermute | solution.py:1195
  276.9 15.1 %collective-permute-start.51 = (f32[8,3200]{1,0:T(8,128)S(1)}, f32[8,3200]{1,0:T(8,128)S(1)}, u32[]{:S(2)}, u32[]{:S(2)}) collective-permute-start(f32[8,3200]{1,0:T(8,128)S(1)} %pad_maximum_fusion.6), channel_id=1, source_target_pairs={{0,16},{8,24},{16,0},{24,8},{1,17},{9,25},{17,1},{25,9},{2,18},{10... | collective-permute-start | bytes 307208 | tf_op jit(solution)/shard_map/ppermute | solution.py:1195
  278.3 14.4 %collective-permute-start.52 = (f32[8,3200]{1,0:T(8,128)S(1)}, f32[8,3200]{1,0:T(8,128)S(1)}, u32[]{:S(2)}, u32[]{:S(2)}) collective-permute-start(f32[8,3200]{1,0:T(8,128)S(1)} %pad_maximum_fusion.6), channel_id=1, source_target_pairs={{0,24},{8,16},{16,8},{24,0},{1,25},{9,17},{17,9},{25,1},{2,26},{10... | collective-permute-start | bytes 307208 | tf_op jit(solution)/shard_map/ppermute | solution.py:1195
  289.1 6.7 %collective-permute-start.42 = (bf16[144,512]{1,0:T(8,128)(2,1)S(1)}, bf16[144,512]{1,0:T(8,128)(2,1)S(1)}, u32[]{:S(2)}, u32[]{:S(2)}) collective-permute-start(bf16[144,512]{1,0:T(8,128)(2,1)S(1)} %add_convert_fusion.13), channel_id=1, source_target_pairs={{0,1},{1,0},{2,3},{3,2},{4,5},{5,4},{6,7},{7,6},{8,9},{9,8},{10,11... | collective-permute-start | bytes 442376 | tf_op jit(solution)/shard_map/ppermute | solution.py:1195
  292.0 12.1 %collective-permute-start.43 = (bf16[144,512]{1,0:T(8,128)(2,1)S(1)}, bf16[144,512]{1,0:T(8,128)(2,1)S(1)}, u32[]{:S(2)}, u32[]{:S(2)}) collective-permute-start(bf16[144,512]{1,0:T(8,128)(2,1)S(1)} %add_convert_fusion.13), channel_id=1, source_target_pairs={{0,2},{1,3},{2,0},{3,1},{4,6},{5,7},{6,4},{7,5},{8,10},{9,11},{10,... | collective-permute-start | bytes 442376 | tf_op jit(solution)/shard_map/ppermute | solution.py:1195
  292.8 11.3 %collective-permute-start.44 = (bf16[144,512]{1,0:T(8,128)(2,1)S(1)}, bf16[144,512]{1,0:T(8,128)(2,1)S(1)}, u32[]{:S(2)}, u32[]{:S(2)}) collective-permute-start(bf16[144,512]{1,0:T(8,128)(2,1)S(1)} %add_convert_fusion.13), channel_id=1, source_target_pairs={{0,3},{1,2},{2,1},{3,0},{4,7},{5,6},{6,5},{7,4},{8,11},{9,10},{10,... | collective-permute-start | bytes 442376 | tf_op jit(solution)/shard_map/ppermute | solution.py:1195
  295.8 16.3 %collective-permute-start.53 = (f32[8,3200]{1,0:T(8,128)S(1)}, f32[8,3200]{1,0:T(8,128)S(1)}, u32[]{:S(2)}, u32[]{:S(2)}) collective-permute-start(f32[8,3200]{1,0:T(8,128)S(1)} %add_add_fusion.1), channel_id=1, source_target_pairs={{0,1},{1,0},{2,3},{3,2},{4,5},{5,4},{6,7},{7,6},{8,9},{9,8},{10,11... | collective-permute-start | bytes 307208 | tf_op jit(solution)/shard_map/ppermute | solution.py:1195
  304.1 9.6 %collective-permute-start.54 = (f32[8,3200]{1,0:T(8,128)S(1)}, f32[8,3200]{1,0:T(8,128)S(1)}, u32[]{:S(2)}, u32[]{:S(2)}) collective-permute-start(f32[8,3200]{1,0:T(8,128)S(1)} %add_add_fusion.1), channel_id=1, source_target_pairs={{0,2},{1,3},{2,0},{3,1},{4,6},{5,7},{6,4},{7,5},{8,10},{9,11},{10,... | collective-permute-start | bytes 307208 | tf_op jit(solution)/shard_map/ppermute | solution.py:1195
  304.1 10.1 %collective-permute-start.55 = (f32[8,3200]{1,0:T(8,128)S(1)}, f32[8,3200]{1,0:T(8,128)S(1)}, u32[]{:S(2)}, u32[]{:S(2)}) collective-permute-start(f32[8,3200]{1,0:T(8,128)S(1)} %add_add_fusion.1), channel_id=1, source_target_pairs={{0,3},{1,2},{2,1},{3,0},{4,7},{5,6},{6,5},{7,4},{8,11},{9,10},{10,... | collective-permute-start | bytes 307208 | tf_op jit(solution)/shard_map/ppermute | solution.py:1195
  307.2 21.5 %copy-start.6 = (bf16[4,144,512]{2,1,0:T(8,128)(2,1)}, bf16[4,144,512]{2,1,0:T(8,128)(2,1)S(1)}, u32[]{:S(2)}) copy-start(bf16[4,144,512]{2,1,0:T(8,128)(2,1)S(1)} %pad_maximum_fusion.5.refs_3_) | copy-start | bytes 1769476
  307.2 21.4 %copy-start.7 = (bf16[4,256,512]{2,1,0:T(8,128)(2,1)}, bf16[4,256,512]{2,1,0:T(8,128)(2,1)S(1)}, u32[]{:S(2)}) copy-start(bf16[4,256,512]{2,1,0:T(8,128)(2,1)S(1)} %collective-permute-done.33.refs_1_) | copy-start | bytes 3145732
  307.2 16.4 %collective-permute-start.45 = (bf16[4,144,512]{2,1,0:T(8,128)(2,1)S(1)}, bf16[4,144,512]{2,1,0:T(8,128)(2,1)S(1)}, u32[]{:S(2)}, u32[]{:S(2)}) collective-permute-start(bf16[4,144,512]{2,1,0:T(8,128)(2,1)S(1)} %pad_maximum_fusion.5.refs_3_), channel_id=1, source_target_pairs={{0,8},{8,0},{16,24},{24,16},{1,9},{9,1},{17,25},{25,17},{2,10},{10... | collective-permute-start | bytes 1769480 | tf_op jit(solution)/shard_map/ppermute | solution.py:1195
  310.3 16.2 %collective-permute-start.47 = (bf16[4,144,512]{2,1,0:T(8,128)(2,1)S(1)}, bf16[4,144,512]{2,1,0:T(8,128)(2,1)S(1)}, u32[]{:S(2)}, u32[]{:S(2)}) collective-permute-start(bf16[4,144,512]{2,1,0:T(8,128)(2,1)S(1)} %pad_maximum_fusion.5.refs_3_), channel_id=1, source_target_pairs={{0,16},{8,24},{16,0},{24,8},{1,17},{9,25},{17,1},{25,9},{2,18},{10... | collective-permute-start | bytes 1769480 | tf_op jit(solution)/shard_map/ppermute | solution.py:1195
  312.2 27.9 %collective-permute-start.34 = (bf16[2,256,512]{2,1,0:T(8,128)(2,1)}, bf16[2,256,512]{2,1,0:T(8,128)(2,1)S(1)}, u32[]{:S(2)}, u32[]{:S(2)}) collective-permute-start(bf16[2,256,512]{2,1,0:T(8,128)(2,1)} %slice.308), channel_id=1, source_target_pairs={{0,16},{8,24},{16,0},{24,8},{1,17},{9,25},{17,1},{25,9},{2,18},{10... | collective-permute-start | bytes 1572872 | tf_op jit(solution)/shard_map/ppermute | solution.py:1195
  313.7 26.4 %collective-permute-start.36 = (bf16[2,256,512]{2,1,0:T(8,128)(2,1)}, bf16[2,256,512]{2,1,0:T(8,128)(2,1)}, u32[]{:S(2)}, u32[]{:S(2)}) collective-permute-start(bf16[2,256,512]{2,1,0:T(8,128)(2,1)} %slice.309), channel_id=1, source_target_pairs={{0,8},{8,0},{16,24},{24,16},{1,9},{9,1},{17,25},{25,17},{2,10},{10... | collective-permute-start | bytes 1572872 | tf_op jit(solution)/shard_map/ppermute | solution.py:1195
  323.7 16.4 %collective-permute-start.46 = (bf16[2,144,512]{2,1,0:T(8,128)(2,1)S(1)}, bf16[2,144,512]{2,1,0:T(8,128)(2,1)}, u32[]{:S(2)}, u32[]{:S(2)}) collective-permute-start(bf16[2,144,512]{2,1,0:T(8,128)(2,1)S(1)} %slice.318), channel_id=1, source_target_pairs={{0,16},{8,24},{16,0},{24,8},{1,17},{9,25},{17,1},{25,9},{2,18},{10... | collective-permute-start | bytes 884744 | tf_op jit(solution)/shard_map/ppermute | solution.py:1195
  327.3 12.7 %collective-permute-start.48 = (bf16[2,144,512]{2,1,0:T(8,128)(2,1)}, bf16[2,144,512]{2,1,0:T(8,128)(2,1)}, u32[]{:S(2)}, u32[]{:S(2)}) collective-permute-start(bf16[2,144,512]{2,1,0:T(8,128)(2,1)} %slice.319), channel_id=1, source_target_pairs={{0,8},{8,0},{16,24},{24,16},{1,9},{9,1},{17,25},{25,17},{2,10},{10... | collective-permute-start | bytes 884744 | tf_op jit(solution)/shard_map/ppermute | solution.py:1195
  (31 other events, 133.5 us)

commit v4 on v3

--- a/solution.py
+++ b/solution.py
@@ -126,7 +126,7 @@
     vecs[...] = jnp.zeros_like(vecs)
     sides = []
     for src, place in ((own, core), (oth, 1 - core)):
-        block = src[...].astype(f32)
+        block = src[...].astype(bf16).astype(f32)
 
         def at(width):
             return pl.ds(pl.multiple_of(place * width, LANE), width)
@@ -173,7 +173,7 @@
 
 def front_kernel(
     scal, tok, halo, gain, w_own, w_oth, r_own, r_oth, taps, heads,
-    n_own, n_oth, u_out, act_out, dact_out, dt_out, sg_out, cum_out, cumt_out, st_out,
+    n_own, n_oth, u_out, act_out, dact_out, dt_out, sg_out, cum_out, cumt_out, st_out, st_low,
     ubuf, bt, ecl,
 ):
     step = pl.program_id(0)
@@ -243,7 +243,9 @@
         ecg = spread_group(head_columns(ecl[...], group))
         xt = (act.astype(f32) * dtg).astype(bf16)
         xw = (xt.astype(f32) * ecg).astype(bf16)
-        st_out[...] = nn(bt[...], xw)
+        state = nn(bt[...], xw)
+        st_out[...] = state
+        st_low[...] = state.astype(bf16)
 
 
 def front(scal, tok, halo, gain, wu_own, wu_oth, taps, heads):
@@ -283,6 +285,7 @@
             const_spec((tok_count, LANE)),
             const_spec((LANE, tok_count)),
             pl.BlockSpec((N, GROUP), lambda j, *_: (0, jnp.maximum(j - 1, 0))),
+            pl.BlockSpec((N, GROUP), lambda j, *_: (0, jnp.maximum(j - 1, 0))),
         ],
         [
             jax.ShapeDtypeStruct((ext, half), bf16),
@@ -295,6 +298,7 @@
             jax.ShapeDtypeStruct((tok_count, LANE), f32),
             jax.ShapeDtypeStruct((LANE, tok_count), f32),
             jax.ShapeDtypeStruct((N, DIN), f32),
+            jax.ShapeDtypeStruct((N, DIN), bf16),
         ],
         [
             pltpu.VMEM((ext, GROUP), f32),
@@ -385,7 +389,7 @@
 
 def gate_kernel(
     scal, yloc, act, z, eg, cum, s_in, vecs,
-    own_out, oth_out, ey_out, ez_out, r_loc, r_dev, dc_out, g_out, gs_out,
+    own_out, oth_out, ey_out, ez_out, r_loc, r_dev, dc_out, g_out, gs_out, g_low,
     pick, vbuf, ytbuf, ydbuf,
 ):
     step = pl.program_id(0)
@@ -465,6 +469,10 @@
     r_dev[...] = rd
     dc_out[...] = dc
 
+    @pl.when(step == pl.num_programs(0) - 1)
+    def _():
+        g_low[...] = g_out[...].astype(bf16)
+
 
 def gate(scal, yloc, act, z, eg, cum, s_in, vecs):
     tok_count = act.shape[0]
@@ -500,6 +508,7 @@
             rowspec(LANE),
             const_spec((N, DIN)),
             const_spec((8, DIN)),
+            const_spec((N, DIN)),
         ],
         [
             out(DIN // 2, bf16),
@@ -511,6 +520,7 @@
             out(LANE, f32),
             jax.ShapeDtypeStruct((N, DIN), f32),
             jax.ShapeDtypeStruct((8, DIN), f32),
+            jax.ShapeDtypeStruct((N, DIN), bf16),
         ],
         [
             pltpu.VMEM((DIN, LANE), bf16),
@@ -968,7 +978,7 @@
         ],
         [const_spec((rows, d)), const_spec((HALO, d)), const_spec((8, d))],
         [
-            jax.ShapeDtypeStruct((rows, d), f32),
+            pltpu.HBM((rows, d), f32),
             jax.ShapeDtypeStruct((HALO, d), f32),
             jax.ShapeDtypeStruct((8, d), f32),
         ],
@@ -1248,7 +1258,7 @@
     return across(by_x[: SIDE // 2], "rep", 2), across(by_y[SIDE // 2 :], "rep", 1)
 
 
-def chain(local, total, logs, by, *cover):
+def chain(local, low, total, logs, by, *cover):
     size = lax.axis_size("tm")
     tm = lax.axis_index("tm")
 
@@ -1265,7 +1275,7 @@
     def inclusive(held):
         return (local + total * held).astype(bf16)
 
-    first = moved(local.astype(bf16), 1)
+    first = moved(low, 1)
     reach = moved(logs, 1)
     total = after(total, *cover)
     held = inside(first, 1)
@@ -1321,7 +1331,7 @@
         + fill(norm_gain)
         + [dt_bias, a_log, d_skip, jnp.zeros((half_conv - 3 * half_heads,), f32)]
     )
-    pack = pack.reshape(8, half_conv).astype(bf16)
+    pack = pack.reshape(8, half_conv)
     pack_oth = swap(pack)
     edge_tok = tok[tok_count - HALO :]
     halo = shifted(edge_tok, 1)
@@ -1335,7 +1345,7 @@
     wo_oth = swap(wo_own)
     up_oth = swap(upstream)
 
-    n_own, n_oth, u, act, dact, dt, sg, cum, cumt, st = front(
+    n_own, n_oth, u, act, dact, dt, sg, cum, cumt, st, st_low = front(
         scal, tok, halo, gain, after(wu_own, wz_own, wo_own), wu_oth, taps, heads
     )
     n_got = swap(n_oth)
@@ -1345,17 +1355,17 @@
     logs = cum[tok_count - 1 :]
     z = gate_proj(scal, n_own, n_oth, wz_own, wz_oth)
     eg = grad_gated(scal, upstream, wo_own, wo_oth)
-    sent, finish = chain(st, total, logs, 1, z, eg)
+    sent, finish = chain(st, st_low, total, logs, 1, z, eg)
     yloc, s0 = intra(scal, after(act, sent), dt, cum, cumt)
     s_in = finish(yloc)
-    g_own, g_oth, ey, ez, r_loc, r_dev, dc_dev, g_loc, gs = gate(
+    g_own, g_oth, ey, ez, r_loc, r_dev, dc_dev, g_loc, gs, g_low = gate(
         scal, yloc, act, z, eg, cum, s_in, vecs
     )
 
     gated_got = swap(g_oth)
     ez_got = swap(ez)
     ab = outer_ab(scal, g_own, gated_got, upstream, up_oth, ez, ez_got, n_own, n_got)
-    sent, finish = chain(g_loc, total, logs, -1, ab[0])
+    sent, finish = chain(g_loc, g_low, total, logs, -1, ab[0])
     dxt, db_loc, dc_loc, r2, cq = back(scal, after(act, sent), dt, cum, cumt, ey, s0)
     g_in = finish(dxt)
     ab_corner = exchange_corner(ab)
@@ -1367,12 +1377,9 @@
     eu_got = [swap(e) for e in eu]
     ab_parts = sum_parts(ab[0], ab_got, gconv)
     *c, g_rates = outer_c(scal, eu, eu_got, after(n_own, *ab_parts), n_got)
-    output = out_proj(scal, g_own, g_oth, wo_own, wo_oth, after(tok, c[0]))
     c_corner = exchange_corner(c)
-    c_got = exchange_sides(c, c_corner, output)
-    ab_piece = reduce_times(ab_parts, output)
     grad_in, edge, ggain = input_back(
-        scal, ez, eu, wz_own, wz_oth, wu_own, wu_oth, after(tok, ab_piece, *c_corner), halo, upstream, gain
+        scal, ez, eu, wz_own, wz_oth, wu_own, wu_oth, after(tok, c[0]), halo, upstream, gain
     )
     grad_skip = jnp.sum(gs[1].reshape(H, P_SIZE), axis=1)
 
@@ -1395,9 +1402,12 @@
         ],
         axis=1,
     )
-    ab_near = gather_times(ab_piece, packed)
-    c_parts = sum_parts(c[0], c_got, ab_near)
-    packed = after(packed, *c_parts)
+    c_got = exchange_sides(c, c_corner, packed)
+    ab_piece = reduce_times(ab_parts, packed)
+    output = out_proj(scal, g_own, g_oth, wo_own, wo_oth, after(tok, ab_piece))
+    c_parts = sum_parts(c[0], c_got, output)
+    ab_near = gather_times(ab_piece, *c_parts)
+    packed = after(packed, *c_corner)
     own = lax.dynamic_index_in_dim(packed, core, 0, keepdims=False)
     small = own + swap(lax.dynamic_index_in_dim(packed, 1 - core, 0, keepdims=False))
     small = jnp.concatenate([small, g_rates.reshape(8, -1)], axis=1)
@@ -1415,7 +1425,7 @@
     c_piece = reduce_times(c_parts)
     c_near = gather_times(c_piece)
     small = total_over(after(small, c_piece), "tm")
-    edge = shifted(edge, -1)
+    edge = shifted(after(edge.astype(bf16), *c_parts), -1).astype(f32)
     edge = jnp.where(tm == tm_size - 1, jnp.zeros_like(edge), edge)
     input_grad = grad_in.at[tok_count - HALO :].add(edge)
     c_x, c_y = gather_replicas(c_near)

time: 346 us -> 341 us (0.986)
  waiting for transfers between devices: 62.5 us -> 51.1 us
  starting transfers between devices: 57.8 us -> 63.4 us
    ppermute x34, waiting for transfers between devices: 51.7 us -> 40.1 us  [across(): lax.ppermute(x, axis, [(i, i ^ mask) for i in range(lax.axis_size(axis))])]
    ppermute x34, starting transfers between devices: 39.2 us -> 42.9 us  [across(): lax.ppermute(x, axis, [(i, i ^ mask) for i in range(lax.axis_size(axis))])]
    unnamed x80 -> x72, local copies, waits for them, and re-layouts: 8.47 us -> 10.3 us
  transfers between devices with their start and end apart: 56 -> 56, of which waited for: 17 -> 14; matrix products, arithmetic and copies ran while one was open for 11% -> 11% of each run, Pallas kernels for 44% -> 44%
where the time goes in v4:
time: 341 us; the launch traced here: 339 us
  Pallas kernels  171 us (50%)
  starting transfers between devices  63.4 us (19%)
  waiting for transfers between devices  51.1 us (15%)
  local copies, waits for them, and re-layouts  30.3 us (9%)
  other arithmetic  20 us (6%)
    ppermute x34, starting transfers between devices, across(): lax.ppermute(x, axis, [(i, i ^ mask) for i in range(lax.axis_size(axis))])  42.9 us
    ppermute x34, waiting for transfers between devices, across(): lax.ppermute(x, axis, [(i, i ^ mask) for i in range(lax.axis_size(axis))])  40.1 us
    pallas_call x1, Pallas kernels, front(): call(front_kernel, (groups,), [const_spec((tok_count, d)), const_spec((HA...  25.7 us
    pallas_call x1, Pallas kernels, tail(): call(tail_kernel, (groups + 2,), [wide, pl.BlockSpec((tok_count, GROUP),...  25.3 us
    pallas_call x1, Pallas kernels, back(): call(back_kernel, (groups,), [wide, pl.BlockSpec((tok_count, GROUP), lamb...  18.3 us
    pallas_call x1, Pallas kernels, gate(): call(gate_kernel, (tok_count // rows,), [rowspec(DIN), rowspec(CONV), row...  17.3 us
    ppermute x8, starting transfers between devices, shifted(): lax.ppermute(x, 'tm', [(i, (i + by) % length) for i in range(length)])  17 us
    pallas_call x1, Pallas kernels, input_back(): call(input_back_kernel, (2 * per,), [const_spec(ez.shape), own(zd), oth(z...  14.5 us
  transfers between devices with their start and end apart: 56, of which 14 were waited for; matrix products, arithmetic and copies ran while one was open for 11% of the time, Pallas kernels for 44%

profile of v4, /device:TPU:0, one launch (start us, length us, event | category | flops | bytes accessed | tf_op | source)
XLA Modules:
  0.0 339.0 jit_solution(6692688748764720505)
XLA Ops:
  1.4 4.1 %convert.6 = bf16[4384,512]{1,0:T(8,128)(2,1)S(1)} convert(f32[4384,512]{1,0:T(8,128)} %bitcast.79) | non-fusion elementwise | flops 2244608 | bytes 13467648 | tf_op jit(solution)/shard_map/convert.3
  6.5 2.4 copy-done.3
  8.8 1.7 convert_element_type.253.w_own
  11.2 1.4 slice.299.w_own.wz_own
  12.6 3.1 collective-permute-start
  18.9 2.3 vectors.1
  21.8 25.7 %front.1 = (bf16[528,512]{1,0:T(8,128)(2,1)}, bf16[528,512]{1,0:T(8,128)(2,1)}, bf16[528,2304]{1,0:T(8,128)(2,1)}, bf16[512,2304]{1,0:T(8,128)(2,1)}, bf16[512,2...) custom-call(s32[4]{0:T(128)} %pad_add_fusion.scal, ...), custom_call_target="tpu_custom_call" | custom-call | flops 2629828 | bytes 13099 | tf_op jit(solution)/shard_map/front/pallas_call | solution.py:263
  47.6 3.0 collective-permute-start.5
  50.5 6.8 %grad_gated.1.eg = bf16[2,512,1024]{2,1,0:T(8,128)(2,1)} custom-call(s32[4]{0:T(128)} %pad_add_fusion.scal, bf16[512,1024]{1,0:T(8,128)(2,1)} %bitcast.75, bf16[1024,1024]{1,0:T(8,128)(2,1)} %convert_element_type.253.w_own, bf16[1024,1024]{1,0:T(8,128)(2,1)} %collective-permute-done.4.w_oth), custom_call_target="tpu_custom_call" | custom-call | flops 2147483 | bytes 4194 | tf_op jit(solution)/shard_map/grad_gated/pallas_call | solution.py:864
  58.2 6.9 %gate_proj.1.z = bf16[512,2048]{1,0:T(8,128)(2,1)} custom-call(s32[4]{0:T(128)} %pad_add_fusion.scal, bf16[528,512]{1,0:T(8,128)(2,1)} %get-tuple-element.154.a_own.rb1.rest_10_, bf16[528,512]{1,0:T(8,128)(2,1)} %get-tuple-element.110.a_oth, bf16[2048,512]{1,0:T(8,128)(2,1)} %slice.299.w_own.wz_own, bf16[2048,512]{1,0:T(8,128)(2,1)} %collective-permute-done.3.w_oth.wz_oth), custom_call_target="tpu_custom_call" | custom-call | flops 2147483 | bytes 4194 | tf_op jit(solution)/shard_map/gate_proj/pallas_call | solution.py:842
  65.3 2.7 collective-permute-start.7
  70.1 14.3 %intra.1 = (f32[512,2048]{1,0:T(8,128)}, bf16[4,128,2048]{2,1,0:T(8,128)(2,1)}) custom-call(s32[4]{0:T(128)} %pad_add_fusion.scal, bf16[512,2304]{1,0:T(8,128)(2,1)} %get-tuple-element.124.x.bc.act, bf16[512,2304]{1,0:T(8,128)(2,1)} %get-tuple-element.124.x.bc.act, f32[512,128]{1,0:T(8,128)} %get-tuple-element.114.dt, f32[512,128]{1,0:T(8,128)} %get-tuple-element.108.cum, ...), custom_call_target="tpu_custom_call" | custom-call | flops 805306 | bytes 8388 | tf_op jit(solution)/shard_map/intra/pallas_call | solution.py:365
  84.6 6.6 %collective-permute-done.7 = bf16[128,2048]{1,0:T(8,128)(2,1)S(1)} collective-permute-done((bf16[128,2048]{1,0:T(8,128)(2,1)S(1)}, bf16[128,2048]{1,0:T(8,128)(2,1)S(1)}, u32[]{:S(2)}, u32[]{:S(2)}) %collective-permute-start.7) | collective-permute-done | bytes 524320 | tf_op jit(solution)/shard_map/ppermute | solution.py:1201
  92.2 17.3 %gate.1 = (bf16[512,1024]{1,0:T(8,128)(2,1)}, bf16[512,1024]{1,0:T(8,128)(2,1)}, bf16[512,2048]{1,0:T(8,128)(2,1)}, bf16[512,2048]{1,0:T(8,128)(2,1)}, f32[512,1...) custom-call(s32[4]{0:T(128)} %pad_add_fusion.scal, ...), custom_call_target="tpu_custom_call" | custom-call | flops 1610612 | bytes 20971 | tf_op jit(solution)/shard_map/gate/pallas_call | solution.py:489
  110.6 2.3 collective-permute-start.14
  112.9 2.5 collective-permute-done.9.ra2
  115.4 2.3 collective-permute-start.15
  118.6 12.7 %outer_ab.1 = (bf16[4,256,512]{2,1,0:T(8,128)(2,1)}, bf16[4,256,512]{2,1,0:T(8,128)(2,1)}, bf16[4,256,512]{2,1,0:T(8,128)(2,1)}, bf16[4,256,512]{2,1,0:T(8,128)(2,1)}) custom-call(s32[4]{0:T(128)} %pad_add_fusion.scal, bf16[512,1024]{1,0:T(8,128)(2,1)} %get-tuple-element.119.a1.a_own, bf16[512,1024]{1,0:T(8,128)(2,1)} %collective-permute-done.8.a2, ...), custom_call_target="tpu_custom_call" | custom-call | flops 4294967 | bytes 10000 | tf_op jit(solution)/shard_map/outer_ab/pallas_call | solution.py:1037
  131.3 2.5 fusion.11
  133.8 1.5 collective-permute-start.13
  136.0 1.5 collective-permute-start.12
  137.7 1.6 collective-permute-start.16
  139.4 18.3 %back.1 = (bf16[512,2048]{1,0:T(8,128)(2,1)}, f32[512,128]{1,0:T(8,128)}, f32[512,128]{1,0:T(8,128)}, f32[512,128]{1,0:T(8,128)}, f32[8,128]{1,0:T(8,128)}) custom-call(s32[4]{0:T(128)} %pad_add_fusion.scal, bf16[512,2304]{1,0:T(8,128)(2,1)} %get-tuple-element.124.x.bc.act, bf16[512,2304]{1,0:T(8,128)(2,1)} %get-tuple-element.124.x.bc.act, ...), custom_call_target="tpu_custom_call" | custom-call | flops 2147483 | bytes 8388 | tf_op jit(solution)/shard_map/back/pallas_call | solution.py:630
  157.8 1.2 add_convert_fusion
  159.6 1.2 add_convert_fusion.1
  163.1 2.1 add_convert_fusion.2.g_in
  165.1 25.3 %tail.1 = (bf16[528,512]{1,0:T(8,128)(2,1)}, bf16[528,512]{1,0:T(8,128)(2,1)}, bf16[528,512]{1,0:T(8,128)(2,1)}, bf16[528,512]{1,0:T(8,128)(2,1)}, bf16[528,512]...) custom-call(s32[4]{0:T(128)} %pad_add_fusion.scal, bf16[512,2304]{1,0:T(8,128)(2,1)} %get-tuple-element.124.x.bc.act, ...), custom_call_target="tpu_custom_call" | custom-call | flops 1073741 | bytes 12582 | tf_op jit(solution)/shard_map/tail/pallas_call | solution.py:779
  193.5 2.7 fusion
  196.2 2.6 collective-permute-start.26
  198.9 1.7 collective-permute-start.24
  202.3 10.4 %outer_c.1 = (bf16[4,144,512]{2,1,0:T(8,128)(2,1)}, bf16[4,144,512]{2,1,0:T(8,128)(2,1)}, bf16[4,144,512]{2,1,0:T(8,128)(2,1)}, bf16[4,144,512]{2,1,0:T(8,128)(2,1)}, f32[32,512]{1,0:T(8,128)}) custom-call(s32[4]{0:T(128)} %pad_add_fusion.scal, bf16[528,512]{1,0:T(8,128)(2,1)} %get-tuple-element.149.rest_0_, bf16[528,512]{1,0:T(8,128)(2,1)} %get-tuple-element.150.rest_1_, ...), custom_call_target="tpu_custom_call" | custom-call | flops 2491416 | bytes 10000 | tf_op jit(solution)/shard_map/outer_c/pallas_call | solution.py:1087
  212.7 14.5 %input_back.1 = (f32[512,1024]{1,0:T(8,128)}, f32[16,1024]{1,0:T(8,128)}, f32[8,1024]{1,0:T(8,128)}) custom-call(s32[4]{0:T(128)} %pad_add_fusion.scal, bf16[512,2048]{1,0:T(8,128)(2,1)} %get-tuple-element.121.b1.ez, bf16[2048,512]{1,0:T(8,128)(2,1)} %slice.299.w_own.wz_own, bf16[2048,512]{1,0:T(8,128)(2,1)} %collective-permute-done.3.w_oth.wz_oth, ...), custom_call_target="tpu_custom_call" | custom-call | flops 4982833 | bytes 13631 | tf_op jit(solution)/shard_map/input_back/pallas_call | solution.py:964
  228.0 1.3 collective-permute-start.29
  229.3 3.3 copy.31
  232.7 1.6 collective-permute-start.27
  234.3 1.2 add_convert_fusion.8
  237.4 2.5 collective-permute-start.32
  240.0 6.7 %out_proj.1 = bf16[512,1024]{1,0:T(8,128)(2,1)} custom-call(s32[4]{0:T(128)} %pad_add_fusion.scal, bf16[512,1024]{1,0:T(8,128)(2,1)} %get-tuple-element.119.a1.a_own, bf16[512,1024]{1,0:T(8,128)(2,1)} %get-tuple-element.120.a_oth, bf16[1024,1024]{1,0:T(8,128)(2,1)} %convert_element_type.253.w_own, bf16[1024,1024]{1,0:T(8,128)(2,1)} %collective-permute-done.4.w_oth, ...), custom_call_target="tpu_custom_call" | custom-call | flops 2147483 | bytes 4194 | tf_op jit(solution)/shard_map/out_proj/pallas_call | solution.py:888
  247.7 1.1 collective-permute-done.49
  249.7 10.6 %collective-permute-done.30 = bf16[4,144,512]{2,1,0:T(8,128)(2,1)S(1)} collective-permute-done((bf16[4,144,512]{2,1,0:T(8,128)(2,1)S(1)}, bf16[4,144,512]{2,1,0:T(8,128)(2,1)S(1)}, u32[]{:S(2)}, u32[]{:S(2)}) %collective-permute-start.30) | collective-permute-done | bytes 589856 | tf_op jit(solution)/shard_map/ppermute | solution.py:1205
  261.1 3.9 %collective-permute-done.28 = bf16[4,144,512]{2,1,0:T(8,128)(2,1)S(1)} collective-permute-done((bf16[4,144,512]{2,1,0:T(8,128)(2,1)S(1)}, bf16[4,144,512]{2,1,0:T(8,128)(2,1)S(1)}, u32[]{:S(2)}, u32[]{:S(2)}) %collective-permute-start.28) | collective-permute-done | bytes 589856 | tf_op jit(solution)/shard_map/ppermute | solution.py:1205
  266.1 1.3 collective-permute-start.51
  267.3 1.2 pad_maximum_fusion.2.refs_0_
  268.6 1.6 collective-permute-start.35
  270.7 2.0 collective-permute-start.41
  272.7 2.4 collective-permute-start.39
  275.1 4.1 %collective-permute-done.41 = bf16[144,512]{1,0:T(8,128)(2,1)S(1)} collective-permute-done((bf16[144,512]{1,0:T(8,128)(2,1)S(1)}, bf16[144,512]{1,0:T(8,128)(2,1)S(1)}, u32[]{:S(2)}, u32[]{:S(2)}) %collective-permute-start.41) | collective-permute-done | bytes 147488 | tf_op jit(solution)/shard_map/ppermute | solution.py:1205
  279.2 2.0 collective-permute-start.31
  281.2 2.9 collective-permute-done.40
  284.1 2.6 collective-permute-start.44
  286.7 1.9 collective-permute-start.42
  288.6 1.5 bitcast_dynamic-update-slice_fusion
  290.0 2.6 collective-permute-done.44
  292.7 2.5 collective-permute-start.55
  295.2 5.7 %collective-permute-done.43 = bf16[144,512]{1,0:T(8,128)(2,1)S(1)} collective-permute-done((bf16[144,512]{1,0:T(8,128)(2,1)S(1)}, bf16[144,512]{1,0:T(8,128)(2,1)S(1)}, u32[]{:S(2)}, u32[]{:S(2)}) %collective-permute-start.43) | collective-permute-done | bytes 147488 | tf_op jit(solution)/shard_map/ppermute | solution.py:1205
  300.9 2.9 collective-permute-start.54
  305.4 1.3 collective-permute-start.47
  308.4 1.4 collective-permute-start.38
  312.2 7.9 %collective-permute-done.45.refs_4_ = bf16[4,144,512]{2,1,0:T(8,128)(2,1)S(1)} collective-permute-done((bf16[4,144,512]{2,1,0:T(8,128)(2,1)S(1)}, bf16[4,144,512]{2,1,0:T(8,128)(2,1)S(1)}, u32[]{:S(2)}, u32[]{:S(2)}) %collective-permute-start.45) | collective-permute-done | bytes 589856 | tf_op jit(solution)/shard_map/ppermute | solution.py:1205
  321.7 1.7 slice.319
  323.5 1.4 collective-permute-start.48
  326.1 6.4 %finish_near.1 = (f32[1024,1024]{1,0:T(8,128)}, f32[4384,512]{1,0:T(8,128)}) custom-call(s32[4]{0:T(128)} %pad_add_fusion.scal, bf16[4,256,512]{2,1,0:T(8,128)(2,1)} %copy-done.2, bf16[4,256,512]{2,1,0:T(8,128)(2,1)} %copy-done.5, bf16[4,256,512]{2,1,0:T(8,128)(2,1)} %copy-done.6, bf16[4,144,512]{2,1,0:T(8,128)(2,1)} %copy-done.4, ...), custom_call_target="tpu_custom_call" | custom-call | bytes 10000 | tf_op jit(solution)/shard_map/finish_near/pallas_call | solution.py:1101
  332.5 1.6 collective-permute-done.46.refs_2_
  335.1 3.7 %finish_far.1 = (f32[1024,1024]{1,0:T(8,128)}, f32[4384,512]{1,0:T(8,128)}) custom-call(s32[4]{0:T(128)} %pad_add_fusion.scal, bf16[2,256,512]{2,1,0:T(8,128)(2,1)} %copy-done.21, bf16[2,256,512]{2,1,0:T(8,128)(2,1)} %copy-done.22, bf16[2,144,512]{2,1,0:T(8,128)(2,1)} %collective-permute-done.46.refs_2_, ...), custom_call_target="tpu_custom_call", output_to_operand_aliasing={{0}: (5, {}), {1}: (6, {})} | custom-call | bytes 10000 | tf_op jit(solution)/shard_map/finish_far/pallas_call | solution.py:1101
  (217 shorter events, 36.3 us)
Async XLA Ops:
  5.9 15.3 %collective-permute-start.2 = (bf16[2560,512]{1,0:T(8,128)(2,1)S(1)}, bf16[2560,512]{1,0:T(8,128)(2,1)}, u32[]{:S(2)}, u32[]{:S(2)}) collective-permute-start(bf16[2560,512]{1,0:T(8,128)(2,1)S(1)} %pad.19.w_own.r_own.wu_own), channel_id=1, source_target_pairs={{0,4},{4,0},{1,5},{5,1},{2,6},{6,2},{3,7},{7,3},{8,12},{12,8},{9,1... | collective-permute-start | bytes 7864328 | tf_op jit(solution)/shard_map/ppermute | solution.py:1196
  10.6 39.9 %collective-permute-start.4 = (bf16[1024,1024]{1,0:T(8,128)(2,1)}, bf16[1024,1024]{1,0:T(8,128)(2,1)}, u32[]{:S(2)}, u32[]{:S(2)}) collective-permute-start(bf16[1024,1024]{1,0:T(8,128)(2,1)} %convert_element_type.253.w_own), channel_id=1, source_target_pairs={{0,4},{4,0},{1,5},{5,1},{2,6},{6,2},{3,7},{7,3},{8,12},{12,8},{9,1... | collective-permute-start | bytes 6291464 | tf_op jit(solution)/shard_map/ppermute | solution.py:1196
  12.6 45.6 %collective-permute-start.3 = (bf16[2048,512]{1,0:T(8,128)(2,1)}, bf16[2048,512]{1,0:T(8,128)(2,1)}, u32[]{:S(2)}, u32[]{:S(2)}) collective-permute-start(bf16[2048,512]{1,0:T(8,128)(2,1)} %slice.299.w_own.wz_own), channel_id=1, source_target_pairs={{0,4},{4,0},{1,5},{5,1},{2,6},{6,2},{3,7},{7,3},{8,12},{12,8},{9,1... | collective-permute-start | bytes 6291464 | tf_op jit(solution)/shard_map/ppermute | solution.py:1196
  12.6 8.6 %collective-permute-start = (bf16[16,1024]{1,0:T(8,128)(2,1)S(1)}, bf16[16,1024]{1,0:T(8,128)(2,1)S(1)}, u32[]{:S(2)}, u32[]{:S(2)}) collective-permute-start(bf16[16,1024]{1,0:T(8,128)(2,1)S(1)} %slice_bitcast_fusion), channel_id=1, source_target_pairs={{0,1},{1,2},{2,3},{3,0},{4,5},{5,6},{6,7},{7,4},{8,9},{9,10},{10,1... | collective-permute-start | bytes 98312 | tf_op jit(solution)/shard_map/ppermute | solution.py:1201
  15.9 2.4 collective-permute-start.1
  47.6 17.5 %collective-permute-start.5 = (bf16[128,2048]{1,0:T(8,128)(2,1)}, bf16[128,2048]{1,0:T(8,128)(2,1)S(1)}, u32[]{:S(2)}, u32[]{:S(2)}) collective-permute-start(bf16[128,2048]{1,0:T(8,128)(2,1)} %get-tuple-element.112), channel_id=1, source_target_pairs={{0,1},{1,2},{2,3},{3,0},{4,5},{5,6},{6,7},{7,4},{8,9},{9,10},{10,1... | collective-permute-start | bytes 1572872 | tf_op jit(solution)/shard_map/ppermute | solution.py:1201
  65.3 25.9 %collective-permute-start.7 = (bf16[128,2048]{1,0:T(8,128)(2,1)S(1)}, bf16[128,2048]{1,0:T(8,128)(2,1)S(1)}, u32[]{:S(2)}, u32[]{:S(2)}) collective-permute-start(bf16[128,2048]{1,0:T(8,128)(2,1)S(1)} %add_convert_fusion.5), channel_id=1, source_target_pairs={{0,2},{1,3},{2,0},{3,1},{4,6},{5,7},{6,4},{7,5},{8,10},{9,11},{10,... | collective-permute-start | bytes 1572872 | tf_op jit(solution)/shard_map/ppermute | solution.py:1201
  68.6 15.8 %collective-permute-start.6 = (f32[1,128]{1,0:T(1,128)S(1)}, f32[1,128]{1,0:T(1,128)S(1)}, u32[]{:S(2)}, u32[]{:S(2)}) collective-permute-start(f32[1,128]{1,0:T(1,128)S(1)} %slice.237), channel_id=1, source_target_pairs={{0,1},{1,2},{2,3},{3,0},{4,5},{5,6},{6,7},{7,4},{8,9},{9,10},{10,1... | collective-permute-start | bytes 1544 | tf_op jit(solution)/shard_map/ppermute | solution.py:1201
  92.2 17.4 %copy-start.1 = (bf16[1,512,1024]{2,1,0:T(8,128)(2,1)S(1)}, bf16[1,512,1024]{2,1,0:T(8,128)(2,1)}, u32[]{:S(2)}) copy-start(bf16[1,512,1024]{2,1,0:T(8,128)(2,1)} %param.27) | copy-start | bytes 3145732
  109.5 8.3 %collective-permute-start.10 = (bf16[512,2048]{1,0:T(8,128)(2,1)}, bf16[512,2048]{1,0:T(8,128)(2,1)}, u32[]{:S(2)}, u32[]{:S(2)}) collective-permute-start(bf16[512,2048]{1,0:T(8,128)(2,1)} %get-tuple-element.121.b1.ez), channel_id=1, source_target_pairs={{0,4},{4,0},{1,5},{5,1},{2,6},{6,2},{3,7},{7,3},{8,12},{12,8},{9,1... | collective-permute-start | bytes 6291464 | tf_op jit(solution)/shard_map/ppermute | solution.py:1196
  109.6 5.8 %collective-permute-start.9 = (bf16[512,1024]{1,0:T(8,128)(2,1)S(1)}, bf16[512,1024]{1,0:T(8,128)(2,1)S(1)}, u32[]{:S(2)}, u32[]{:S(2)}) collective-permute-start(bf16[512,1024]{1,0:T(8,128)(2,1)S(1)} %bitcast.78), channel_id=1, source_target_pairs={{0,4},{4,0},{1,5},{5,1},{2,6},{6,2},{3,7},{7,3},{8,12},{12,8},{9,1... | collective-permute-start | bytes 3145736 | tf_op jit(solution)/shard_map/ppermute | solution.py:1196
  110.1 7.7 %collective-permute-start.8 = (bf16[512,1024]{1,0:T(8,128)(2,1)}, bf16[512,1024]{1,0:T(8,128)(2,1)}, u32[]{:S(2)}, u32[]{:S(2)}) collective-permute-start(bf16[512,1024]{1,0:T(8,128)(2,1)} %get-tuple-element.120.a_oth), channel_id=1, source_target_pairs={{0,4},{4,0},{1,5},{5,1},{2,6},{6,2},{3,7},{7,3},{8,12},{12,8},{9,1... | collective-permute-start | bytes 3145736 | tf_op jit(solution)/shard_map/ppermute | solution.py:1196
  110.2 7.6 %collective-permute-start.11 = (bf16[528,512]{1,0:T(8,128)(2,1)}, bf16[528,512]{1,0:T(8,128)(2,1)S(1)}, u32[]{:S(2)}, u32[]{:S(2)}) collective-permute-start(bf16[528,512]{1,0:T(8,128)(2,1)} %get-tuple-element.110.a_oth), channel_id=1, source_target_pairs={{0,4},{4,0},{1,5},{5,1},{2,6},{6,2},{3,7},{7,3},{8,12},{12,8},{9,1... | collective-permute-start | bytes 1622024 | tf_op jit(solution)/shard_map/ppermute | solution.py:1196
  110.6 27.0 %collective-permute-start.14 = (bf16[128,2048]{1,0:T(8,128)(2,1)}, bf16[128,2048]{1,0:T(8,128)(2,1)S(1)}, u32[]{:S(2)}, u32[]{:S(2)}) collective-permute-start(bf16[128,2048]{1,0:T(8,128)(2,1)} %get-tuple-element.130), channel_id=1, source_target_pairs={{0,3},{1,0},{2,1},{3,2},{4,7},{5,4},{6,5},{7,6},{8,11},{9,8},{10,9... | collective-permute-start | bytes 1572872 | tf_op jit(solution)/shard_map/ppermute | solution.py:1201
  115.4 47.1 %collective-permute-start.15 = (f32[1,128]{1,0:T(1,128)S(1)}, f32[1,128]{1,0:T(1,128)S(1)}, u32[]{:S(2)}, u32[]{:S(2)}) collective-permute-start(f32[1,128]{1,0:T(1,128)S(1)} %slice.237), channel_id=1, source_target_pairs={{0,3},{1,0},{2,1},{3,2},{4,7},{5,4},{6,5},{7,6},{8,11},{9,8},{10,9... | collective-permute-start | bytes 1544 | tf_op jit(solution)/shard_map/ppermute | solution.py:1201
  133.8 24.0 %collective-permute-start.13 = (bf16[2,256,512]{2,1,0:T(8,128)(2,1)}, bf16[2,256,512]{2,1,0:T(8,128)(2,1)}, u32[]{:S(2)}, u32[]{:S(2)}) collective-permute-start(bf16[2,256,512]{2,1,0:T(8,128)(2,1)} %get-tuple-element.186), channel_id=1, source_target_pairs={{0,8},{8,0},{16,24},{24,16},{1,9},{9,1},{17,25},{25,17},{2,10},{10... | collective-permute-start | bytes 1572872 | tf_op jit(solution)/shard_map/ppermute | solution.py:1205
  136.0 23.6 %collective-permute-start.12 = (bf16[2,256,512]{2,1,0:T(8,128)(2,1)}, bf16[2,256,512]{2,1,0:T(8,128)(2,1)}, u32[]{:S(2)}, u32[]{:S(2)}) collective-permute-start(bf16[2,256,512]{2,1,0:T(8,128)(2,1)} %get-tuple-element.185), channel_id=1, source_target_pairs={{0,16},{8,24},{16,0},{24,8},{1,17},{9,25},{17,1},{25,9},{2,18},{10... | collective-permute-start | bytes 1572872 | tf_op jit(solution)/shard_map/ppermute | solution.py:1205
  137.7 25.3 %collective-permute-start.16 = (bf16[128,2048]{1,0:T(8,128)(2,1)S(1)}, bf16[128,2048]{1,0:T(8,128)(2,1)}, u32[]{:S(2)}, u32[]{:S(2)}) collective-permute-start(bf16[128,2048]{1,0:T(8,128)(2,1)S(1)} %add_convert_fusion.3), channel_id=1, source_target_pairs={{0,2},{1,3},{2,0},{3,1},{4,6},{5,7},{6,4},{7,5},{8,10},{9,11},{10,... | collective-permute-start | bytes 1572872 | tf_op jit(solution)/shard_map/ppermute | solution.py:1201
  139.4 18.3 %copy-start.11 = (bf16[4,256,512]{2,1,0:T(8,128)(2,1)S(1)}, bf16[4,256,512]{2,1,0:T(8,128)(2,1)}, u32[]{:S(2)}) copy-start(bf16[4,256,512]{2,1,0:T(8,128)(2,1)} %get-tuple-element.146) | copy-start | bytes 3145732
  159.0 32.6 %collective-permute-start.18 = (bf16[4,256,512]{2,1,0:T(8,128)(2,1)S(1)}, bf16[4,256,512]{2,1,0:T(8,128)(2,1)}, u32[]{:S(2)}, u32[]{:S(2)}) collective-permute-start(bf16[4,256,512]{2,1,0:T(8,128)(2,1)S(1)} %pad_maximum_fusion.1), channel_id=1, source_target_pairs={{0,16},{8,24},{16,0},{24,8},{1,17},{9,25},{17,1},{25,9},{2,18},{10... | collective-permute-start | bytes 3145736 | tf_op jit(solution)/shard_map/ppermute | solution.py:1205
  160.9 31.3 %collective-permute-start.17 = (bf16[4,256,512]{2,1,0:T(8,128)(2,1)S(1)}, bf16[4,256,512]{2,1,0:T(8,128)(2,1)}, u32[]{:S(2)}, u32[]{:S(2)}) collective-permute-start(bf16[4,256,512]{2,1,0:T(8,128)(2,1)S(1)} %pad_maximum_fusion), channel_id=1, source_target_pairs={{0,8},{8,0},{16,24},{24,16},{1,9},{9,1},{17,25},{25,17},{2,10},{10... | collective-permute-start | bytes 3145736 | tf_op jit(solution)/shard_map/ppermute | solution.py:1205
  165.1 28.4 %copy-start.14 = (bf16[4,256,512]{2,1,0:T(8,128)(2,1)S(1)}, bf16[4,256,512]{2,1,0:T(8,128)(2,1)}, u32[]{:S(2)}) copy-start(bf16[4,256,512]{2,1,0:T(8,128)(2,1)} %get-tuple-element.144) | copy-start | bytes 3145732
  191.1 5.1 %collective-permute-start.19 = (bf16[528,512]{1,0:T(8,128)(2,1)}, bf16[528,512]{1,0:T(8,128)(2,1)}, u32[]{:S(2)}, u32[]{:S(2)}) collective-permute-start(bf16[528,512]{1,0:T(8,128)(2,1)} %get-tuple-element.149.rest_0_), channel_id=1, source_target_pairs={{0,4},{4,0},{1,5},{5,1},{2,6},{6,2},{3,7},{7,3},{8,12},{12,8},{9,1... | collective-permute-start | bytes 1622024 | tf_op jit(solution)/shard_map/ppermute | solution.py:1196
  191.1 7.7 %collective-permute-start.20 = (bf16[528,512]{1,0:T(8,128)(2,1)}, bf16[528,512]{1,0:T(8,128)(2,1)}, u32[]{:S(2)}, u32[]{:S(2)}) collective-permute-start(bf16[528,512]{1,0:T(8,128)(2,1)} %get-tuple-element.150.rest_1_), channel_id=1, source_target_pairs={{0,4},{4,0},{1,5},{5,1},{2,6},{6,2},{3,7},{7,3},{8,12},{12,8},{9,1... | collective-permute-start | bytes 1622024 | tf_op jit(solution)/shard_map/ppermute | solution.py:1196
  191.6 7.3 %collective-permute-start.21 = (bf16[528,512]{1,0:T(8,128)(2,1)}, bf16[528,512]{1,0:T(8,128)(2,1)}, u32[]{:S(2)}, u32[]{:S(2)}) collective-permute-start(bf16[528,512]{1,0:T(8,128)(2,1)} %get-tuple-element.151.rest_2_), channel_id=1, source_target_pairs={{0,4},{4,0},{1,5},{5,1},{2,6},{6,2},{3,7},{7,3},{8,12},{12,8},{9,1... | collective-permute-start | bytes 1622024 | tf_op jit(solution)/shard_map/ppermute | solution.py:1196
  191.7 9.0 %collective-permute-start.22 = (bf16[528,512]{1,0:T(8,128)(2,1)}, bf16[528,512]{1,0:T(8,128)(2,1)S(1)}, u32[]{:S(2)}, u32[]{:S(2)}) collective-permute-start(bf16[528,512]{1,0:T(8,128)(2,1)} %get-tuple-element.152.rest_3_), channel_id=1, source_target_pairs={{0,4},{4,0},{1,5},{5,1},{2,6},{6,2},{3,7},{7,3},{8,12},{12,8},{9,1... | collective-permute-start | bytes 1622024 | tf_op jit(solution)/shard_map/ppermute | solution.py:1196
  192.2 8.4 %collective-permute-start.23 = (bf16[528,512]{1,0:T(8,128)(2,1)}, bf16[528,512]{1,0:T(8,128)(2,1)S(1)}, u32[]{:S(2)}, u32[]{:S(2)}) collective-permute-start(bf16[528,512]{1,0:T(8,128)(2,1)} %get-tuple-element.153.rest_4_), channel_id=1, source_target_pairs={{0,4},{4,0},{1,5},{5,1},{2,6},{6,2},{3,7},{7,3},{8,12},{12,8},{9,1... | collective-permute-start | bytes 1622024 | tf_op jit(solution)/shard_map/ppermute | solution.py:1196
  196.2 38.0 %collective-permute-start.26 = (bf16[256,512]{1,0:T(8,128)(2,1)}, bf16[256,512]{1,0:T(8,128)(2,1)}, u32[]{:S(2)}, u32[]{:S(2)}) collective-permute-start(bf16[256,512]{1,0:T(8,128)(2,1)} %get-tuple-element.178), channel_id=1, source_target_pairs={{0,3},{1,2},{2,1},{3,0},{4,7},{5,6},{6,5},{7,4},{8,11},{9,10},{10,... | collective-permute-start | bytes 786440 | tf_op jit(solution)/shard_map/ppermute | solution.py:1205
  198.9 35.4 %collective-permute-start.25 = (bf16[256,512]{1,0:T(8,128)(2,1)}, bf16[256,512]{1,0:T(8,128)(2,1)}, u32[]{:S(2)}, u32[]{:S(2)}) collective-permute-start(bf16[256,512]{1,0:T(8,128)(2,1)} %get-tuple-element.179), channel_id=1, source_target_pairs={{0,2},{1,3},{2,0},{3,1},{4,6},{5,7},{6,4},{7,5},{8,10},{9,11},{10,... | collective-permute-start | bytes 786440 | tf_op jit(solution)/shard_map/ppermute | solution.py:1205
  198.9 35.4 %collective-permute-start.24 = (bf16[256,512]{1,0:T(8,128)(2,1)}, bf16[256,512]{1,0:T(8,128)(2,1)}, u32[]{:S(2)}, u32[]{:S(2)}) collective-permute-start(bf16[256,512]{1,0:T(8,128)(2,1)} %get-tuple-element.180), channel_id=1, source_target_pairs={{0,1},{1,0},{2,3},{3,2},{4,5},{5,4},{6,7},{7,6},{8,9},{9,8},{10,11... | collective-permute-start | bytes 786440 | tf_op jit(solution)/shard_map/ppermute | solution.py:1205
  212.7 15.3 %copy-start.17 = (bf16[4,144,512]{2,1,0:T(8,128)(2,1)S(1)}, bf16[4,144,512]{2,1,0:T(8,128)(2,1)}, u32[]{:S(2)}) copy-start(bf16[4,144,512]{2,1,0:T(8,128)(2,1)} %get-tuple-element.166) | copy-start | bytes 1769476
  228.0 18.7 %collective-permute-start.29 = (bf16[2,144,512]{2,1,0:T(8,128)(2,1)S(1)}, bf16[2,144,512]{2,1,0:T(8,128)(2,1)S(1)}, u32[]{:S(2)}, u32[]{:S(2)}) collective-permute-start(bf16[2,144,512]{2,1,0:T(8,128)(2,1)S(1)} %get-tuple-element.188), channel_id=1, source_target_pairs={{0,8},{8,0},{16,24},{24,16},{1,9},{9,1},{17,25},{25,17},{2,10},{10... | collective-permute-start | bytes 884744 | tf_op jit(solution)/shard_map/ppermute | solution.py:1205
  232.7 14.8 %collective-permute-start.27 = (bf16[2,144,512]{2,1,0:T(8,128)(2,1)S(1)}, bf16[2,144,512]{2,1,0:T(8,128)(2,1)S(1)}, u32[]{:S(2)}, u32[]{:S(2)}) collective-permute-start(bf16[2,144,512]{2,1,0:T(8,128)(2,1)S(1)} %get-tuple-element.187), channel_id=1, source_target_pairs={{0,16},{8,24},{16,0},{24,8},{1,17},{9,25},{17,1},{25,9},{2,18},{10... | collective-permute-start | bytes 884744 | tf_op jit(solution)/shard_map/ppermute | solution.py:1205
  235.5 30.5 %collective-permute-start.34 = (bf16[256,512]{1,0:T(8,128)(2,1)S(1)}, bf16[256,512]{1,0:T(8,128)(2,1)}, u32[]{:S(2)}, u32[]{:S(2)}) collective-permute-start(bf16[256,512]{1,0:T(8,128)(2,1)S(1)} %add_convert_fusion.8), channel_id=1, source_target_pairs={{0,3},{1,2},{2,1},{3,0},{4,7},{5,6},{6,5},{7,4},{8,11},{9,10},{10,... | collective-permute-start | bytes 786440 | tf_op jit(solution)/shard_map/ppermute | solution.py:1205
  236.6 30.8 %collective-permute-start.33 = (bf16[256,512]{1,0:T(8,128)(2,1)S(1)}, bf16[256,512]{1,0:T(8,128)(2,1)}, u32[]{:S(2)}, u32[]{:S(2)}) collective-permute-start(bf16[256,512]{1,0:T(8,128)(2,1)S(1)} %add_convert_fusion.8), channel_id=1, source_target_pairs={{0,2},{1,3},{2,0},{3,1},{4,6},{5,7},{6,4},{7,5},{8,10},{9,11},{10,... | collective-permute-start | bytes 786440 | tf_op jit(solution)/shard_map/ppermute | solution.py:1205
  237.4 29.9 %collective-permute-start.32 = (bf16[256,512]{1,0:T(8,128)(2,1)S(1)}, bf16[256,512]{1,0:T(8,128)(2,1)}, u32[]{:S(2)}, u32[]{:S(2)}) collective-permute-start(bf16[256,512]{1,0:T(8,128)(2,1)S(1)} %add_convert_fusion.8), channel_id=1, source_target_pairs={{0,1},{1,0},{2,3},{3,2},{4,5},{5,4},{6,7},{7,6},{8,9},{9,8},{10,11... | collective-permute-start | bytes 786440 | tf_op jit(solution)/shard_map/ppermute | solution.py:1205
  246.8 19.1 %copy-start.18 = (bf16[4,144,512]{2,1,0:T(8,128)(2,1)S(1)}, bf16[4,144,512]{2,1,0:T(8,128)(2,1)}, u32[]{:S(2)}) copy-start(bf16[4,144,512]{2,1,0:T(8,128)(2,1)} %get-tuple-element.163) | copy-start | bytes 1769476
  246.8 13.5 %collective-permute-start.30 = (bf16[4,144,512]{2,1,0:T(8,128)(2,1)S(1)}, bf16[4,144,512]{2,1,0:T(8,128)(2,1)S(1)}, u32[]{:S(2)}, u32[]{:S(2)}) collective-permute-start(bf16[4,144,512]{2,1,0:T(8,128)(2,1)S(1)} %pad_maximum_fusion.4), channel_id=1, source_target_pairs={{0,16},{8,24},{16,0},{24,8},{1,17},{9,25},{17,1},{25,9},{2,18},{10... | collective-permute-start | bytes 1769480 | tf_op jit(solution)/shard_map/ppermute | solution.py:1205
  247.5 1.3 collective-permute-start.49
  248.8 16.2 %collective-permute-start.28 = (bf16[4,144,512]{2,1,0:T(8,128)(2,1)S(1)}, bf16[4,144,512]{2,1,0:T(8,128)(2,1)S(1)}, u32[]{:S(2)}, u32[]{:S(2)}) collective-permute-start(bf16[4,144,512]{2,1,0:T(8,128)(2,1)S(1)} %pad_maximum_fusion.3), channel_id=1, source_target_pairs={{0,8},{8,0},{16,24},{24,16},{1,9},{9,1},{17,25},{25,17},{2,10},{10... | collective-permute-start | bytes 1769480 | tf_op jit(solution)/shard_map/ppermute | solution.py:1205
  260.3 10.4 %collective-permute-start.52 = (f32[8,3200]{1,0:T(8,128)S(1)}, f32[8,3200]{1,0:T(8,128)S(1)}, u32[]{:S(2)}, u32[]{:S(2)}) collective-permute-start(f32[8,3200]{1,0:T(8,128)S(1)} %pad_maximum_fusion.6), channel_id=1, source_target_pairs={{0,24},{8,16},{16,8},{24,0},{1,25},{9,17},{17,9},{25,1},{2,26},{10... | collective-permute-start | bytes 307208 | tf_op jit(solution)/shard_map/ppermute | solution.py:1205
  265.0 7.7 %collective-permute-start.50 = (f32[8,3200]{1,0:T(8,128)S(1)}, f32[8,3200]{1,0:T(8,128)S(1)}, u32[]{:S(2)}, u32[]{:S(2)}) collective-permute-start(f32[8,3200]{1,0:T(8,128)S(1)} %pad_maximum_fusion.6), channel_id=1, source_target_pairs={{0,8},{8,0},{16,24},{24,16},{1,9},{9,1},{17,25},{25,17},{2,10},{10... | collective-permute-start | bytes 307208 | tf_op jit(solution)/shard_map/ppermute | solution.py:1205
  266.1 6.6 %collective-permute-start.51 = (f32[8,3200]{1,0:T(8,128)S(1)}, f32[8,3200]{1,0:T(8,128)S(1)}, u32[]{:S(2)}, u32[]{:S(2)}) collective-permute-start(f32[8,3200]{1,0:T(8,128)S(1)} %pad_maximum_fusion.6), channel_id=1, source_target_pairs={{0,16},{8,24},{16,0},{24,8},{1,17},{9,25},{17,1},{25,9},{2,18},{10... | collective-permute-start | bytes 307208 | tf_op jit(solution)/shard_map/ppermute | solution.py:1205
  268.6 39.0 %copy-start.2 = (bf16[4,256,512]{2,1,0:T(8,128)(2,1)}, bf16[4,256,512]{2,1,0:T(8,128)(2,1)S(1)}, u32[]{:S(2)}) copy-start(bf16[4,256,512]{2,1,0:T(8,128)(2,1)S(1)} %pad_maximum_fusion.2.refs_0_) | copy-start | bytes 3145732
  268.6 35.2 %collective-permute-start.35 = (bf16[4,256,512]{2,1,0:T(8,128)(2,1)S(1)}, bf16[4,256,512]{2,1,0:T(8,128)(2,1)S(1)}, u32[]{:S(2)}, u32[]{:S(2)}) collective-permute-start(bf16[4,256,512]{2,1,0:T(8,128)(2,1)S(1)} %pad_maximum_fusion.2.refs_0_), channel_id=1, source_target_pairs={{0,8},{8,0},{16,24},{24,16},{1,9},{9,1},{17,25},{25,17},{2,10},{10... | collective-permute-start | bytes 3145736 | tf_op jit(solution)/shard_map/ppermute | solution.py:1205
  270.1 35.3 %collective-permute-start.37 = (bf16[4,256,512]{2,1,0:T(8,128)(2,1)S(1)}, bf16[4,256,512]{2,1,0:T(8,128)(2,1)S(1)}, u32[]{:S(2)}, u32[]{:S(2)}) collective-permute-start(bf16[4,256,512]{2,1,0:T(8,128)(2,1)S(1)} %pad_maximum_fusion.2.refs_0_), channel_id=1, source_target_pairs={{0,16},{8,24},{16,0},{24,8},{1,17},{9,25},{17,1},{25,9},{2,18},{10... | collective-permute-start | bytes 3145736 | tf_op jit(solution)/shard_map/ppermute | solution.py:1205
  270.7 8.5 %collective-permute-start.41 = (bf16[144,512]{1,0:T(8,128)(2,1)S(1)}, bf16[144,512]{1,0:T(8,128)(2,1)S(1)}, u32[]{:S(2)}, u32[]{:S(2)}) collective-permute-start(bf16[144,512]{1,0:T(8,128)(2,1)S(1)} %get-tuple-element.181), channel_id=1, source_target_pairs={{0,3},{1,2},{2,1},{3,0},{4,7},{5,6},{6,5},{7,4},{8,11},{9,10},{10,... | collective-permute-start | bytes 442376 | tf_op jit(solution)/shard_map/ppermute | solution.py:1205
  272.7 11.3 %collective-permute-start.40 = (bf16[144,512]{1,0:T(8,128)(2,1)S(1)}, bf16[144,512]{1,0:T(8,128)(2,1)S(1)}, u32[]{:S(2)}, u32[]{:S(2)}) collective-permute-start(bf16[144,512]{1,0:T(8,128)(2,1)S(1)} %get-tuple-element.182), channel_id=1, source_target_pairs={{0,2},{1,3},{2,0},{3,1},{4,6},{5,7},{6,4},{7,5},{8,10},{9,11},{10,... | collective-permute-start | bytes 442376 | tf_op jit(solution)/shard_map/ppermute | solution.py:1205
  272.7 11.3 %collective-permute-start.39 = (bf16[144,512]{1,0:T(8,128)(2,1)S(1)}, bf16[144,512]{1,0:T(8,128)(2,1)S(1)}, u32[]{:S(2)}, u32[]{:S(2)}) collective-permute-start(bf16[144,512]{1,0:T(8,128)(2,1)S(1)} %get-tuple-element.183), channel_id=1, source_target_pairs={{0,1},{1,0},{2,3},{3,2},{4,5},{5,4},{6,7},{7,6},{8,9},{9,8},{10,11... | collective-permute-start | bytes 442376 | tf_op jit(solution)/shard_map/ppermute | solution.py:1205
  279.2 7.5 %collective-permute-start.31 = (bf16[16,1024]{1,0:T(8,128)(2,1)S(1)}, bf16[16,1024]{1,0:T(8,128)(2,1)S(1)}, u32[]{:S(2)}, u32[]{:S(2)}) collective-permute-start(bf16[16,1024]{1,0:T(8,128)(2,1)S(1)} %convert_element_type.293), channel_id=1, source_target_pairs={{0,3},{1,0},{2,1},{3,2},{4,7},{5,4},{6,5},{7,6},{8,11},{9,8},{10,9... | collective-permute-start | bytes 98312 | tf_op jit(solution)/shard_map/ppermute | solution.py:1201
  284.1 8.6 %collective-permute-start.44 = (bf16[144,512]{1,0:T(8,128)(2,1)S(1)}, bf16[144,512]{1,0:T(8,128)(2,1)S(1)}, u32[]{:S(2)}, u32[]{:S(2)}) collective-permute-start(bf16[144,512]{1,0:T(8,128)(2,1)S(1)} %add_convert_fusion.13), channel_id=1, source_target_pairs={{0,3},{1,2},{2,1},{3,0},{4,7},{5,6},{6,5},{7,4},{8,11},{9,10},{10,... | collective-permute-start | bytes 442376 | tf_op jit(solution)/shard_map/ppermute | solution.py:1205
  286.7 14.2 %collective-permute-start.43 = (bf16[144,512]{1,0:T(8,128)(2,1)S(1)}, bf16[144,512]{1,0:T(8,128)(2,1)S(1)}, u32[]{:S(2)}, u32[]{:S(2)}) collective-permute-start(bf16[144,512]{1,0:T(8,128)(2,1)S(1)} %add_convert_fusion.13), channel_id=1, source_target_pairs={{0,2},{1,3},{2,0},{3,1},{4,6},{5,7},{6,4},{7,5},{8,10},{9,11},{10,... | collective-permute-start | bytes 442376 | tf_op jit(solution)/shard_map/ppermute | solution.py:1205
  286.7 14.2 %collective-permute-start.42 = (bf16[144,512]{1,0:T(8,128)(2,1)S(1)}, bf16[144,512]{1,0:T(8,128)(2,1)S(1)}, u32[]{:S(2)}, u32[]{:S(2)}) collective-permute-start(bf16[144,512]{1,0:T(8,128)(2,1)S(1)} %add_convert_fusion.13), channel_id=1, source_target_pairs={{0,1},{1,0},{2,3},{3,2},{4,5},{5,4},{6,7},{7,6},{8,9},{9,8},{10,11... | collective-permute-start | bytes 442376 | tf_op jit(solution)/shard_map/ppermute | solution.py:1205
  292.7 14.9 %collective-permute-start.55 = (f32[8,3200]{1,0:T(8,128)S(1)}, f32[8,3200]{1,0:T(8,128)S(1)}, u32[]{:S(2)}, u32[]{:S(2)}) collective-permute-start(f32[8,3200]{1,0:T(8,128)S(1)} %add_add_fusion.1), channel_id=1, source_target_pairs={{0,3},{1,2},{2,1},{3,0},{4,7},{5,6},{6,5},{7,4},{8,11},{9,10},{10,... | collective-permute-start | bytes 307208 | tf_op jit(solution)/shard_map/ppermute | solution.py:1205
  300.9 7.5 %collective-permute-start.53 = (f32[8,3200]{1,0:T(8,128)S(1)}, f32[8,3200]{1,0:T(8,128)S(1)}, u32[]{:S(2)}, u32[]{:S(2)}) collective-permute-start(f32[8,3200]{1,0:T(8,128)S(1)} %add_add_fusion.1), channel_id=1, source_target_pairs={{0,1},{1,0},{2,3},{3,2},{4,5},{5,4},{6,7},{7,6},{8,9},{9,8},{10,11... | collective-permute-start | bytes 307208 | tf_op jit(solution)/shard_map/ppermute | solution.py:1205
  300.9 8.9 %collective-permute-start.54 = (f32[8,3200]{1,0:T(8,128)S(1)}, f32[8,3200]{1,0:T(8,128)S(1)}, u32[]{:S(2)}, u32[]{:S(2)}) collective-permute-start(f32[8,3200]{1,0:T(8,128)S(1)} %add_add_fusion.1), channel_id=1, source_target_pairs={{0,2},{1,3},{2,0},{3,1},{4,6},{5,7},{6,4},{7,5},{8,10},{9,11},{10,... | collective-permute-start | bytes 307208 | tf_op jit(solution)/shard_map/ppermute | solution.py:1205
  303.8 22.2 %copy-start.4 = (bf16[4,144,512]{2,1,0:T(8,128)(2,1)}, bf16[4,144,512]{2,1,0:T(8,128)(2,1)S(1)}, u32[]{:S(2)}) copy-start(bf16[4,144,512]{2,1,0:T(8,128)(2,1)S(1)} %pad_maximum_fusion.5.refs_3_) | copy-start | bytes 1769476
  303.8 22.2 %copy-start.5 = (bf16[4,256,512]{2,1,0:T(8,128)(2,1)}, bf16[4,256,512]{2,1,0:T(8,128)(2,1)S(1)}, u32[]{:S(2)}) copy-start(bf16[4,256,512]{2,1,0:T(8,128)(2,1)S(1)} %collective-permute-done.35.refs_1_) | copy-start | bytes 3145732
  303.9 16.3 %collective-permute-start.45 = (bf16[4,144,512]{2,1,0:T(8,128)(2,1)S(1)}, bf16[4,144,512]{2,1,0:T(8,128)(2,1)S(1)}, u32[]{:S(2)}, u32[]{:S(2)}) collective-permute-start(bf16[4,144,512]{2,1,0:T(8,128)(2,1)S(1)} %pad_maximum_fusion.5.refs_3_), channel_id=1, source_target_pairs={{0,8},{8,0},{16,24},{24,16},{1,9},{9,1},{17,25},{25,17},{2,10},{10... | collective-permute-start | bytes 1769480 | tf_op jit(solution)/shard_map/ppermute | solution.py:1205
  305.4 16.3 %collective-permute-start.47 = (bf16[4,144,512]{2,1,0:T(8,128)(2,1)S(1)}, bf16[4,144,512]{2,1,0:T(8,128)(2,1)}, u32[]{:S(2)}, u32[]{:S(2)}) collective-permute-start(bf16[4,144,512]{2,1,0:T(8,128)(2,1)S(1)} %pad_maximum_fusion.5.refs_3_), channel_id=1, source_target_pairs={{0,16},{8,24},{16,0},{24,8},{1,17},{9,25},{17,1},{25,9},{2,18},{10... | collective-permute-start | bytes 1769480 | tf_op jit(solution)/shard_map/ppermute | solution.py:1205
  307.6 26.5 %collective-permute-start.36 = (bf16[2,256,512]{2,1,0:T(8,128)(2,1)}, bf16[2,256,512]{2,1,0:T(8,128)(2,1)S(1)}, u32[]{:S(2)}, u32[]{:S(2)}) collective-permute-start(bf16[2,256,512]{2,1,0:T(8,128)(2,1)} %slice.316), channel_id=1, source_target_pairs={{0,16},{8,24},{16,0},{24,8},{1,17},{9,25},{17,1},{25,9},{2,18},{10... | collective-permute-start | bytes 1572872 | tf_op jit(solution)/shard_map/ppermute | solution.py:1205
  308.4 25.8 %collective-permute-start.38 = (bf16[2,256,512]{2,1,0:T(8,128)(2,1)}, bf16[2,256,512]{2,1,0:T(8,128)(2,1)S(1)}, u32[]{:S(2)}, u32[]{:S(2)}) collective-permute-start(bf16[2,256,512]{2,1,0:T(8,128)(2,1)} %slice.317), channel_id=1, source_target_pairs={{0,8},{8,0},{16,24},{24,16},{1,9},{9,1},{17,25},{25,17},{2,10},{10... | collective-permute-start | bytes 1572872 | tf_op jit(solution)/shard_map/ppermute | solution.py:1205
  320.1 14.0 %collective-permute-start.46 = (bf16[2,144,512]{2,1,0:T(8,128)(2,1)S(1)}, bf16[2,144,512]{2,1,0:T(8,128)(2,1)}, u32[]{:S(2)}, u32[]{:S(2)}) collective-permute-start(bf16[2,144,512]{2,1,0:T(8,128)(2,1)S(1)} %slice.318), channel_id=1, source_target_pairs={{0,16},{8,24},{16,0},{24,8},{1,17},{9,25},{17,1},{25,9},{2,18},{10... | collective-permute-start | bytes 884744 | tf_op jit(solution)/shard_map/ppermute | solution.py:1205
  323.5 10.6 %collective-permute-start.48 = (bf16[2,144,512]{2,1,0:T(8,128)(2,1)}, bf16[2,144,512]{2,1,0:T(8,128)(2,1)}, u32[]{:S(2)}, u32[]{:S(2)}) collective-permute-start(bf16[2,144,512]{2,1,0:T(8,128)(2,1)} %slice.319), channel_id=1, source_target_pairs={{0,8},{8,0},{16,24},{24,16},{1,9},{9,1},{17,25},{25,17},{2,10},{10... | collective-permute-start | bytes 884744 | tf_op jit(solution)/shard_map/ppermute | solution.py:1205
  (27 other events, 98.3 us)

commit v5 on v4

--- a/solution.py
+++ b/solution.py
@@ -1353,10 +1353,10 @@
     total = jnp.exp(jnp.repeat(cum[tok_count - 1, :H], P_SIZE))[None]
 
     logs = cum[tok_count - 1 :]
-    z = gate_proj(scal, n_own, n_oth, wz_own, wz_oth)
     eg = grad_gated(scal, upstream, wo_own, wo_oth)
-    sent, finish = chain(st, st_low, total, logs, 1, z, eg)
-    yloc, s0 = intra(scal, after(act, sent), dt, cum, cumt)
+    sent, finish = chain(st, st_low, total, logs, 1, eg)
+    z = gate_proj(scal, after(n_own, sent), n_oth, wz_own, wz_oth)
+    yloc, s0 = intra(scal, after(act, z), dt, cum, cumt)
     s_in = finish(yloc)
     g_own, g_oth, ey, ez, r_loc, r_dev, dc_dev, g_loc, gs, g_low = gate(
         scal, yloc, act, z, eg, cum, s_in, vecs

time: 341 us -> 340 us (level)
  no operation moved by 1% of the time
where the time goes in v5:
time: 340 us; the launch traced here: 338 us
  Pallas kernels  171 us (50%)
  starting transfers between devices  63.8 us (19%)
  waiting for transfers between devices  50 us (15%)
  local copies, waits for them, and re-layouts  30.3 us (9%)
  other arithmetic  20 us (6%)
    ppermute x34, starting transfers between devices, across(): lax.ppermute(x, axis, [(i, i ^ mask) for i in range(lax.axis_size(axis))])  44.4 us
    ppermute x34, waiting for transfers between devices, across(): lax.ppermute(x, axis, [(i, i ^ mask) for i in range(lax.axis_size(axis))])  37.5 us
    pallas_call x1, Pallas kernels, front(): call(front_kernel, (groups,), [const_spec((tok_count, d)), const_spec((HA...  25.7 us
    pallas_call x1, Pallas kernels, tail(): call(tail_kernel, (groups + 2,), [wide, pl.BlockSpec((tok_count, GROUP),...  25.3 us
    pallas_call x1, Pallas kernels, back(): call(back_kernel, (groups,), [wide, pl.BlockSpec((tok_count, GROUP), lamb...  18.3 us
    pallas_call x1, Pallas kernels, gate(): call(gate_kernel, (tok_count // rows,), [rowspec(DIN), rowspec(CONV), row...  17.3 us
    ppermute x8, starting transfers between devices, shifted(): lax.ppermute(x, 'tm', [(i, (i + by) % length) for i in range(length)])  15.9 us
    pallas_call x1, Pallas kernels, input_back(): call(input_back_kernel, (2 * per,), [const_spec(ez.shape), own(zd), oth(z...  14.5 us
  transfers between devices with their start and end apart: 56, of which 14 were waited for; matrix products, arithmetic and copies ran while one was open for 11% of the time, Pallas kernels for 44%

profile of v5, /device:TPU:0, one launch (start us, length us, event | category | flops | bytes accessed | tf_op | source)
XLA Modules:
  0.0 338.4 jit_solution(1475018881603861952)
XLA Ops:
  1.4 4.1 %convert.6 = bf16[4384,512]{1,0:T(8,128)(2,1)S(1)} convert(f32[4384,512]{1,0:T(8,128)} %bitcast.79) | non-fusion elementwise | flops 2244608 | bytes 13467648 | tf_op jit(solution)/shard_map/convert.3
  6.5 2.4 copy-done.3
  8.8 1.7 convert_element_type.253.w_own
  11.2 1.4 slice.299.w_own.wz_own
  12.6 3.1 collective-permute-start
  18.9 2.3 vectors.1
  21.8 25.7 %front.1 = (bf16[528,512]{1,0:T(8,128)(2,1)}, bf16[528,512]{1,0:T(8,128)(2,1)}, bf16[528,2304]{1,0:T(8,128)(2,1)}, bf16[512,2304]{1,0:T(8,128)(2,1)}, bf16[512,2...) custom-call(s32[4]{0:T(128)} %pad_add_fusion.scal, ...), custom_call_target="tpu_custom_call" | custom-call | flops 2629828 | bytes 13099 | tf_op jit(solution)/shard_map/front/pallas_call | solution.py:263
  47.6 3.0 collective-permute-start.4
  50.5 6.9 %grad_gated.1.eg = bf16[2,512,1024]{2,1,0:T(8,128)(2,1)} custom-call(s32[4]{0:T(128)} %pad_add_fusion.scal, bf16[512,1024]{1,0:T(8,128)(2,1)} %bitcast.75, bf16[1024,1024]{1,0:T(8,128)(2,1)} %convert_element_type.253.w_own, bf16[1024,1024]{1,0:T(8,128)(2,1)} %collective-permute-done.3.w_oth), custom_call_target="tpu_custom_call" | custom-call | flops 2147483 | bytes 4194 | tf_op jit(solution)/shard_map/grad_gated/pallas_call | solution.py:864
  58.3 6.7 %collective-permute-done.4 = bf16[128,2048]{1,0:T(8,128)(2,1)S(1)} collective-permute-done((bf16[128,2048]{1,0:T(8,128)(2,1)}, bf16[128,2048]{1,0:T(8,128)(2,1)S(1)}, u32[]{:S(2)}, u32[]{:S(2)}) %collective-permute-start.4) | collective-permute-done | bytes 524320 | tf_op jit(solution)/shard_map/ppermute | solution.py:1201
  68.1 1.6 collective-permute-start.6
  69.7 6.8 %gate_proj.1.z = bf16[512,2048]{1,0:T(8,128)(2,1)} custom-call(s32[4]{0:T(128)} %pad_add_fusion.scal, bf16[528,512]{1,0:T(8,128)(2,1)} %get-tuple-element.156.a_own.rb1.rest_10_, bf16[528,512]{1,0:T(8,128)(2,1)} %get-tuple-element.114.a_oth, bf16[2048,512]{1,0:T(8,128)(2,1)} %slice.299.w_own.wz_own, bf16[2048,512]{1,0:T(8,128)(2,1)} %collective-permute-done.5.w_oth.wz_oth), custom_call_target="tpu_custom_call" | custom-call | flops 2147483 | bytes 4194 | tf_op jit(solution)/shard_map/gate_proj/pallas_call | solution.py:842
  76.5 14.3 %intra.1 = (f32[512,2048]{1,0:T(8,128)}, bf16[4,128,2048]{2,1,0:T(8,128)(2,1)}) custom-call(s32[4]{0:T(128)} %pad_add_fusion.scal, bf16[512,2304]{1,0:T(8,128)(2,1)} %get-tuple-element.126.x.bc.act, bf16[512,2304]{1,0:T(8,128)(2,1)} %get-tuple-element.126.x.bc.act, f32[512,128]{1,0:T(8,128)} %get-tuple-element.116.dt, f32[512,128]{1,0:T(8,128)} %get-tuple-element.110.cum, ...), custom_call_target="tpu_custom_call" | custom-call | flops 805306 | bytes 8388 | tf_op jit(solution)/shard_map/intra/pallas_call | solution.py:365
  92.0 17.3 %gate.1 = (bf16[512,1024]{1,0:T(8,128)(2,1)}, bf16[512,1024]{1,0:T(8,128)(2,1)}, bf16[512,2048]{1,0:T(8,128)(2,1)}, bf16[512,2048]{1,0:T(8,128)(2,1)}, f32[512,1...) custom-call(s32[4]{0:T(128)} %pad_add_fusion.scal, ...), custom_call_target="tpu_custom_call" | custom-call | flops 1610612 | bytes 20971 | tf_op jit(solution)/shard_map/gate/pallas_call | solution.py:489
  110.4 2.2 collective-permute-start.14
  112.6 2.6 collective-permute-done.9.ra2
  115.2 2.2 collective-permute-start.15
  118.3 12.7 %outer_ab.1 = (bf16[4,256,512]{2,1,0:T(8,128)(2,1)}, bf16[4,256,512]{2,1,0:T(8,128)(2,1)}, bf16[4,256,512]{2,1,0:T(8,128)(2,1)}, bf16[4,256,512]{2,1,0:T(8,128)(2,1)}) custom-call(s32[4]{0:T(128)} %pad_add_fusion.scal, bf16[512,1024]{1,0:T(8,128)(2,1)} %get-tuple-element.121.a1.a_own, bf16[512,1024]{1,0:T(8,128)(2,1)} %collective-permute-done.8.a2, ...), custom_call_target="tpu_custom_call" | custom-call | flops 4294967 | bytes 10000 | tf_op jit(solution)/shard_map/outer_ab/pallas_call | solution.py:1037
  131.0 2.5 fusion.11
  133.5 1.5 collective-permute-start.13
  135.8 1.5 collective-permute-start.12
  138.2 18.3 %back.1 = (bf16[512,2048]{1,0:T(8,128)(2,1)}, f32[512,128]{1,0:T(8,128)}, f32[512,128]{1,0:T(8,128)}, f32[512,128]{1,0:T(8,128)}, f32[8,128]{1,0:T(8,128)}) custom-call(s32[4]{0:T(128)} %pad_add_fusion.scal, bf16[512,2304]{1,0:T(8,128)(2,1)} %get-tuple-element.126.x.bc.act, bf16[512,2304]{1,0:T(8,128)(2,1)} %get-tuple-element.126.x.bc.act, ...), custom_call_target="tpu_custom_call" | custom-call | flops 2147483 | bytes 8388 | tf_op jit(solution)/shard_map/back/pallas_call | solution.py:630
  156.6 1.2 add_convert_fusion
  158.4 1.2 add_convert_fusion.1
  161.5 1.6 collective-permute-done.16
  163.2 2.1 add_convert_fusion.2.g_in
  165.2 25.3 %tail.1 = (bf16[528,512]{1,0:T(8,128)(2,1)}, bf16[528,512]{1,0:T(8,128)(2,1)}, bf16[528,512]{1,0:T(8,128)(2,1)}, bf16[528,512]{1,0:T(8,128)(2,1)}, bf16[528,512]...) custom-call(s32[4]{0:T(128)} %pad_add_fusion.scal, bf16[512,2304]{1,0:T(8,128)(2,1)} %get-tuple-element.126.x.bc.act, ...), custom_call_target="tpu_custom_call" | custom-call | flops 1073741 | bytes 12582 | tf_op jit(solution)/shard_map/tail/pallas_call | solution.py:779
  193.6 2.7 fusion
  196.4 1.5 collective-permute-start.26
  198.4 2.4 collective-permute-start.24
  202.4 10.4 %outer_c.1 = (bf16[4,144,512]{2,1,0:T(8,128)(2,1)}, bf16[4,144,512]{2,1,0:T(8,128)(2,1)}, bf16[4,144,512]{2,1,0:T(8,128)(2,1)}, bf16[4,144,512]{2,1,0:T(8,128)(2,1)}, f32[32,512]{1,0:T(8,128)}) custom-call(s32[4]{0:T(128)} %pad_add_fusion.scal, bf16[528,512]{1,0:T(8,128)(2,1)} %get-tuple-element.151.rest_0_, bf16[528,512]{1,0:T(8,128)(2,1)} %get-tuple-element.152.rest_1_, ...), custom_call_target="tpu_custom_call" | custom-call | flops 2491416 | bytes 10000 | tf_op jit(solution)/shard_map/outer_c/pallas_call | solution.py:1087
  212.8 14.5 %input_back.1 = (f32[512,1024]{1,0:T(8,128)}, f32[16,1024]{1,0:T(8,128)}, f32[8,1024]{1,0:T(8,128)}) custom-call(s32[4]{0:T(128)} %pad_add_fusion.scal, bf16[512,2048]{1,0:T(8,128)(2,1)} %get-tuple-element.123.b1.ez, bf16[2048,512]{1,0:T(8,128)(2,1)} %slice.299.w_own.wz_own, bf16[2048,512]{1,0:T(8,128)(2,1)} %collective-permute-done.5.w_oth.wz_oth, ...), custom_call_target="tpu_custom_call" | custom-call | flops 4982833 | bytes 13631 | tf_op jit(solution)/shard_map/input_back/pallas_call | solution.py:964
  228.8 3.3 copy.31
  233.1 1.2 add_convert_fusion.8
  234.3 3.0 collective-permute-start.34
  237.3 1.5 collective-permute-start.32
  238.8 6.7 %out_proj.1 = bf16[512,1024]{1,0:T(8,128)(2,1)} custom-call(s32[4]{0:T(128)} %pad_add_fusion.scal, bf16[512,1024]{1,0:T(8,128)(2,1)} %get-tuple-element.121.a1.a_own, bf16[512,1024]{1,0:T(8,128)(2,1)} %get-tuple-element.122.a_oth, bf16[1024,1024]{1,0:T(8,128)(2,1)} %convert_element_type.253.w_own, bf16[1024,1024]{1,0:T(8,128)(2,1)} %collective-permute-done.3.w_oth, ...), custom_call_target="tpu_custom_call" | custom-call | flops 2147483 | bytes 4194 | tf_op jit(solution)/shard_map/out_proj/pallas_call | solution.py:888
  245.6 1.2 collective-permute-start.30
  248.2 1.5 collective-permute-start.28
  249.8 9.4 %collective-permute-done.30 = bf16[4,144,512]{2,1,0:T(8,128)(2,1)S(1)} collective-permute-done((bf16[4,144,512]{2,1,0:T(8,128)(2,1)S(1)}, bf16[4,144,512]{2,1,0:T(8,128)(2,1)S(1)}, u32[]{:S(2)}, u32[]{:S(2)}) %collective-permute-start.30) | collective-permute-done | bytes 589856 | tf_op jit(solution)/shard_map/ppermute | solution.py:1205
  259.1 2.1 collective-permute-start.52
  261.2 3.2 collective-permute-done.28
  264.4 1.5 collective-permute-start.50
  266.8 1.2 pad_maximum_fusion.2.refs_0_
  269.0 1.2 collective-permute-start.37
  270.1 2.3 collective-permute-start.41
  272.4 2.1 collective-permute-start.39
  274.6 4.1 %collective-permute-done.41 = bf16[144,512]{1,0:T(8,128)(2,1)S(1)} collective-permute-done((bf16[144,512]{1,0:T(8,128)(2,1)S(1)}, bf16[144,512]{1,0:T(8,128)(2,1)S(1)}, u32[]{:S(2)}, u32[]{:S(2)}) %collective-permute-start.41) | collective-permute-done | bytes 147488 | tf_op jit(solution)/shard_map/ppermute | solution.py:1205
  278.6 2.3 collective-permute-start.31
  280.9 2.4 collective-permute-done.40
  283.4 3.6 %collective-permute-start.44 = (bf16[144,512]{1,0:T(8,128)(2,1)S(1)}, bf16[144,512]{1,0:T(8,128)(2,1)S(1)}, u32[]{:S(2)}, u32[]{:S(2)}) collective-permute-start(bf16[144,512]{1,0:T(8,128)(2,1)S(1)} %add_convert_fusion.13), channel_id=1, source_target_pairs={{0,3},{1,2},{2,1},{3,0},{4,7},{5,6},{6,5},{7,4},{8,11},{9,10},{10,... | collective-permute-start | bytes 442376 | tf_op jit(solution)/shard_map/ppermute | solution.py:1205
  287.9 1.5 bitcast_dynamic-update-slice_fusion
  289.3 2.6 collective-permute-done.44
  292.0 3.2 collective-permute-start.55
  295.1 5.4 %collective-permute-done.43 = bf16[144,512]{1,0:T(8,128)(2,1)S(1)} collective-permute-done((bf16[144,512]{1,0:T(8,128)(2,1)S(1)}, bf16[144,512]{1,0:T(8,128)(2,1)S(1)}, u32[]{:S(2)}, u32[]{:S(2)}) %collective-permute-start.43) | collective-permute-done | bytes 147488 | tf_op jit(solution)/shard_map/ppermute | solution.py:1205
  300.5 2.5 collective-permute-start.54
  303.1 1.3 collective-permute-start.45
  306.8 1.3 collective-permute-start.36
  311.4 7.9 %collective-permute-done.45.refs_4_ = bf16[4,144,512]{2,1,0:T(8,128)(2,1)S(1)} collective-permute-done((bf16[4,144,512]{2,1,0:T(8,128)(2,1)S(1)}, bf16[4,144,512]{2,1,0:T(8,128)(2,1)S(1)}, u32[]{:S(2)}, u32[]{:S(2)}) %collective-permute-start.45) | collective-permute-done | bytes 589856 | tf_op jit(solution)/shard_map/ppermute | solution.py:1205
  319.4 1.4 collective-permute-start.46
  321.5 1.7 slice.319
  325.3 6.4 %finish_near.1 = (f32[1024,1024]{1,0:T(8,128)}, f32[4384,512]{1,0:T(8,128)}) custom-call(s32[4]{0:T(128)} %pad_add_fusion.scal, bf16[4,256,512]{2,1,0:T(8,128)(2,1)} %copy-done.2, bf16[4,256,512]{2,1,0:T(8,128)(2,1)} %copy-done.5, bf16[4,256,512]{2,1,0:T(8,128)(2,1)} %copy-done.6, bf16[4,144,512]{2,1,0:T(8,128)(2,1)} %copy-done.4, ...), custom_call_target="tpu_custom_call" | custom-call | bytes 10000 | tf_op jit(solution)/shard_map/finish_near/pallas_call | solution.py:1101
  331.7 1.7 collective-permute-done.46.refs_2_
  334.4 3.7 %finish_far.1 = (f32[1024,1024]{1,0:T(8,128)}, f32[4384,512]{1,0:T(8,128)}) custom-call(s32[4]{0:T(128)} %pad_add_fusion.scal, bf16[2,256,512]{2,1,0:T(8,128)(2,1)} %copy-done.21, bf16[2,256,512]{2,1,0:T(8,128)(2,1)} %copy-done.22, bf16[2,144,512]{2,1,0:T(8,128)(2,1)} %collective-permute-done.46.refs_2_, ...), custom_call_target="tpu_custom_call", output_to_operand_aliasing={{0}: (5, {}), {1}: (6, {})} | custom-call | bytes 10000 | tf_op jit(solution)/shard_map/finish_far/pallas_call | solution.py:1101
  (217 shorter events, 37.4 us)
Async XLA Ops:
  5.9 15.3 %collective-permute-start.2 = (bf16[2560,512]{1,0:T(8,128)(2,1)S(1)}, bf16[2560,512]{1,0:T(8,128)(2,1)}, u32[]{:S(2)}, u32[]{:S(2)}) collective-permute-start(bf16[2560,512]{1,0:T(8,128)(2,1)S(1)} %pad.19.w_own.r_own.wu_own), channel_id=1, source_target_pairs={{0,4},{4,0},{1,5},{5,1},{2,6},{6,2},{3,7},{7,3},{8,12},{12,8},{9,1... | collective-permute-start | bytes 7864328 | tf_op jit(solution)/shard_map/ppermute | solution.py:1196
  10.6 39.9 %collective-permute-start.3 = (bf16[1024,1024]{1,0:T(8,128)(2,1)}, bf16[1024,1024]{1,0:T(8,128)(2,1)}, u32[]{:S(2)}, u32[]{:S(2)}) collective-permute-start(bf16[1024,1024]{1,0:T(8,128)(2,1)} %convert_element_type.253.w_own), channel_id=1, source_target_pairs={{0,4},{4,0},{1,5},{5,1},{2,6},{6,2},{3,7},{7,3},{8,12},{12,8},{9,1... | collective-permute-start | bytes 6291464 | tf_op jit(solution)/shard_map/ppermute | solution.py:1196
  12.6 57.1 %collective-permute-start.5 = (bf16[2048,512]{1,0:T(8,128)(2,1)}, bf16[2048,512]{1,0:T(8,128)(2,1)}, u32[]{:S(2)}, u32[]{:S(2)}) collective-permute-start(bf16[2048,512]{1,0:T(8,128)(2,1)} %slice.299.w_own.wz_own), channel_id=1, source_target_pairs={{0,4},{4,0},{1,5},{5,1},{2,6},{6,2},{3,7},{7,3},{8,12},{12,8},{9,1... | collective-permute-start | bytes 6291464 | tf_op jit(solution)/shard_map/ppermute | solution.py:1196
  12.6 8.6 %collective-permute-start = (bf16[16,1024]{1,0:T(8,128)(2,1)S(1)}, bf16[16,1024]{1,0:T(8,128)(2,1)S(1)}, u32[]{:S(2)}, u32[]{:S(2)}) collective-permute-start(bf16[16,1024]{1,0:T(8,128)(2,1)S(1)} %slice_bitcast_fusion), channel_id=1, source_target_pairs={{0,1},{1,2},{2,3},{3,0},{4,5},{5,6},{6,7},{7,4},{8,9},{9,10},{10,1... | collective-permute-start | bytes 98312 | tf_op jit(solution)/shard_map/ppermute | solution.py:1201
  15.9 2.4 collective-permute-start.1
  47.6 17.4 %collective-permute-start.4 = (bf16[128,2048]{1,0:T(8,128)(2,1)}, bf16[128,2048]{1,0:T(8,128)(2,1)S(1)}, u32[]{:S(2)}, u32[]{:S(2)}) collective-permute-start(bf16[128,2048]{1,0:T(8,128)(2,1)} %get-tuple-element.112), channel_id=1, source_target_pairs={{0,1},{1,2},{2,3},{3,0},{4,5},{5,6},{6,7},{7,4},{8,9},{9,10},{10,1... | collective-permute-start | bytes 1572872 | tf_op jit(solution)/shard_map/ppermute | solution.py:1201
  65.2 25.8 %collective-permute-start.7 = (bf16[128,2048]{1,0:T(8,128)(2,1)S(1)}, bf16[128,2048]{1,0:T(8,128)(2,1)S(1)}, u32[]{:S(2)}, u32[]{:S(2)}) collective-permute-start(bf16[128,2048]{1,0:T(8,128)(2,1)S(1)} %add_convert_fusion.5), channel_id=1, source_target_pairs={{0,2},{1,3},{2,0},{3,1},{4,6},{5,7},{6,4},{7,5},{8,10},{9,11},{10,... | collective-permute-start | bytes 1572872 | tf_op jit(solution)/shard_map/ppermute | solution.py:1201
  68.1 22.7 %collective-permute-start.6 = (f32[1,128]{1,0:T(1,128)S(1)}, f32[1,128]{1,0:T(1,128)S(1)}, u32[]{:S(2)}, u32[]{:S(2)}) collective-permute-start(f32[1,128]{1,0:T(1,128)S(1)} %slice.237), channel_id=1, source_target_pairs={{0,1},{1,2},{2,3},{3,0},{4,5},{5,6},{6,7},{7,4},{8,9},{9,10},{10,1... | collective-permute-start | bytes 1544 | tf_op jit(solution)/shard_map/ppermute | solution.py:1201
  92.0 17.4 %copy-start.1 = (bf16[1,512,1024]{2,1,0:T(8,128)(2,1)S(1)}, bf16[1,512,1024]{2,1,0:T(8,128)(2,1)}, u32[]{:S(2)}) copy-start(bf16[1,512,1024]{2,1,0:T(8,128)(2,1)} %param.27) | copy-start | bytes 3145732
  109.3 8.2 %collective-permute-start.10 = (bf16[512,2048]{1,0:T(8,128)(2,1)}, bf16[512,2048]{1,0:T(8,128)(2,1)}, u32[]{:S(2)}, u32[]{:S(2)}) collective-permute-start(bf16[512,2048]{1,0:T(8,128)(2,1)} %get-tuple-element.123.b1.ez), channel_id=1, source_target_pairs={{0,4},{4,0},{1,5},{5,1},{2,6},{6,2},{3,7},{7,3},{8,12},{12,8},{9,1... | collective-permute-start | bytes 6291464 | tf_op jit(solution)/shard_map/ppermute | solution.py:1196
  109.4 5.8 %collective-permute-start.9 = (bf16[512,1024]{1,0:T(8,128)(2,1)S(1)}, bf16[512,1024]{1,0:T(8,128)(2,1)S(1)}, u32[]{:S(2)}, u32[]{:S(2)}) collective-permute-start(bf16[512,1024]{1,0:T(8,128)(2,1)S(1)} %bitcast.78), channel_id=1, source_target_pairs={{0,4},{4,0},{1,5},{5,1},{2,6},{6,2},{3,7},{7,3},{8,12},{12,8},{9,1... | collective-permute-start | bytes 3145736 | tf_op jit(solution)/shard_map/ppermute | solution.py:1196
  109.9 7.6 %collective-permute-start.8 = (bf16[512,1024]{1,0:T(8,128)(2,1)}, bf16[512,1024]{1,0:T(8,128)(2,1)}, u32[]{:S(2)}, u32[]{:S(2)}) collective-permute-start(bf16[512,1024]{1,0:T(8,128)(2,1)} %get-tuple-element.122.a_oth), channel_id=1, source_target_pairs={{0,4},{4,0},{1,5},{5,1},{2,6},{6,2},{3,7},{7,3},{8,12},{12,8},{9,1... | collective-permute-start | bytes 3145736 | tf_op jit(solution)/shard_map/ppermute | solution.py:1196
  110.0 7.5 %collective-permute-start.11 = (bf16[528,512]{1,0:T(8,128)(2,1)}, bf16[528,512]{1,0:T(8,128)(2,1)S(1)}, u32[]{:S(2)}, u32[]{:S(2)}) collective-permute-start(bf16[528,512]{1,0:T(8,128)(2,1)} %get-tuple-element.114.a_oth), channel_id=1, source_target_pairs={{0,4},{4,0},{1,5},{5,1},{2,6},{6,2},{3,7},{7,3},{8,12},{12,8},{9,1... | collective-permute-start | bytes 1622024 | tf_op jit(solution)/shard_map/ppermute | solution.py:1196
  110.4 26.9 %collective-permute-start.14 = (bf16[128,2048]{1,0:T(8,128)(2,1)}, bf16[128,2048]{1,0:T(8,128)(2,1)S(1)}, u32[]{:S(2)}, u32[]{:S(2)}) collective-permute-start(bf16[128,2048]{1,0:T(8,128)(2,1)} %get-tuple-element.132), channel_id=1, source_target_pairs={{0,3},{1,0},{2,1},{3,2},{4,7},{5,4},{6,5},{7,6},{8,11},{9,8},{10,9... | collective-permute-start | bytes 1572872 | tf_op jit(solution)/shard_map/ppermute | solution.py:1201
  115.2 46.2 %collective-permute-start.15 = (f32[1,128]{1,0:T(1,128)S(1)}, f32[1,128]{1,0:T(1,128)S(1)}, u32[]{:S(2)}, u32[]{:S(2)}) collective-permute-start(f32[1,128]{1,0:T(1,128)S(1)} %slice.237), channel_id=1, source_target_pairs={{0,3},{1,0},{2,1},{3,2},{4,7},{5,4},{6,5},{7,6},{8,11},{9,8},{10,9... | collective-permute-start | bytes 1544 | tf_op jit(solution)/shard_map/ppermute | solution.py:1201
  133.5 23.1 %collective-permute-start.13 = (bf16[2,256,512]{2,1,0:T(8,128)(2,1)}, bf16[2,256,512]{2,1,0:T(8,128)(2,1)}, u32[]{:S(2)}, u32[]{:S(2)}) collective-permute-start(bf16[2,256,512]{2,1,0:T(8,128)(2,1)} %get-tuple-element.188), channel_id=1, source_target_pairs={{0,8},{8,0},{16,24},{24,16},{1,9},{9,1},{17,25},{25,17},{2,10},{10... | collective-permute-start | bytes 1572872 | tf_op jit(solution)/shard_map/ppermute | solution.py:1205
  135.8 22.7 %collective-permute-start.12 = (bf16[2,256,512]{2,1,0:T(8,128)(2,1)}, bf16[2,256,512]{2,1,0:T(8,128)(2,1)}, u32[]{:S(2)}, u32[]{:S(2)}) collective-permute-start(bf16[2,256,512]{2,1,0:T(8,128)(2,1)} %get-tuple-element.187), channel_id=1, source_target_pairs={{0,16},{8,24},{16,0},{24,8},{1,17},{9,25},{17,1},{25,9},{2,18},{10... | collective-permute-start | bytes 1572872 | tf_op jit(solution)/shard_map/ppermute | solution.py:1205
  137.5 25.7 %collective-permute-start.16 = (bf16[128,2048]{1,0:T(8,128)(2,1)S(1)}, bf16[128,2048]{1,0:T(8,128)(2,1)}, u32[]{:S(2)}, u32[]{:S(2)}) collective-permute-start(bf16[128,2048]{1,0:T(8,128)(2,1)S(1)} %add_convert_fusion.3), channel_id=1, source_target_pairs={{0,2},{1,3},{2,0},{3,1},{4,6},{5,7},{6,4},{7,5},{8,10},{9,11},{10,... | collective-permute-start | bytes 1572872 | tf_op jit(solution)/shard_map/ppermute | solution.py:1201
  138.2 18.3 %copy-start.11 = (bf16[4,256,512]{2,1,0:T(8,128)(2,1)S(1)}, bf16[4,256,512]{2,1,0:T(8,128)(2,1)}, u32[]{:S(2)}) copy-start(bf16[4,256,512]{2,1,0:T(8,128)(2,1)} %get-tuple-element.148) | copy-start | bytes 3145732
  157.9 33.9 %collective-permute-start.18 = (bf16[4,256,512]{2,1,0:T(8,128)(2,1)S(1)}, bf16[4,256,512]{2,1,0:T(8,128)(2,1)}, u32[]{:S(2)}, u32[]{:S(2)}) collective-permute-start(bf16[4,256,512]{2,1,0:T(8,128)(2,1)S(1)} %pad_maximum_fusion.1), channel_id=1, source_target_pairs={{0,16},{8,24},{16,0},{24,8},{1,17},{9,25},{17,1},{25,9},{2,18},{10... | collective-permute-start | bytes 3145736 | tf_op jit(solution)/shard_map/ppermute | solution.py:1205
  159.7 32.6 %collective-permute-start.17 = (bf16[4,256,512]{2,1,0:T(8,128)(2,1)S(1)}, bf16[4,256,512]{2,1,0:T(8,128)(2,1)}, u32[]{:S(2)}, u32[]{:S(2)}) collective-permute-start(bf16[4,256,512]{2,1,0:T(8,128)(2,1)S(1)} %pad_maximum_fusion), channel_id=1, source_target_pairs={{0,8},{8,0},{16,24},{24,16},{1,9},{9,1},{17,25},{25,17},{2,10},{10... | collective-permute-start | bytes 3145736 | tf_op jit(solution)/shard_map/ppermute | solution.py:1205
  165.2 28.4 %copy-start.14 = (bf16[4,256,512]{2,1,0:T(8,128)(2,1)S(1)}, bf16[4,256,512]{2,1,0:T(8,128)(2,1)}, u32[]{:S(2)}) copy-start(bf16[4,256,512]{2,1,0:T(8,128)(2,1)} %get-tuple-element.146) | copy-start | bytes 3145732
  191.2 5.1 %collective-permute-start.19 = (bf16[528,512]{1,0:T(8,128)(2,1)}, bf16[528,512]{1,0:T(8,128)(2,1)}, u32[]{:S(2)}, u32[]{:S(2)}) collective-permute-start(bf16[528,512]{1,0:T(8,128)(2,1)} %get-tuple-element.151.rest_0_), channel_id=1, source_target_pairs={{0,4},{4,0},{1,5},{5,1},{2,6},{6,2},{3,7},{7,3},{8,12},{12,8},{9,1... | collective-permute-start | bytes 1622024 | tf_op jit(solution)/shard_map/ppermute | solution.py:1196
  191.2 6.6 %collective-permute-start.20 = (bf16[528,512]{1,0:T(8,128)(2,1)}, bf16[528,512]{1,0:T(8,128)(2,1)}, u32[]{:S(2)}, u32[]{:S(2)}) collective-permute-start(bf16[528,512]{1,0:T(8,128)(2,1)} %get-tuple-element.152.rest_1_), channel_id=1, source_target_pairs={{0,4},{4,0},{1,5},{5,1},{2,6},{6,2},{3,7},{7,3},{8,12},{12,8},{9,1... | collective-permute-start | bytes 1622024 | tf_op jit(solution)/shard_map/ppermute | solution.py:1196
  191.7 6.7 %collective-permute-start.21 = (bf16[528,512]{1,0:T(8,128)(2,1)}, bf16[528,512]{1,0:T(8,128)(2,1)}, u32[]{:S(2)}, u32[]{:S(2)}) collective-permute-start(bf16[528,512]{1,0:T(8,128)(2,1)} %get-tuple-element.153.rest_2_), channel_id=1, source_target_pairs={{0,4},{4,0},{1,5},{5,1},{2,6},{6,2},{3,7},{7,3},{8,12},{12,8},{9,1... | collective-permute-start | bytes 1622024 | tf_op jit(solution)/shard_map/ppermute | solution.py:1196
  191.8 9.0 %collective-permute-start.22 = (bf16[528,512]{1,0:T(8,128)(2,1)}, bf16[528,512]{1,0:T(8,128)(2,1)S(1)}, u32[]{:S(2)}, u32[]{:S(2)}) collective-permute-start(bf16[528,512]{1,0:T(8,128)(2,1)} %get-tuple-element.154.rest_3_), channel_id=1, source_target_pairs={{0,4},{4,0},{1,5},{5,1},{2,6},{6,2},{3,7},{7,3},{8,12},{12,8},{9,1... | collective-permute-start | bytes 1622024 | tf_op jit(solution)/shard_map/ppermute | solution.py:1196
  192.3 8.4 %collective-permute-start.23 = (bf16[528,512]{1,0:T(8,128)(2,1)}, bf16[528,512]{1,0:T(8,128)(2,1)S(1)}, u32[]{:S(2)}, u32[]{:S(2)}) collective-permute-start(bf16[528,512]{1,0:T(8,128)(2,1)} %get-tuple-element.155.rest_4_), channel_id=1, source_target_pairs={{0,4},{4,0},{1,5},{5,1},{2,6},{6,2},{3,7},{7,3},{8,12},{12,8},{9,1... | collective-permute-start | bytes 1622024 | tf_op jit(solution)/shard_map/ppermute | solution.py:1196
  196.4 36.7 %collective-permute-start.26 = (bf16[256,512]{1,0:T(8,128)(2,1)}, bf16[256,512]{1,0:T(8,128)(2,1)}, u32[]{:S(2)}, u32[]{:S(2)}) collective-permute-start(bf16[256,512]{1,0:T(8,128)(2,1)} %get-tuple-element.180), channel_id=1, source_target_pairs={{0,3},{1,2},{2,1},{3,0},{4,7},{5,6},{6,5},{7,4},{8,11},{9,10},{10,... | collective-permute-start | bytes 786440 | tf_op jit(solution)/shard_map/ppermute | solution.py:1205
  197.9 35.2 %collective-permute-start.25 = (bf16[256,512]{1,0:T(8,128)(2,1)}, bf16[256,512]{1,0:T(8,128)(2,1)}, u32[]{:S(2)}, u32[]{:S(2)}) collective-permute-start(bf16[256,512]{1,0:T(8,128)(2,1)} %get-tuple-element.181), channel_id=1, source_target_pairs={{0,2},{1,3},{2,0},{3,1},{4,6},{5,7},{6,4},{7,5},{8,10},{9,11},{10,... | collective-permute-start | bytes 786440 | tf_op jit(solution)/shard_map/ppermute | solution.py:1205
  198.4 34.7 %collective-permute-start.24 = (bf16[256,512]{1,0:T(8,128)(2,1)}, bf16[256,512]{1,0:T(8,128)(2,1)}, u32[]{:S(2)}, u32[]{:S(2)}) collective-permute-start(bf16[256,512]{1,0:T(8,128)(2,1)} %get-tuple-element.182), channel_id=1, source_target_pairs={{0,1},{1,0},{2,3},{3,2},{4,5},{5,4},{6,7},{7,6},{8,9},{9,8},{10,11... | collective-permute-start | bytes 786440 | tf_op jit(solution)/shard_map/ppermute | solution.py:1205
  212.8 15.3 %copy-start.17 = (bf16[4,144,512]{2,1,0:T(8,128)(2,1)S(1)}, bf16[4,144,512]{2,1,0:T(8,128)(2,1)}, u32[]{:S(2)}) copy-start(bf16[4,144,512]{2,1,0:T(8,128)(2,1)} %get-tuple-element.168) | copy-start | bytes 1769476
  228.1 17.4 %collective-permute-start.29 = (bf16[2,144,512]{2,1,0:T(8,128)(2,1)S(1)}, bf16[2,144,512]{2,1,0:T(8,128)(2,1)S(1)}, u32[]{:S(2)}, u32[]{:S(2)}) collective-permute-start(bf16[2,144,512]{2,1,0:T(8,128)(2,1)S(1)} %get-tuple-element.190), channel_id=1, source_target_pairs={{0,8},{8,0},{16,24},{24,16},{1,9},{9,1},{17,25},{25,17},{2,10},{10... | collective-permute-start | bytes 884744 | tf_op jit(solution)/shard_map/ppermute | solution.py:1205
  232.1 14.8 %collective-permute-start.27 = (bf16[2,144,512]{2,1,0:T(8,128)(2,1)S(1)}, bf16[2,144,512]{2,1,0:T(8,128)(2,1)S(1)}, u32[]{:S(2)}, u32[]{:S(2)}) collective-permute-start(bf16[2,144,512]{2,1,0:T(8,128)(2,1)S(1)} %get-tuple-element.189), channel_id=1, source_target_pairs={{0,16},{8,24},{16,0},{24,8},{1,17},{9,25},{17,1},{25,9},{2,18},{10... | collective-permute-start | bytes 884744 | tf_op jit(solution)/shard_map/ppermute | solution.py:1205
  234.3 31.8 %collective-permute-start.34 = (bf16[256,512]{1,0:T(8,128)(2,1)S(1)}, bf16[256,512]{1,0:T(8,128)(2,1)}, u32[]{:S(2)}, u32[]{:S(2)}) collective-permute-start(bf16[256,512]{1,0:T(8,128)(2,1)S(1)} %add_convert_fusion.8), channel_id=1, source_target_pairs={{0,3},{1,2},{2,1},{3,0},{4,7},{5,6},{6,5},{7,4},{8,11},{9,10},{10,... | collective-permute-start | bytes 786440 | tf_op jit(solution)/shard_map/ppermute | solution.py:1205
  237.3 29.4 %collective-permute-start.33 = (bf16[256,512]{1,0:T(8,128)(2,1)S(1)}, bf16[256,512]{1,0:T(8,128)(2,1)}, u32[]{:S(2)}, u32[]{:S(2)}) collective-permute-start(bf16[256,512]{1,0:T(8,128)(2,1)S(1)} %add_convert_fusion.8), channel_id=1, source_target_pairs={{0,2},{1,3},{2,0},{3,1},{4,6},{5,7},{6,4},{7,5},{8,10},{9,11},{10,... | collective-permute-start | bytes 786440 | tf_op jit(solution)/shard_map/ppermute | solution.py:1205
  237.3 29.4 %collective-permute-start.32 = (bf16[256,512]{1,0:T(8,128)(2,1)S(1)}, bf16[256,512]{1,0:T(8,128)(2,1)}, u32[]{:S(2)}, u32[]{:S(2)}) collective-permute-start(bf16[256,512]{1,0:T(8,128)(2,1)S(1)} %add_convert_fusion.8), channel_id=1, source_target_pairs={{0,1},{1,0},{2,3},{3,2},{4,5},{5,4},{6,7},{7,6},{8,9},{9,8},{10,11... | collective-permute-start | bytes 786440 | tf_op jit(solution)/shard_map/ppermute | solution.py:1205
  245.6 20.4 %copy-start.18 = (bf16[4,144,512]{2,1,0:T(8,128)(2,1)S(1)}, bf16[4,144,512]{2,1,0:T(8,128)(2,1)}, u32[]{:S(2)}) copy-start(bf16[4,144,512]{2,1,0:T(8,128)(2,1)} %get-tuple-element.165) | copy-start | bytes 1769476
  245.6 13.5 %collective-permute-start.30 = (bf16[4,144,512]{2,1,0:T(8,128)(2,1)S(1)}, bf16[4,144,512]{2,1,0:T(8,128)(2,1)S(1)}, u32[]{:S(2)}, u32[]{:S(2)}) collective-permute-start(bf16[4,144,512]{2,1,0:T(8,128)(2,1)S(1)} %pad_maximum_fusion.4), channel_id=1, source_target_pairs={{0,16},{8,24},{16,0},{24,8},{1,17},{9,25},{17,1},{25,9},{2,18},{10... | collective-permute-start | bytes 1769480 | tf_op jit(solution)/shard_map/ppermute | solution.py:1205
  247.0 1.3 collective-permute-start.49
  248.2 16.2 %collective-permute-start.28 = (bf16[4,144,512]{2,1,0:T(8,128)(2,1)S(1)}, bf16[4,144,512]{2,1,0:T(8,128)(2,1)S(1)}, u32[]{:S(2)}, u32[]{:S(2)}) collective-permute-start(bf16[4,144,512]{2,1,0:T(8,128)(2,1)S(1)} %pad_maximum_fusion.3), channel_id=1, source_target_pairs={{0,8},{8,0},{16,24},{24,16},{1,9},{9,1},{17,25},{25,17},{2,10},{10... | collective-permute-start | bytes 1769480 | tf_op jit(solution)/shard_map/ppermute | solution.py:1205
  259.1 11.0 %collective-permute-start.52 = (f32[8,3200]{1,0:T(8,128)S(1)}, f32[8,3200]{1,0:T(8,128)S(1)}, u32[]{:S(2)}, u32[]{:S(2)}) collective-permute-start(f32[8,3200]{1,0:T(8,128)S(1)} %pad_maximum_fusion.6), channel_id=1, source_target_pairs={{0,24},{8,16},{16,8},{24,0},{1,25},{9,17},{17,9},{25,1},{2,26},{10... | collective-permute-start | bytes 307208 | tf_op jit(solution)/shard_map/ppermute | solution.py:1205
  264.4 8.0 %collective-permute-start.50 = (f32[8,3200]{1,0:T(8,128)S(1)}, f32[8,3200]{1,0:T(8,128)S(1)}, u32[]{:S(2)}, u32[]{:S(2)}) collective-permute-start(f32[8,3200]{1,0:T(8,128)S(1)} %pad_maximum_fusion.6), channel_id=1, source_target_pairs={{0,8},{8,0},{16,24},{24,16},{1,9},{9,1},{17,25},{25,17},{2,10},{10... | collective-permute-start | bytes 307208 | tf_op jit(solution)/shard_map/ppermute | solution.py:1205
  266.2 6.2 %collective-permute-start.51 = (f32[8,3200]{1,0:T(8,128)S(1)}, f32[8,3200]{1,0:T(8,128)S(1)}, u32[]{:S(2)}, u32[]{:S(2)}) collective-permute-start(f32[8,3200]{1,0:T(8,128)S(1)} %pad_maximum_fusion.6), channel_id=1, source_target_pairs={{0,16},{8,24},{16,0},{24,8},{1,17},{9,25},{17,1},{25,9},{2,18},{10... | collective-permute-start | bytes 307208 | tf_op jit(solution)/shard_map/ppermute | solution.py:1205
  268.0 38.8 %copy-start.2 = (bf16[4,256,512]{2,1,0:T(8,128)(2,1)}, bf16[4,256,512]{2,1,0:T(8,128)(2,1)S(1)}, u32[]{:S(2)}) copy-start(bf16[4,256,512]{2,1,0:T(8,128)(2,1)S(1)} %pad_maximum_fusion.2.refs_0_) | copy-start | bytes 3145732
  268.0 35.0 %collective-permute-start.35 = (bf16[4,256,512]{2,1,0:T(8,128)(2,1)S(1)}, bf16[4,256,512]{2,1,0:T(8,128)(2,1)S(1)}, u32[]{:S(2)}, u32[]{:S(2)}) collective-permute-start(bf16[4,256,512]{2,1,0:T(8,128)(2,1)S(1)} %pad_maximum_fusion.2.refs_0_), channel_id=1, source_target_pairs={{0,8},{8,0},{16,24},{24,16},{1,9},{9,1},{17,25},{25,17},{2,10},{10... | collective-permute-start | bytes 3145736 | tf_op jit(solution)/shard_map/ppermute | solution.py:1205
  269.0 36.2 %collective-permute-start.37 = (bf16[4,256,512]{2,1,0:T(8,128)(2,1)S(1)}, bf16[4,256,512]{2,1,0:T(8,128)(2,1)S(1)}, u32[]{:S(2)}, u32[]{:S(2)}) collective-permute-start(bf16[4,256,512]{2,1,0:T(8,128)(2,1)S(1)} %pad_maximum_fusion.2.refs_0_), channel_id=1, source_target_pairs={{0,16},{8,24},{16,0},{24,8},{1,17},{9,25},{17,1},{25,9},{2,18},{10... | collective-permute-start | bytes 3145736 | tf_op jit(solution)/shard_map/ppermute | solution.py:1205
  270.1 8.5 %collective-permute-start.41 = (bf16[144,512]{1,0:T(8,128)(2,1)S(1)}, bf16[144,512]{1,0:T(8,128)(2,1)S(1)}, u32[]{:S(2)}, u32[]{:S(2)}) collective-permute-start(bf16[144,512]{1,0:T(8,128)(2,1)S(1)} %get-tuple-element.183), channel_id=1, source_target_pairs={{0,3},{1,2},{2,1},{3,0},{4,7},{5,6},{6,5},{7,4},{8,11},{9,10},{10,... | collective-permute-start | bytes 442376 | tf_op jit(solution)/shard_map/ppermute | solution.py:1205
  272.4 10.9 %collective-permute-start.40 = (bf16[144,512]{1,0:T(8,128)(2,1)S(1)}, bf16[144,512]{1,0:T(8,128)(2,1)S(1)}, u32[]{:S(2)}, u32[]{:S(2)}) collective-permute-start(bf16[144,512]{1,0:T(8,128)(2,1)S(1)} %get-tuple-element.184), channel_id=1, source_target_pairs={{0,2},{1,3},{2,0},{3,1},{4,6},{5,7},{6,4},{7,5},{8,10},{9,11},{10,... | collective-permute-start | bytes 442376 | tf_op jit(solution)/shard_map/ppermute | solution.py:1205
  272.4 10.9 %collective-permute-start.39 = (bf16[144,512]{1,0:T(8,128)(2,1)S(1)}, bf16[144,512]{1,0:T(8,128)(2,1)S(1)}, u32[]{:S(2)}, u32[]{:S(2)}) collective-permute-start(bf16[144,512]{1,0:T(8,128)(2,1)S(1)} %get-tuple-element.185), channel_id=1, source_target_pairs={{0,1},{1,0},{2,3},{3,2},{4,5},{5,4},{6,7},{7,6},{8,9},{9,8},{10,11... | collective-permute-start | bytes 442376 | tf_op jit(solution)/shard_map/ppermute | solution.py:1205
  278.6 8.4 %collective-permute-start.31 = (bf16[16,1024]{1,0:T(8,128)(2,1)S(1)}, bf16[16,1024]{1,0:T(8,128)(2,1)S(1)}, u32[]{:S(2)}, u32[]{:S(2)}) collective-permute-start(bf16[16,1024]{1,0:T(8,128)(2,1)S(1)} %convert_element_type.293), channel_id=1, source_target_pairs={{0,3},{1,0},{2,1},{3,2},{4,7},{5,4},{6,5},{7,6},{8,11},{9,8},{10,9... | collective-permute-start | bytes 98312 | tf_op jit(solution)/shard_map/ppermute | solution.py:1201
  283.4 8.6 %collective-permute-start.44 = (bf16[144,512]{1,0:T(8,128)(2,1)S(1)}, bf16[144,512]{1,0:T(8,128)(2,1)S(1)}, u32[]{:S(2)}, u32[]{:S(2)}) collective-permute-start(bf16[144,512]{1,0:T(8,128)(2,1)S(1)} %add_convert_fusion.13), channel_id=1, source_target_pairs={{0,3},{1,2},{2,1},{3,0},{4,7},{5,6},{6,5},{7,4},{8,11},{9,10},{10,... | collective-permute-start | bytes 442376 | tf_op jit(solution)/shard_map/ppermute | solution.py:1205
  287.0 13.5 %collective-permute-start.43 = (bf16[144,512]{1,0:T(8,128)(2,1)S(1)}, bf16[144,512]{1,0:T(8,128)(2,1)S(1)}, u32[]{:S(2)}, u32[]{:S(2)}) collective-permute-start(bf16[144,512]{1,0:T(8,128)(2,1)S(1)} %add_convert_fusion.13), channel_id=1, source_target_pairs={{0,2},{1,3},{2,0},{3,1},{4,6},{5,7},{6,4},{7,5},{8,10},{9,11},{10,... | collective-permute-start | bytes 442376 | tf_op jit(solution)/shard_map/ppermute | solution.py:1205
  287.0 13.5 %collective-permute-start.42 = (bf16[144,512]{1,0:T(8,128)(2,1)S(1)}, bf16[144,512]{1,0:T(8,128)(2,1)S(1)}, u32[]{:S(2)}, u32[]{:S(2)}) collective-permute-start(bf16[144,512]{1,0:T(8,128)(2,1)S(1)} %add_convert_fusion.13), channel_id=1, source_target_pairs={{0,1},{1,0},{2,3},{3,2},{4,5},{5,4},{6,7},{7,6},{8,9},{9,8},{10,11... | collective-permute-start | bytes 442376 | tf_op jit(solution)/shard_map/ppermute | solution.py:1205
  292.0 14.8 %collective-permute-start.55 = (f32[8,3200]{1,0:T(8,128)S(1)}, f32[8,3200]{1,0:T(8,128)S(1)}, u32[]{:S(2)}, u32[]{:S(2)}) collective-permute-start(f32[8,3200]{1,0:T(8,128)S(1)} %add_add_fusion.1), channel_id=1, source_target_pairs={{0,3},{1,2},{2,1},{3,0},{4,7},{5,6},{6,5},{7,4},{8,11},{9,10},{10,... | collective-permute-start | bytes 307208 | tf_op jit(solution)/shard_map/ppermute | solution.py:1205
  300.5 7.6 %collective-permute-start.53 = (f32[8,3200]{1,0:T(8,128)S(1)}, f32[8,3200]{1,0:T(8,128)S(1)}, u32[]{:S(2)}, u32[]{:S(2)}) collective-permute-start(f32[8,3200]{1,0:T(8,128)S(1)} %add_add_fusion.1), channel_id=1, source_target_pairs={{0,1},{1,0},{2,3},{3,2},{4,5},{5,4},{6,7},{7,6},{8,9},{9,8},{10,11... | collective-permute-start | bytes 307208 | tf_op jit(solution)/shard_map/ppermute | solution.py:1205
  300.5 8.4 %collective-permute-start.54 = (f32[8,3200]{1,0:T(8,128)S(1)}, f32[8,3200]{1,0:T(8,128)S(1)}, u32[]{:S(2)}, u32[]{:S(2)}) collective-permute-start(f32[8,3200]{1,0:T(8,128)S(1)} %add_add_fusion.1), channel_id=1, source_target_pairs={{0,2},{1,3},{2,0},{3,1},{4,6},{5,7},{6,4},{7,5},{8,10},{9,11},{10,... | collective-permute-start | bytes 307208 | tf_op jit(solution)/shard_map/ppermute | solution.py:1205
  303.0 22.2 %copy-start.4 = (bf16[4,144,512]{2,1,0:T(8,128)(2,1)}, bf16[4,144,512]{2,1,0:T(8,128)(2,1)S(1)}, u32[]{:S(2)}) copy-start(bf16[4,144,512]{2,1,0:T(8,128)(2,1)S(1)} %pad_maximum_fusion.5.refs_3_) | copy-start | bytes 1769476
  303.1 22.2 %copy-start.5 = (bf16[4,256,512]{2,1,0:T(8,128)(2,1)}, bf16[4,256,512]{2,1,0:T(8,128)(2,1)S(1)}, u32[]{:S(2)}) copy-start(bf16[4,256,512]{2,1,0:T(8,128)(2,1)S(1)} %collective-permute-done.35.refs_1_) | copy-start | bytes 3145732
  303.1 16.3 %collective-permute-start.45 = (bf16[4,144,512]{2,1,0:T(8,128)(2,1)S(1)}, bf16[4,144,512]{2,1,0:T(8,128)(2,1)S(1)}, u32[]{:S(2)}, u32[]{:S(2)}) collective-permute-start(bf16[4,144,512]{2,1,0:T(8,128)(2,1)S(1)} %pad_maximum_fusion.5.refs_3_), channel_id=1, source_target_pairs={{0,8},{8,0},{16,24},{24,16},{1,9},{9,1},{17,25},{25,17},{2,10},{10... | collective-permute-start | bytes 1769480 | tf_op jit(solution)/shard_map/ppermute | solution.py:1205
  305.2 16.3 %collective-permute-start.47 = (bf16[4,144,512]{2,1,0:T(8,128)(2,1)S(1)}, bf16[4,144,512]{2,1,0:T(8,128)(2,1)}, u32[]{:S(2)}, u32[]{:S(2)}) collective-permute-start(bf16[4,144,512]{2,1,0:T(8,128)(2,1)S(1)} %pad_maximum_fusion.5.refs_3_), channel_id=1, source_target_pairs={{0,16},{8,24},{16,0},{24,8},{1,17},{9,25},{17,1},{25,9},{2,18},{10... | collective-permute-start | bytes 1769480 | tf_op jit(solution)/shard_map/ppermute | solution.py:1205
  306.8 26.7 %collective-permute-start.36 = (bf16[2,256,512]{2,1,0:T(8,128)(2,1)}, bf16[2,256,512]{2,1,0:T(8,128)(2,1)S(1)}, u32[]{:S(2)}, u32[]{:S(2)}) collective-permute-start(bf16[2,256,512]{2,1,0:T(8,128)(2,1)} %slice.316), channel_id=1, source_target_pairs={{0,16},{8,24},{16,0},{24,8},{1,17},{9,25},{17,1},{25,9},{2,18},{10... | collective-permute-start | bytes 1572872 | tf_op jit(solution)/shard_map/ppermute | solution.py:1205
  308.1 25.3 %collective-permute-start.38 = (bf16[2,256,512]{2,1,0:T(8,128)(2,1)}, bf16[2,256,512]{2,1,0:T(8,128)(2,1)S(1)}, u32[]{:S(2)}, u32[]{:S(2)}) collective-permute-start(bf16[2,256,512]{2,1,0:T(8,128)(2,1)} %slice.317), channel_id=1, source_target_pairs={{0,8},{8,0},{16,24},{24,16},{1,9},{9,1},{17,25},{25,17},{2,10},{10... | collective-permute-start | bytes 1572872 | tf_op jit(solution)/shard_map/ppermute | solution.py:1205
  319.4 14.1 %collective-permute-start.46 = (bf16[2,144,512]{2,1,0:T(8,128)(2,1)S(1)}, bf16[2,144,512]{2,1,0:T(8,128)(2,1)}, u32[]{:S(2)}, u32[]{:S(2)}) collective-permute-start(bf16[2,144,512]{2,1,0:T(8,128)(2,1)S(1)} %slice.318), channel_id=1, source_target_pairs={{0,16},{8,24},{16,0},{24,8},{1,17},{9,25},{17,1},{25,9},{2,18},{10... | collective-permute-start | bytes 884744 | tf_op jit(solution)/shard_map/ppermute | solution.py:1205
  323.2 10.2 %collective-permute-start.48 = (bf16[2,144,512]{2,1,0:T(8,128)(2,1)}, bf16[2,144,512]{2,1,0:T(8,128)(2,1)}, u32[]{:S(2)}, u32[]{:S(2)}) collective-permute-start(bf16[2,144,512]{2,1,0:T(8,128)(2,1)} %slice.319), channel_id=1, source_target_pairs={{0,8},{8,0},{16,24},{24,16},{1,9},{9,1},{17,25},{25,17},{2,10},{10... | collective-permute-start | bytes 884744 | tf_op jit(solution)/shard_map/ppermute | solution.py:1205
  (27 other events, 103.7 us)
